TPU v7x, 32 devices: a whole 2x2x4 slice. The times are simulated.
32 devices in a mesh: dp: 8 (over z, y), tensor: 4 (over x, core).
Axes of the slice: x: 2, y: 2, z: 4, core: 2. Of those that a mesh axis runs over, the one named last changes fastest.
Arguments:
- query_tokens: float32 [2048, 768], P('dp'), may hold values from -6 to 6
- passage_tokens: float32 [6144, 768], P('dp'), may hold values from -6 to 6
- query_mask: int32 [64, 32], P('dp'), may hold values from 0 to 1, as said below
- passage_lengths: int32 [24], replicated, may hold values from 64 to 256, as said below
- positives: int32 [64], replicated, may hold values from 0 to 23
- qkv_weight: float32 [2, 3, 768, 768], P(None, None, 'dp', 'tensor'), may hold values from -0.21875 to 0.21875
- qkv_moment: float32 [2, 3, 768, 768], P(None, None, 'dp', 'tensor'), may hold values from -0.18 to 0.18
- qkv_second: float32 [2, 3, 768, 768], P(None, None, 'dp', 'tensor'), may hold values from 5e-05 to 0.0005
- out_weight: float32 [2, 768, 768], P(None, 'tensor', 'dp'), may hold values from -0.875 to 0.875
- out_moment: float32 [2, 768, 768], P(None, 'tensor', 'dp'), may hold values from -0.09 to 0.09
- out_second: float32 [2, 768, 768], P(None, 'tensor', 'dp'), may hold values from 7e-06 to 7e-05
- up_weight: float32 [2, 768, 3072], P(None, 'dp', 'tensor'), may hold values from -0.21875 to 0.21875
- up_moment: float32 [2, 768, 3072], P(None, 'dp', 'tensor'), may hold values from -0.12 to 0.12
- up_second: float32 [2, 768, 3072], P(None, 'dp', 'tensor'), may hold values from 1.5e-05 to 0.00015
- down_weight: float32 [2, 3072, 768], P(None, 'tensor', 'dp'), may hold values from -0.15625 to 0.15625
- down_moment: float32 [2, 3072, 768], P(None, 'tensor', 'dp'), may hold values from -0.15 to 0.15
- down_second: float32 [2, 3072, 768], P(None, 'tensor', 'dp'), may hold values from 3e-05 to 0.0003
- projection: float32 [768, 128], P('dp'), may hold values from -0.21875 to 0.21875
- projection_moment: float32 [768, 128], P('dp'), may hold values from -0.6 to 0.6
- projection_second: float32 [768, 128], P('dp'), may hold values from 0.0004 to 0.004
- bias_pair: float32 [2, 2, 768], P(None, None, 'tensor'), may hold values from -3 to 3
- bias_pair_moment: float32 [2, 2, 768], P(None, None, 'tensor'), may hold values from -0.36 to 0.36
- bias_pair_second: float32 [2, 2, 768], P(None, None, 'tensor'), may hold values from 0.0002 to 0.002
- bias_up: float32 [2, 3072], P(None, 'tensor'), may hold values from -3 to 3
- bias_up_moment: float32 [2, 3072], P(None, 'tensor'), may hold values from -0.072 to 0.072
- bias_up_second: float32 [2, 3072], P(None, 'tensor'), may hold values from 5e-06 to 5e-05
- norm_terms: float32 [2, 6, 768], replicated, may hold values from -2 to 2, as said below
- norm_terms_moment: float32 [2, 6, 768], replicated, may hold values from -0.18 to 0.18
- norm_terms_second: float32 [2, 6, 768], replicated, may hold values from 5e-05 to 0.0005
Outputs:
- loss_mean: float32 [], replicated
- query_grad: float32 [2048, 768], P(('dp', 'tensor'))
- passage_grad: float32 [6144, 768], P(('dp', 'tensor'))
- qkv_grad: float32 [2, 3, 768, 768], P(None, None, 'dp', 'tensor')
- qkv_moment_new: float32 [2, 3, 768, 768], P(None, None, 'dp', 'tensor')
- qkv_second_new: float32 [2, 3, 768, 768], P(None, None, 'dp', 'tensor')
- qkv_update: float32 [2, 3, 768, 768], P(None, None, 'dp', 'tensor')
- out_grad: float32 [2, 768, 768], P(None, 'tensor', 'dp')
- out_moment_new: float32 [2, 768, 768], P(None, 'tensor', 'dp')
- out_second_new: float32 [2, 768, 768], P(None, 'tensor', 'dp')
- out_update: float32 [2, 768, 768], P(None, 'tensor', 'dp')
- up_grad: float32 [2, 768, 3072], P(None, 'dp', 'tensor')
- up_moment_new: float32 [2, 768, 3072], P(None, 'dp', 'tensor')
- up_second_new: float32 [2, 768, 3072], P(None, 'dp', 'tensor')
- up_update: float32 [2, 768, 3072], P(None, 'dp', 'tensor')
- down_grad: float32 [2, 3072, 768], P(None, 'tensor', 'dp')
- down_moment_new: float32 [2, 3072, 768], P(None, 'tensor', 'dp')
- down_second_new: float32 [2, 3072, 768], P(None, 'tensor', 'dp')
- down_update: float32 [2, 3072, 768], P(None, 'tensor', 'dp')
- projection_grad: float32 [768, 128], P('dp')
- projection_moment_new: float32 [768, 128], P('dp')
- projection_second_new: float32 [768, 128], P('dp')
- projection_update: float32 [768, 128], P('dp')
- bias_pair_grad: float32 [2, 2, 768], P(None, None, 'tensor')
- bias_pair_moment_new: float32 [2, 2, 768], P(None, None, 'tensor')
- bias_pair_second_new: float32 [2, 2, 768], P(None, None, 'tensor')
- bias_pair_update: float32 [2, 2, 768], P(None, None, 'tensor')
- bias_up_grad: float32 [2, 3072], P(None, 'tensor')
- bias_up_moment_new: float32 [2, 3072], P(None, 'tensor')
- bias_up_second_new: float32 [2, 3072], P(None, 'tensor')
- bias_up_update: float32 [2, 3072], P(None, 'tensor')
- norm_terms_grad: float32 [2, 6, 768], replicated
- norm_terms_moment_new: float32 [2, 6, 768], replicated
- norm_terms_second_new: float32 [2, 6, 768], replicated
- norm_terms_update: float32 [2, 6, 768], replicated
Inputs may be any that keep to these rules, and one draw needn't show every extreme that they name: `query_mask`: each row holds ones at its first 4 to 32 positions and zeros after them; some row is all ones. `passage_lengths`: some passage has all 256 tokens. `norm_terms`: rows 1 and 4 of each layer are gains between 0.4 and 1.6; the other rows lie between -2 and 2.
All inputs are finite; a program needn't handle non-finite values.
Results may differ from a plain program's by a relative error of at most 0.034.
Values may be sent and summed in bfloat16 or wider, within the bound.
No kernel may reach another device: no remote copies, remote signals or barrier semaphores. Data moves between devices by JAX's collectives and lax.ppermute only.
A program may use at most 192 MiB of HBM per device.

v0:
```python
import math

import jax
import jax.numpy as jnp
from jax import lax
from jax.sharding import PartitionSpec as P

HEAD = 64
DIM = 128
QLEN = 32
PLEN = 256
LAYERS = 2
STEP = 10
QDEV = 8
PDEV = 3


MASKED = -1e30
SHARPNESS = 24.0
SCORE_SCALE = 4.0
LN_EPS = 1e-12
NORM_EPS = 1e-12
BETA_ONE = 0.9
BETA_TWO = 0.999
ADAM_EPS = 1e-08
LEARN_RATE = 0.02
WEIGHT_DECAY = 0.01


def layer_norm_keep(values, gains, shifts):
    average = jnp.mean(values, -1, keepdims=True)
    centred = values - average
    factor = lax.rsqrt(jnp.mean(centred * centred, -1, keepdims=True) + LN_EPS)
    normal = centred * factor
    return (normal * gains + shifts, normal, factor)


def layer_norm_back(upstream, normal, factor, gains):
    scaled = upstream * gains
    average = jnp.mean(scaled, -1, keepdims=True)
    cross = jnp.mean(scaled * normal, -1, keepdims=True)
    return (
        factor * (scaled - average - normal * cross),
        jnp.sum(upstream * normal, 0),
        jnp.sum(upstream, 0),
    )


def gelu_slope(pre_act):
    return (
        0.5 * (1.0 + lax.erf(pre_act * 0.7071067811865476))
        + pre_act * jnp.exp(-0.5 * pre_act * pre_act) * 0.3989422804014327
    )


def slice_own(full):
    tensor_count = lax.axis_size("tensor")
    tensor_at = lax.axis_index("tensor")
    query_rows = QDEV * QLEN
    query_each = query_rows // tensor_count
    passage_each = PDEV * PLEN // tensor_count
    front = lax.dynamic_slice_in_dim(full, tensor_at * query_each, query_each, 0)
    behind = lax.dynamic_slice_in_dim(full, query_rows + tensor_at * passage_each, passage_each, 0)
    return jnp.concatenate([front, behind], 0)


def output_rows(local):
    return slice_own(local)


def branch_total(partial_value):
    return lax.psum(partial_value.astype(jnp.bfloat16), "tensor").astype(jnp.float32)


def input_total(partial_value):
    return lax.psum(partial_value.astype(jnp.bfloat16), "tensor").astype(jnp.float32)


def by_heads(packed, seq_count, length):
    return packed.reshape(packed.shape[0], seq_count, length, -1, HEAD)


def key_scores(queries, keys_all, key_valid):
    scores = (
        jnp.einsum("sqhd,skhd->shqk", queries, keys_all, preferred_element_type=jnp.float32) * 0.125
    )
    return jnp.where(key_valid[:, None, None, :], scores, MASKED)


def attend(queries, keys_all, values, key_valid):
    scores = key_scores(queries, keys_all, key_valid)
    highest = jnp.max(scores, -1, keepdims=True)
    powers = jnp.exp(scores - highest)
    summed = jnp.sum(powers, -1, keepdims=True)
    chances = (powers / summed).astype(jnp.bfloat16)
    mixture = jnp.einsum("shqk,skhd->sqhd", chances, values, preferred_element_type=jnp.float32)
    return (mixture, highest + jnp.log(summed))


def attend_back(queries, keys_all, values, key_valid, log_total, upstream):
    chances = jnp.exp(key_scores(queries, keys_all, key_valid) - log_total)
    grad_values = jnp.einsum(
        "shqk,sqhd->skhd",
        chances.astype(jnp.bfloat16),
        upstream,
        preferred_element_type=jnp.float32,
    )
    grad_chances = jnp.einsum(
        "sqhd,skhd->shqk", upstream, values, preferred_element_type=jnp.float32
    )
    grad_scores = (
        chances * (grad_chances - jnp.sum(chances * grad_chances, -1, keepdims=True))
    ).astype(jnp.bfloat16)
    grad_queries = (
        jnp.einsum("shqk,skhd->sqhd", grad_scores, keys_all, preferred_element_type=jnp.float32)
        * 0.125
    )
    grad_keys = (
        jnp.einsum("shqk,sqhd->skhd", grad_scores, queries, preferred_element_type=jnp.float32)
        * 0.125
    )
    return jnp.stack([grad_queries, grad_keys, grad_values])


def layer_forward(hidden, inputs, weights, vectors, masks):
    qkv_low, out_low, up_low, down_low = weights
    bias_pair, bias_up, norm_terms = vectors
    q_rows = QDEV * QLEN
    bias_rows = jnp.stack([bias_pair[0], jnp.zeros_like(bias_pair[0]), bias_pair[1]])
    packed = (
        jnp.einsum("rd,tdc->trc", inputs, qkv_low, preferred_element_type=jnp.float32)
        + bias_rows[:, None, :]
    ).astype(jnp.bfloat16)
    width_local = packed.shape[2]
    front = by_heads(packed[:, :q_rows], QDEV, QLEN)
    behind = by_heads(packed[:, q_rows:], PDEV, PLEN)
    mix_front, sums_front = attend(front[0], front[1], front[2], masks[0])
    mix_behind, sums_behind = attend(behind[0], behind[1], behind[2], masks[1])
    mixture = jnp.concatenate(
        [mix_front.reshape(q_rows, width_local), mix_behind.reshape(-1, width_local)]
    ).astype(jnp.bfloat16)
    attended = branch_total(jnp.dot(mixture, out_low, preferred_element_type=jnp.float32))
    first, normal_one, factor_one = layer_norm_keep(
        hidden + attended + norm_terms[0], norm_terms[1], norm_terms[2]
    )
    first_low = first.astype(jnp.bfloat16)
    pre_act = jnp.dot(first_low, up_low, preferred_element_type=jnp.float32) + bias_up
    activated = jax.nn.gelu(pre_act, approximate=False).astype(jnp.bfloat16)
    spread = branch_total(jnp.dot(activated, down_low, preferred_element_type=jnp.float32))
    second, normal_two, factor_two = layer_norm_keep(
        first + spread + norm_terms[3], norm_terms[4], norm_terms[5]
    )
    saved = (
        inputs,
        packed,
        sums_front,
        sums_behind,
        mixture,
        normal_one,
        factor_one,
        first_low,
        pre_act,
        activated,
        normal_two,
        factor_two,
    )
    return (second, saved)


def layer_backward(upstream, saved, weights, vectors, masks):
    (
        inputs,
        packed,
        sums_front,
        sums_behind,
        mixture,
        normal_one,
        factor_one,
        first_low,
        pre_act,
        activated,
        normal_two,
        factor_two,
    ) = saved
    qkv_low, out_low, up_low, down_low = weights
    bias_pair, bias_up, norm_terms = vectors
    q_rows = QDEV * QLEN
    grad_two, gain_two, shift_two = layer_norm_back(upstream, normal_two, factor_two, norm_terms[4])
    spread_low = grad_two.astype(jnp.bfloat16)
    grad_down = jnp.einsum("rf,rd->fd", activated, spread_low, preferred_element_type=jnp.float32)
    grad_act = jnp.einsum("rd,fd->rf", spread_low, down_low, preferred_element_type=jnp.float32)
    pre_low = (grad_act * gelu_slope(pre_act)).astype(jnp.bfloat16)
    grad_up = jnp.einsum("rd,rf->df", first_low, pre_low, preferred_element_type=jnp.float32)
    grad_bias_up = jnp.sum(pre_low, 0, dtype=jnp.float32)
    grad_first = grad_two + input_total(
        jnp.einsum("rf,df->rd", pre_low, up_low, preferred_element_type=jnp.float32)
    )
    grad_one, gain_one, shift_one = layer_norm_back(
        grad_first, normal_one, factor_one, norm_terms[1]
    )
    attended_low = grad_one.astype(jnp.bfloat16)
    grad_out = jnp.einsum("rc,rd->cd", mixture, attended_low, preferred_element_type=jnp.float32)
    grad_mix = jnp.einsum(
        "rd,cd->rc", attended_low, out_low, preferred_element_type=jnp.float32
    ).astype(jnp.bfloat16)
    width_local = packed.shape[2]
    front = by_heads(packed[:, :q_rows], QDEV, QLEN)
    behind = by_heads(packed[:, q_rows:], PDEV, PLEN)
    grad_front = attend_back(
        front[0],
        front[1],
        front[2],
        masks[0],
        sums_front,
        grad_mix[:q_rows].reshape(QDEV, QLEN, -1, HEAD),
    )
    grad_behind = attend_back(
        behind[0],
        behind[1],
        behind[2],
        masks[1],
        sums_behind,
        grad_mix[q_rows:].reshape(PDEV, PLEN, -1, HEAD),
    )
    grad_packed = jnp.concatenate(
        [grad_front.reshape(3, q_rows, width_local), grad_behind.reshape(3, -1, width_local)], 1
    ).astype(jnp.bfloat16)
    grad_qkv = jnp.einsum("rd,trc->tdc", inputs, grad_packed, preferred_element_type=jnp.float32)
    bias_sums = jnp.sum(grad_packed, 1, dtype=jnp.float32)
    grad_input = grad_one + input_total(
        jnp.einsum("trc,tdc->rd", grad_packed, qkv_low, preferred_element_type=jnp.float32)
    )
    grad_pair = jnp.stack([bias_sums[0], bias_sums[2]])
    grad_norms = jnp.stack(
        [jnp.sum(grad_one, 0), gain_one, shift_one, jnp.sum(grad_two, 0), gain_two, shift_two]
    )
    return (
        grad_input,
        (grad_qkv, grad_out, grad_up, grad_down),
        (grad_pair, grad_bias_up, grad_norms),
    )


def similarity(queries, passages, lengths):
    similar = jnp.einsum("qid,pjd->qipj", queries, passages, preferred_element_type=jnp.float32)
    valid = lax.broadcasted_iota(jnp.int32, (lengths.shape[0], PLEN), 1) < lengths[:, None]
    sharp = jnp.where(valid[None, None], SHARPNESS * similar, MASKED)
    highest = jnp.max(sharp, -1, keepdims=True)
    powers = jnp.exp(sharp - highest)
    summed = jnp.sum(powers, -1, keepdims=True)
    log_counts = jnp.log(lengths.astype(jnp.float32))
    smooth = (highest[..., 0] + jnp.log(summed[..., 0]) - log_counts[None, None, :]) / SHARPNESS
    return (SCORE_SCALE * jnp.sum(smooth, 1), powers / summed)


def pulled(queries, passages, lengths, steer):
    ignored, shares = similarity(queries, passages, lengths)
    return (steer[:, None, :, None] * shares).astype(jnp.bfloat16)


def block_split(amount, unit):
    size_each = math.gcd(amount, unit)
    return (amount // size_each, size_each)


def scores_by_passages(queries, passages, lengths, unit):
    blocks, size_each = block_split(passages.shape[0], unit)

    def single(pieces):
        return similarity(queries, pieces[0], pieces[1])[0]

    parts = lax.map(
        single, (passages.reshape(blocks, size_each, PLEN, DIM), lengths.reshape(blocks, size_each))
    )
    return jnp.transpose(parts, (1, 0, 2)).reshape(queries.shape[0], blocks * size_each)


def both_by_passages(queries, passages, lengths, steer, unit):
    blocks, size_each = block_split(passages.shape[0], unit)
    steer_blocks = jnp.transpose(steer.reshape(steer.shape[0], blocks, size_each), (1, 0, 2))

    def advance(running, pieces):
        shares = pulled(queries, pieces[0], pieces[1], pieces[2])
        running = running + jnp.einsum(
            "qipj,pjd->qid", shares, pieces[0], preferred_element_type=jnp.float32
        )
        return (
            running,
            jnp.einsum("qipj,qid->pjd", shares, queries, preferred_element_type=jnp.float32),
        )

    result, terms = lax.scan(
        advance,
        jnp.zeros(queries.shape, jnp.float32),
        (
            passages.reshape(blocks, size_each, PLEN, DIM),
            lengths.reshape(blocks, size_each),
            steer_blocks,
        ),
    )
    return (result, terms.reshape(blocks * size_each, PLEN, DIM))


def cross_entropy(logits, chosen):
    highest = jnp.max(logits, -1, keepdims=True)
    powers = jnp.exp(logits - highest)
    summed = jnp.sum(powers, -1, keepdims=True)
    losses = highest[:, 0] + jnp.log(summed[:, 0]) - jnp.sum(jnp.where(chosen, logits, 0.0), -1)
    return (powers / summed - chosen.astype(jnp.float32), losses)


def adam_step(master, moment, second, gradient, decay):
    moment_new = BETA_ONE * moment + (1.0 - BETA_ONE) * gradient
    second_new = BETA_TWO * second + (1.0 - BETA_TWO) * gradient * gradient
    rising = moment_new / (1.0 - BETA_ONE**STEP)
    spread = jnp.sqrt(second_new / (1.0 - BETA_TWO**STEP))
    return (moment_new, second_new, -LEARN_RATE * (rising / (spread + ADAM_EPS) + decay * master))


def body(
    query_tokens,
    passage_tokens,
    query_mask,
    passage_lengths,
    positives,
    qkv_weight,
    qkv_moment,
    qkv_second,
    out_weight,
    out_moment,
    out_second,
    up_weight,
    up_moment,
    up_second,
    down_weight,
    down_moment,
    down_second,
    projection,
    projection_moment,
    projection_second,
    bias_pair,
    bias_pair_moment,
    bias_pair_second,
    bias_up,
    bias_up_moment,
    bias_up_second,
    norm_terms,
    norm_terms_moment,
    norm_terms_second,
):
    qkv_all, out_all, up_all, down_all, proj_all = (
        lax.all_gather(qkv_weight.astype(jnp.bfloat16), "dp", axis=2, tiled=True),
        lax.all_gather(out_weight.astype(jnp.bfloat16), "dp", axis=2, tiled=True),
        lax.all_gather(up_weight.astype(jnp.bfloat16), "dp", axis=1, tiled=True),
        lax.all_gather(down_weight.astype(jnp.bfloat16), "dp", axis=2, tiled=True),
        lax.all_gather(projection.astype(jnp.bfloat16), "dp", axis=0, tiled=True),
    )
    devices = lax.axis_size("dp")
    dev_index = lax.axis_index("dp")
    own_lengths = lax.dynamic_slice_in_dim(passage_lengths, dev_index * PDEV, PDEV, 0)
    own_positives = lax.dynamic_slice_in_dim(positives, dev_index * QDEV, QDEV, 0)
    masks = (
        query_mask == 1,
        lax.broadcasted_iota(jnp.int32, (PDEV, PLEN), 1) < own_lengths[:, None],
    )
    q_rows = QDEV * QLEN
    full_input = jnp.concatenate([query_tokens, passage_tokens], 0)
    hidden = full_input
    inputs = full_input.astype(jnp.bfloat16)
    saved_list = []
    for layer_at in range(LAYERS):
        if layer_at > 0:
            inputs = hidden.astype(jnp.bfloat16)
        weights = (qkv_all[layer_at], out_all[layer_at], up_all[layer_at], down_all[layer_at])
        vectors = (bias_pair[layer_at], bias_up[layer_at], norm_terms[layer_at])
        hidden, saved = layer_forward(hidden, inputs, weights, vectors, masks)
        saved_list.append(saved)
    top_low = hidden.astype(jnp.bfloat16)
    embedded = jnp.dot(top_low, proj_all, preferred_element_type=jnp.float32)
    factor = lax.rsqrt(jnp.sum(embedded * embedded, -1, keepdims=True) + NORM_EPS)
    normed = embedded * factor
    normed_low = normed.astype(jnp.bfloat16)
    query_emb = normed_low[:q_rows].reshape(QDEV, QLEN, DIM)
    passage_emb = normed_low[q_rows:].reshape(PDEV, PLEN, DIM)
    all_passages = lax.all_gather(passage_emb, "dp", axis=0, tiled=True)
    logits = scores_by_passages(query_emb, all_passages, passage_lengths, 4 * PDEV)
    chosen = lax.broadcasted_iota(jnp.int32, logits.shape, 1) == own_positives[:, None]
    deltas, losses = cross_entropy(logits, chosen)
    loss_mean = lax.psum(jnp.sum(losses), "dp") / (QDEV * devices)
    steer = SCORE_SCALE * deltas
    grad_query, passage_terms = both_by_passages(
        query_emb, all_passages, passage_lengths, steer, 4 * PDEV
    )
    grad_passage = lax.psum_scatter(passage_terms, "dp", scatter_dimension=0, tiled=True)
    grad_normed = jnp.concatenate([grad_query.reshape(-1, DIM), grad_passage.reshape(-1, DIM)], 0)
    grad_embedded = (
        factor * (grad_normed - normed * jnp.sum(grad_normed * normed, -1, keepdims=True))
    ).astype(jnp.bfloat16)
    grad_proj_terms = jnp.einsum(
        "rd,rk->dk", top_low, grad_embedded, preferred_element_type=jnp.float32
    )
    upstream = jnp.einsum("rk,dk->rd", grad_embedded, proj_all, preferred_element_type=jnp.float32)
    mat_list = []
    vec_list = []
    for layer_at in range(LAYERS - 1, -1, -1):
        weights = (qkv_all[layer_at], out_all[layer_at], up_all[layer_at], down_all[layer_at])
        vectors = (bias_pair[layer_at], bias_up[layer_at], norm_terms[layer_at])
        upstream, layer_mats, layer_vecs = layer_backward(
            upstream, saved_list[layer_at], weights, vectors, masks
        )
        mat_list.insert(0, layer_mats)
        vec_list.insert(0, layer_vecs)
    qkv_grad, out_grad, up_grad, down_grad, projection_grad = (
        lax.psum_scatter(
            jnp.stack([layer_mats[0] for layer_mats in mat_list]),
            "dp",
            scatter_dimension=2,
            tiled=True,
        ),
        lax.psum_scatter(
            jnp.stack([layer_mats[1] for layer_mats in mat_list]),
            "dp",
            scatter_dimension=2,
            tiled=True,
        ),
        lax.psum_scatter(
            jnp.stack([layer_mats[2] for layer_mats in mat_list]),
            "dp",
            scatter_dimension=1,
            tiled=True,
        ),
        lax.psum_scatter(
            jnp.stack([layer_mats[3] for layer_mats in mat_list]),
            "dp",
            scatter_dimension=2,
            tiled=True,
        ),
        lax.psum_scatter(grad_proj_terms, "dp", scatter_dimension=0, tiled=True),
    )
    pair_stack = jnp.stack([layer_vecs[0] for layer_vecs in vec_list])
    bias_stack = jnp.stack([layer_vecs[1] for layer_vecs in vec_list])
    norm_stack = jnp.stack([layer_vecs[2] for layer_vecs in vec_list])
    pair_grad, bias_grad, norms_grad = lax.psum((pair_stack, bias_stack, norm_stack), "dp")
    qkv_m, qkv_v, qkv_u = adam_step(qkv_weight, qkv_moment, qkv_second, qkv_grad, WEIGHT_DECAY)
    out_m, out_v, out_u = adam_step(out_weight, out_moment, out_second, out_grad, WEIGHT_DECAY)
    up_m, up_v, up_u = adam_step(up_weight, up_moment, up_second, up_grad, WEIGHT_DECAY)
    down_m, down_v, down_u = adam_step(
        down_weight, down_moment, down_second, down_grad, WEIGHT_DECAY
    )
    proj_m, proj_v, proj_u = adam_step(
        projection, projection_moment, projection_second, projection_grad, WEIGHT_DECAY
    )
    pair_m, pair_v, pair_u = adam_step(
        bias_pair, bias_pair_moment, bias_pair_second, pair_grad, 0.0
    )
    bias_m, bias_v, bias_u = adam_step(bias_up, bias_up_moment, bias_up_second, bias_grad, 0.0)
    norm_m, norm_v, norm_u = adam_step(
        norm_terms, norm_terms_moment, norm_terms_second, norms_grad, 0.0
    )
    final_grad = output_rows(upstream)
    query_share = QDEV * QLEN // lax.axis_size("tensor")
    return (
        loss_mean,
        final_grad[:query_share],
        final_grad[query_share:],
        qkv_grad,
        qkv_m,
        qkv_v,
        qkv_u,
        out_grad,
        out_m,
        out_v,
        out_u,
        up_grad,
        up_m,
        up_v,
        up_u,
        down_grad,
        down_m,
        down_v,
        down_u,
        projection_grad,
        proj_m,
        proj_v,
        proj_u,
        pair_grad,
        pair_m,
        pair_v,
        pair_u,
        bias_grad,
        bias_m,
        bias_v,
        bias_u,
        norms_grad,
        norm_m,
        norm_v,
        norm_u,
    )


def solution(mesh):
    placed = (
        P("dp", None),
        P("dp", None),
        P("dp", None),
        P(),
        P(),
        P(None, None, "dp", "tensor"),
        P(None, None, "dp", "tensor"),
        P(None, None, "dp", "tensor"),
        P(None, "tensor", "dp"),
        P(None, "tensor", "dp"),
        P(None, "tensor", "dp"),
        P(None, "dp", "tensor"),
        P(None, "dp", "tensor"),
        P(None, "dp", "tensor"),
        P(None, "tensor", "dp"),
        P(None, "tensor", "dp"),
        P(None, "tensor", "dp"),
        P("dp", None),
        P("dp", None),
        P("dp", None),
        P(None, None, "tensor"),
        P(None, None, "tensor"),
        P(None, None, "tensor"),
        P(None, "tensor"),
        P(None, "tensor"),
        P(None, "tensor"),
        P(),
        P(),
        P(),
    )
    return jax.shard_map(
        body,
        mesh=mesh,
        in_specs=placed,
        out_specs=(
            P(),
            P(("dp", "tensor"), None),
            P(("dp", "tensor"), None),
            P(None, None, "dp", "tensor"),
            P(None, None, "dp", "tensor"),
            P(None, None, "dp", "tensor"),
            P(None, None, "dp", "tensor"),
            P(None, "tensor", "dp"),
            P(None, "tensor", "dp"),
            P(None, "tensor", "dp"),
            P(None, "tensor", "dp"),
            P(None, "dp", "tensor"),
            P(None, "dp", "tensor"),
            P(None, "dp", "tensor"),
            P(None, "dp", "tensor"),
            P(None, "tensor", "dp"),
            P(None, "tensor", "dp"),
            P(None, "tensor", "dp"),
            P(None, "tensor", "dp"),
            P("dp", None),
            P("dp", None),
            P("dp", None),
            P("dp", None),
            P(None, None, "tensor"),
            P(None, None, "tensor"),
            P(None, None, "tensor"),
            P(None, None, "tensor"),
            P(None, "tensor"),
            P(None, "tensor"),
            P(None, "tensor"),
            P(None, "tensor"),
            P(),
            P(),
            P(),
            P(),
        ),
        check_vma=False,
    )
```

profile of v0, /device:TPU:0, one launch (start us, length us, event | category | flops | bytes accessed | tf_op | source)
XLA Modules:
  0.0 1296.8 jit_solution(4007897964645691240)
XLA Ops:
  10.7 34.6 %all_gather.19 = bf16[2,192,768]{1,0,2:T(2,128)(2,1)S(1)} all-gather(bf16[2,192,96]{1,0,2:T(2,128)(2,1)S(1)} %copy.453), channel_id=1, replica_groups=mesh['dp'=8,'tensor'=4] {'dp'}, dimensions={2}, use_global_device_ids=true | all-gather | bytes 663552 | tf_op jit(solution)/shard_map/all_gather | solution.py:353
  51.2 18.0 %all-gather.5.cloned.1.call-done = bf16[2,3,768,192]{3,0,1,2:T(2,128)(2,1)} async-done(((bf16[2,3,96,192]{3,0,1,2:T(2,128)(2,1)}), bf16[2,3,768,192]{3,0,1,2:T(2,128)(2,1)}) %all-gather.5.cloned.1.call-update) | async-done | bytes 1769488 | tf_op jit(solution)/shard_map/all_gather | solution.py:352
  69.2 8.8 fusion.203
  78.0 6.3 copy.590
  99.4 38.2 %all-reduce.12.cloned.1.call-done = bf16[1024,768]{1,0:T(8,128)(2,1)} async-done(((bf16[1024,768]{1,0:T(8,128)(2,1)}), bf16[1024,768]{1,0:T(8,128)(2,1)}) %all-reduce.12.cloned.1.call-update) | async-done | bytes 1572880 | tf_op jit(solution)/shard_map/psum | solution.py:72
  137.6 2.8 fusion.201
  141.0 51.6 %all-gather.7.cloned.1.call-done = bf16[2,768,768]{2,1,0:T(8,128)(2,1)} async-done(((bf16[2,96,768]{2,1,0:T(8,128)(2,1)}), bf16[2,768,768]{2,1,0:T(8,128)(2,1)}) %all-gather.7.cloned.1.call-update) | async-done | bytes 2359312 | tf_op jit(solution)/shard_map/all_gather | solution.py:354
  192.6 10.8 fusion.31
  203.4 42.5 %all-gather.9.cloned.1.call-done = bf16[2,768,768]{1,2,0:T(8,128)(2,1)} async-done(((bf16[2,768,96]{1,2,0:T(8,128)(2,1)}), bf16[2,768,768]{1,2,0:T(8,128)(2,1)}) %all-gather.9.cloned.1.call-update) | async-done | bytes 2359312 | tf_op jit(solution)/shard_map/all_gather | solution.py:355
  245.8 4.3 convolution_convert_fusion.4
  250.6 2.8 copy.593
  253.5 6.4 copy.592
  259.9 31.8 %all-reduce.14.cloned.1.call-done = bf16[1024,768]{1,0:T(8,128)(2,1)} async-done(((bf16[1024,768]{1,0:T(8,128)(2,1)}), bf16[1024,768]{1,0:T(8,128)(2,1)}) %all-reduce.14.cloned.1.call-update) | async-done | bytes 1572880 | tf_op jit(solution)/shard_map/psum | solution.py:72
  291.8 2.5 fusion.200
  307.8 42.8 %all-reduce.16.cloned.1.call-done = bf16[1024,768]{1,0:T(8,128)(2,1)} async-done(((bf16[1024,768]{1,0:T(8,128)(2,1)}), bf16[1024,768]{1,0:T(8,128)(2,1)}) %all-reduce.16.cloned.1.call-update) | async-done | bytes 1572880 | tf_op jit(solution)/shard_map/psum | solution.py:72
  350.7 2.5 fusion.199
  356.0 9.4 fusion.34
  366.6 2.6 convolution_convert_fusion.2
  370.1 32.7 %all_gather.22 = bf16[768,128]{1,0:T(8,128)(2,1)} all-gather(bf16[96,128]{1,0:T(8,128)(2,1)S(1)} %convert_element_type.220), channel_id=1, replica_groups=mesh['dp'=8,'tensor'=4] {'dp'}, dimensions={0}, use_global_device_ids=true | all-gather | bytes 221184 | tf_op jit(solution)/shard_map/all_gather | solution.py:356
  402.8 9.5 all-reduce.18.cloned.1.call-done
  412.3 2.5 fusion.198
  419.9 43.9 %all-gather.11.cloned.1.call-done = bf16[24,256,128]{2,1,0:T(8,128)(2,1)} async-done(((bf16[3,256,128]{2,1,0:T(8,128)(2,1)}), bf16[24,256,128]{2,1,0:T(8,128)(2,1)}) %all-gather.11.cloned.1.call-update) | async-done | bytes 1572880 | tf_op jit(solution)/shard_map/all_gather | solution.py:385
  463.9 6.6 while.23
  471.8 23.7 %while.24 = (s32[]{:T(128)}, f32[8,32,128]{2,1,0:T(8,128)}, f32[2,12,256,128]{3,2,1,0:T(8,128)}, f32[2,8,12]{2,1,0:T(8,128)S(1)}, s32[2,12]{1,0:T(2,128)S(1)}, /...) while((s32[]{:T(128)}, f32[8,32,128]{2,1,0:T(8,128)}, ...), condition=%wide.region_34.35_spmd.clone, body=%wide.region_31.34_spmd.clone.sunk | while | flops 611126528 | bytes 27690012 | solution.py:292
  473.6 3.1 fusion.282
  476.8 2.4 multiply_convert_fusion.8
  480.5 2.7 bitcast_dynamic-update-slice_fusion.5
  485.0 3.1 fusion.282
  488.2 2.4 multiply_convert_fusion.8
  492.7 2.7 bitcast_dynamic-update-slice_fusion.5
  495.6 73.1 %reduce-scatter.10.cloned.1.call-done = f32[3,256,128]{2,1,0:T(8,128)} async-done(((f32[24,256,128]{2,1,0:T(8,128)}), f32[3,256,128]{2,1,0:T(8,128)}) %reduce-scatter.10.cloned.1.call-update) | async-done | bytes 393232 | tf_op jit(solution)/shard_map/reduce_scatter | solution.py:394
  571.8 3.0 multiply_reduce_fusion.1
  578.5 3.1 convert_reduce_fusion
  582.8 2.6 convolution_convert_fusion.1
  588.0 39.6 %all-reduce.20.cloned.1.call-done = bf16[1024,768]{1,0:T(8,128)(2,1)} async-done(((bf16[1024,768]{1,0:T(8,128)(2,1)}), bf16[1024,768]{1,0:T(8,128)(2,1)}) %all-reduce.20.cloned.1.call-update) | async-done | bytes 1572880 | tf_op jit(solution)/shard_map/psum | solution.py:76
  627.6 4.2 multiply_reduce_fusion.2
  651.1 4.2 bitcast_convert_fusion.1
  655.3 43.0 %all-reduce.22.cloned.1.call-done = bf16[1024,768]{1,0:T(8,128)(2,1)} async-done(((bf16[1024,768]{1,0:T(8,128)(2,1)}), bf16[1024,768]{1,0:T(8,128)(2,1)}) %all-reduce.22.cloned.1.call-update) | async-done | bytes 1572880 | tf_op jit(solution)/shard_map/psum | solution.py:76
  698.4 4.2 multiply_reduce_fusion.3
  706.0 3.1 convert_reduce_fusion.1
  710.4 2.6 convolution_convert_fusion
  713.7 3.0 fusion.215
  716.9 39.1 %all-reduce.24.cloned.1.call-done = bf16[1024,768]{1,0:T(8,128)(2,1)} async-done(((bf16[1024,768]{1,0:T(8,128)(2,1)}), bf16[1024,768]{1,0:T(8,128)(2,1)}) %all-reduce.24.cloned.1.call-update) | async-done | bytes 1572880 | tf_op jit(solution)/shard_map/psum | solution.py:76
  756.1 4.2 multiply_reduce_fusion.4
  767.1 3.0 fusion.97
  782.1 2.6 multiply_reduce_fusion.21
  810.3 4.1 bitcast_convert_fusion
  814.8 2.5 convolution_bitcast_fusion.5
  819.3 3.5 copy.563
  822.7 3.3 reshape.505
  826.1 4.2 convolution_bitcast_fusion.1
  831.9 2.5 pad_maximum_fusion.1
  834.3 8.3 copy.522
  843.7 3.6 fusion.75
  850.4 6.9 copy.561
  857.3 8.0 reshape.503
  866.1 4.3 convolution_bitcast_fusion.3
  872.3 2.5 pad_maximum_fusion
  902.1 37.8 %all-reduce.1 = (f32[]{:T(128)}, f32[2,2,192]{2,1,0:T(2,128)S(1)}, f32[2,768]{1,0:T(2,128)S(1)}, f32[2,6,768]{2,1,0:T(8,128)S(1)}) all-reduce(f32[]{:T(128)} %subtract_reduce_fusion, f32[2,2,192]{2,1,0:T(2,128)S(1)} %pad_maximum_fusion.9, f32[2,768]{1,0:T(2,128)S(1)} %pad_maximum_fusion.6, ...), channel_id=1, replica_groups=mesh['dp'=8,'tensor'=4] {'dp'}, use_global_device_ids=true, to_apply=%region_30.31 | all-reduce | flops 11521 | bytes 92168 | tf_op jit(solution)/shard_map/psum | solution.py:389
  953.3 151.9 %all-reduce.28.cloned.1.call-done = f32[2,768,768]{1,0,2:T(2,128)} async-done(((f32[2,768,768]{1,0,2:T(2,128)}), f32[2,768,768]{1,0,2:T(2,128)}) %all-reduce.28.cloned.1.call-update) | async-done | bytes 4718608
  1107.9 79.0 %reduce-scatter.16.cloned.1.call-done = f32[96,1152]{1,0:T(8,128)} async-done(((f32[768,1152]{1,0:T(8,128)}), f32[96,1152]{1,0:T(8,128)}) %reduce-scatter.16.cloned.1.call-update) | async-done | bytes 442384
  1190.6 2.6 add_multiply_fusion.2
  1198.6 87.2 %reduce-scatter.12.cloned.1.call-done = f32[2,96,768]{2,1,0:T(8,128)} async-done(((f32[2,768,768]{2,1,0:T(8,128)}), f32[2,96,768]{2,1,0:T(8,128)}) %reduce-scatter.12.cloned.1.call-update) | async-done | bytes 589840 | tf_op jit(solution)/shard_map/reduce_scatter | solution.py:426
  1285.8 2.5 add_multiply_fusion.1
  (685 shorter events, 203.9 us)
Async XLA Ops:
  7.2 40.7 %copy-start.182 = (s32[24]{0:T(128)S(1)}, s32[24]{0:T(128)}, u32[]{:S(2)}) copy-start(s32[24]{0:T(128)} %param.36) | copy-start | bytes 292
  7.2 62.0 %all-gather.5.cloned.1.call-start = ((), (), s32[]{:S(2)}) async-start(), calls=%async_computation.5 | async-start | bytes 2654208 | tf_op jit(solution)/shard_map/all_gather | solution.py:352
  9.5 128.1 %all-reduce.12.cloned.1.call-start = ((), (), s32[]{:S(2)}) async-start(), calls=%async_computation.6 | async-start | bytes 3145728 | tf_op jit(solution)/shard_map/psum | solution.py:72
  47.8 46.5 %copy-start.36 = (bf16[1,192,768]{2,1,0:T(8,128)(2,1)}, bf16[1,192,768]{2,1,0:T(8,128)(2,1)S(1)}, u32[]{:S(2)}) copy-start(bf16[1,192,768]{2,1,0:T(8,128)(2,1)S(1)} %copy.591) | copy-start | bytes 884740
  51.1 40.2 %copy-start.168 = (pred[3,256]{1,0:T(4,128)(4,1)}, pred[3,256]{1,0:T(4,128)(4,1)S(1)}, u32[]{:S(2)}) copy-start(pred[3,256]{1,0:T(4,128)(4,1)S(1)} %iota_compare_fusion.2) | copy-start | bytes 2308
  96.1 96.4 %all-gather.7.cloned.1.call-start = ((), (), s32[]{:S(2)}) async-start(), calls=%async_computation.7 | async-start | bytes 2654208 | tf_op jit(solution)/shard_map/all_gather | solution.py:354
  97.0 148.9 %all-gather.9.cloned.1.call-start = ((), (), s32[]{:S(2)}) async-start(), calls=%async_computation.8 | async-start | bytes 2654208 | tf_op jit(solution)/shard_map/all_gather | solution.py:355
  97.8 193.9 %all-reduce.14.cloned.1.call-start = ((), (), s32[]{:S(2)}) async-start(), calls=%async_computation.9 | async-start | bytes 3145728 | tf_op jit(solution)/shard_map/psum | solution.py:72
  98.7 93.9 %copy-start.170 = (f32[768]{0:T(1024)}, f32[768]{0:T(1024)S(1)}, u32[]{:S(2)}) copy-start(f32[768]{0:T(1024)S(1)} %get-tuple-element.336) | copy-start | bytes 9220
  99.4 192.4 %copy-start.136 = (f32[768]{0:T(1024)}, f32[768]{0:T(1024)S(1)}, u32[]{:S(2)}) copy-start(f32[768]{0:T(1024)S(1)} %get-tuple-element.330) | copy-start | bytes 9220
  99.4 192.4 %copy-start.153 = (f32[768]{0:T(1024)}, f32[768]{0:T(1024)S(1)}, u32[]{:S(2)}) copy-start(f32[768]{0:T(1024)S(1)} %get-tuple-element.329) | copy-start | bytes 9220
  99.4 195.5 %copy-start.156 = (f32[768]{0:T(1024)}, f32[768]{0:T(1024)S(1)}, u32[]{:S(2)}) copy-start(f32[768]{0:T(1024)S(1)} %get-tuple-element.326) | copy-start | bytes 9220
  99.4 251.3 %copy-start.126 = (f32[768]{0:T(1024)}, f32[768]{0:T(1024)S(1)}, u32[]{:S(2)}) copy-start(f32[768]{0:T(1024)S(1)} %get-tuple-element.327) | copy-start | bytes 9220
  99.4 312.9 %copy-start.123 = (f32[768]{0:T(1024)}, f32[768]{0:T(1024)S(1)}, u32[]{:S(2)}) copy-start(f32[768]{0:T(1024)S(1)} %get-tuple-element.324) | copy-start | bytes 9220
  140.4 151.3 %copy-start.1 = (f32[1024,768]{1,0:T(8,128)}, f32[1024,768]{1,0:T(8,128)S(1)}, u32[]{:S(2)}) copy-start(f32[1024,768]{1,0:T(8,128)S(1)} %get-tuple-element.401) | copy-start | bytes 9437188
  140.5 151.3 %copy-start.114 = (f32[1024]{0:T(1024)}, f32[1024]{0:T(1024)S(1)}, u32[]{:S(2)}) copy-start(f32[1024]{0:T(1024)S(1)} %broadcast_multiply_fusion.11) | copy-start | bytes 12292
  141.0 150.8 %copy-start.129 = (f32[1024]{0:T(1024)}, f32[1024]{0:T(1024)S(1)}, u32[]{:S(2)}) copy-start(f32[1024]{0:T(1024)S(1)} %add_rsqrt_fusion.4) | copy-start | bytes 12292
  250.2 100.5 %all-reduce.16.cloned.1.call-start = ((), (), s32[]{:S(2)}) async-start(), calls=%async_computation.10 | async-start | bytes 3145728 | tf_op jit(solution)/shard_map/psum | solution.py:72
  294.3 56.3 %copy-start.108 = (f32[1024]{0:T(1024)}, f32[1024]{0:T(1024)S(1)}, u32[]{:S(2)}) copy-start(f32[1024]{0:T(1024)S(1)} %broadcast_multiply_fusion.10) | copy-start | bytes 12292
  294.8 55.8 %copy-start.117 = (f32[1024]{0:T(1024)}, f32[1024]{0:T(1024)S(1)}, u32[]{:S(2)}) copy-start(f32[1024]{0:T(1024)S(1)} %add_rsqrt_fusion.3) | copy-start | bytes 12292
  304.5 46.2 %copy-start.4 = (f32[1024,768]{1,0:T(8,128)S(1)}, f32[1024,768]{1,0:T(8,128)}, u32[]{:S(2)}) copy-start(f32[1024,768]{1,0:T(8,128)} %copy-done.3) | copy-start | bytes 9437188
  307.6 104.7 %all-reduce.18.cloned.1.call-start = ((), (), s32[]{:S(2)}) async-start(), calls=%async_computation.11 | async-start | bytes 3145728 | tf_op jit(solution)/shard_map/psum | solution.py:72
  353.2 59.0 %copy-start.111 = (f32[1024]{0:T(1024)}, f32[1024]{0:T(1024)S(1)}, u32[]{:S(2)}) copy-start(f32[1024]{0:T(1024)S(1)} %broadcast_multiply_fusion.9) | copy-start | bytes 12292
  353.8 58.5 %copy-start.120 = (f32[1024]{0:T(1024)}, f32[1024]{0:T(1024)S(1)}, u32[]{:S(2)}) copy-start(f32[1024]{0:T(1024)S(1)} %add_rsqrt_fusion.2) | copy-start | bytes 12292
  366.6 45.7 %copy-start.7 = (f32[1024,768]{1,0:T(8,128)S(1)}, f32[1024,768]{1,0:T(8,128)}, u32[]{:S(2)}) copy-start(f32[1024,768]{1,0:T(8,128)} %copy-done.6) | copy-start | bytes 9437188
  369.2 94.6 %all-gather.11.cloned.1.call-start = ((), (), s32[]{:S(2)}) async-start(), calls=%async_computation.12 | async-start | bytes 1769472 | tf_op jit(solution)/shard_map/all_gather | solution.py:385
  417.7 46.1 %copy-start.134 = (f32[1024]{0:T(1024)}, f32[1024]{0:T(1024)S(1)}, u32[]{:S(2)}) copy-start(f32[1024]{0:T(1024)S(1)} %add_rsqrt_fusion) | copy-start | bytes 12292
  419.5 149.2 %reduce-scatter.10.cloned.1.call-start = ((), (), s32[]{:S(2)}) async-start(), calls=%async_computation.13 | async-start | bytes 3538944 | tf_op jit(solution)/shard_map/reduce_scatter | solution.py:394
  495.4 73.2 %copy-start.135 = (f32[1024]{0:T(1024)S(1)}, f32[1024]{0:T(1024)}, u32[]{:S(2)}) copy-start(f32[1024]{0:T(1024)} %copy-done.134) | copy-start | bytes 12292
  495.4 76.3 %copy-start.16 = (f32[1024,768]{1,0:T(8,128)S(1)}, f32[1024,768]{1,0:T(8,128)}, u32[]{:S(2)}) copy-start(f32[1024,768]{1,0:T(8,128)} %copy-done.15) | copy-start | bytes 9437188
  495.5 76.3 %copy-start.133 = (f32[1024]{0:T(1024)S(1)}, f32[1024]{0:T(1024)}, u32[]{:S(2)}) copy-start(f32[1024]{0:T(1024)} %copy-done.132) | copy-start | bytes 12292
  495.5 76.3 %copy-start.146 = (f32[1024]{0:T(1024)S(1)}, f32[1024]{0:T(1024)}, u32[]{:S(2)}) copy-start(f32[1024]{0:T(1024)} %copy-done.145) | copy-start | bytes 12292
  495.5 76.3 %copy-start.148 = (f32[768]{0:T(1024)S(1)}, f32[768]{0:T(1024)}, u32[]{:S(2)}) copy-start(f32[768]{0:T(1024)} %get-tuple-element.321) | copy-start | bytes 9220
  495.5 132.0 %all-reduce.20.cloned.1.call-start = ((), (), s32[]{:S(2)}) async-start(), calls=%async_computation.14 | async-start | bytes 3145728 | tf_op jit(solution)/shard_map/psum | solution.py:76
  582.8 44.7 %copy-start.8 = (f32[1024,768]{1,0:T(8,128)S(1)}, f32[1024,768]{1,0:T(8,128)}, u32[]{:S(2)}) copy-start(f32[1024,768]{1,0:T(8,128)} %copy-done.6) | copy-start | bytes 9437188
  585.5 112.9 %all-reduce.22.cloned.1.call-start = ((), (), s32[]{:S(2)}) async-start(), calls=%async_computation.15 | async-start | bytes 3145728 | tf_op jit(solution)/shard_map/psum | solution.py:76
  651.1 47.3 %copy-start.5 = (f32[1024,768]{1,0:T(8,128)S(1)}, f32[1024,768]{1,0:T(8,128)}, u32[]{:S(2)}) copy-start(f32[1024,768]{1,0:T(8,128)} %copy-done.3) | copy-start | bytes 9437188
  651.1 47.3 %copy-start.109 = (f32[1024]{0:T(1024)S(1)}, f32[1024]{0:T(1024)}, u32[]{:S(2)}) copy-start(f32[1024]{0:T(1024)} %copy-done.108) | copy-start | bytes 12292
  651.1 47.3 %copy-start.118 = (f32[1024]{0:T(1024)S(1)}, f32[1024]{0:T(1024)}, u32[]{:S(2)}) copy-start(f32[1024]{0:T(1024)} %copy-done.117) | copy-start | bytes 12292
  651.1 47.3 %copy-start.127 = (f32[768]{0:T(1024)S(1)}, f32[768]{0:T(1024)}, u32[]{:S(2)}) copy-start(f32[768]{0:T(1024)} %copy-done.126) | copy-start | bytes 9220
  655.3 100.8 %all-reduce.24.cloned.1.call-start = ((), (), s32[]{:S(2)}) async-start(), calls=%async_computation.16 | async-start | bytes 3145728 | tf_op jit(solution)/shard_map/psum | solution.py:76
  712.9 43.1 %copy-start.2 = (f32[1024,768]{1,0:T(8,128)S(1)}, f32[1024,768]{1,0:T(8,128)}, u32[]{:S(2)}) copy-start(f32[1024,768]{1,0:T(8,128)} %copy-done.1) | copy-start | bytes 9437188
  713.0 43.1 %copy-start.115 = (f32[1024]{0:T(1024)S(1)}, f32[1024]{0:T(1024)}, u32[]{:S(2)}) copy-start(f32[1024]{0:T(1024)} %copy-done.114) | copy-start | bytes 12292
  713.0 43.1 %copy-start.130 = (f32[1024]{0:T(1024)S(1)}, f32[1024]{0:T(1024)}, u32[]{:S(2)}) copy-start(f32[1024]{0:T(1024)} %copy-done.129) | copy-start | bytes 12292
  713.0 43.1 %copy-start.137 = (f32[768]{0:T(1024)S(1)}, f32[768]{0:T(1024)}, u32[]{:S(2)}) copy-start(f32[768]{0:T(1024)} %copy-done.136) | copy-start | bytes 9220
  713.0 187.6 %reduce-scatter.14.cloned.1.call-start = ((), (), s32[]{:S(2)}) async-start(), calls=%async_computation.19 | async-start | bytes 442368 | tf_op jit(solution)/shard_map/reduce_scatter | solution.py:438
  716.7 230.0 %all-reduce.26.cloned.1.call-start = ((), (), s32[]{:S(2)}) async-start(), calls=%async_computation.17 | async-start | bytes 3145728 | tf_op jit(solution)/shard_map/psum | solution.py:76
  814.5 135.6 %reduce-scatter.18.cloned.1.call-start = ((), (), s32[]{:S(2)}) async-start(), calls=%async_computation.21 | async-start | bytes 1327104
  826.1 279.1 %all-reduce.28.cloned.1.call-start = ((), (), s32[]{:S(2)}) async-start(), calls=%async_computation.22 | async-start | bytes 9437184
  842.6 344.2 %reduce-scatter.16.cloned.1.call-start = ((), (), s32[]{:S(2)}) async-start(), calls=%async_computation.20 | async-start | bytes 3981312
  865.4 420.4 %reduce-scatter.12.cloned.1.call-start = ((), (), s32[]{:S(2)}) async-start(), calls=%async_computation.18 | async-start | bytes 5308416 | tf_op jit(solution)/shard_map/reduce_scatter | solution.py:426
  876.9 68.5 %copy-start.150 = (f32[2,768]{1,0:T(2,128)S(1)}, f32[2,768]{1,0:T(2,128)}, u32[]{:S(2)}) copy-start(f32[2,768]{1,0:T(2,128)} %param.56) | copy-start | bytes 18436
  876.9 69.9 %copy-start.19 = (f32[1024,768]{1,0:T(8,128)S(1)}, f32[1024,768]{1,0:T(8,128)}, u32[]{:S(2)}) copy-start(f32[1024,768]{1,0:T(8,128)} %copy-done.17) | copy-start | bytes 9437188
  890.1 54.0 %copy-start.160 = (f32[2,2,192]{2,1,0:T(2,128)S(1)}, f32[2,2,192]{2,1,0:T(2,128)}, u32[]{:S(2)}) copy-start(f32[2,2,192]{2,1,0:T(2,128)} %param.53) | copy-start | bytes 9220
  948.5 157.8 %copy-start.49 = (f32[2,768,96]{1,2,0:T(8,128)S(1)}, f32[2,768,96]{1,2,0:T(8,128)}, u32[]{:S(2)}) copy-start(f32[2,768,96]{1,2,0:T(8,128)} %param.47) | copy-start | bytes 1769476
  948.5 157.8 %copy-start.89 = (f32[2,768,96]{1,2,0:T(8,128)S(1)}, f32[2,768,96]{1,2,0:T(8,128)}, u32[]{:S(2)}) copy-start(f32[2,768,96]{1,2,0:T(8,128)} %param.49) | copy-start | bytes 1769476
  948.5 157.8 %copy-start.90 = (f32[2,768,96]{1,2,0:T(8,128)S(1)}, f32[2,768,96]{1,2,0:T(8,128)}, u32[]{:S(2)}) copy-start(f32[2,768,96]{1,2,0:T(8,128)} %param.48) | copy-start | bytes 1769476
  951.3 156.6 %copy-start.88 = (f32[2,192,96]{2,1,0:T(8,128)}, f32[2,192,96]{2,1,0:T(8,128)S(1)}, u32[]{:S(2)}) copy-start(f32[2,192,96]{2,1,0:T(8,128)S(1)} %copy.564) | copy-start | bytes 442372
  1107.9 82.7 %copy-start.53 = (f32[2,3,96,192]{2,3,1,0:T(8,128)S(1)}, f32[2,3,96,192]{2,3,1,0:T(8,128)}, u32[]{:S(2)}) copy-start(f32[2,3,96,192]{2,3,1,0:T(8,128)} %copy.521) | copy-start | bytes 1327108
  1107.9 82.7 %copy-start.54 = (f32[2,3,96,192]{2,3,1,0:T(8,128)S(1)}, f32[2,3,96,192]{2,3,1,0:T(8,128)}, u32[]{:S(2)}) copy-start(f32[2,3,96,192]{2,3,1,0:T(8,128)} %copy.520) | copy-start | bytes 1327108
  1107.9 82.7 %copy-start.55 = (f32[2,3,96,192]{2,3,1,0:T(8,128)S(1)}, f32[2,3,96,192]{2,3,1,0:T(8,128)}, u32[]{:S(2)}) copy-start(f32[2,3,96,192]{2,3,1,0:T(8,128)} %copy.519) | copy-start | bytes 1327108
  1190.6 95.2 %copy-start.52 = (f32[2,96,768]{2,1,0:T(8,128)S(1)}, f32[2,96,768]{2,1,0:T(8,128)}, u32[]{:S(2)}) copy-start(f32[2,96,768]{2,1,0:T(8,128)} %param.44) | copy-start | bytes 1769476
  1193.1 92.7 %copy-start.91 = (f32[2,96,768]{2,1,0:T(8,128)S(1)}, f32[2,96,768]{2,1,0:T(8,128)}, u32[]{:S(2)}) copy-start(f32[2,96,768]{2,1,0:T(8,128)} %param.46) | copy-start | bytes 1769476
  1193.1 92.7 %copy-start.92 = (f32[2,96,768]{2,1,0:T(8,128)S(1)}, f32[2,96,768]{2,1,0:T(8,128)}, u32[]{:S(2)}) copy-start(f32[2,96,768]{2,1,0:T(8,128)} %param.45) | copy-start | bytes 1769476
  (152 other events, 494.0 us)
Sparse Core Ops, SparseCore 0:
  10.8 58.3 all-gather.4
  96.2 41.3 all-reduce.11
  140.4 52.1 all-gather.6
  195.2 50.6 all-gather.8
  250.3 41.3 all-reduce.13
  307.7 42.8 all-reduce.15
  369.3 42.8 all-reduce.17
  419.6 44.2 all-gather.10
  495.6 72.9 reduce-scatter.9
  585.6 41.9 all-reduce.19
  655.4 42.8 all-reduce.21
  713.1 42.8 all-reduce.23
  759.9 61.4 reduce-scatter.13
  823.6 41.8 all-reduce.25
  868.8 64.3 reduce-scatter.17
  936.7 168.4 all-reduce.27
  1108.7 78.1 reduce-scatter.15
  1191.0 94.7 reduce-scatter.11
where the time goes:
time: 1310 us; the launch traced here: 1300 us
  waiting for transfers between devices  792 us (60%)
  local copies, waits for them, and re-layouts  171 us (13%)
  matrix products  121 us (9%)
  blocking collectives  105 us (8%)
  other arithmetic  86 us (7%)
  between operations  19.6 us (1%)
    unnamed x21, waiting for transfers between devices  231 us
    psum x4, waiting for transfers between devices, branch_total(): lax.psum(partial_value.astype(jnp.bfloat16), 'tensor').astype(jnp.float32)  122 us
    psum x4, waiting for transfers between devices, input_total(): lax.psum(partial_value.astype(jnp.bfloat16), 'tensor').astype(jnp.float32)  122 us
    unnamed x406, local copies, waits for them, and re-layouts  92.1 us
    reduce_scatter x1, waiting for transfers between devices, body(): lax.psum_scatter(jnp.stack([layer_mats[2] for layer_mats in mat_list]), '...  87.2 us
    reduce_scatter x1, waiting for transfers between devices, body(): lax.psum_scatter(passage_terms, 'dp', scatter_dimension=0, tiled=True)  73.1 us
    all_gather x1, waiting for transfers between devices, body(): lax.all_gather(up_weight.astype(jnp.bfloat16), 'dp', axis=1, tiled=True)  51.6 us
    all_gather x1, waiting for transfers between devices, body(): all_passages = lax.all_gather(passage_emb, 'dp', axis=0, tiled=True)  43.9 us
  transfers between devices with their start and end apart: 18, of which 15 were waited for; matrix products, arithmetic and copies ran while one was open for 16% of the time, Pallas kernels for 0%

commit v1 on v0

v1 whole, which is shorter than its diff:
```python
import functools

import jax
import jax.numpy as jnp
from jax import lax
from jax.experimental import pallas as pl
from jax.experimental.pallas import tpu as pltpu
from jax.sharding import PartitionSpec as P

WIDTH = 768
HEAD = 64
DIM = 128
QLEN = 32
PLEN = 256
LAYERS = 2
STEP = 10
QDEV = 8
PDEV = 3
ROWS = 256
PARTS = 4
HEADS_EACH = 3
OWN = HEADS_EACH * HEAD
SLAB = 768
HELD = 640
PACK = 3 * SLAB

MASKED = -1e30
SHARPNESS = 24.0
SCORE_SCALE = 4.0
LN_EPS = 1e-12
NORM_EPS = 1e-12
BETA_ONE = 0.9
BETA_TWO = 0.999
ADAM_EPS = 1e-08
LEARN_RATE = 0.02
WEIGHT_DECAY = 0.01
VMEM_BYTES = 60 * 1024 * 1024

BF = jnp.bfloat16
F32 = jnp.float32
BOTH = ("dp", "tensor")


def nn(left, right):
    return jnp.dot(left, right, preferred_element_type=F32)


def nt(left, right):
    return lax.dot_general(left, right, (((1,), (1,)), ((), ())), preferred_element_type=F32)


def norm_forward(values):
    average = jnp.mean(values, -1, keepdims=True)
    centred = values - average
    factor = lax.rsqrt(jnp.mean(centred * centred, -1, keepdims=True) + LN_EPS)
    return centred * factor, factor


def norm_backward(upstream, normal, factor, gains):
    scaled = upstream * gains
    average = jnp.mean(scaled, -1, keepdims=True)
    cross = jnp.mean(scaled * normal, -1, keepdims=True)
    return factor * (scaled - average - normal * cross)


def column_sum(values):
    return jnp.sum(values.astype(F32), 0, keepdims=True)


def part_order(place, split):
    if not split:
        return list(range(PARTS))
    x_at, c_at = place[0], place[1]
    return [
        (x_at ^ x_rel) * 2 + (c_at ^ c_rel) for c_rel in range(2) for x_rel in range(2)
    ]


def weight_copies(w_ref, held, sems, parts, base):
    return [
        pltpu.make_async_copy(
            w_ref.at[:, part, :, pl.ds(base, SLAB)], held.at[slot], sems.at[slot]
        )
        for slot, part in enumerate(parts)
    ]


def projection_copy(w_ref, proj, sem):
    return pltpu.make_async_copy(w_ref.at[:, 0, :, pl.ds(LAYERS * PACK, DIM)], proj, sem)


def stored(refs, slot, value):
    refs[slot // 2 if len(refs) > 1 else 0][slot % 2 if len(refs) > 1 else slot] = value


def attention_kernel(base, split, place, *refs):
    x_ref, mask_ref, pair_ref, norm_ref, w_ref = refs[:5]
    first_ref, low_t_ref, packed_ref, chances_ref, normal_ref, factor_ref, first_t_ref = refs[5:12]
    mixture_refs = refs[12:-2]
    held, sems = refs[-2:]
    parts = part_order(place, split)
    copies = weight_copies(w_ref, held, sems, parts, base)
    for copy in copies:
        copy.start()
    hidden = x_ref[...]
    low = hidden.astype(BF)
    low_t_ref[...] = low.T
    mask = mask_ref[...]
    attended = jnp.zeros((ROWS, WIDTH), F32)
    for slot in range(PARTS):
        copies[slot].wait()
        weight = held[slot, :, :, :HELD].reshape(WIDTH, HELD)
        packed = (nn(low, weight) + pair_ref[parts[slot]]).astype(BF)
        packed_ref[slot] = packed
        values_t = packed[:, 2 * OWN : 3 * OWN].T
        mixed = [jnp.zeros((HEAD, ROWS), F32)]
        for head in range(HEADS_EACH):
            queries = packed[:, head * HEAD : (head + 1) * HEAD]
            keys = packed[:, OWN + head * HEAD : OWN + (head + 1) * HEAD]
            scores = nt(keys, queries) * 0.125 + mask
            powers = jnp.exp(scores - jnp.max(scores, 0, keepdims=True))
            chances = (powers * (1.0 / jnp.sum(powers, 0, keepdims=True))).astype(BF)
            chances_ref[slot * HEADS_EACH + head] = chances
            mixed.append(nn(values_t[head * HEAD : (head + 1) * HEAD], chances))
        mixture = jnp.concatenate(mixed, 0).astype(BF).T
        stored(mixture_refs, slot, mixture)
        attended = attended + nt(
            mixture, held[slot, :, :, SLAB - ROWS :].reshape(WIDTH, ROWS)
        )
    normal, factor = norm_forward(hidden + attended + norm_ref[0:1])
    normal_ref[...] = normal
    factor_ref[...] = jnp.broadcast_to(factor, factor_ref.shape)
    first = normal * norm_ref[1:2] + norm_ref[2:3]
    first_ref[...] = first
    first_t_ref[...] = first.astype(BF).T


def mlp_kernel(base, top, split, place, *refs):
    first_ref, up_bias_ref, norm_ref, w_ref = refs[:4]
    out_ref, slope_ref, normal_ref, factor_ref = refs[4:8]
    act_refs = refs[8 : 10 if split else 9]
    refs = refs[8 + len(act_refs) :]
    if top:
        emb_ref, unit_ref, scale_ref, top_t_ref = refs[:4]
        refs = refs[4:]
    up_held, down_held, up_sems, down_sems = refs[:4]
    parts = part_order(place, split)
    ups = weight_copies(w_ref, up_held, up_sems, parts, base + SLAB)
    downs = weight_copies(w_ref, down_held, down_sems, parts, base + 2 * SLAB)
    for slot in range(PARTS):
        ups[slot].start()
        downs[slot].start()
    if top:
        proj, proj_sem = refs[4:]
        proj_load = projection_copy(w_ref, proj, proj_sem)
        proj_load.start()
    first = first_ref[...]
    first_low = first.astype(BF)
    spread = jnp.zeros((ROWS, WIDTH), F32)
    for slot in range(PARTS):
        ups[slot].wait()
        pre_act = nn(first_low, up_held[slot].reshape(WIDTH, SLAB)) + up_bias_ref[parts[slot]]
        chance = 0.5 * (1.0 + lax.erf(pre_act * 0.7071067811865476))
        act = (pre_act * chance).astype(BF)
        stored(act_refs, slot, act)
        slope_ref[slot] = (
            chance + pre_act * jnp.exp(-0.5 * pre_act * pre_act) * 0.3989422804014327
        ).astype(BF)
        downs[slot].wait()
        spread = spread + nt(act, down_held[slot].reshape(WIDTH, SLAB))
    normal, factor = norm_forward(first + spread + norm_ref[3:4])
    normal_ref[...] = normal
    factor_ref[...] = jnp.broadcast_to(factor, factor_ref.shape)
    second = normal * norm_ref[4:5] + norm_ref[5:6]
    out_ref[...] = second
    if top:
        second_low = second.astype(BF)
        top_t_ref[...] = second_low.T
        proj_load.wait()
        embedded = nn(second_low, proj[...].reshape(WIDTH, DIM))
        scale = lax.rsqrt(jnp.sum(embedded * embedded, -1, keepdims=True) + NORM_EPS)
        unit = embedded * scale
        unit_ref[...] = unit
        emb_ref[...] = unit.astype(BF)
        scale_ref[...] = jnp.broadcast_to(scale, scale_ref.shape)


def mlp_pull_kernel(base, top, split, place, *refs):
    if top:
        grad_emb_ref, unit_ref, scale_ref, top_t_ref = refs[:4]
        refs = refs[4:]
    else:
        dy_ref = refs[0]
        refs = refs[1:]
    slope_ref, normal_ref, factor_ref, norm_ref, w_ref = refs[:5]
    grad_ref, sum_ref, low_t_ref = refs[5:8]
    pre_refs = refs[8 : 10 if split else 9]
    refs = refs[8 + len(pre_refs) :]
    if top:
        proj_grad_ref = refs[0]
        refs = refs[1:]
    up_held, down_held, up_sems, down_sems = refs[:4]
    parts = part_order(place, split)
    ups = weight_copies(w_ref, up_held, up_sems, parts, base + SLAB)
    downs = weight_copies(w_ref, down_held, down_sems, parts, base + 2 * SLAB)
    if top:
        proj, proj_sem = refs[4:]
        proj_load = projection_copy(w_ref, proj, proj_sem)
        proj_load.start()
    order = (2, 3, 0, 1) if split else (0, 1, 2, 3)
    for slot in order:
        downs[slot].start()
        ups[slot].start()
    if top:
        grad_emb = grad_emb_ref[...]
        unit = unit_ref[...]
        low_emb = (
            scale_ref[:, :1] * (grad_emb - unit * jnp.sum(grad_emb * unit, -1, keepdims=True))
        ).astype(BF)
        proj_grad_ref[...] = nn(top_t_ref[...], low_emb)
        proj_load.wait()
        dy = nt(low_emb, proj[...].reshape(WIDTH, DIM))
    else:
        dy = dy_ref[...]
    normal = normal_ref[...]
    grad_two = norm_backward(dy, normal, factor_ref[:, :1], norm_ref[4:5])
    sum_ref[0:1] = column_sum(grad_two)
    sum_ref[1:2] = column_sum(dy * normal)
    sum_ref[2:3] = column_sum(dy)
    sum_ref[7:8] = jnp.zeros((1, WIDTH), F32)
    low = grad_two.astype(BF)
    low_t_ref[...] = low.T
    grad_first = grad_two
    for slot in order:
        downs[slot].wait()
        grad_act = nn(low, down_held[slot].reshape(WIDTH, SLAB))
        pre_low = (grad_act * slope_ref[slot].astype(F32)).astype(BF)
        sum_ref[pl.ds(3 + parts[slot], 1), :] = column_sum(pre_low)
        stored(pre_refs, slot, pre_low)
        ups[slot].wait()
        grad_first = grad_first + nt(pre_low, up_held[slot].reshape(WIDTH, SLAB))
    grad_ref[...] = grad_first


def attention_pull_kernel(base, split, place, *refs):
    grad_first_ref, packed_ref, chances_ref, normal_ref, factor_ref, norm_ref, w_ref = refs[:7]
    dx_ref, sum_ref, low_t_ref = refs[7:10]
    packed_grad_refs = refs[10:-2]
    held, sems = refs[-2:]
    parts = part_order(place, split)
    copies = weight_copies(w_ref, held, sems, parts, base)
    order = (2, 3, 0, 1) if split else (0, 1, 2, 3)
    for slot in order:
        copies[slot].start()
    normal = normal_ref[...]
    grad_first = grad_first_ref[...]
    grad_one = norm_backward(grad_first, normal, factor_ref[:, :1], norm_ref[1:2])
    sum_ref[0:1] = column_sum(grad_one)
    sum_ref[1:2] = column_sum(grad_first * normal)
    sum_ref[2:3] = column_sum(grad_first)
    sum_ref[7:8] = jnp.zeros((1, WIDTH), F32)
    low = grad_one.astype(BF)
    low_t_ref[...] = low.T
    grad_input = grad_one
    for slot in order:
        copies[slot].wait()
        grad_mix = nn(low, held[slot, :, :, SLAB - ROWS :].reshape(WIDTH, ROWS)).astype(BF)
        packed = packed_ref[slot]
        keys_t = packed[:, OWN : 2 * OWN].T
        grad_queries, grad_keys, grad_values = [], [], []
        for head in range(HEADS_EACH):
            queries = packed[:, head * HEAD : (head + 1) * HEAD]
            values = packed[:, 2 * OWN + head * HEAD : 2 * OWN + (head + 1) * HEAD]
            upstream = grad_mix[:, (head + 1) * HEAD : (head + 2) * HEAD]
            chances = chances_ref[slot * HEADS_EACH + head]
            grad_values.append(nn(chances, upstream).astype(BF))
            wide = chances.astype(F32)
            product = wide * nt(values, upstream)
            grad_scores = (product - wide * jnp.sum(product, 0, keepdims=True)).astype(BF)
            grad_keys.append((nn(grad_scores, queries) * 0.125).astype(BF))
            grad_queries.append(nn(keys_t[head * HEAD : (head + 1) * HEAD], grad_scores) * 0.125)
        grad_packed = jnp.concatenate(
            [jnp.concatenate(grad_queries, 0).astype(BF).T]
            + grad_keys
            + grad_values
            + [jnp.zeros((ROWS, SLAB - 3 * OWN), BF)],
            1,
        )
        sum_ref[pl.ds(3 + parts[slot], 1), :] = column_sum(grad_packed)
        stored(packed_grad_refs, slot, grad_packed)
        grad_input = grad_input + nt(grad_packed, held[slot].reshape(WIDTH, SLAB))
    dx_ref[...] = grad_input


def rows_of(refs):
    return jnp.concatenate([ref[...] for ref in refs], 1)


def rows_at(refs, slot):
    return jnp.concatenate([ref[slot] for ref in refs], 0)


def block_sends(stage, slot, targets, sems, place, y_first, base):
    width = stage.shape[-1]
    lanes = pl.ds(base, width)
    if len(targets) == 1:
        copies = [
            pltpu.make_async_copy(
                stage.at[0, 0], targets[0].at[slot, :, lanes], sems.at[0, 0]
            )
        ]
    else:
        copies = []
        for y_rel in range(2):
            first, second = (y_rel, slot) if y_first else (slot, y_rel)
            for z_rel in range(4):
                copies.append(
                    pltpu.make_async_copy(
                        stage.at[(place[3] + z_rel) & 3, place[2] ^ y_rel],
                        targets[first].at[second, z_rel, :, lanes],
                        sems.at[y_rel, z_rel],
                    )
                )
    for copy in copies:
        copy.start()
    return copies


def mlp_grad_kernel(top, split, place, *refs):
    sides = 2 if split else 1
    groups = []
    for _ in range(4):
        groups.append(refs[:sides])
        refs = refs[sides:]
    first_t_refs, pre_refs, low_t_refs, act_refs = groups
    if top:
        proj_refs, refs = refs[:sides], refs[sides:]
    up_targets, refs = refs[:sides], refs[sides:]
    down_targets, refs = refs[:sides], refs[sides:]
    stage, sems = refs[:2]
    fold = stage.shape[2:]
    slots = PARTS // sides
    sends = []
    if top:
        proj_stage, proj_sems = refs[2:]
        total = proj_refs[0][...]
        for ref in proj_refs[1:]:
            total = total + ref[...]
        proj_stage[...] = total.astype(BF).reshape(proj_stage.shape)
        for slot in range(slots):
            sends += block_sends(
                proj_stage, slot, down_targets, proj_sems.at[slot], place, True, SLAB
            )
    first_t = rows_of(first_t_refs)
    low_t = rows_of(low_t_refs)
    for slot in reversed(range(slots)):
        stage[0, slot] = nn(first_t, rows_at(pre_refs, slot)).astype(BF).reshape(*fold)
        sends += block_sends(stage.at[0, slot], slot, up_targets, sems.at[0, slot], place, False, 0)
        stage[1, slot] = nn(low_t, rows_at(act_refs, slot)).astype(BF).reshape(*fold)
        sends += block_sends(stage.at[1, slot], slot, down_targets, sems.at[1, slot], place, True, 0)
    for copy in sends:
        copy.wait()


def attention_grad_kernel(y_first, split, place, *refs):
    sides = 2 if split else 1
    groups = []
    for _ in range(4):
        groups.append(refs[:sides])
        refs = refs[sides:]
    x_t_refs, packed_refs, low_t_refs, mixture_refs = groups
    targets, refs = refs[:sides], refs[sides:]
    stage, sems = refs
    fold = stage.shape[1:]
    sends = []
    x_t = rows_of(x_t_refs)
    low_t = rows_of(low_t_refs)
    for slot in reversed(range(PARTS // sides)):
        grad_weight = nn(x_t, rows_at(packed_refs, slot))
        grad_out = nn(low_t, rows_at(mixture_refs, slot))
        stage[slot] = (
            jnp.concatenate(
                [grad_weight[:, : SLAB - ROWS], grad_weight[:, SLAB - ROWS :] + grad_out], 1
            )
            .astype(BF)
            .reshape(*fold)
        )
        sends += block_sends(stage.at[slot], slot, targets, sems.at[slot], place, y_first, 0)
    for copy in sends:
        copy.wait()


def any_spec():
    return pl.BlockSpec(memory_space=pl.ANY)


def vmem_spec():
    return pl.BlockSpec(memory_space=pltpu.VMEM)


def shaped(shape, kind):
    return jax.ShapeDtypeStruct(shape, kind)


def price(micros):
    return pl.CostEstimate(
        flops=int(micros * 1e6), bytes_accessed=int(micros * 3e3), transcendentals=0
    )


def params():
    return pltpu.CompilerParams(vmem_limit_bytes=VMEM_BYTES)


def smem_spec():
    return pl.BlockSpec(memory_space=pltpu.SMEM)


def sided(split, shape, kind):
    if split:
        return [shaped((2, *shape), kind)] * 2
    return [shaped((PARTS, *shape), kind)]


def held_scratch(gathered, count):
    depth = (gathered.shape[0], gathered.shape[2])
    return [pltpu.VMEM((PARTS, *depth, SLAB), BF)] * count + [
        pltpu.SemaphoreType.DMA((PARTS,))
    ] * count


def projection_scratch(gathered):
    depth = (gathered.shape[0], gathered.shape[2])
    return [pltpu.VMEM((*depth, DIM), BF), pltpu.SemaphoreType.DMA]


def call(kernel, name, micros, place, args, outs, scratch, in_hbm=(), out_hbm=()):
    return pl.pallas_call(
        kernel,
        out_shape=outs,
        in_specs=[smem_spec()]
        + [any_spec() if at in in_hbm else vmem_spec() for at in range(len(args))],
        out_specs=[any_spec() if at in out_hbm else vmem_spec() for at in range(len(outs))],
        scratch_shapes=scratch,
        compiler_params=params(),
        cost_estimate=price(micros),
        name=name,
    )(place, *args)


def run_attention(layer_at, place, hidden, mask, pair_rows, norms, gathered, split):
    outs = [
        shaped((ROWS, WIDTH), F32),
        shaped((WIDTH, ROWS), BF),
        shaped((PARTS, ROWS, HELD), BF),
        shaped((PARTS * HEADS_EACH, ROWS, ROWS), BF),
        shaped((ROWS, WIDTH), F32),
        shaped((ROWS, DIM), F32),
        shaped((WIDTH, ROWS), BF),
    ] + sided(split, (ROWS, ROWS), BF)
    return call(
        functools.partial(attention_kernel, layer_at * PACK, split),
        f"attention_{layer_at}",
        9,
        place,
        [hidden, mask, pair_rows, norms, gathered],
        outs,
        held_scratch(gathered, 1),
        in_hbm=(4,),
    )


def run_mlp(layer_at, place, first, up_rows, norms, gathered, split):
    top = layer_at == LAYERS - 1
    outs = [
        shaped((ROWS, WIDTH), F32),
        shaped((PARTS, ROWS, SLAB), BF),
        shaped((ROWS, WIDTH), F32),
        shaped((ROWS, DIM), F32),
    ] + sided(split, (ROWS, SLAB), BF)
    scratch = held_scratch(gathered, 2)
    if top:
        outs += [
            shaped((ROWS, DIM), BF),
            shaped((ROWS, DIM), F32),
            shaped((ROWS, DIM), F32),
            shaped((WIDTH, ROWS), BF),
        ]
        scratch += projection_scratch(gathered)
    return call(
        functools.partial(mlp_kernel, layer_at * PACK, top, split),
        f"mlp_{layer_at}",
        9,
        place,
        [first, up_rows, norms, gathered],
        outs,
        scratch,
        in_hbm=(3,),
    )


def run_mlp_pull(layer_at, place, upstream, saved, norms, gathered, split):
    top = layer_at == LAYERS - 1
    outs = [
        shaped((ROWS, WIDTH), F32),
        shaped((8, WIDTH), F32),
        shaped((WIDTH, ROWS), BF),
    ] + sided(split, (ROWS, SLAB), BF)
    scratch = held_scratch(gathered, 2)
    if top:
        outs += [shaped((WIDTH, DIM), F32)]
        scratch += projection_scratch(gathered)
    args = [*upstream, *saved, norms, gathered]
    return call(
        functools.partial(mlp_pull_kernel, layer_at * PACK, top, split),
        f"pull_mlp_{layer_at}",
        8,
        place,
        args,
        outs,
        scratch,
        in_hbm=(len(args) - 1,),
    )


def run_attention_pull(layer_at, place, grad_first, saved, norms, gathered, split):
    outs = [
        shaped((ROWS, WIDTH), F32),
        shaped((8, WIDTH), F32),
        shaped((WIDTH, ROWS), BF),
    ] + sided(split, (ROWS, SLAB), BF)
    args = [grad_first, *saved, norms, gathered]
    return call(
        functools.partial(attention_pull_kernel, layer_at * PACK, split),
        f"pull_attention_{layer_at}",
        10,
        place,
        args,
        outs,
        held_scratch(gathered, 1),
        in_hbm=(len(args) - 1,),
    )


def grad_shapes(split, rows_each, width):
    if split:
        return [shaped((2, 4, rows_each, width), BF)] * 2
    return [shaped((PARTS, WIDTH, width), BF)]


def run_mlp_grad(layer_at, place, groups, split, rows_each):
    top = layer_at == LAYERS - 1
    args = [value for group in groups for value in group]
    sides = 2 if split else 1
    outs = grad_shapes(split, rows_each, SLAB)
    outs += grad_shapes(split, rows_each, SLAB + (DIM if top else 0))
    fold = (4, 2, rows_each) if split else (1, 1, WIDTH)
    slots = PARTS // sides
    scratch = [
        pltpu.VMEM((2, slots, *fold, SLAB), BF),
        pltpu.SemaphoreType.DMA((2, slots, 2, 4)),
    ]
    if top:
        scratch += [pltpu.VMEM((*fold, DIM), BF), pltpu.SemaphoreType.DMA((slots, 2, 4))]
    results = call(
        functools.partial(mlp_grad_kernel, top, split),
        f"grad_mlp_{layer_at}",
        8,
        place,
        args,
        outs,
        scratch,
        out_hbm=range(len(outs)),
    )
    return results[:sides], results[sides:]


def run_attention_grad(layer_at, y_first, place, groups, split, rows_each):
    args = [value for group in groups for value in group]
    outs = grad_shapes(split, rows_each, SLAB)
    fold = (4, 2, rows_each) if split else (1, 1, WIDTH)
    slots = PARTS // (2 if split else 1)
    return call(
        functools.partial(attention_grad_kernel, y_first, split),
        f"grad_attention_{layer_at}",
        5,
        place,
        args,
        outs,
        [pltpu.VMEM((slots, *fold, SLAB), BF), pltpu.SemaphoreType.DMA((slots, 2, 4))],
        out_hbm=range(len(outs)),
    )


CORE_SWAP = [(at, at ^ 1) for at in range(PARTS)]
X_SWAP = [(at, at ^ 2) for at in range(PARTS)]
Y_SWAP = [(at, at ^ 1) for at in range(8)]
Z_GROUPS = [[0, 2, 4, 6], [1, 3, 5, 7]]


def added(*terms):
    total = terms[0].astype(F32)
    for term in terms[1:]:
        total = total + term.astype(F32)
    return total


def over_x(value, name):
    with jax.named_scope(f"x_{name}"):
        return lax.ppermute(value, "tensor", X_SWAP)


def over_y(value, name):
    with jax.named_scope(f"y_{name}"):
        return lax.ppermute(value, "dp", Y_SWAP)


def over_core(value, name="pair"):
    with jax.named_scope(f"core_{name}"):
        return lax.ppermute(value, "tensor", CORE_SWAP)


def along_z(value, step, name):
    pairs = [(at, ((at // 2 + step) % 4) * 2 + at % 2) for at in range(8)]
    with jax.named_scope(f"z_{name}_{step}"):
        return lax.ppermute(value, "dp", pairs)


def tied(*values):
    return lax.optimization_barrier(values)


class Reduction:
    def __init__(self, name, pieces, y_first):
        self.name = name
        self.keep, self.send = pieces
        self.first, self.second = (over_y, over_x) if y_first else (over_x, over_y)

    def start(self):
        self.one = self.first(self.send, self.name + "_first")

    def add_second(self):
        with jax.named_scope(f"add_{self.name}_second"):
            self.terms = added(self.keep[1], self.one[1]).astype(BF)

    def start_second(self):
        self.two = self.second(self.terms, self.name + "_second")

    def add_third(self):
        with jax.named_scope(f"add_{self.name}_third"):
            self.blocks = [
                added(self.keep[0, step], self.one[0, step], self.two[step]).astype(BF)
                for step in range(1, 4)
            ]

    def start_third(self):
        self.arrived = [
            along_z(block, step + 1, self.name) for step, block in enumerate(self.blocks)
        ]

    def total(self):
        with jax.named_scope(f"add_{self.name}_last"):
            return added(self.keep[0, 0], self.one[0, 0], self.two[0], *self.arrived)


def reduce_whole(grads, devices):
    grads = grads.reshape(PARTS, devices, WIDTH // devices, -1)
    grads = jnp.transpose(grads, (1, 0, 2, 3)).reshape(devices * PARTS, WIDTH // devices, -1)
    return lax.psum_scatter(grads, BOTH, scatter_dimension=0, tiled=True)[0].astype(F32)


def total_over_all(value, split):
    if not split:
        return lax.psum(value, BOTH)
    value = value + over_core(value)
    value = value + over_x(value, "sums")
    value = value + over_y(value, "sums")
    value = value + lax.ppermute(value, "dp", [(at, at ^ 2) for at in range(8)])
    return value + lax.ppermute(value, "dp", [(at, at ^ 4) for at in range(8)])


def score_kernel(count, lengths_ref, log_ref, queries_ref, passages_ref, powers_ref, sums_ref, logit_ref):
    queries = queries_ref[...]

    def single(at, carry):
        similar = nt(passages_ref[at], queries)
        spot = lax.broadcasted_iota(jnp.int32, (PLEN, ROWS), 0)
        powers = jnp.where(spot < lengths_ref[at], jnp.exp(SHARPNESS * similar), 0.0)
        powers_ref[at] = powers.astype(BF)
        sums_ref[pl.ds(at, 1), :] = jnp.sum(powers, 0, keepdims=True)
        return carry

    lax.fori_loop(0, count, single, 0)
    smooth = (jnp.log(sums_ref[...]) - log_ref[...]) / SHARPNESS
    token = lax.broadcasted_iota(jnp.int32, (ROWS, DIM), 0) // QLEN
    query = lax.broadcasted_iota(jnp.int32, (ROWS, DIM), 1)
    pick = (token == query).astype(F32)
    logit_ref[...] = SCORE_SCALE * jnp.dot(
        smooth, pick, precision=lax.Precision.HIGHEST, preferred_element_type=F32
    )


def pull_kernel(count, powers_ref, steer_ref, queries_ref, passages_ref, passage_out, query_out, total):
    queries = queries_ref[...]
    total[...] = jnp.zeros_like(total)

    def single(at, carry):
        shares = (powers_ref[at].astype(F32) * steer_ref[pl.ds(at, 1), :]).astype(BF)
        passage_out[at] = nn(shares, queries).astype(BF)
        total[...] += nn(passages_ref[at].T, shares)
        return carry

    lax.fori_loop(0, count, single, 0)
    query_out[...] = total[...].T


def scores_of(queries, passages, lengths):
    count = passages.shape[0]
    return pl.pallas_call(
        functools.partial(score_kernel, count),
        out_shape=[
            shaped((count, PLEN, ROWS), BF),
            shaped((count, ROWS), F32),
            shaped((count, DIM), F32),
        ],
        in_specs=[pl.BlockSpec(memory_space=pltpu.SMEM)] + [vmem_spec()] * 3,
        out_specs=[vmem_spec()] * 3,
        compiler_params=params(),
        cost_estimate=price(4),
        name="scores",
    )(lengths, jnp.log(lengths.astype(F32))[:, None], queries, passages)


def pulls_of(powers, steer, queries, passages):
    count = passages.shape[0]
    return pl.pallas_call(
        functools.partial(pull_kernel, count),
        out_shape=[shaped((count, PLEN, DIM), BF), shaped((ROWS, DIM), F32)],
        in_specs=[vmem_spec()] * 4,
        out_specs=[vmem_spec()] * 2,
        scratch_shapes=[pltpu.VMEM((DIM, ROWS), F32)],
        compiler_params=params(),
        cost_estimate=price(4),
        name="score_pulls",
    )(powers, steer, queries, passages)


def adam_step(master, moment, second, gradient, decay):
    moment_new = BETA_ONE * moment + (1.0 - BETA_ONE) * gradient
    second_new = BETA_TWO * second + (1.0 - BETA_TWO) * gradient * gradient
    rising = moment_new / (1.0 - BETA_ONE**STEP)
    spread = jnp.sqrt(second_new / (1.0 - BETA_TWO**STEP))
    return (moment_new, second_new, -LEARN_RATE * (rising / (spread + ADAM_EPS) + decay * master))


def pack_weights(qkv, out, up, down, proj):
    pieces = []
    for layer_at in range(LAYERS):
        pieces += [qkv[layer_at, 0], qkv[layer_at, 1], qkv[layer_at, 2]]
        pieces += [out[layer_at].T, up[layer_at], down[layer_at].T]
    pieces.append(proj)
    return jnp.concatenate([piece.astype(BF) for piece in pieces], 1)


def unpack_grads(att_list, up_list, down_list):
    qkv = jnp.stack(
        [
            jnp.stack([att[:, kind * OWN : (kind + 1) * OWN] for kind in range(3)])
            for att in att_list
        ]
    )
    out = jnp.stack([att[:, 3 * OWN :].T for att in att_list])
    return qkv, out, jnp.stack(up_list), jnp.stack([down[:, :SLAB].T for down in down_list])


def to_output_rows(grad, tensor_at):
    rows = PDEV * PLEN // PARTS
    query_rows = QDEV * QLEN // PARTS
    start = jnp.where(tensor_at == PARTS - 1, 0, ROWS - rows)
    step = lax.ppermute(
        lax.dynamic_slice_in_dim(grad, start, rows, 0),
        "tensor",
        [(at, (at + 1) % PARTS) for at in range(PARTS)],
    )
    last = PARTS - 1
    one = lax.ppermute(grad[query_rows : 2 * query_rows], "tensor", [(last, 1)])
    two = lax.ppermute(grad[2 * query_rows : 3 * query_rows], "tensor", [(last, 2)])
    own = grad[last * query_rows :]
    query = jnp.where(
        tensor_at == 0,
        step[:query_rows],
        jnp.where(tensor_at == 1, one, jnp.where(tensor_at == 2, two, own)),
    )
    unit = query_rows
    passage = jnp.where(
        tensor_at == 0,
        grad[:rows],
        jnp.where(
            tensor_at == 1,
            jnp.concatenate([step[2 * unit :], grad[: 2 * unit]]),
            jnp.where(tensor_at == 2, jnp.concatenate([step[unit:], grad[:unit]]), step),
        ),
    )
    return query, passage


def body(
    query_tokens,
    passage_tokens,
    query_mask,
    passage_lengths,
    positives,
    qkv_weight,
    qkv_moment,
    qkv_second,
    out_weight,
    out_moment,
    out_second,
    up_weight,
    up_moment,
    up_second,
    down_weight,
    down_moment,
    down_second,
    projection,
    projection_moment,
    projection_second,
    bias_pair,
    bias_pair_moment,
    bias_pair_second,
    bias_up,
    bias_up_moment,
    bias_up_second,
    norm_terms,
    norm_terms_moment,
    norm_terms_second,
):
    devices = lax.axis_size("dp")
    dev_index = lax.axis_index("dp")
    tensor_at = lax.axis_index("tensor")
    last = PARTS - 1
    is_query = tensor_at == last
    rows_each = WIDTH // devices
    pack = pack_weights(qkv_weight, out_weight, up_weight, down_weight, projection)
    gathered = lax.all_gather(pack, BOTH, axis=0, tiled=False)
    gathered = gathered.reshape(devices, PARTS, rows_each, -1)
    split = devices == 8
    if not split:
        gathered = jnp.transpose(gathered, (1, 0, 2, 3)).reshape(1, PARTS, WIDTH, -1)
    small = jnp.concatenate([bias_pair.reshape(-1), bias_up.reshape(-1)])
    small_all = lax.all_gather(small, "tensor", axis=0, tiled=False)
    pair_all = small_all[:, : LAYERS * 2 * OWN].reshape(PARTS, LAYERS, 2, OWN)
    up_all = small_all[:, LAYERS * 2 * OWN :].reshape(PARTS, LAYERS, 1, SLAB)
    pair_rows = jnp.concatenate(
        [
            pair_all[:, :, 0],
            jnp.zeros((PARTS, LAYERS, OWN), F32),
            pair_all[:, :, 1],
            jnp.zeros((PARTS, LAYERS, HELD - 3 * OWN), F32),
        ],
        -1,
    )[:, :, None, :]

    passage_at = jnp.minimum(tensor_at, last - 1)
    own_passage = lax.dynamic_slice_in_dim(passage_tokens, passage_at * PLEN, PLEN, 0)
    hidden = jnp.where(is_query, query_tokens, own_passage)
    own_length = lax.dynamic_slice_in_dim(passage_lengths, dev_index * PDEV + passage_at, 1, 0)
    spot = jnp.arange(ROWS, dtype=jnp.int32)
    key_valid = jnp.where(is_query, query_mask.reshape(ROWS) == 1, spot < own_length)
    together = jnp.logical_or(
        jnp.logical_not(is_query), spot[:, None] // QLEN == spot[None, :] // QLEN
    )
    mask = jnp.where(jnp.logical_and(key_valid[:, None], together), 0.0, MASKED).astype(F32)

    place = jnp.stack([tensor_at // 2, tensor_at % 2, dev_index % 2, dev_index // 2]).astype(jnp.int32)

    def sides_of(keep, send):
        return [keep, over_core(send)] if split else [keep]

    def shared(value):
        return [value, over_core(value)] if split else [value]

    saved_list = []
    for layer_at in range(LAYERS):
        outs = run_attention(
            layer_at,
            place,
            hidden,
            mask,
            pair_rows[:, layer_at],
            norm_terms[layer_at],
            gathered,
            split,
        )
        first, x_t, packed, chances, normal_one, factor_one, first_t = outs[:7]
        mixtures = sides_of(outs[7], outs[-1])
        outs = run_mlp(
            layer_at, place, first, up_all[:, layer_at], norm_terms[layer_at], gathered, split
        )
        hidden, slope, normal_two, factor_two = outs[:4]
        acts = sides_of(outs[4], outs[5 if split else 4])
        saved_list.append(
            dict(
                mlp=(slope, normal_two, factor_two),
                attention=(packed, chances, normal_one, factor_one),
                x_t=shared(x_t),
                first_t=shared(first_t),
                mixtures=mixtures,
                acts=acts,
            )
        )
    embedding, unit, scale, top_t = outs[-4:]

    passages = lax.all_to_all(
        jnp.broadcast_to(embedding[None], (devices, ROWS, DIM)), "dp", 0, 0, tiled=True
    )
    queries = embedding
    arrived = [lax.ppermute(embedding, "tensor", [(last, at)]) for at in range(last)]
    for at in range(last):
        queries = jnp.where(tensor_at == at, arrived[at], queries)
    length_table = passage_lengths.reshape(devices, PDEV)
    own_lengths = lax.dynamic_slice_in_dim(length_table, passage_at, 1, 1)[:, 0]
    powers, sums, logit_part = scores_of(queries, passages, own_lengths)
    logits = lax.all_gather(logit_part[:, :QDEV], "tensor", axis=0, tiled=False)[:last]
    own_positives = lax.dynamic_slice_in_dim(positives, dev_index * QDEV, QDEV, 0)
    ids = (
        lax.broadcasted_iota(jnp.int32, logits.shape, 1) * PDEV
        + lax.broadcasted_iota(jnp.int32, logits.shape, 0)
    )
    chosen = ids == own_positives[None, None, :]
    highest = jnp.max(logits, (0, 1), keepdims=True)
    raised = jnp.exp(logits - highest)
    summed = jnp.sum(raised, (0, 1), keepdims=True)
    losses = highest + jnp.log(summed) - jnp.sum(jnp.where(chosen, logits, 0.0), (0, 1), keepdims=True)
    deltas = raised / summed - chosen.astype(F32)
    own_deltas = lax.dynamic_slice_in_dim(deltas, passage_at, 1, 0)[0]
    steer = jnp.where(is_query, 0.0, SCORE_SCALE) * jnp.repeat(own_deltas, QLEN, axis=1) / sums
    passage_terms, query_terms = pulls_of(powers, steer, queries, passages)
    passage_back = lax.all_to_all(passage_terms, "dp", 0, 0, tiled=True)
    grad_passage = jnp.sum(passage_back.astype(F32), 0)
    returned = [lax.ppermute(query_terms, "tensor", [(at, last)]) for at in range(last)]
    grad_query = returned[0] + returned[1] + returned[2]
    grad_emb = jnp.where(is_query, grad_query, grad_passage)

    upstream = (grad_emb, unit, scale, top_t)
    mlp_sums, attention_sums = [None] * LAYERS, [None] * LAYERS

    def mlp_pull(layer_at, upstream):
        saved = saved_list[layer_at]
        outs = run_mlp_pull(
            layer_at, place, upstream, saved["mlp"], norm_terms[layer_at], gathered, split
        )
        grad_first, mlp_sums[layer_at], low_t = outs[:3]
        groups = [
            saved["first_t"],
            sides_of(outs[3], outs[4 if split else 3]),
            shared(low_t),
            saved["acts"],
        ]
        if layer_at == LAYERS - 1:
            groups.append(shared(outs[-1]))
        return grad_first, groups

    def attention_pull(layer_at, grad_first):
        saved = saved_list[layer_at]
        outs = run_attention_pull(
            layer_at,
            place,
            grad_first,
            saved["attention"],
            norm_terms[layer_at],
            gathered,
            split,
        )
        dx, attention_sums[layer_at], low_t = outs[:3]
        return dx, [
            saved["x_t"],
            sides_of(outs[3], outs[-1]),
            shared(low_t),
            saved["mixtures"],
        ]

    def mlp_grad(layer_at, groups):
        return run_mlp_grad(layer_at, place, groups, split, rows_each)

    def attention_grad(layer_at, y_first, groups):
        return run_attention_grad(layer_at, y_first, place, groups, split, rows_each)

    if split:
        grad_first, mlp_groups = mlp_pull(1, upstream)
        up_grads, down_grads = mlp_grad(1, mlp_groups)
        up_one, down_one = Reduction("up_1", up_grads, False), Reduction("down_1", down_grads, True)
        grad_first, up_one.send, down_one.send = tied(grad_first, up_one.send, down_one.send)
        up_one.start()
        down_one.start()
        dx, att_groups = attention_pull(1, grad_first)
        att_one = Reduction("att_1", attention_grad(1, False, att_groups), False)
        dx, att_one.send = tied(dx, att_one.send)
        att_one.start()
        grad_first, mlp_groups = mlp_pull(0, (dx,))
        up_one.add_second()
        down_one.add_second()
        mlp_groups[0][0], up_one.terms, down_one.terms = tied(
            mlp_groups[0][0], up_one.terms, down_one.terms
        )
        up_one.start_second()
        down_one.start_second()
        up_grads, down_grads = mlp_grad(0, mlp_groups)
        up_zero = Reduction("up_0", up_grads, False)
        down_zero = Reduction("down_0", down_grads, True)
        grad_first, up_zero.send, down_zero.send = tied(grad_first, up_zero.send, down_zero.send)
        up_zero.start()
        down_zero.start()
        dx, att_groups = attention_pull(0, grad_first)
        att_one.add_second()
        att_groups[0][0], att_one.terms = tied(att_groups[0][0], att_one.terms)
        att_one.start_second()
        up_one.add_third()
        down_one.add_third()
        up_zero.add_second()
        down_zero.add_second()
        att_groups[0][0], up_zero.terms, down_zero.terms = tied(
            att_groups[0][0], up_zero.terms, down_zero.terms
        )
        att_zero = Reduction("att_0", attention_grad(0, True, att_groups), True)
        att_zero.start()
        att_one.add_third()
        att_zero.add_second()
        for item in (up_one, down_one, att_one):
            item.start_third()
        for item in (up_zero, down_zero, att_zero):
            item.start_second()
        for item in (up_zero, down_zero, att_zero):
            item.add_third()
            item.start_third()
        attention_sums[0] = tied(attention_sums[0], att_zero.terms)[0]
        att_list = [att_zero.total(), att_one.total()]
        up_list = [up_zero.total(), up_one.total()]
        down_list = [down_zero.total(), down_one.total()]
    else:
        att_list, up_list, down_list = [], [], []
        dx = None
        for layer_at in range(LAYERS - 1, -1, -1):
            grad_first, groups = mlp_pull(layer_at, (dx,) if upstream is None else upstream)
            upstream = None
            up_grads, down_grads = mlp_grad(layer_at, groups)
            dx, groups = attention_pull(layer_at, grad_first)
            att_grads = attention_grad(layer_at, False, groups)
            up_list.insert(0, reduce_whole(up_grads[0], devices))
            down_list.insert(0, reduce_whole(down_grads[0], devices))
            att_list.insert(0, reduce_whole(att_grads[0], devices))
    loss_part = jnp.where(tensor_at == 0, jnp.sum(losses), 0.0)
    sums = jnp.stack([attention_sums[0], mlp_sums[0], attention_sums[1], mlp_sums[1]])
    row_ids = lax.broadcasted_iota(jnp.int32, sums.shape, 1)
    sums = sums + jnp.where(row_ids == 7, loss_part, 0.0)
    sums = total_over_all(sums, split).reshape(LAYERS, 2, 8, WIDTH)
    norms_grad = sums[:, :, :3].reshape(LAYERS, 6, WIDTH)
    own_sums = lax.dynamic_slice_in_dim(sums, 3 + tensor_at, 1, 2)[:, :, 0]
    pair_grad = jnp.stack([own_sums[:, 0, :OWN], own_sums[:, 0, 2 * OWN : 3 * OWN]], 1)
    bias_grad = own_sums[:, 1]
    loss_mean = sums[0, 0, 7, 0] / (QDEV * devices)
    projection_grad = down_list[LAYERS - 1][:, SLAB:]
    qkv_grad, out_grad, up_grad, down_grad = unpack_grads(att_list, up_list, down_list)
    qkv_m, qkv_v, qkv_u = adam_step(qkv_weight, qkv_moment, qkv_second, qkv_grad, WEIGHT_DECAY)
    out_m, out_v, out_u = adam_step(out_weight, out_moment, out_second, out_grad, WEIGHT_DECAY)
    up_m, up_v, up_u = adam_step(up_weight, up_moment, up_second, up_grad, WEIGHT_DECAY)
    down_m, down_v, down_u = adam_step(
        down_weight, down_moment, down_second, down_grad, WEIGHT_DECAY
    )
    proj_m, proj_v, proj_u = adam_step(
        projection, projection_moment, projection_second, projection_grad, WEIGHT_DECAY
    )
    pair_m, pair_v, pair_u = adam_step(
        bias_pair, bias_pair_moment, bias_pair_second, pair_grad, 0.0
    )
    bias_m, bias_v, bias_u = adam_step(bias_up, bias_up_moment, bias_up_second, bias_grad, 0.0)
    norm_m, norm_v, norm_u = adam_step(
        norm_terms, norm_terms_moment, norm_terms_second, norms_grad, 0.0
    )
    query_grad, passage_grad = to_output_rows(dx, tensor_at)
    return (
        loss_mean,
        query_grad,
        passage_grad,
        qkv_grad,
        qkv_m,
        qkv_v,
        qkv_u,
        out_grad,
        out_m,
        out_v,
        out_u,
        up_grad,
        up_m,
        up_v,
        up_u,
        down_grad,
        down_m,
        down_v,
        down_u,
        projection_grad,
        proj_m,
        proj_v,
        proj_u,
        pair_grad,
        pair_m,
        pair_v,
        pair_u,
        bias_grad,
        bias_m,
        bias_v,
        bias_u,
        norms_grad,
        norm_m,
        norm_v,
        norm_u,
    )


def solution(mesh):
    placed = (
        P("dp", None),
        P("dp", None),
        P("dp", None),
        P(),
        P(),
        P(None, None, "dp", "tensor"),
        P(None, None, "dp", "tensor"),
        P(None, None, "dp", "tensor"),
        P(None, "tensor", "dp"),
        P(None, "tensor", "dp"),
        P(None, "tensor", "dp"),
        P(None, "dp", "tensor"),
        P(None, "dp", "tensor"),
        P(None, "dp", "tensor"),
        P(None, "tensor", "dp"),
        P(None, "tensor", "dp"),
        P(None, "tensor", "dp"),
        P("dp", None),
        P("dp", None),
        P("dp", None),
        P(None, None, "tensor"),
        P(None, None, "tensor"),
        P(None, None, "tensor"),
        P(None, "tensor"),
        P(None, "tensor"),
        P(None, "tensor"),
        P(),
        P(),
        P(),
    )
    return jax.shard_map(
        body,
        mesh=mesh,
        in_specs=placed,
        out_specs=(
            P(),
            P(("dp", "tensor"), None),
            P(("dp", "tensor"), None),
            P(None, None, "dp", "tensor"),
            P(None, None, "dp", "tensor"),
            P(None, None, "dp", "tensor"),
            P(None, None, "dp", "tensor"),
            P(None, "tensor", "dp"),
            P(None, "tensor", "dp"),
            P(None, "tensor", "dp"),
            P(None, "tensor", "dp"),
            P(None, "dp", "tensor"),
            P(None, "dp", "tensor"),
            P(None, "dp", "tensor"),
            P(None, "dp", "tensor"),
            P(None, "tensor", "dp"),
            P(None, "tensor", "dp"),
            P(None, "tensor", "dp"),
            P(None, "tensor", "dp"),
            P("dp", None),
            P("dp", None),
            P("dp", None),
            P("dp", None),
            P(None, None, "tensor"),
            P(None, None, "tensor"),
            P(None, None, "tensor"),
            P(None, None, "tensor"),
            P(None, "tensor"),
            P(None, "tensor"),
            P(None, "tensor"),
            P(None, "tensor"),
            P(),
            P(),
            P(),
            P(),
        ),
        check_vma=False,
    )
```

time: 1310 us -> 542 us (0.41)
  waiting for transfers between devices: 792 us -> 244 us
  local copies, waits for them, and re-layouts: 171 us -> 25.3 us
  matrix products: 121 us -> 0 us
  Pallas kernels: 0 us -> 114 us
  blocking collectives: 105 us -> 11.6 us
  starting transfers between devices: 2.79 us -> 78.6 us
  other arithmetic: 86 us -> 39.9 us
    psum x8 -> x0, waiting for transfers between devices: 244 us -> none  [the longest x4 122 us: branch_total(): lax.psum(partial_value.astype(jnp.bfloat16), 'tensor').astype(jnp.float32)]
    unnamed x21 -> x1, waiting for transfers between devices: 231 us -> 0.02 us
    reduce_scatter x3 -> x0, waiting for transfers between devices: 160 us -> none  [the longest x1 87.2 us: body(): lax.psum_scatter(jnp.stack([layer_mats[2] for layer_mats in mat_list]), '...]
    dot_general x57 -> x0, matrix products: 117 us -> none  [the longest x2 20.2 us: layer_forward(): jnp.dot(first_low, up_low, preferred_element_type=jnp.float32) + bias_up]
    pallas_call x0 -> x14, Pallas kernels: none -> 114 us  [the longest x12 106 us: call(): pl.pallas_call(kernel, out_shape=outs, in_specs=[smem_spec()] + [any_spec...]
    unnamed x406 -> x159, local copies, waits for them, and re-layouts: 92.1 us -> 16.3 us
    ppermute x0 -> x61, starting transfers between devices: none -> 71.2 us  [the longest x18 25.3 us: along_z(): return lax.ppermute(value, 'dp', pairs)]
    ppermute x0 -> x61, waiting for transfers between devices: none -> 66 us  [the longest x18 23.7 us: along_z(): return lax.ppermute(value, 'dp', pairs)]
  transfers between devices with their start and end apart: 18 -> 64, of which waited for: 15 -> 26; matrix products, arithmetic and copies ran while one was open for 16% -> 9% of each run, Pallas kernels for 0% -> 11%
where the time goes in v1:
time: 542 us; the launch traced here: 532 us
  waiting for transfers between devices  244 us (45%)
  Pallas kernels  114 us (21%)
  starting transfers between devices  78.6 us (15%)
  other arithmetic  39.9 us (7%)
  local copies, waits for them, and re-layouts  25.3 us (5%)
  between operations  18.2 us (3%)
  blocking collectives  11.6 us (2%)
    all_gather x1, waiting for transfers between devices, body(): gathered = lax.all_gather(pack, BOTH, axis=0, tiled=False)  163 us
    pallas_call x12, Pallas kernels, call(): pl.pallas_call(kernel, out_shape=outs, in_specs=[smem_spec()] + [any_spec...  106 us
    ppermute x18, starting transfers between devices, along_z(): return lax.ppermute(value, 'dp', pairs)  25.3 us
    ppermute x18, waiting for transfers between devices, along_z(): return lax.ppermute(value, 'dp', pairs)  23.7 us
    ppermute x18, starting transfers between devices, over_core(): return lax.ppermute(value, 'tensor', CORE_SWAP)  22.1 us
    unnamed x159, local copies, waits for them, and re-layouts  16.3 us
    ppermute x7, waiting for transfers between devices, over_y(): return lax.ppermute(value, 'dp', Y_SWAP)  14.5 us
  transfers between devices with their start and end apart: 64, of which 26 were waited for; matrix products, arithmetic and copies ran while one was open for 9% of the time, Pallas kernels for 11%

profile of v1, /device:TPU:0, one launch (start us, length us, event | category | flops | bytes accessed | tf_op | source)
XLA Modules:
  0.0 531.7 jit_solution(1139608247501181162)
XLA Ops:
  11.1 6.3 %all-gather.3 = f32[4,1,2304]{2,1,0:T(1,128)S(1)} all-gather(f32[1,1,2304]{2,1,0:T(1,128)S(1)} %reshape.391), channel_id=2, replica_groups=mesh['dp'=8,'tensor'=4] {'tensor'}, dimensions={0}, use_global_device_ids=true | all-gather | bytes 46080 | tf_op jit(solution)/shard_map/all_gather | solution.py:851
  22.5 2.2 dynamic-slice_select_fusion.refs_0_
  24.7 162.6 %all-gather.6.cloned.1.call-done = bf16[3072,4736]{1,0:T(8,128)(2,1)} async-done(((bf16[96,4736]{1,0:T(8,128)(2,1)}), bf16[3072,4736]{1,0:T(8,128)(2,1)}) %all-gather.6.cloned.1.call-update) | async-done | bytes 29098000 | tf_op jit(solution)/shard_map/all_gather | solution.py:845
  187.3 10.6 %attention_0.1 = (f32[256,768]{1,0:T(8,128)}, bf16[768,256]{1,0:T(8,128)(2,1)}, bf16[4,256,640]{2,1,0:T(8,128)(2,1)}, bf16[12,256,256]{2,1,0:T(8,128)(2,1)}, f32...) custom-call(s32[4]{0:T(128)} %pad_add_fusion.place, ...), custom_call_target="tpu_custom_call" | custom-call | flops 9000000 | bytes 27000 | tf_op jit(solution)/shard_map/attention_0/pallas_call | solution.py:438
  197.9 8.9 %mlp_0.1 = (f32[256,768]{1,0:T(8,128)}, bf16[4,256,768]{2,1,0:T(8,128)(2,1)}, f32[256,768]{1,0:T(8,128)}, f32[256,128]{1,0:T(8,128)}, bf16[2,256,768]{2,1,0:T(8,128)(2,1)}, /*index=5*/bf16[2,256,768]{2,1,0:T(8,128)(2,1)}) custom-call(s32[4]{0:T(128)} %pad_add_fusion.place, f32[256,768]{1,0:T(8,128)} %get-tuple-element.123.refs_0_, ...), custom_call_target="tpu_custom_call" | custom-call | flops 9000000 | bytes 27000 | tf_op jit(solution)/shard_map/mlp_0/pallas_call | solution.py:438
  206.8 10.8 %attention_1.1 = (f32[256,768]{1,0:T(8,128)}, bf16[768,256]{1,0:T(8,128)(2,1)}, bf16[4,256,640]{2,1,0:T(8,128)(2,1)}, bf16[12,256,256]{2,1,0:T(8,128)(2,1)}, f32...) custom-call(s32[4]{0:T(128)} %pad_add_fusion.place, ...), custom_call_target="tpu_custom_call" | custom-call | flops 9000000 | bytes 27000 | tf_op jit(solution)/shard_map/attention_1/pallas_call | solution.py:438
  217.6 10.1 %mlp_1.1 = (f32[256,768]{1,0:T(8,128)}, bf16[4,256,768]{2,1,0:T(8,128)(2,1)}, f32[256,768]{1,0:T(8,128)}, f32[256,128]{1,0:T(8,128)}, bf16[2,256,768]{2,1,0:T(8,...) custom-call(s32[4]{0:T(128)} %pad_add_fusion.place, ...), custom_call_target="tpu_custom_call" | custom-call | flops 9000000 | bytes 27000 | tf_op jit(solution)/shard_map/mlp_1/pallas_call | solution.py:438
  227.7 1.8 broadcast_in_dim.51
  229.5 3.7 all-to-all-start
  237.4 4.5 collective-permute-done.2
  242.5 5.5 %all-to-all-done.passages_ref = bf16[8,256,128]{2,1,0:T(8,128)(2,1)S(1)} async-done(((bf16[8,256,128]{2,1,0:T(8,128)(2,1)}), bf16[8,256,128]{2,1,0:T(8,128)(2,1)S(1)}, u32[]{:S(2)}, u32[]{:S(2)}) %all-to-all-start) | async-done | bytes 524320 | tf_op jit(solution)/shard_map/all_to_all | solution.py:914
  248.8 4.0 scores.1
  252.8 5.3 all-gather.2
  260.2 4.0 score_pulls.1
  264.2 3.6 all-to-all-start.1
  268.0 3.2 collective-permute-start.3
  273.0 9.8 %all-to-all-done.1 = bf16[8,256,128]{2,1,0:T(8,128)(2,1)S(1)} async-done(((bf16[8,256,128]{2,1,0:T(8,128)(2,1)}), bf16[8,256,128]{2,1,0:T(8,128)(2,1)S(1)}, u32[]{:S(2)}, u32[]{:S(2)}) %all-to-all-start.1) | async-done | bytes 524320 | tf_op jit(solution)/shard_map/all_to_all | solution.py:939
  283.6 9.2 %pull_mlp_1.1 = (f32[256,768]{1,0:T(8,128)}, f32[8,768]{1,0:T(8,128)}, bf16[768,256]{1,0:T(8,128)(2,1)}, bf16[2,256,768]{2,1,0:T(8,128)(2,1)}, bf16[2,256,768]{2,1,0:T(8,128)(2,1)}, /*index=5*/f32[768,128]{1,0:T(8,128)}) custom-call(s32[4]{0:T(128)} %pad_add_fusion.place, f32[256,128]{1,0:T(8,128)} %add_select_fusion.refs_0_, ...), custom_call_target="tpu_custom_call" | custom-call | flops 8000000 | bytes 24000 | tf_op jit(solution)/shard_map/pull_mlp_1/pallas_call | solution.py:438
  293.9 2.1 collective-permute-done.6.refs_1_
  298.1 6.7 %grad_mlp_1.1 = (bf16[2,4,96,768]{3,2,1,0:T(8,128)(2,1)}, bf16[2,4,96,768]{3,2,1,0:T(8,128)(2,1)}, bf16[2,4,96,896]{3,2,1,0:T(8,128)(2,1)}, bf16[2,4,96,896]{3,2,1,0:T(8,128)(2,1)}) custom-call(s32[4]{0:T(128)} %pad_add_fusion.place, bf16[768,256]{1,0:T(8,128)(2,1)} %get-tuple-element.139.refs_0_, bf16[768,256]{1,0:T(8,128)(2,1)} %copy-done.31, ...), custom_call_target="tpu_custom_call" | custom-call | flops 8000000 | bytes 24000 | tf_op jit(solution)/shard_map/grad_mlp_1/pallas_call | solution.py:438
  304.9 1.5 collective-permute-start.16
  307.8 12.4 %pull_attention_1.1 = (f32[256,768]{1,0:T(8,128)}, f32[8,768]{1,0:T(8,128)}, bf16[768,256]{1,0:T(8,128)(2,1)}, bf16[2,256,768]{2,1,0:T(8,128)(2,1)}, bf16[2,256,768]{2,1,0:T(8,128)(2,1)}) custom-call(s32[4]{0:T(128)} %pad_add_fusion.place, f32[256,768]{1,0:T(8,128)} %get-tuple-element.148.refs_0_, bf16[4,256,640]{2,1,0:T(8,128)(2,1)} %get-tuple-element.149.refs_1_, ...), custom_call_target="tpu_custom_call" | custom-call | flops 10000000 | bytes 30000 | tf_op jit(solution)/shard_map/pull_attention_1/pallas_call | solution.py:438
  321.1 1.9 collective-permute-done.14.refs_7_
  325.9 4.9 grad_attention_1.1
  331.6 8.7 %pull_mlp_0.1 = (f32[256,768]{1,0:T(8,128)}, f32[8,768]{1,0:T(8,128)}, bf16[768,256]{1,0:T(8,128)(2,1)}, bf16[2,256,768]{2,1,0:T(8,128)(2,1)}, bf16[2,256,768]{2,1,0:T(8,128)(2,1)}) custom-call(s32[4]{0:T(128)} %pad_add_fusion.place, f32[256,768]{1,0:T(8,128)} %get-tuple-element.161.refs_0_, bf16[4,256,768]{2,1,0:T(8,128)(2,1)} %get-tuple-element.162.refs_1_, ...), custom_call_target="tpu_custom_call" | custom-call | flops 8000000 | bytes 24000 | tf_op jit(solution)/shard_map/pull_mlp_0/pallas_call | solution.py:438
  341.7 1.8 copy.110
  346.0 2.2 fusion.4
  348.2 2.1 fusion
  352.6 6.3 %grad_mlp_0.1 = (bf16[2,4,96,768]{3,2,1,0:T(8,128)(2,1)}, bf16[2,4,96,768]{3,2,1,0:T(8,128)(2,1)}, bf16[2,4,96,768]{3,2,1,0:T(8,128)(2,1)}, bf16[2,4,96,768]{3,2,1,0:T(8,128)(2,1)}) custom-call(s32[4]{0:T(128)} %pad_add_fusion.place, bf16[768,256]{1,0:T(8,128)(2,1)} %get-tuple-element.171.refs_0_, bf16[768,256]{1,0:T(8,128)(2,1)} %copy-done.30, ...), custom_call_target="tpu_custom_call" | custom-call | flops 8000000 | bytes 24000 | tf_op jit(solution)/shard_map/grad_mlp_0/pallas_call | solution.py:438
  360.2 12.5 %pull_attention_0.1 = (f32[256,768]{1,0:T(8,128)}, f32[8,768]{1,0:T(8,128)}, bf16[768,256]{1,0:T(8,128)(2,1)}, bf16[2,256,768]{2,1,0:T(8,128)(2,1)}, bf16[2,256,768]{2,1,0:T(8,128)(2,1)}) custom-call(s32[4]{0:T(128)} %pad_add_fusion.place, f32[256,768]{1,0:T(8,128)} %get-tuple-element.179.refs_0_, bf16[4,256,640]{2,1,0:T(8,128)(2,1)} %get-tuple-element.180.refs_1_, ...), custom_call_target="tpu_custom_call" | custom-call | flops 10000000 | bytes 30000 | tf_op jit(solution)/shard_map/pull_attention_0/pallas_call | solution.py:438
  375.3 2.0 fusion.5
  378.9 1.9 collective-permute-start.51
  380.8 1.8 collective-permute-start.52
  382.6 1.5 fusion.12
  384.1 3.3 collective-permute-done.50
  388.0 4.4 collective-permute-done.51
  394.9 2.1 collective-permute-start.58
  397.9 1.6 collective-permute-start.60
  402.3 14.8 %collective-permute-start.24 = (bf16[768,256]{1,0:T(8,128)(2,1)S(1)}, bf16[768,256]{1,0:T(8,128)(2,1)S(1)}, u32[]{:S(2)}, u32[]{:S(2)}) collective-permute-start(bf16[768,256]{1,0:T(8,128)(2,1)S(1)} %copy-done.34), channel_id=1, source_target_pairs={{0,1},{1,0},{2,3},{3,2},{4,5},{5,4},{6,7},{7,6},{8,9},{9,8},{10,11... | collective-permute-start | bytes 1179656 | tf_op jit(solution)/shard_map/core_pair/ppermute | solution.py:620
  417.1 2.9 collective-permute-start.25
  422.6 2.0 fusion.7
  428.2 4.9 grad_attention_0.1
  434.4 1.9 collective-permute-done.41
  436.3 1.5 fusion.39
  438.0 3.0 collective-permute-start.43
  442.5 4.0 collective-permute-done.42
  446.5 5.1 collective-permute-done.43
  454.2 2.8 collective-permute-done.53
  460.1 2.8 collective-permute-start.56
  463.2 10.9 %collective-permute-done.45 = bf16[4,96,768]{2,1,0:T(8,128)(2,1)S(1)} collective-permute-done((bf16[4,96,768]{2,1,0:T(8,128)(2,1)S(1)}, bf16[4,96,768]{2,1,0:T(8,128)(2,1)S(1)}, u32[]{:S(2)}, u32[]{:S(2)}) %collective-permute-start.45) | collective-permute-done | bytes 589856 | tf_op jit(solution)/shard_map/y_up_0_second/ppermute | solution.py:615
  475.7 2.2 collective-permute-start.47
  479.4 3.6 collective-permute-done.30
  484.5 1.5 add_multiply_fusion
  486.0 1.7 collective-permute-done.31
  487.7 1.9 collective-permute-start.32
  489.8 3.7 collective-permute-done.32
  494.6 1.5 add_multiply_fusion.1
  496.1 3.0 collective-permute-done.33
  503.7 3.4 collective-permute-done.37
  507.3 1.9 collective-permute-start.38
  509.2 2.1 collective-permute-start.39
  512.3 2.1 collective-permute-done.38
  514.4 3.4 collective-permute-done.39
  521.8 1.6 add_multiply_fusion.2
  (343 shorter events, 75.2 us)
Async XLA Ops:
  7.2 180.0 %all-gather.6.cloned.1.call-start = ((), (), s32[]{:S(2)}) async-start(), calls=%async_computation.2 | async-start | bytes 30007296 | tf_op jit(solution)/shard_map/all_gather | solution.py:845
  229.5 18.6 %all-to-all-start = ((bf16[8,256,128]{2,1,0:T(8,128)(2,1)}), bf16[8,256,128]{2,1,0:T(8,128)(2,1)S(1)}, u32[]{:S(2)}, u32[]{:S(2)}) async-start(bf16[8,256,128]{2,1,0:T(8,128)(2,1)} %broadcast_in_dim.51), calls=%async_computation | async-start | bytes 1048576 | tf_op jit(solution)/shard_map/all_to_all | solution.py:914
  234.1 3.3 collective-permute-start
  234.7 2.7 collective-permute-start.1
  235.4 6.5 %collective-permute-start.2 = (bf16[256,128]{1,0:T(8,128)(2,1)S(1)}, bf16[256,128]{1,0:T(8,128)(2,1)S(1)}, u32[]{:S(2)}, u32[]{:S(2)}) collective-permute-start(bf16[256,128]{1,0:T(8,128)(2,1)S(1)} %copy-done.41), channel_id=1, source_target_pairs={{3,0},{7,4},{11,8},{15,12},{19,16},{23,20},{27,24},{31,28}} | collective-permute-start | bytes 196616 | tf_op jit(solution)/shard_map/ppermute | solution.py:918
  264.2 18.7 %all-to-all-start.1 = ((bf16[8,256,128]{2,1,0:T(8,128)(2,1)}), bf16[8,256,128]{2,1,0:T(8,128)(2,1)S(1)}, u32[]{:S(2)}, u32[]{:S(2)}) async-start(bf16[8,256,128]{2,1,0:T(8,128)(2,1)} %get-tuple-element.131), calls=%async_computation.1 | async-start | bytes 1048576 | tf_op jit(solution)/shard_map/all_to_all | solution.py:939
  267.8 28.3 %collective-permute-start.9 = (bf16[2,256,768]{2,1,0:T(8,128)(2,1)}, bf16[2,256,768]{2,1,0:T(8,128)(2,1)S(1)}, u32[]{:S(2)}, u32[]{:S(2)}) collective-permute-start(bf16[2,256,768]{2,1,0:T(8,128)(2,1)} %get-tuple-element.144), channel_id=1, source_target_pairs={{0,1},{1,0},{2,3},{3,2},{4,5},{5,4},{6,7},{7,6},{8,9},{9,8},{10,11... | collective-permute-start | bytes 2359304 | tf_op jit(solution)/shard_map/core_pair/ppermute | solution.py:620
  268.0 14.9 %collective-permute-start.3 = (f32[256,128]{1,0:T(8,128)}, f32[256,128]{1,0:T(8,128)S(1)}, u32[]{:S(2)}, u32[]{:S(2)}) collective-permute-start(f32[256,128]{1,0:T(8,128)} %get-tuple-element.130), channel_id=1, source_target_pairs={{0,3},{4,7},{8,11},{12,15},{16,19},{20,23},{24,27},{28,31}} | collective-permute-start | bytes 393224 | tf_op jit(solution)/shard_map/ppermute | solution.py:941
  271.2 11.7 %collective-permute-start.4 = (f32[256,128]{1,0:T(8,128)}, f32[256,128]{1,0:T(8,128)S(1)}, u32[]{:S(2)}, u32[]{:S(2)}) collective-permute-start(f32[256,128]{1,0:T(8,128)} %get-tuple-element.130), channel_id=1, source_target_pairs={{1,3},{5,7},{9,11},{13,15},{17,19},{21,23},{25,27},{29,31}} | collective-permute-start | bytes 393224 | tf_op jit(solution)/shard_map/ppermute | solution.py:941
  271.9 11.0 %collective-permute-start.5 = (f32[256,128]{1,0:T(8,128)}, f32[256,128]{1,0:T(8,128)S(1)}, u32[]{:S(2)}, u32[]{:S(2)}) collective-permute-start(f32[256,128]{1,0:T(8,128)} %get-tuple-element.130), channel_id=1, source_target_pairs={{2,3},{6,7},{10,11},{14,15},{18,19},{22,23},{26,27},{30,31}} | collective-permute-start | bytes 393224 | tf_op jit(solution)/shard_map/ppermute | solution.py:941
  292.8 4.3 collective-permute-start.7
  292.9 3.1 collective-permute-start.6
  293.4 3.1 collective-permute-start.10
  293.5 3.6 collective-permute-start.8
  304.9 40.7 %collective-permute-start.16 = (bf16[2,4,96,896]{3,2,1,0:T(8,128)(2,1)}, bf16[2,4,96,896]{3,2,1,0:T(8,128)(2,1)}, u32[]{:S(2)}, u32[]{:S(2)}) collective-permute-start(bf16[2,4,96,896]{3,2,1,0:T(8,128)(2,1)} %get-tuple-element.170), channel_id=1, source_target_pairs={{0,4},{4,0},{8,12},{12,8},{16,20},{20,16},{24,28},{28,24},{1,5},{5... | collective-permute-start | bytes 4128776 | tf_op jit(solution)/shard_map/y_down_1_first/ppermute | solution.py:615
  306.4 39.0 %collective-permute-start.15 = (bf16[2,4,96,768]{3,2,1,0:T(8,128)(2,1)}, bf16[2,4,96,768]{3,2,1,0:T(8,128)(2,1)}, u32[]{:S(2)}, u32[]{:S(2)}) collective-permute-start(bf16[2,4,96,768]{3,2,1,0:T(8,128)(2,1)} %get-tuple-element.168), channel_id=1, source_target_pairs={{0,2},{1,3},{2,0},{3,1},{4,6},{5,7},{6,4},{7,5},{8,10},{9,11},{10,... | collective-permute-start | bytes 3538952 | tf_op jit(solution)/shard_map/x_up_1_first/ppermute | solution.py:610
  320.2 4.7 collective-permute-start.12
  320.3 2.6 collective-permute-start.14
  321.0 2.5 collective-permute-start.11
  322.9 1.9 collective-permute-start.13
  330.9 43.3 %collective-permute-start.21 = (bf16[2,4,96,768]{3,2,1,0:T(8,128)(2,1)}, bf16[2,4,96,768]{3,2,1,0:T(8,128)(2,1)}, u32[]{:S(2)}, u32[]{:S(2)}) collective-permute-start(bf16[2,4,96,768]{3,2,1,0:T(8,128)(2,1)} %get-tuple-element.187), channel_id=1, source_target_pairs={{0,2},{1,3},{2,0},{3,1},{4,6},{5,7},{6,4},{7,5},{8,10},{9,11},{10,... | collective-permute-start | bytes 3538952 | tf_op jit(solution)/shard_map/x_att_1_first/ppermute | solution.py:610
  331.5 20.2 %collective-permute-start.20 = (bf16[2,256,768]{2,1,0:T(8,128)(2,1)}, bf16[2,256,768]{2,1,0:T(8,128)(2,1)S(1)}, u32[]{:S(2)}, u32[]{:S(2)}) collective-permute-start(bf16[2,256,768]{2,1,0:T(8,128)(2,1)} %get-tuple-element.176), channel_id=1, source_target_pairs={{0,1},{1,0},{2,3},{3,2},{4,5},{5,4},{6,7},{7,6},{8,9},{9,8},{10,11... | collective-permute-start | bytes 2359304 | tf_op jit(solution)/shard_map/core_pair/ppermute | solution.py:620
  340.3 12.1 %collective-permute-start.18 = (bf16[2,256,768]{2,1,0:T(8,128)(2,1)}, bf16[2,256,768]{2,1,0:T(8,128)(2,1)}, u32[]{:S(2)}, u32[]{:S(2)}) collective-permute-start(bf16[2,256,768]{2,1,0:T(8,128)(2,1)} %get-tuple-element.173), channel_id=1, source_target_pairs={{0,1},{1,0},{2,3},{3,2},{4,5},{5,4},{6,7},{7,6},{8,9},{9,8},{10,11... | collective-permute-start | bytes 2359304 | tf_op jit(solution)/shard_map/core_pair/ppermute | solution.py:620
  345.5 4.9 collective-permute-start.17
  345.6 6.8 %collective-permute-start.19 = (bf16[768,256]{1,0:T(8,128)(2,1)}, bf16[768,256]{1,0:T(8,128)(2,1)}, u32[]{:S(2)}, u32[]{:S(2)}) collective-permute-start(bf16[768,256]{1,0:T(8,128)(2,1)} %get-tuple-element.174.refs_4_), channel_id=1, source_target_pairs={{0,1},{1,0},{2,3},{3,2},{4,5},{5,4},{6,7},{7,6},{8,9},{9,8},{10,11... | collective-permute-start | bytes 1179656 | tf_op jit(solution)/shard_map/core_pair/ppermute | solution.py:620
  350.3 30.5 %collective-permute-start.57 = (bf16[4,96,896]{2,1,0:T(8,128)(2,1)}, bf16[4,96,896]{2,1,0:T(8,128)(2,1)}, u32[]{:S(2)}, u32[]{:S(2)}) collective-permute-start(bf16[4,96,896]{2,1,0:T(8,128)(2,1)} %fusion), channel_id=1, source_target_pairs={{0,2},{1,3},{2,0},{3,1},{4,6},{5,7},{6,4},{7,5},{8,10},{9,11},{10,... | collective-permute-start | bytes 2064392 | tf_op jit(solution)/shard_map/x_down_1_second/ppermute | solution.py:610
  351.8 25.5 %collective-permute-start.49 = (bf16[4,96,768]{2,1,0:T(8,128)(2,1)}, bf16[4,96,768]{2,1,0:T(8,128)(2,1)}, u32[]{:S(2)}, u32[]{:S(2)}) collective-permute-start(bf16[4,96,768]{2,1,0:T(8,128)(2,1)} %fusion.4), channel_id=1, source_target_pairs={{0,4},{4,0},{8,12},{12,8},{16,20},{20,16},{24,28},{28,24},{1,5},{5... | collective-permute-start | bytes 1769480 | tf_op jit(solution)/shard_map/y_up_1_second/ppermute | solution.py:615
  359.0 62.9 %collective-permute-start.23 = (bf16[2,4,96,768]{3,2,1,0:T(8,128)(2,1)}, bf16[2,4,96,768]{3,2,1,0:T(8,128)(2,1)}, u32[]{:S(2)}, u32[]{:S(2)}) collective-permute-start(bf16[2,4,96,768]{3,2,1,0:T(8,128)(2,1)} %get-tuple-element.192), channel_id=1, source_target_pairs={{0,4},{4,0},{8,12},{12,8},{16,20},{20,16},{24,28},{28,24},{1,5},{5... | collective-permute-start | bytes 3538952 | tf_op jit(solution)/shard_map/y_down_0_first/ppermute | solution.py:615
  374.1 20.8 %collective-permute-start.34 = (f32[192,768]{1,0:T(8,128)S(1)}, f32[192,768]{1,0:T(8,128)S(1)}, u32[]{:S(2)}, u32[]{:S(2)}) collective-permute-start(f32[192,768]{1,0:T(8,128)S(1)} %constant_dynamic-slice_fusion.1), channel_id=1, source_target_pairs={{0,1},{1,2},{2,3},{3,0},{4,5},{5,6},{6,7},{7,4},{8,9},{9,10},{10,1... | collective-permute-start | bytes 1769480 | tf_op jit(solution)/shard_map/ppermute | solution.py:780
  378.7 8.7 %collective-permute-start.50 = (bf16[96,768]{1,0:T(8,128)(2,1)S(1)}, bf16[96,768]{1,0:T(8,128)(2,1)S(1)}, u32[]{:S(2)}, u32[]{:S(2)}) collective-permute-start(bf16[96,768]{1,0:T(8,128)(2,1)S(1)} %get-tuple-element.356), channel_id=1, source_target_pairs={{0,8},{4,12},{8,16},{12,20},{16,24},{20,28},{24,0},{28,4},{1,9},{5... | collective-permute-start | bytes 442376 | tf_op jit(solution)/shard_map/z_up_1_1/ppermute | solution.py:626
  378.9 13.5 %collective-permute-start.51 = (bf16[96,768]{1,0:T(8,128)(2,1)S(1)}, bf16[96,768]{1,0:T(8,128)(2,1)S(1)}, u32[]{:S(2)}, u32[]{:S(2)}) collective-permute-start(bf16[96,768]{1,0:T(8,128)(2,1)S(1)} %get-tuple-element.358), channel_id=1, source_target_pairs={{0,16},{4,20},{8,24},{12,28},{16,0},{20,4},{24,8},{28,12},{1,17},{... | collective-permute-start | bytes 442376 | tf_op jit(solution)/shard_map/z_up_1_2/ppermute | solution.py:626
  380.8 12.3 %collective-permute-start.52 = (bf16[96,768]{1,0:T(8,128)(2,1)S(1)}, bf16[96,768]{1,0:T(8,128)(2,1)S(1)}, u32[]{:S(2)}, u32[]{:S(2)}) collective-permute-start(bf16[96,768]{1,0:T(8,128)(2,1)S(1)} %get-tuple-element.357), channel_id=1, source_target_pairs={{0,24},{4,28},{8,0},{12,4},{16,8},{20,12},{24,16},{28,20},{1,25},{... | collective-permute-start | bytes 442376 | tf_op jit(solution)/shard_map/z_up_1_3/ppermute | solution.py:626
  387.4 37.2 %collective-permute-start.22 = (bf16[2,4,96,768]{3,2,1,0:T(8,128)(2,1)S(1)}, bf16[2,4,96,768]{3,2,1,0:T(8,128)(2,1)S(1)}, u32[]{:S(2)}, u32[]{:S(2)}) collective-permute-start(bf16[2,4,96,768]{3,2,1,0:T(8,128)(2,1)S(1)} %copy-done.68), channel_id=1, source_target_pairs={{0,2},{1,3},{2,0},{3,1},{4,6},{5,7},{6,4},{7,5},{8,10},{9,11},{10,... | collective-permute-start | bytes 3538952 | tf_op jit(solution)/shard_map/x_up_0_first/ppermute | solution.py:610
  392.4 4.6 collective-permute-start.35
  393.1 4.8 collective-permute-start.36
  394.9 7.4 %collective-permute-start.58 = (bf16[96,896]{1,0:T(8,128)(2,1)S(1)}, bf16[96,896]{1,0:T(8,128)(2,1)S(1)}, u32[]{:S(2)}, u32[]{:S(2)}) collective-permute-start(bf16[96,896]{1,0:T(8,128)(2,1)S(1)} %get-tuple-element.347), channel_id=1, source_target_pairs={{0,8},{4,12},{8,16},{12,20},{16,24},{20,28},{24,0},{28,4},{1,9},{5... | collective-permute-start | bytes 516104 | tf_op jit(solution)/shard_map/z_down_1_1/ppermute | solution.py:626
  397.0 20.1 %collective-permute-start.59 = (bf16[96,896]{1,0:T(8,128)(2,1)S(1)}, bf16[96,896]{1,0:T(8,128)(2,1)S(1)}, u32[]{:S(2)}, u32[]{:S(2)}) collective-permute-start(bf16[96,896]{1,0:T(8,128)(2,1)S(1)} %get-tuple-element.349), channel_id=1, source_target_pairs={{0,16},{4,20},{8,24},{12,28},{16,0},{20,4},{24,8},{28,12},{1,17},{... | collective-permute-start | bytes 516104 | tf_op jit(solution)/shard_map/z_down_1_2/ppermute | solution.py:626
  397.9 22.2 %collective-permute-start.60 = (bf16[96,896]{1,0:T(8,128)(2,1)S(1)}, bf16[96,896]{1,0:T(8,128)(2,1)S(1)}, u32[]{:S(2)}, u32[]{:S(2)}) collective-permute-start(bf16[96,896]{1,0:T(8,128)(2,1)S(1)} %get-tuple-element.348), channel_id=1, source_target_pairs={{0,24},{4,28},{8,0},{12,4},{16,8},{20,12},{24,16},{28,20},{1,25},{... | collective-permute-start | bytes 516104 | tf_op jit(solution)/shard_map/z_down_1_3/ppermute | solution.py:626
  402.3 24.3 %collective-permute-start.24 = (bf16[768,256]{1,0:T(8,128)(2,1)S(1)}, bf16[768,256]{1,0:T(8,128)(2,1)S(1)}, u32[]{:S(2)}, u32[]{:S(2)}) collective-permute-start(bf16[768,256]{1,0:T(8,128)(2,1)S(1)} %copy-done.34), channel_id=1, source_target_pairs={{0,1},{1,0},{2,3},{3,2},{4,5},{5,4},{6,7},{7,6},{8,9},{9,8},{10,11... | collective-permute-start | bytes 1179656 | tf_op jit(solution)/shard_map/core_pair/ppermute | solution.py:620
  417.1 10.3 %collective-permute-start.25 = (bf16[2,256,768]{2,1,0:T(8,128)(2,1)S(1)}, bf16[2,256,768]{2,1,0:T(8,128)(2,1)}, u32[]{:S(2)}, u32[]{:S(2)}) collective-permute-start(bf16[2,256,768]{2,1,0:T(8,128)(2,1)S(1)} %copy-done.69), channel_id=1, source_target_pairs={{0,1},{1,0},{2,3},{3,2},{4,5},{5,4},{6,7},{7,6},{8,9},{9,8},{10,11... | collective-permute-start | bytes 2359304 | tf_op jit(solution)/shard_map/core_pair/ppermute | solution.py:620
  420.1 16.2 %collective-permute-start.41 = (bf16[4,96,768]{2,1,0:T(8,128)(2,1)}, bf16[4,96,768]{2,1,0:T(8,128)(2,1)}, u32[]{:S(2)}, u32[]{:S(2)}) collective-permute-start(bf16[4,96,768]{2,1,0:T(8,128)(2,1)} %fusion.5), channel_id=1, source_target_pairs={{0,4},{4,0},{8,12},{12,8},{16,20},{20,16},{24,28},{28,24},{1,5},{5... | collective-permute-start | bytes 1769480 | tf_op jit(solution)/shard_map/y_att_1_second/ppermute | solution.py:615
  421.9 4.7 collective-permute-start.26
  424.6 2.0 collective-permute-start.27
  433.1 29.8 %collective-permute-start.28 = (bf16[2,4,96,768]{3,2,1,0:T(8,128)(2,1)}, bf16[2,4,96,768]{3,2,1,0:T(8,128)(2,1)S(1)}, u32[]{:S(2)}, u32[]{:S(2)}) collective-permute-start(bf16[2,4,96,768]{3,2,1,0:T(8,128)(2,1)} %get-tuple-element.200), channel_id=1, source_target_pairs={{0,4},{4,0},{8,12},{12,8},{16,20},{20,16},{24,28},{28,24},{1,5},{5... | collective-permute-start | bytes 3538952 | tf_op jit(solution)/shard_map/y_att_0_first/ppermute | solution.py:615
  437.8 8.7 %collective-permute-start.42 = (bf16[96,768]{1,0:T(8,128)(2,1)S(1)}, bf16[96,768]{1,0:T(8,128)(2,1)S(1)}, u32[]{:S(2)}, u32[]{:S(2)}) collective-permute-start(bf16[96,768]{1,0:T(8,128)(2,1)S(1)} %get-tuple-element.362), channel_id=1, source_target_pairs={{0,8},{4,12},{8,16},{12,20},{16,24},{20,28},{24,0},{28,4},{1,9},{5... | collective-permute-start | bytes 442376 | tf_op jit(solution)/shard_map/z_att_1_1/ppermute | solution.py:626
  438.0 13.7 %collective-permute-start.43 = (bf16[96,768]{1,0:T(8,128)(2,1)S(1)}, bf16[96,768]{1,0:T(8,128)(2,1)S(1)}, u32[]{:S(2)}, u32[]{:S(2)}) collective-permute-start(bf16[96,768]{1,0:T(8,128)(2,1)S(1)} %get-tuple-element.364), channel_id=1, source_target_pairs={{0,16},{4,20},{8,24},{12,28},{16,0},{20,4},{24,8},{28,12},{1,17},{... | collective-permute-start | bytes 442376 | tf_op jit(solution)/shard_map/z_att_1_2/ppermute | solution.py:626
  440.9 10.7 %collective-permute-start.44 = (bf16[96,768]{1,0:T(8,128)(2,1)S(1)}, bf16[96,768]{1,0:T(8,128)(2,1)S(1)}, u32[]{:S(2)}, u32[]{:S(2)}) collective-permute-start(bf16[96,768]{1,0:T(8,128)(2,1)S(1)} %get-tuple-element.363), channel_id=1, source_target_pairs={{0,24},{4,28},{8,0},{12,4},{16,8},{20,12},{24,16},{28,20},{1,25},{... | collective-permute-start | bytes 442376 | tf_op jit(solution)/shard_map/z_att_1_3/ppermute | solution.py:626
  442.4 14.5 %collective-permute-start.53 = (bf16[4,96,768]{2,1,0:T(8,128)(2,1)S(1)}, bf16[4,96,768]{2,1,0:T(8,128)(2,1)S(1)}, u32[]{:S(2)}, u32[]{:S(2)}) collective-permute-start(bf16[4,96,768]{2,1,0:T(8,128)(2,1)S(1)} %copy-done.28), channel_id=1, source_target_pairs={{0,2},{1,3},{2,0},{3,1},{4,6},{5,7},{6,4},{7,5},{8,10},{9,11},{10,... | collective-permute-start | bytes 1769480 | tf_op jit(solution)/shard_map/x_down_0_second/ppermute | solution.py:610
  453.0 21.1 %collective-permute-start.45 = (bf16[4,96,768]{2,1,0:T(8,128)(2,1)S(1)}, bf16[4,96,768]{2,1,0:T(8,128)(2,1)S(1)}, u32[]{:S(2)}, u32[]{:S(2)}) collective-permute-start(bf16[4,96,768]{2,1,0:T(8,128)(2,1)S(1)} %copy-done.27), channel_id=1, source_target_pairs={{0,4},{4,0},{8,12},{12,8},{16,20},{20,16},{24,28},{28,24},{1,5},{5... | collective-permute-start | bytes 1769480 | tf_op jit(solution)/shard_map/y_up_0_second/ppermute | solution.py:615
  458.2 19.8 %collective-permute-start.54 = (bf16[96,768]{1,0:T(8,128)(2,1)S(1)}, bf16[96,768]{1,0:T(8,128)(2,1)S(1)}, u32[]{:S(2)}, u32[]{:S(2)}) collective-permute-start(bf16[96,768]{1,0:T(8,128)(2,1)S(1)} %get-tuple-element.350), channel_id=1, source_target_pairs={{0,8},{4,12},{8,16},{12,20},{16,24},{20,28},{24,0},{28,4},{1,9},{5... | collective-permute-start | bytes 442376 | tf_op jit(solution)/shard_map/z_down_0_1/ppermute | solution.py:626
  458.8 19.5 %collective-permute-start.55 = (bf16[96,768]{1,0:T(8,128)(2,1)S(1)}, bf16[96,768]{1,0:T(8,128)(2,1)S(1)}, u32[]{:S(2)}, u32[]{:S(2)}) collective-permute-start(bf16[96,768]{1,0:T(8,128)(2,1)S(1)} %get-tuple-element.352), channel_id=1, source_target_pairs={{0,16},{4,20},{8,24},{12,28},{16,0},{20,4},{24,8},{28,12},{1,17},{... | collective-permute-start | bytes 442376 | tf_op jit(solution)/shard_map/z_down_0_2/ppermute | solution.py:626
  460.1 18.3 %collective-permute-start.56 = (bf16[96,768]{1,0:T(8,128)(2,1)S(1)}, bf16[96,768]{1,0:T(8,128)(2,1)S(1)}, u32[]{:S(2)}, u32[]{:S(2)}) collective-permute-start(bf16[96,768]{1,0:T(8,128)(2,1)S(1)} %get-tuple-element.351), channel_id=1, source_target_pairs={{0,24},{4,28},{8,0},{12,4},{16,8},{20,12},{24,16},{28,20},{1,25},{... | collective-permute-start | bytes 442376 | tf_op jit(solution)/shard_map/z_down_0_3/ppermute | solution.py:626
  463.2 12.5 %collective-permute-start.29 = (f32[4,8,768]{2,1,0:T(8,128)S(1)}, f32[4,8,768]{2,1,0:T(8,128)S(1)}, u32[]{:S(2)}, u32[]{:S(2)}) collective-permute-start(f32[4,8,768]{2,1,0:T(8,128)S(1)} %maximum_add_fusion), channel_id=1, source_target_pairs={{0,1},{1,0},{2,3},{3,2},{4,5},{5,4},{6,7},{7,6},{8,9},{9,8},{10,11... | collective-permute-start | bytes 294920 | tf_op jit(solution)/shard_map/core_pair/ppermute | solution.py:620
  474.3 15.3 %collective-permute-start.46 = (bf16[96,768]{1,0:T(8,128)(2,1)S(1)}, bf16[96,768]{1,0:T(8,128)(2,1)S(1)}, u32[]{:S(2)}, u32[]{:S(2)}) collective-permute-start(bf16[96,768]{1,0:T(8,128)(2,1)S(1)} %get-tuple-element.353), channel_id=1, source_target_pairs={{0,8},{4,12},{8,16},{12,20},{16,24},{20,28},{24,0},{28,4},{1,9},{5... | collective-permute-start | bytes 442376 | tf_op jit(solution)/shard_map/z_up_0_1/ppermute | solution.py:626
  475.7 13.9 %collective-permute-start.47 = (bf16[96,768]{1,0:T(8,128)(2,1)S(1)}, bf16[96,768]{1,0:T(8,128)(2,1)S(1)}, u32[]{:S(2)}, u32[]{:S(2)}) collective-permute-start(bf16[96,768]{1,0:T(8,128)(2,1)S(1)} %get-tuple-element.355), channel_id=1, source_target_pairs={{0,16},{4,20},{8,24},{12,28},{16,0},{20,4},{24,8},{28,12},{1,17},{... | collective-permute-start | bytes 442376 | tf_op jit(solution)/shard_map/z_up_0_2/ppermute | solution.py:626
  478.1 11.6 %collective-permute-start.48 = (bf16[96,768]{1,0:T(8,128)(2,1)S(1)}, bf16[96,768]{1,0:T(8,128)(2,1)S(1)}, u32[]{:S(2)}, u32[]{:S(2)}) collective-permute-start(bf16[96,768]{1,0:T(8,128)(2,1)S(1)} %get-tuple-element.354), channel_id=1, source_target_pairs={{0,24},{4,28},{8,0},{12,4},{16,8},{20,12},{24,16},{28,20},{1,25},{... | collective-permute-start | bytes 442376 | tf_op jit(solution)/shard_map/z_up_0_3/ppermute | solution.py:626
  478.3 4.6 collective-permute-start.30
  483.0 4.7 collective-permute-start.31
  487.7 5.7 %collective-permute-start.32 = (f32[4,8,768]{2,1,0:T(8,128)S(1)}, f32[4,8,768]{2,1,0:T(8,128)S(1)}, u32[]{:S(2)}, u32[]{:S(2)}) collective-permute-start(f32[4,8,768]{2,1,0:T(8,128)S(1)} %add.513), channel_id=1, source_target_pairs={{0,8},{4,12},{8,0},{12,4},{16,24},{20,28},{24,16},{28,20},{1,9},{5... | collective-permute-start | bytes 294920 | tf_op jit(solution)/shard_map/ppermute | solution.py:678
  493.6 5.6 %collective-permute-start.33 = (f32[4,8,768]{2,1,0:T(8,128)S(1)}, f32[4,8,768]{2,1,0:T(8,128)S(1)}, u32[]{:S(2)}, u32[]{:S(2)}) collective-permute-start(f32[4,8,768]{2,1,0:T(8,128)S(1)} %add.514), channel_id=1, source_target_pairs={{0,16},{4,20},{8,24},{12,28},{16,0},{20,4},{24,8},{28,12},{1,17},{... | collective-permute-start | bytes 294920 | tf_op jit(solution)/shard_map/ppermute | solution.py:679
  496.1 10.9 %collective-permute-start.37 = (bf16[4,96,768]{2,1,0:T(8,128)(2,1)S(1)}, bf16[4,96,768]{2,1,0:T(8,128)(2,1)S(1)}, u32[]{:S(2)}, u32[]{:S(2)}) collective-permute-start(bf16[4,96,768]{2,1,0:T(8,128)(2,1)S(1)} %fusion.8), channel_id=1, source_target_pairs={{0,2},{1,3},{2,0},{3,1},{4,6},{5,7},{6,4},{7,5},{8,10},{9,11},{10,... | collective-permute-start | bytes 1769480 | tf_op jit(solution)/shard_map/x_att_0_second/ppermute | solution.py:610
  507.3 7.1 %collective-permute-start.38 = (bf16[96,768]{1,0:T(8,128)(2,1)S(1)}, bf16[96,768]{1,0:T(8,128)(2,1)S(1)}, u32[]{:S(2)}, u32[]{:S(2)}) collective-permute-start(bf16[96,768]{1,0:T(8,128)(2,1)S(1)} %get-tuple-element.359), channel_id=1, source_target_pairs={{0,8},{4,12},{8,16},{12,20},{16,24},{20,28},{24,0},{28,4},{1,9},{5... | collective-permute-start | bytes 442376 | tf_op jit(solution)/shard_map/z_att_0_1/ppermute | solution.py:626
  509.2 8.5 %collective-permute-start.39 = (bf16[96,768]{1,0:T(8,128)(2,1)S(1)}, bf16[96,768]{1,0:T(8,128)(2,1)S(1)}, u32[]{:S(2)}, u32[]{:S(2)}) collective-permute-start(bf16[96,768]{1,0:T(8,128)(2,1)S(1)} %get-tuple-element.361), channel_id=1, source_target_pairs={{0,16},{4,20},{8,24},{12,28},{16,0},{20,4},{24,8},{28,12},{1,17},{... | collective-permute-start | bytes 442376 | tf_op jit(solution)/shard_map/z_att_0_2/ppermute | solution.py:626
  511.3 6.7 %collective-permute-start.40 = (bf16[96,768]{1,0:T(8,128)(2,1)S(1)}, bf16[96,768]{1,0:T(8,128)(2,1)S(1)}, u32[]{:S(2)}, u32[]{:S(2)}) collective-permute-start(bf16[96,768]{1,0:T(8,128)(2,1)S(1)} %get-tuple-element.360), channel_id=1, source_target_pairs={{0,24},{4,28},{8,0},{12,4},{16,8},{20,12},{24,16},{28,20},{1,25},{... | collective-permute-start | bytes 442376 | tf_op jit(solution)/shard_map/z_att_0_3/ppermute | solution.py:626
  (73 other events, 470.8 us)
Sparse Core Ops, SparseCore 0:
  11.0 176.2 all-gather.5

commit v2 on v1

--- a/solution.py
+++ b/solution.py
@@ -76,30 +76,59 @@
     ]
 
 
-def weight_copies(w_ref, held, sems, parts, base):
-    return [
-        pltpu.make_async_copy(
-            w_ref.at[:, part, :, pl.ds(base, SLAB)], held.at[slot], sems.at[slot]
-        )
-        for slot, part in enumerate(parts)
-    ]
-
-
-def projection_copy(w_ref, proj, sem):
-    return pltpu.make_async_copy(w_ref.at[:, 0, :, pl.ds(LAYERS * PACK, DIM)], proj, sem)
+class Copies:
+    def __init__(self, copies):
+        self.copies = copies
+
+    def start(self):
+        for copy in self.copies:
+            copy.start()
+
+    def wait(self):
+        for copy in self.copies:
+            copy.wait()
+
+
+def weight_copies(refs, plan, held, sems, parts, place):
+    kind, base = plan
+    groups = []
+    for slot, part in enumerate(parts):
+        copies = []
+        if kind == "whole":
+            source = refs[0].at[:, :, part, :, pl.ds(base, SLAB)]
+            copies.append(pltpu.make_async_copy(source, held.at[slot], sems.at[slot, 0]))
+        else:
+            c_rel, x_rel = divmod(slot, 2)
+            for y_rel in range(2):
+                outer, inner = (x_rel, y_rel) if kind == "x_last" else (y_rel, x_rel)
+                for back in range(4):
+                    copies.append(
+                        pltpu.make_async_copy(
+                            refs[2 * c_rel + outer].at[inner, back],
+                            held.at[slot, (place[3] - back) & 3, place[2] ^ y_rel],
+                            sems.at[slot, 4 * y_rel + back],
+                        )
+                    )
+        groups.append(Copies(copies))
+    return groups
+
+
+def projection_copy(w_ref, proj, sem, base):
+    return pltpu.make_async_copy(w_ref.at[:, :, 0, :, pl.ds(base, DIM)], proj, sem)
 
 
 def stored(refs, slot, value):
     refs[slot // 2 if len(refs) > 1 else 0][slot % 2 if len(refs) > 1 else slot] = value
 
 
-def attention_kernel(base, split, place, *refs):
-    x_ref, mask_ref, pair_ref, norm_ref, w_ref = refs[:5]
-    first_ref, low_t_ref, packed_ref, chances_ref, normal_ref, factor_ref, first_t_ref = refs[5:12]
-    mixture_refs = refs[12:-2]
+def attention_kernel(plan, count, split, place, *refs):
+    x_ref, mask_ref, pair_ref, norm_ref = refs[:4]
+    w_refs, refs = refs[4 : 4 + count], refs[4 + count :]
+    first_ref, low_t_ref, packed_ref, chances_ref, normal_ref, factor_ref, first_t_ref = refs[:7]
+    mixture_refs = refs[7:-2]
     held, sems = refs[-2:]
     parts = part_order(place, split)
-    copies = weight_copies(w_ref, held, sems, parts, base)
+    copies = weight_copies(w_refs, plan, held, sems, parts, place)
     for copy in copies:
         copy.start()
     hidden = x_ref[...]
@@ -109,8 +138,8 @@
     attended = jnp.zeros((ROWS, WIDTH), F32)
     for slot in range(PARTS):
         copies[slot].wait()
-        weight = held[slot, :, :, :HELD].reshape(WIDTH, HELD)
-        packed = (nn(low, weight) + pair_ref[parts[slot]]).astype(BF)
+        weight = held[slot, :, :, :, :HELD].reshape(WIDTH, HELD)
+        packed = (nn(low, weight) + pair_ref[slot]).astype(BF)
         packed_ref[slot] = packed
         values_t = packed[:, 2 * OWN : 3 * OWN].T
         mixed = [jnp.zeros((HEAD, ROWS), F32)]
@@ -125,7 +154,7 @@
         mixture = jnp.concatenate(mixed, 0).astype(BF).T
         stored(mixture_refs, slot, mixture)
         attended = attended + nt(
-            mixture, held[slot, :, :, SLAB - ROWS :].reshape(WIDTH, ROWS)
+            mixture, held[slot, :, :, :, SLAB - ROWS :].reshape(WIDTH, ROWS)
         )
     normal, factor = norm_forward(hidden + attended + norm_ref[0:1])
     normal_ref[...] = normal
@@ -135,31 +164,33 @@
     first_t_ref[...] = first.astype(BF).T
 
 
-def mlp_kernel(base, top, split, place, *refs):
-    first_ref, up_bias_ref, norm_ref, w_ref = refs[:4]
-    out_ref, slope_ref, normal_ref, factor_ref = refs[4:8]
-    act_refs = refs[8 : 10 if split else 9]
-    refs = refs[8 + len(act_refs) :]
+def mlp_kernel(up_plan, down_plan, proj_base, count, top, split, place, *refs):
+    first_ref, up_bias_ref, norm_ref = refs[:3]
+    up_refs, down_refs = refs[3 : 3 + count], refs[3 + count : 3 + 2 * count]
+    refs = refs[3 + 2 * count :]
+    out_ref, slope_ref, normal_ref, factor_ref = refs[:4]
+    act_refs = refs[4 : 6 if split else 5]
+    refs = refs[4 + len(act_refs) :]
     if top:
         emb_ref, unit_ref, scale_ref, top_t_ref = refs[:4]
         refs = refs[4:]
     up_held, down_held, up_sems, down_sems = refs[:4]
     parts = part_order(place, split)
-    ups = weight_copies(w_ref, up_held, up_sems, parts, base + SLAB)
-    downs = weight_copies(w_ref, down_held, down_sems, parts, base + 2 * SLAB)
+    ups = weight_copies(up_refs, up_plan, up_held, up_sems, parts, place)
+    downs = weight_copies(down_refs, down_plan, down_held, down_sems, parts, place)
     for slot in range(PARTS):
         ups[slot].start()
         downs[slot].start()
     if top:
         proj, proj_sem = refs[4:]
-        proj_load = projection_copy(w_ref, proj, proj_sem)
+        proj_load = projection_copy(up_refs[0], proj, proj_sem, proj_base)
         proj_load.start()
     first = first_ref[...]
     first_low = first.astype(BF)
     spread = jnp.zeros((ROWS, WIDTH), F32)
     for slot in range(PARTS):
         ups[slot].wait()
-        pre_act = nn(first_low, up_held[slot].reshape(WIDTH, SLAB)) + up_bias_ref[parts[slot]]
+        pre_act = nn(first_low, up_held[slot].reshape(WIDTH, SLAB)) + up_bias_ref[slot]
         chance = 0.5 * (1.0 + lax.erf(pre_act * 0.7071067811865476))
         act = (pre_act * chance).astype(BF)
         stored(act_refs, slot, act)
@@ -185,27 +216,29 @@
         scale_ref[...] = jnp.broadcast_to(scale, scale_ref.shape)
 
 
-def mlp_pull_kernel(base, top, split, place, *refs):
+def mlp_pull_kernel(up_plan, down_plan, proj_base, count, top, split, place, *refs):
     if top:
         grad_emb_ref, unit_ref, scale_ref, top_t_ref = refs[:4]
         refs = refs[4:]
     else:
         dy_ref = refs[0]
         refs = refs[1:]
-    slope_ref, normal_ref, factor_ref, norm_ref, w_ref = refs[:5]
-    grad_ref, sum_ref, low_t_ref = refs[5:8]
-    pre_refs = refs[8 : 10 if split else 9]
-    refs = refs[8 + len(pre_refs) :]
+    slope_ref, normal_ref, factor_ref, norm_ref = refs[:4]
+    up_refs, down_refs = refs[4 : 4 + count], refs[4 + count : 4 + 2 * count]
+    refs = refs[4 + 2 * count :]
+    grad_ref, sum_ref, low_t_ref = refs[:3]
+    pre_refs = refs[3 : 5 if split else 4]
+    refs = refs[3 + len(pre_refs) :]
     if top:
         proj_grad_ref = refs[0]
         refs = refs[1:]
     up_held, down_held, up_sems, down_sems = refs[:4]
     parts = part_order(place, split)
-    ups = weight_copies(w_ref, up_held, up_sems, parts, base + SLAB)
-    downs = weight_copies(w_ref, down_held, down_sems, parts, base + 2 * SLAB)
+    ups = weight_copies(up_refs, up_plan, up_held, up_sems, parts, place)
+    downs = weight_copies(down_refs, down_plan, down_held, down_sems, parts, place)
     if top:
         proj, proj_sem = refs[4:]
-        proj_load = projection_copy(w_ref, proj, proj_sem)
+        proj_load = projection_copy(up_refs[0], proj, proj_sem, proj_base)
         proj_load.start()
     order = (2, 3, 0, 1) if split else (0, 1, 2, 3)
     for slot in order:
@@ -242,13 +275,14 @@
     grad_ref[...] = grad_first
 
 
-def attention_pull_kernel(base, split, place, *refs):
-    grad_first_ref, packed_ref, chances_ref, normal_ref, factor_ref, norm_ref, w_ref = refs[:7]
-    dx_ref, sum_ref, low_t_ref = refs[7:10]
-    packed_grad_refs = refs[10:-2]
+def attention_pull_kernel(plan, count, split, place, *refs):
+    grad_first_ref, packed_ref, chances_ref, normal_ref, factor_ref, norm_ref = refs[:6]
+    w_refs, refs = refs[6 : 6 + count], refs[6 + count :]
+    dx_ref, sum_ref, low_t_ref = refs[:3]
+    packed_grad_refs = refs[3:-2]
     held, sems = refs[-2:]
     parts = part_order(place, split)
-    copies = weight_copies(w_ref, held, sems, parts, base)
+    copies = weight_copies(w_refs, plan, held, sems, parts, place)
     order = (2, 3, 0, 1) if split else (0, 1, 2, 3)
     for slot in order:
         copies[slot].start()
@@ -264,7 +298,7 @@
     grad_input = grad_one
     for slot in order:
         copies[slot].wait()
-        grad_mix = nn(low, held[slot, :, :, SLAB - ROWS :].reshape(WIDTH, ROWS)).astype(BF)
+        grad_mix = nn(low, held[slot, :, :, :, SLAB - ROWS :].reshape(WIDTH, ROWS)).astype(BF)
         packed = packed_ref[slot]
         keys_t = packed[:, OWN : 2 * OWN].T
         grad_queries, grad_keys, grad_values = [], [], []
@@ -422,16 +456,14 @@
     return [shaped((PARTS, *shape), kind)]
 
 
-def held_scratch(gathered, count):
-    depth = (gathered.shape[0], gathered.shape[2])
-    return [pltpu.VMEM((PARTS, *depth, SLAB), BF)] * count + [
-        pltpu.SemaphoreType.DMA((PARTS,))
+def held_scratch(fold, count):
+    return [pltpu.VMEM((PARTS, *fold, SLAB), BF)] * count + [
+        pltpu.SemaphoreType.DMA((PARTS, 8))
     ] * count
 
 
-def projection_scratch(gathered):
-    depth = (gathered.shape[0], gathered.shape[2])
-    return [pltpu.VMEM((*depth, DIM), BF), pltpu.SemaphoreType.DMA]
+def projection_scratch(fold):
+    return [pltpu.VMEM((*fold, DIM), BF), pltpu.SemaphoreType.DMA]
 
 
 def call(kernel, name, micros, place, args, outs, scratch, in_hbm=(), out_hbm=()):
@@ -448,7 +480,8 @@
     )(place, *args)
 
 
-def run_attention(layer_at, place, hidden, mask, pair_rows, norms, gathered, split):
+def run_attention(layer_at, place, hidden, mask, pair_rows, norms, weights, split):
+    arrays, plan = weights["att"]
     outs = [
         shaped((ROWS, WIDTH), F32),
         shaped((WIDTH, ROWS), BF),
@@ -458,27 +491,30 @@
         shaped((ROWS, DIM), F32),
         shaped((WIDTH, ROWS), BF),
     ] + sided(split, (ROWS, ROWS), BF)
+    args = [hidden, mask, pair_rows, norms, *arrays]
     return call(
-        functools.partial(attention_kernel, layer_at * PACK, split),
+        functools.partial(attention_kernel, plan, len(arrays), split),
         f"attention_{layer_at}",
         9,
         place,
-        [hidden, mask, pair_rows, norms, gathered],
+        args,
         outs,
-        held_scratch(gathered, 1),
-        in_hbm=(4,),
-    )
-
-
-def run_mlp(layer_at, place, first, up_rows, norms, gathered, split):
+        held_scratch(weights["fold"], 1),
+        in_hbm=range(4, len(args)),
+    )
+
+
+def run_mlp(layer_at, place, first, up_rows, norms, weights, split):
     top = layer_at == LAYERS - 1
+    ups, up_plan = weights["up"]
+    downs, down_plan = weights["down"]
     outs = [
         shaped((ROWS, WIDTH), F32),
         shaped((PARTS, ROWS, SLAB), BF),
         shaped((ROWS, WIDTH), F32),
         shaped((ROWS, DIM), F32),
     ] + sided(split, (ROWS, SLAB), BF)
-    scratch = held_scratch(gathered, 2)
+    scratch = held_scratch(weights["fold"], 2)
     if top:
         outs += [
             shaped((ROWS, DIM), BF),
@@ -486,59 +522,69 @@
             shaped((ROWS, DIM), F32),
             shaped((WIDTH, ROWS), BF),
         ]
-        scratch += projection_scratch(gathered)
+        scratch += projection_scratch(weights["fold"])
+    args = [first, up_rows, norms, *ups, *downs]
     return call(
-        functools.partial(mlp_kernel, layer_at * PACK, top, split),
+        functools.partial(
+            mlp_kernel, up_plan, down_plan, weights.get("proj"), len(ups), top, split
+        ),
         f"mlp_{layer_at}",
         9,
         place,
-        [first, up_rows, norms, gathered],
+        args,
         outs,
         scratch,
-        in_hbm=(3,),
-    )
-
-
-def run_mlp_pull(layer_at, place, upstream, saved, norms, gathered, split):
+        in_hbm=range(3, len(args)),
+    )
+
+
+def run_mlp_pull(layer_at, place, upstream, saved, norms, weights, split):
     top = layer_at == LAYERS - 1
+    ups, up_plan = weights["up"]
+    downs, down_plan = weights["down"]
     outs = [
         shaped((ROWS, WIDTH), F32),
         shaped((8, WIDTH), F32),
         shaped((WIDTH, ROWS), BF),
     ] + sided(split, (ROWS, SLAB), BF)
-    scratch = held_scratch(gathered, 2)
+    scratch = held_scratch(weights["fold"], 2)
     if top:
         outs += [shaped((WIDTH, DIM), F32)]
-        scratch += projection_scratch(gathered)
-    args = [*upstream, *saved, norms, gathered]
+        scratch += projection_scratch(weights["fold"])
+    inputs = [*upstream, *saved, norms]
+    args = [*inputs, *ups, *downs]
     return call(
-        functools.partial(mlp_pull_kernel, layer_at * PACK, top, split),
+        functools.partial(
+            mlp_pull_kernel, up_plan, down_plan, weights.get("proj"), len(ups), top, split
+        ),
         f"pull_mlp_{layer_at}",
         8,
         place,
         args,
         outs,
         scratch,
-        in_hbm=(len(args) - 1,),
-    )
-
-
-def run_attention_pull(layer_at, place, grad_first, saved, norms, gathered, split):
+        in_hbm=range(len(inputs), len(args)),
+    )
+
+
+def run_attention_pull(layer_at, place, grad_first, saved, norms, weights, split):
+    arrays, plan = weights["att"]
     outs = [
         shaped((ROWS, WIDTH), F32),
         shaped((8, WIDTH), F32),
         shaped((WIDTH, ROWS), BF),
     ] + sided(split, (ROWS, SLAB), BF)
-    args = [grad_first, *saved, norms, gathered]
+    inputs = [grad_first, *saved, norms]
+    args = [*inputs, *arrays]
     return call(
-        functools.partial(attention_pull_kernel, layer_at * PACK, split),
+        functools.partial(attention_pull_kernel, plan, len(arrays), split),
         f"pull_attention_{layer_at}",
         10,
         place,
         args,
         outs,
-        held_scratch(gathered, 1),
-        in_hbm=(len(args) - 1,),
+        held_scratch(weights["fold"], 1),
+        in_hbm=range(len(inputs), len(args)),
     )
 
 
@@ -753,13 +799,52 @@
     return (moment_new, second_new, -LEARN_RATE * (rising / (spread + ADAM_EPS) + decay * master))
 
 
-def pack_weights(qkv, out, up, down, proj):
-    pieces = []
-    for layer_at in range(LAYERS):
-        pieces += [qkv[layer_at, 0], qkv[layer_at, 1], qkv[layer_at, 2]]
-        pieces += [out[layer_at].T, up[layer_at], down[layer_at].T]
-    pieces.append(proj)
+def joined(*pieces):
     return jnp.concatenate([piece.astype(BF) for piece in pieces], 1)
+
+
+def attention_shard(qkv, out):
+    return joined(qkv[0], qkv[1], qkv[2], out.T)
+
+
+class Gathering:
+    def __init__(self, name, shard, x_last):
+        self.name = name
+        self.shard = shard
+        self.plan = ("x_last" if x_last else "y_last", 0)
+        self.first, self.second = (over_y, over_x) if x_last else (over_x, over_y)
+
+    def column(self):
+        arrived = [along_z(self.shard, step, self.name) for step in range(1, 4)]
+        self.held = jnp.stack([self.shard, *arrived])
+
+    def plane(self):
+        self.held = jnp.stack([self.held, self.first(self.held, self.name + "_first")])
+
+    def cross(self):
+        self.other = self.second(self.held, self.name + "_second")
+
+    def all(self):
+        pairs = [over_core(self.held, self.name), over_core(self.other, self.name)]
+        return [self.held, self.other, *pairs], self.plan
+
+
+def gather_whole(shard, devices):
+    rows_each = shard.shape[0]
+    value = lax.all_gather(shard, BOTH, axis=0, tiled=False)
+    if devices == 8:
+        return value.reshape(4, 2, PARTS, rows_each, -1)
+    value = value.reshape(devices, PARTS, rows_each, -1)
+    return jnp.transpose(value, (1, 0, 2, 3)).reshape(1, 1, PARTS, WIDTH, -1)
+
+
+def whole_weights(value):
+    return {
+        "att": ([value], ("whole", 0)),
+        "up": ([value], ("whole", SLAB)),
+        "down": ([value], ("whole", 2 * SLAB)),
+        "proj": PACK,
+    }
 
 
 def unpack_grads(att_list, up_list, down_list):
@@ -841,26 +926,58 @@
     last = PARTS - 1
     is_query = tensor_at == last
     rows_each = WIDTH // devices
-    pack = pack_weights(qkv_weight, out_weight, up_weight, down_weight, projection)
-    gathered = lax.all_gather(pack, BOTH, axis=0, tiled=False)
-    gathered = gathered.reshape(devices, PARTS, rows_each, -1)
     split = devices == 8
-    if not split:
-        gathered = jnp.transpose(gathered, (1, 0, 2, 3)).reshape(1, PARTS, WIDTH, -1)
-    small = jnp.concatenate([bias_pair.reshape(-1), bias_up.reshape(-1)])
-    small_all = lax.all_gather(small, "tensor", axis=0, tiled=False)
-    pair_all = small_all[:, : LAYERS * 2 * OWN].reshape(PARTS, LAYERS, 2, OWN)
-    up_all = small_all[:, LAYERS * 2 * OWN :].reshape(PARTS, LAYERS, 1, SLAB)
-    pair_rows = jnp.concatenate(
+    pair_own = jnp.concatenate(
         [
-            pair_all[:, :, 0],
-            jnp.zeros((PARTS, LAYERS, OWN), F32),
-            pair_all[:, :, 1],
-            jnp.zeros((PARTS, LAYERS, HELD - 3 * OWN), F32),
+            bias_pair[:, 0],
+            jnp.zeros((LAYERS, OWN), F32),
+            bias_pair[:, 1],
+            jnp.zeros((LAYERS, HELD - 3 * OWN), F32),
         ],
         -1,
-    )[:, :, None, :]
-
+    )
+    small = jnp.concatenate([pair_own, bias_up], -1)
+    if split:
+        crossed = over_x(small, "biases")
+        small_all = [small, crossed, over_core(small, "biases"), over_core(crossed, "biases")]
+        small_all = jnp.stack(small_all)
+    else:
+        small_all = lax.all_gather(small, "tensor", axis=0, tiled=False)
+
+    shards = [
+        (
+            attention_shard(qkv_weight[at], out_weight[at]),
+            up_weight[at].astype(BF),
+            down_weight[at].T.astype(BF),
+        )
+        for at in range(LAYERS)
+    ]
+    if split:
+        last_layer = whole_weights(gather_whole(joined(*shards[1], projection), devices))
+        att = Gathering("att_0", shards[0][0], True)
+        up = Gathering("up_0", shards[0][1], False)
+        down = Gathering("down_0", shards[0][2], True)
+        att.column()
+        att.held, up.shard, down.shard, small_all = tied(
+            att.held, up.shard, down.shard, small_all
+        )
+        att.plane()
+        up.column()
+        down.column()
+        up.plane()
+        down.plane()
+        att.cross()
+        up.cross()
+        down.cross()
+        first_layer = {"att": att.all()}
+    else:
+        first_layer = whole_weights(gather_whole(joined(*shards[0]), devices))
+        last_layer = whole_weights(gather_whole(joined(*shards[1], projection), devices))
+    weights = [first_layer, last_layer]
+    for layer in weights:
+        layer["fold"] = (4, 2, rows_each) if split else (1, 1, WIDTH)
+    pair_rows = small_all[:, :, None, :HELD]
+    up_all = small_all[:, :, None, HELD:]
     passage_at = jnp.minimum(tensor_at, last - 1)
     own_passage = lax.dynamic_slice_in_dim(passage_tokens, passage_at * PLEN, PLEN, 0)
     hidden = jnp.where(is_query, query_tokens, own_passage)
@@ -889,13 +1006,18 @@
             mask,
             pair_rows[:, layer_at],
             norm_terms[layer_at],
-            gathered,
+            weights[layer_at],
             split,
         )
         first, x_t, packed, chances, normal_one, factor_one, first_t = outs[:7]
+        if split and layer_at == 0:
+            first, up.held, up.other, down.held, down.other = tied(
+                first, up.held, up.other, down.held, down.other
+            )
+            weights[0].update(up=up.all(), down=down.all())
         mixtures = sides_of(outs[7], outs[-1])
         outs = run_mlp(
-            layer_at, place, first, up_all[:, layer_at], norm_terms[layer_at], gathered, split
+            layer_at, place, first, up_all[:, layer_at], norm_terms[layer_at], weights[layer_at], split
         )
         hidden, slope, normal_two, factor_two = outs[:4]
         acts = sides_of(outs[4], outs[5 if split else 4])
@@ -948,7 +1070,7 @@
     def mlp_pull(layer_at, upstream):
         saved = saved_list[layer_at]
         outs = run_mlp_pull(
-            layer_at, place, upstream, saved["mlp"], norm_terms[layer_at], gathered, split
+            layer_at, place, upstream, saved["mlp"], norm_terms[layer_at], weights[layer_at], split
         )
         grad_first, mlp_sums[layer_at], low_t = outs[:3]
         groups = [
@@ -969,7 +1091,7 @@
             grad_first,
             saved["attention"],
             norm_terms[layer_at],
-            gathered,
+            weights[layer_at],
             split,
         )
         dx, attention_sums[layer_at], low_t = outs[:3]

time: 542 us -> 510 us (0.941); the launches traced: 532 us -> 506 us
  waiting for transfers between devices: 244 us -> 153 us
  starting transfers between devices: 78.6 us -> 140 us
  blocking collectives: 11.6 us -> 5.31 us
    all_gather x1, waiting for transfers between devices: 163 us -> 0.02 us  [gather_whole(): value = lax.all_gather(shard, BOTH, axis=0, tiled=False)]
    ppermute x7 -> x11, waiting for transfers between devices: 9.75 us -> 57.9 us  [over_x(): return lax.ppermute(value, 'tensor', X_SWAP)]
    ppermute x18 -> x27, starting transfers between devices: 25.3 us -> 71 us  [along_z(): return lax.ppermute(value, 'dp', pairs)]
    ppermute x18 -> x27, waiting for transfers between devices: 23.7 us -> 36.4 us  [along_z(): return lax.ppermute(value, 'dp', pairs)]
    all_to_all x1, starting transfers between devices: 3.68 us -> 13 us  [body(): lax.all_to_all(jnp.broadcast_to(embedding[None], (devices, ROWS, DIM)), '...]
    ppermute x18 -> x26, waiting for transfers between devices: 6.86 us -> 14.8 us  [over_core(): return lax.ppermute(value, 'tensor', CORE_SWAP)]
    all_gather x1 -> x0, blocking collectives: 6.31 us -> none  [body(): small_all = lax.all_gather(small, 'tensor', axis=0, tiled=False)]
    ppermute x7 -> x10, waiting for transfers between devices: 14.5 us -> 18.9 us  [over_y(): return lax.ppermute(value, 'dp', Y_SWAP)]
  transfers between devices with their start and end apart: 64 -> 88, of which waited for: 26 -> 37; matrix products, arithmetic and copies ran while one was open for 9% -> 10% of each run, Pallas kernels for 11% -> 16%
where the time goes in v2:
time: 510 us; the launch traced here: 506 us
  waiting for transfers between devices  153 us (30%)
  starting transfers between devices  140 us (27%)
  Pallas kernels  119 us (23%)
  other arithmetic  41.6 us (8%)
  local copies, waits for them, and re-layouts  28.5 us (6%)
  between operations  18.2 us (4%)
  blocking collectives  5.31 us (1%)
    pallas_call x12, Pallas kernels, call(): pl.pallas_call(kernel, out_shape=outs, in_specs=[smem_spec()] + [any_spec...  111 us
    ppermute x27, starting transfers between devices, along_z(): return lax.ppermute(value, 'dp', pairs)  71 us
    ppermute x11, waiting for transfers between devices, over_x(): return lax.ppermute(value, 'tensor', X_SWAP)  57.9 us
    ppermute x27, waiting for transfers between devices, along_z(): return lax.ppermute(value, 'dp', pairs)  36.4 us
    ppermute x26, starting transfers between devices, over_core(): return lax.ppermute(value, 'tensor', CORE_SWAP)  24.1 us
    ppermute x10, waiting for transfers between devices, over_y(): return lax.ppermute(value, 'dp', Y_SWAP)  18.9 us
    unnamed x188, local copies, waits for them, and re-layouts  18.3 us
    ppermute x26, waiting for transfers between devices, over_core(): return lax.ppermute(value, 'tensor', CORE_SWAP)  14.8 us
  transfers between devices with their start and end apart: 88, of which 37 were waited for; matrix products, arithmetic and copies ran while one was open for 10% of the time, Pallas kernels for 16%

profile of v2, /device:TPU:0, one launch (start us, length us, event | category | flops | bytes accessed | tf_op | source)
XLA Modules:
  0.0 506.2 jit_solution(9033685535844734274)
XLA Ops:
  10.8 2.9 collective-permute-start.3
  15.5 2.6 collective-permute-start.1
  22.6 5.8 %collective-permute-done.1 = bf16[96,768]{1,0:T(8,128)(2,1)S(1)} collective-permute-done((bf16[96,768]{1,0:T(8,128)(2,1)S(1)}, bf16[96,768]{1,0:T(8,128)(2,1)S(1)}, u32[]{:S(2)}, u32[]{:S(2)}) %collective-permute-start.1) | collective-permute-done | bytes 147488 | tf_op jit(solution)/shard_map/z_att_0_2/ppermute | solution.py:672
  28.5 1.7 collective-permute-start.6
  30.2 12.2 %collective-permute-start.15 = (bf16[96,768]{1,0:T(8,128)(2,1)S(1)}, bf16[96,768]{1,0:T(8,128)(2,1)S(1)}, u32[]{:S(2)}, u32[]{:S(2)}) collective-permute-start(bf16[96,768]{1,0:T(8,128)(2,1)S(1)} %get-tuple-element.136), channel_id=1, source_target_pairs={{0,8},{4,12},{8,16},{12,20},{16,24},{20,28},{24,0},{28,4},{1,9},{5... | collective-permute-start | bytes 442376 | tf_op jit(solution)/shard_map/z_down_0_1/ppermute | solution.py:672
  45.0 13.0 %collective-permute-start.10 = (bf16[96,768]{1,0:T(8,128)(2,1)S(1)}, bf16[96,768]{1,0:T(8,128)(2,1)S(1)}, u32[]{:S(2)}, u32[]{:S(2)}) collective-permute-start(bf16[96,768]{1,0:T(8,128)(2,1)S(1)} %get-tuple-element.135), channel_id=1, source_target_pairs={{0,8},{4,12},{8,16},{12,20},{16,24},{20,28},{24,0},{28,4},{1,9},{5... | collective-permute-start | bytes 442376 | tf_op jit(solution)/shard_map/z_up_0_1/ppermute | solution.py:672
  57.9 12.3 %collective-permute-start.12 = (bf16[96,768]{1,0:T(8,128)(2,1)S(1)}, bf16[96,768]{1,0:T(8,128)(2,1)S(1)}, u32[]{:S(2)}, u32[]{:S(2)}) collective-permute-start(bf16[96,768]{1,0:T(8,128)(2,1)S(1)} %get-tuple-element.135), channel_id=1, source_target_pairs={{0,24},{4,28},{8,0},{12,4},{16,8},{20,12},{24,16},{28,20},{1,25},{... | collective-permute-start | bytes 442376 | tf_op jit(solution)/shard_map/z_up_0_3/ppermute | solution.py:672
  70.5 6.0 %collective-permute-done.11 = bf16[96,768]{1,0:T(8,128)(2,1)S(1)} collective-permute-done((bf16[96,768]{1,0:T(8,128)(2,1)S(1)}, bf16[96,768]{1,0:T(8,128)(2,1)S(1)}, u32[]{:S(2)}, u32[]{:S(2)}) %collective-permute-start.11) | collective-permute-done | bytes 147488 | tf_op jit(solution)/shard_map/z_up_0_2/ppermute | solution.py:672
  77.9 2.5 collective-permute-done.18
  81.7 22.8 %collective-permute-done.13 = bf16[4,96,768]{2,1,0:T(8,128)(2,1)S(1)} collective-permute-done((bf16[4,96,768]{2,1,0:T(8,128)(2,1)S(1)}, bf16[4,96,768]{2,1,0:T(8,128)(2,1)S(1)}, u32[]{:S(2)}, u32[]{:S(2)}) %collective-permute-start.13) | collective-permute-done | bytes 589856 | tf_op jit(solution)/shard_map/x_up_0_first/ppermute | solution.py:656
  110.8 2.1 dynamic-slice_select_fusion.refs_0_
  113.6 10.9 %attention_0.1 = (f32[256,768]{1,0:T(8,128)}, bf16[768,256]{1,0:T(8,128)(2,1)}, bf16[4,256,640]{2,1,0:T(8,128)(2,1)}, bf16[12,256,256]{2,1,0:T(8,128)(2,1)}, f32...) custom-call(s32[4]{0:T(128)} %pad_add_fusion.place, ...), custom_call_target="tpu_custom_call" | custom-call | flops 9000000 | bytes 27000 | tf_op jit(solution)/shard_map/attention_0/pallas_call | solution.py:470
  124.6 24.6 %collective-permute-done.19.refs_8_.refs_10_ = bf16[2,4,96,768]{3,2,1,0:T(8,128)(2,1)} collective-permute-done((bf16[2,4,96,768]{3,2,1,0:T(8,128)(2,1)S(1)}, bf16[2,4,96,768]{3,2,1,0:T(8,128)(2,1)}, u32[]{:S(2)}, u32[]{:S(2)}) %collective-permute-start.19) | collective-permute-done | bytes 1179680 | tf_op jit(solution)/shard_map/x_down_0_second/ppermute | solution.py:656
  153.0 2.3 collective-permute-done.21.refs_6_.refs_8_
  156.4 1.7 collective-permute-done.23.refs_10_.refs_12_
  159.2 9.9 %mlp_0.1 = (f32[256,768]{1,0:T(8,128)}, bf16[4,256,768]{2,1,0:T(8,128)(2,1)}, f32[256,768]{1,0:T(8,128)}, f32[256,128]{1,0:T(8,128)}, bf16[2,256,768]{2,1,0:T(8,128)(2,1)}, /*index=5*/bf16[2,256,768]{2,1,0:T(8,128)(2,1)}) custom-call(s32[4]{0:T(128)} %pad_add_fusion.place, f32[256,768]{1,0:T(8,128)} %get-tuple-element.137.refs_0_, ...), custom_call_target="tpu_custom_call" | custom-call | flops 9000000 | bytes 27000 | tf_op jit(solution)/shard_map/mlp_0/pallas_call | solution.py:470
  169.1 11.0 %attention_1.1 = (f32[256,768]{1,0:T(8,128)}, bf16[768,256]{1,0:T(8,128)(2,1)}, bf16[4,256,640]{2,1,0:T(8,128)(2,1)}, bf16[12,256,256]{2,1,0:T(8,128)(2,1)}, f32...) custom-call(s32[4]{0:T(128)} %pad_add_fusion.place, ...), custom_call_target="tpu_custom_call" | custom-call | flops 9000000 | bytes 27000 | tf_op jit(solution)/shard_map/attention_1/pallas_call | solution.py:470
  180.1 10.5 %mlp_1.1 = (f32[256,768]{1,0:T(8,128)}, bf16[4,256,768]{2,1,0:T(8,128)(2,1)}, f32[256,768]{1,0:T(8,128)}, f32[256,128]{1,0:T(8,128)}, bf16[2,256,768]{2,1,0:T(8,...) custom-call(s32[4]{0:T(128)} %pad_add_fusion.place, ...), custom_call_target="tpu_custom_call" | custom-call | flops 9000000 | bytes 27000 | tf_op jit(solution)/shard_map/mlp_1/pallas_call | solution.py:470
  190.7 1.8 broadcast_in_dim.55
  192.5 13.0 %all-to-all-start = ((bf16[8,256,128]{2,1,0:T(8,128)(2,1)}), bf16[8,256,128]{2,1,0:T(8,128)(2,1)S(1)}, u32[]{:S(2)}, u32[]{:S(2)}) async-start(bf16[8,256,128]{2,1,0:T(8,128)(2,1)} %broadcast_in_dim.55), calls=%async_computation | async-start | bytes 1048576 | tf_op jit(solution)/shard_map/all_to_all | solution.py:1036
  209.7 3.9 collective-permute-done.26
  214.3 6.2 %all-to-all-done.passages_ref = bf16[8,256,128]{2,1,0:T(8,128)(2,1)S(1)} async-done(((bf16[8,256,128]{2,1,0:T(8,128)(2,1)}), bf16[8,256,128]{2,1,0:T(8,128)(2,1)S(1)}, u32[]{:S(2)}, u32[]{:S(2)}) %all-to-all-start) | async-done | bytes 524320 | tf_op jit(solution)/shard_map/all_to_all | solution.py:1036
  221.3 4.0 scores.1
  225.3 5.3 %all-gather.1 = f32[32,8]{1,0:T(8,128)S(1)} all-gather(f32[8,8]{1,0:T(8,128)} %bitcast.376), channel_id=3, replica_groups=mesh['dp'=8,'tensor'=4] {'tensor'}, dimensions={0}, use_global_device_ids=true | all-gather | bytes 1280 | tf_op jit(solution)/shard_map/all_gather | solution.py:1046
  232.7 4.0 score_pulls.1
  236.7 3.6 all-to-all-start.1
  240.6 2.3 collective-permute-start.27
  244.4 10.9 %all-to-all-done.1 = bf16[8,256,128]{2,1,0:T(8,128)(2,1)S(1)} async-done(((bf16[8,256,128]{2,1,0:T(8,128)(2,1)}), bf16[8,256,128]{2,1,0:T(8,128)(2,1)S(1)}, u32[]{:S(2)}, u32[]{:S(2)}) %all-to-all-start.1) | async-done | bytes 524320 | tf_op jit(solution)/shard_map/all_to_all | solution.py:1061
  256.1 9.7 %pull_mlp_1.1 = (f32[256,768]{1,0:T(8,128)}, f32[8,768]{1,0:T(8,128)}, bf16[768,256]{1,0:T(8,128)(2,1)}, bf16[2,256,768]{2,1,0:T(8,128)(2,1)}, bf16[2,256,768]{2,1,0:T(8,128)(2,1)}, /*index=5*/f32[768,128]{1,0:T(8,128)}) custom-call(s32[4]{0:T(128)} %pad_add_fusion.place, f32[256,128]{1,0:T(8,128)} %add_select_fusion.refs_0_, ...), custom_call_target="tpu_custom_call" | custom-call | flops 8000000 | bytes 24000 | tf_op jit(solution)/shard_map/pull_mlp_1/pallas_call | solution.py:470
  266.9 2.1 collective-permute-done.30.refs_1_
  271.1 6.7 %grad_mlp_1.1 = (bf16[2,4,96,768]{3,2,1,0:T(8,128)(2,1)}, bf16[2,4,96,768]{3,2,1,0:T(8,128)(2,1)}, bf16[2,4,96,896]{3,2,1,0:T(8,128)(2,1)}, bf16[2,4,96,896]{3,2,1,0:T(8,128)(2,1)}) custom-call(s32[4]{0:T(128)} %pad_add_fusion.place, bf16[768,256]{1,0:T(8,128)(2,1)} %get-tuple-element.157.refs_0_, bf16[768,256]{1,0:T(8,128)(2,1)} %copy-done.43, ...), custom_call_target="tpu_custom_call" | custom-call | flops 8000000 | bytes 24000 | tf_op jit(solution)/shard_map/grad_mlp_1/pallas_call | solution.py:470
  279.9 13.1 %pull_attention_1.1 = (f32[256,768]{1,0:T(8,128)}, f32[8,768]{1,0:T(8,128)}, bf16[768,256]{1,0:T(8,128)(2,1)}, bf16[2,256,768]{2,1,0:T(8,128)(2,1)}, bf16[2,256,768]{2,1,0:T(8,128)(2,1)}) custom-call(s32[4]{0:T(128)} %pad_add_fusion.place, f32[256,768]{1,0:T(8,128)} %get-tuple-element.166.refs_0_, bf16[4,256,640]{2,1,0:T(8,128)(2,1)} %get-tuple-element.167.refs_1_, ...), custom_call_target="tpu_custom_call" | custom-call | flops 10000000 | bytes 30000 | tf_op jit(solution)/shard_map/pull_attention_1/pallas_call | solution.py:470
  293.6 2.1 collective-permute-done.38.refs_7_
  298.7 4.9 grad_attention_1.1
  305.3 9.7 %pull_mlp_0.1 = (f32[256,768]{1,0:T(8,128)}, f32[8,768]{1,0:T(8,128)}, bf16[768,256]{1,0:T(8,128)(2,1)}, bf16[2,256,768]{2,1,0:T(8,128)(2,1)}, bf16[2,256,768]{2,1,0:T(8,128)(2,1)}) custom-call(s32[4]{0:T(128)} %pad_add_fusion.place, f32[256,768]{1,0:T(8,128)} %get-tuple-element.179.refs_0_, bf16[4,256,768]{2,1,0:T(8,128)(2,1)} %get-tuple-element.180.refs_1_, ...), custom_call_target="tpu_custom_call" | custom-call | flops 8000000 | bytes 24000 | tf_op jit(solution)/shard_map/pull_mlp_0/pallas_call | solution.py:470
  316.3 1.8 copy.91
  320.7 2.2 fusion.4
  325.4 6.4 %grad_mlp_0.1 = (bf16[2,4,96,768]{3,2,1,0:T(8,128)(2,1)}, bf16[2,4,96,768]{3,2,1,0:T(8,128)(2,1)}, bf16[2,4,96,768]{3,2,1,0:T(8,128)(2,1)}, bf16[2,4,96,768]{3,2,1,0:T(8,128)(2,1)}) custom-call(s32[4]{0:T(128)} %pad_add_fusion.place, bf16[768,256]{1,0:T(8,128)(2,1)} %get-tuple-element.189.refs_0_, bf16[768,256]{1,0:T(8,128)(2,1)} %copy-done.42, ...), custom_call_target="tpu_custom_call" | custom-call | flops 8000000 | bytes 24000 | tf_op jit(solution)/shard_map/grad_mlp_0/pallas_call | solution.py:470
  332.9 12.8 %pull_attention_0.1 = (f32[256,768]{1,0:T(8,128)}, f32[8,768]{1,0:T(8,128)}, bf16[768,256]{1,0:T(8,128)(2,1)}, bf16[2,256,768]{2,1,0:T(8,128)(2,1)}, bf16[2,256,768]{2,1,0:T(8,128)(2,1)}) custom-call(s32[4]{0:T(128)} %pad_add_fusion.place, f32[256,768]{1,0:T(8,128)} %get-tuple-element.197.refs_0_, bf16[4,256,640]{2,1,0:T(8,128)(2,1)} %get-tuple-element.198.refs_1_, ...), custom_call_target="tpu_custom_call" | custom-call | flops 10000000 | bytes 30000 | tf_op jit(solution)/shard_map/pull_attention_0/pallas_call | solution.py:470
  348.3 2.0 fusion.5
  352.0 1.8 collective-permute-start.75
  353.8 1.8 collective-permute-start.76
  356.9 3.5 collective-permute-done.74
  362.0 4.0 collective-permute-done.75
  368.5 2.5 collective-permute-start.82
  376.4 15.3 %collective-permute-start.48 = (bf16[768,256]{1,0:T(8,128)(2,1)S(1)}, bf16[768,256]{1,0:T(8,128)(2,1)S(1)}, u32[]{:S(2)}, u32[]{:S(2)}) collective-permute-start(bf16[768,256]{1,0:T(8,128)(2,1)S(1)} %copy-done.46), channel_id=1, source_target_pairs={{0,1},{1,0},{2,3},{3,2},{4,5},{5,4},{6,7},{7,6},{8,9},{9,8},{10,11... | collective-permute-start | bytes 1179656 | tf_op jit(solution)/shard_map/core_pair/ppermute | solution.py:666
  391.7 3.1 collective-permute-start.49
  397.5 2.0 fusion.7
  402.4 5.0 grad_attention_0.1
  408.6 2.7 collective-permute-done.65
  413.0 2.8 collective-permute-start.67
  417.4 4.1 collective-permute-done.66
  421.4 5.2 %collective-permute-done.67 = bf16[96,768]{1,0:T(8,128)(2,1)S(1)} collective-permute-done((bf16[96,768]{1,0:T(8,128)(2,1)S(1)}, bf16[96,768]{1,0:T(8,128)(2,1)S(1)}, u32[]{:S(2)}, u32[]{:S(2)}) %collective-permute-start.67) | collective-permute-done | bytes 147488 | tf_op jit(solution)/shard_map/z_att_1_2/ppermute | solution.py:672
  428.9 2.3 collective-permute-done.77
  434.3 2.8 collective-permute-start.80
  437.5 11.6 %collective-permute-done.69 = bf16[4,96,768]{2,1,0:T(8,128)(2,1)S(1)} collective-permute-done((bf16[4,96,768]{2,1,0:T(8,128)(2,1)S(1)}, bf16[4,96,768]{2,1,0:T(8,128)(2,1)S(1)}, u32[]{:S(2)}, u32[]{:S(2)}) %collective-permute-start.69) | collective-permute-done | bytes 589856 | tf_op jit(solution)/shard_map/y_up_0_second/ppermute | solution.py:661
  450.2 2.2 collective-permute-start.71
  454.3 3.6 collective-permute-done.54
  460.5 2.1 collective-permute-done.55
  464.1 3.2 collective-permute-done.56
  467.4 2.6 collective-permute-start.57
  477.6 4.6 collective-permute-done.61
  487.3 2.2 collective-permute-done.62
  489.6 3.1 collective-permute-done.63
  (418 shorter events, 110.2 us)
Async XLA Ops:
  7.2 161.9 %all-gather.4.cloned.1.call-start = ((), (), s32[]{:S(2)}) async-start(), calls=%async_computation.2 | async-start | bytes 15409152 | tf_op jit(solution)/shard_map/all_gather | solution.py:834
  10.8 8.6 %collective-permute-start.3 = (f32[2,1408]{1,0:T(2,128)S(1)}, f32[2,1408]{1,0:T(2,128)S(1)}, u32[]{:S(2)}, u32[]{:S(2)}) collective-permute-start(f32[2,1408]{1,0:T(2,128)S(1)} %concatenate.16), channel_id=1, source_target_pairs={{0,2},{1,3},{2,0},{3,1},{4,6},{5,7},{6,4},{7,5},{8,10},{9,11},{10,... | collective-permute-start | bytes 33800 | tf_op jit(solution)/shard_map/x_biases/ppermute | solution.py:656
  13.9 8.7 %collective-permute-start = (bf16[96,768]{1,0:T(8,128)(2,1)S(1)}, bf16[96,768]{1,0:T(8,128)(2,1)S(1)}, u32[]{:S(2)}, u32[]{:S(2)}) collective-permute-start(bf16[96,768]{1,0:T(8,128)(2,1)S(1)} %pad_maximum_fusion.10), channel_id=1, source_target_pairs={{0,8},{4,12},{8,16},{12,20},{16,24},{20,28},{24,0},{28,4},{1,9},{5... | collective-permute-start | bytes 442376 | tf_op jit(solution)/shard_map/z_att_0_1/ppermute | solution.py:672
  15.5 12.9 %collective-permute-start.1 = (bf16[96,768]{1,0:T(8,128)(2,1)S(1)}, bf16[96,768]{1,0:T(8,128)(2,1)S(1)}, u32[]{:S(2)}, u32[]{:S(2)}) collective-permute-start(bf16[96,768]{1,0:T(8,128)(2,1)S(1)} %pad_maximum_fusion.10), channel_id=1, source_target_pairs={{0,16},{4,20},{8,24},{12,28},{16,0},{20,4},{24,8},{28,12},{1,17},{... | collective-permute-start | bytes 442376 | tf_op jit(solution)/shard_map/z_att_0_2/ppermute | solution.py:672
  18.1 10.3 %collective-permute-start.2 = (bf16[96,768]{1,0:T(8,128)(2,1)S(1)}, bf16[96,768]{1,0:T(8,128)(2,1)S(1)}, u32[]{:S(2)}, u32[]{:S(2)}) collective-permute-start(bf16[96,768]{1,0:T(8,128)(2,1)S(1)} %pad_maximum_fusion.10), channel_id=1, source_target_pairs={{0,24},{4,28},{8,0},{12,4},{16,8},{20,12},{24,16},{28,20},{1,25},{... | collective-permute-start | bytes 442376 | tf_op jit(solution)/shard_map/z_att_0_3/ppermute | solution.py:672
  28.5 16.2 %collective-permute-start.6 = (bf16[4,96,768]{2,1,0:T(8,128)(2,1)S(1)}, bf16[4,96,768]{2,1,0:T(8,128)(2,1)S(1)}, u32[]{:S(2)}, u32[]{:S(2)}) collective-permute-start(bf16[4,96,768]{2,1,0:T(8,128)(2,1)S(1)} %pad_maximum_fusion.3), channel_id=1, source_target_pairs={{0,4},{4,0},{8,12},{12,8},{16,20},{20,16},{24,28},{28,24},{1,5},{5... | collective-permute-start | bytes 1769480 | tf_op jit(solution)/shard_map/y_att_0_first/ppermute | solution.py:661
  30.2 27.7 %collective-permute-start.15 = (bf16[96,768]{1,0:T(8,128)(2,1)S(1)}, bf16[96,768]{1,0:T(8,128)(2,1)S(1)}, u32[]{:S(2)}, u32[]{:S(2)}) collective-permute-start(bf16[96,768]{1,0:T(8,128)(2,1)S(1)} %get-tuple-element.136), channel_id=1, source_target_pairs={{0,8},{4,12},{8,16},{12,20},{16,24},{20,28},{24,0},{28,4},{1,9},{5... | collective-permute-start | bytes 442376 | tf_op jit(solution)/shard_map/z_down_0_1/ppermute | solution.py:672
  42.4 15.5 %collective-permute-start.16 = (bf16[96,768]{1,0:T(8,128)(2,1)S(1)}, bf16[96,768]{1,0:T(8,128)(2,1)S(1)}, u32[]{:S(2)}, u32[]{:S(2)}) collective-permute-start(bf16[96,768]{1,0:T(8,128)(2,1)S(1)} %get-tuple-element.136), channel_id=1, source_target_pairs={{0,16},{4,20},{8,24},{12,28},{16,0},{20,4},{24,8},{28,12},{1,17},{... | collective-permute-start | bytes 442376 | tf_op jit(solution)/shard_map/z_down_0_2/ppermute | solution.py:672
  43.7 26.6 %collective-permute-start.17 = (bf16[96,768]{1,0:T(8,128)(2,1)S(1)}, bf16[96,768]{1,0:T(8,128)(2,1)S(1)}, u32[]{:S(2)}, u32[]{:S(2)}) collective-permute-start(bf16[96,768]{1,0:T(8,128)(2,1)S(1)} %get-tuple-element.136), channel_id=1, source_target_pairs={{0,24},{4,28},{8,0},{12,4},{16,8},{20,12},{24,16},{28,20},{1,25},{... | collective-permute-start | bytes 442376 | tf_op jit(solution)/shard_map/z_down_0_3/ppermute | solution.py:672
  44.9 59.8 %collective-permute-start.7 = (bf16[2,4,96,768]{3,2,1,0:T(8,128)(2,1)S(1)}, bf16[2,4,96,768]{3,2,1,0:T(8,128)(2,1)}, u32[]{:S(2)}, u32[]{:S(2)}) collective-permute-start(bf16[2,4,96,768]{3,2,1,0:T(8,128)(2,1)S(1)} %pad_maximum_fusion.refs_4_.refs_6_), channel_id=1, source_target_pairs={{0,2},{1,3},{2,0},{3,1},{4,6},{5,7},{6,4},{7,5},{8,10},{9,11},{10,... | collective-permute-start | bytes 3538952 | tf_op jit(solution)/shard_map/x_att_0_second/ppermute | solution.py:656
  45.0 25.5 %collective-permute-start.10 = (bf16[96,768]{1,0:T(8,128)(2,1)S(1)}, bf16[96,768]{1,0:T(8,128)(2,1)S(1)}, u32[]{:S(2)}, u32[]{:S(2)}) collective-permute-start(bf16[96,768]{1,0:T(8,128)(2,1)S(1)} %get-tuple-element.135), channel_id=1, source_target_pairs={{0,8},{4,12},{8,16},{12,20},{16,24},{20,28},{24,0},{28,4},{1,9},{5... | collective-permute-start | bytes 442376 | tf_op jit(solution)/shard_map/z_up_0_1/ppermute | solution.py:672
  57.9 18.6 %collective-permute-start.11 = (bf16[96,768]{1,0:T(8,128)(2,1)S(1)}, bf16[96,768]{1,0:T(8,128)(2,1)S(1)}, u32[]{:S(2)}, u32[]{:S(2)}) collective-permute-start(bf16[96,768]{1,0:T(8,128)(2,1)S(1)} %get-tuple-element.135), channel_id=1, source_target_pairs={{0,16},{4,20},{8,24},{12,28},{16,0},{20,4},{24,8},{28,12},{1,17},{... | collective-permute-start | bytes 442376 | tf_op jit(solution)/shard_map/z_up_0_2/ppermute | solution.py:672
  57.9 18.6 %collective-permute-start.12 = (bf16[96,768]{1,0:T(8,128)(2,1)S(1)}, bf16[96,768]{1,0:T(8,128)(2,1)S(1)}, u32[]{:S(2)}, u32[]{:S(2)}) collective-permute-start(bf16[96,768]{1,0:T(8,128)(2,1)S(1)} %get-tuple-element.135), channel_id=1, source_target_pairs={{0,24},{4,28},{8,0},{12,4},{16,8},{20,12},{24,16},{28,20},{1,25},{... | collective-permute-start | bytes 442376 | tf_op jit(solution)/shard_map/z_up_0_3/ppermute | solution.py:672
  70.4 10.1 %collective-permute-start.18 = (bf16[4,96,768]{2,1,0:T(8,128)(2,1)S(1)}, bf16[4,96,768]{2,1,0:T(8,128)(2,1)}, u32[]{:S(2)}, u32[]{:S(2)}) collective-permute-start(bf16[4,96,768]{2,1,0:T(8,128)(2,1)S(1)} %get-tuple-element.354), channel_id=1, source_target_pairs={{0,4},{4,0},{8,12},{12,8},{16,20},{20,16},{24,28},{28,24},{1,5},{5... | collective-permute-start | bytes 1769480 | tf_op jit(solution)/shard_map/y_down_0_first/ppermute | solution.py:661
  76.6 27.8 %collective-permute-start.13 = (bf16[4,96,768]{2,1,0:T(8,128)(2,1)S(1)}, bf16[4,96,768]{2,1,0:T(8,128)(2,1)S(1)}, u32[]{:S(2)}, u32[]{:S(2)}) collective-permute-start(bf16[4,96,768]{2,1,0:T(8,128)(2,1)S(1)} %get-tuple-element.356), channel_id=1, source_target_pairs={{0,2},{1,3},{2,0},{3,1},{4,6},{5,7},{6,4},{7,5},{8,10},{9,11},{10,... | collective-permute-start | bytes 1769480 | tf_op jit(solution)/shard_map/x_up_0_first/ppermute | solution.py:656
  77.9 35.7 %collective-permute-start.8 = (bf16[2,4,96,768]{3,2,1,0:T(8,128)(2,1)S(1)}, bf16[2,4,96,768]{3,2,1,0:T(8,128)(2,1)}, u32[]{:S(2)}, u32[]{:S(2)}) collective-permute-start(bf16[2,4,96,768]{3,2,1,0:T(8,128)(2,1)S(1)} %pad_maximum_fusion.refs_4_.refs_6_), channel_id=1, source_target_pairs={{0,1},{1,0},{2,3},{3,2},{4,5},{5,4},{6,7},{7,6},{8,9},{9,8},{10,11... | collective-permute-start | bytes 3538952 | tf_op jit(solution)/shard_map/core_att_0/ppermute | solution.py:666
  81.6 67.6 %collective-permute-start.19 = (bf16[2,4,96,768]{3,2,1,0:T(8,128)(2,1)S(1)}, bf16[2,4,96,768]{3,2,1,0:T(8,128)(2,1)}, u32[]{:S(2)}, u32[]{:S(2)}) collective-permute-start(bf16[2,4,96,768]{3,2,1,0:T(8,128)(2,1)S(1)} %pad_maximum_fusion.2.refs_7_.refs_9_), channel_id=1, source_target_pairs={{0,2},{1,3},{2,0},{3,1},{4,6},{5,7},{6,4},{7,5},{8,10},{9,11},{10,... | collective-permute-start | bytes 3538952 | tf_op jit(solution)/shard_map/x_down_0_second/ppermute | solution.py:656
  104.6 44.6 %collective-permute-start.14 = (bf16[2,4,96,768]{3,2,1,0:T(8,128)(2,1)S(1)}, bf16[2,4,96,768]{3,2,1,0:T(8,128)(2,1)}, u32[]{:S(2)}, u32[]{:S(2)}) collective-permute-start(bf16[2,4,96,768]{3,2,1,0:T(8,128)(2,1)S(1)} %pad_maximum_fusion.1.refs_3_.refs_5_), channel_id=1, source_target_pairs={{0,4},{4,0},{8,12},{12,8},{16,20},{20,16},{24,28},{28,24},{1,5},{5... | collective-permute-start | bytes 3538952 | tf_op jit(solution)/shard_map/y_up_0_second/ppermute | solution.py:661
  104.7 8.9 %collective-permute-start.9 = (bf16[2,4,96,768]{3,2,1,0:T(8,128)(2,1)}, bf16[2,4,96,768]{3,2,1,0:T(8,128)(2,1)}, u32[]{:S(2)}, u32[]{:S(2)}) collective-permute-start(bf16[2,4,96,768]{3,2,1,0:T(8,128)(2,1)} %collective-permute-done.7.refs_5_.refs_7_), channel_id=1, source_target_pairs={{0,1},{1,0},{2,3},{3,2},{4,5},{5,4},{6,7},{7,6},{8,9},{9,8},{10,11... | collective-permute-start | bytes 3538952 | tf_op jit(solution)/shard_map/core_att_0/ppermute | solution.py:666
  149.2 6.1 %collective-permute-start.21 = (bf16[2,4,96,768]{3,2,1,0:T(8,128)(2,1)}, bf16[2,4,96,768]{3,2,1,0:T(8,128)(2,1)S(1)}, u32[]{:S(2)}, u32[]{:S(2)}) collective-permute-start(bf16[2,4,96,768]{3,2,1,0:T(8,128)(2,1)} %collective-permute-done.14.refs_4_.refs_6_), channel_id=1, source_target_pairs={{0,1},{1,0},{2,3},{3,2},{4,5},{5,4},{6,7},{7,6},{8,9},{9,8},{10,11... | collective-permute-start | bytes 3538952 | tf_op jit(solution)/shard_map/core_up_0/ppermute | solution.py:666
  149.7 6.6 %collective-permute-start.22 = (bf16[2,4,96,768]{3,2,1,0:T(8,128)(2,1)S(1)}, bf16[2,4,96,768]{3,2,1,0:T(8,128)(2,1)S(1)}, u32[]{:S(2)}, u32[]{:S(2)}) collective-permute-start(bf16[2,4,96,768]{3,2,1,0:T(8,128)(2,1)S(1)} %pad_maximum_fusion.2.refs_7_.refs_9_), channel_id=1, source_target_pairs={{0,1},{1,0},{2,3},{3,2},{4,5},{5,4},{6,7},{7,6},{8,9},{9,8},{10,11... | collective-permute-start | bytes 3538952 | tf_op jit(solution)/shard_map/core_down_0/ppermute | solution.py:666
  149.8 8.3 %collective-permute-start.23 = (bf16[2,4,96,768]{3,2,1,0:T(8,128)(2,1)}, bf16[2,4,96,768]{3,2,1,0:T(8,128)(2,1)S(1)}, u32[]{:S(2)}, u32[]{:S(2)}) collective-permute-start(bf16[2,4,96,768]{3,2,1,0:T(8,128)(2,1)} %collective-permute-done.19.refs_8_.refs_10_), channel_id=1, source_target_pairs={{0,1},{1,0},{2,3},{3,2},{4,5},{5,4},{6,7},{7,6},{8,9},{9,8},{10,11... | collective-permute-start | bytes 3538952 | tf_op jit(solution)/shard_map/core_down_0/ppermute | solution.py:666
  192.5 28.0 %all-to-all-start = ((bf16[8,256,128]{2,1,0:T(8,128)(2,1)}), bf16[8,256,128]{2,1,0:T(8,128)(2,1)S(1)}, u32[]{:S(2)}, u32[]{:S(2)}) async-start(bf16[8,256,128]{2,1,0:T(8,128)(2,1)} %broadcast_in_dim.55), calls=%async_computation | async-start | bytes 1048576 | tf_op jit(solution)/shard_map/all_to_all | solution.py:1036
  236.7 18.7 %all-to-all-start.1 = ((bf16[8,256,128]{2,1,0:T(8,128)(2,1)}), bf16[8,256,128]{2,1,0:T(8,128)(2,1)S(1)}, u32[]{:S(2)}, u32[]{:S(2)}) async-start(bf16[8,256,128]{2,1,0:T(8,128)(2,1)} %get-tuple-element.149), calls=%async_computation.1 | async-start | bytes 1048576 | tf_op jit(solution)/shard_map/all_to_all | solution.py:1061
  240.3 28.8 %collective-permute-start.33 = (bf16[2,256,768]{2,1,0:T(8,128)(2,1)}, bf16[2,256,768]{2,1,0:T(8,128)(2,1)S(1)}, u32[]{:S(2)}, u32[]{:S(2)}) collective-permute-start(bf16[2,256,768]{2,1,0:T(8,128)(2,1)} %get-tuple-element.162), channel_id=1, source_target_pairs={{0,1},{1,0},{2,3},{3,2},{4,5},{5,4},{6,7},{7,6},{8,9},{9,8},{10,11... | collective-permute-start | bytes 2359304 | tf_op jit(solution)/shard_map/core_pair/ppermute | solution.py:666
  240.6 14.9 %collective-permute-start.27 = (f32[256,128]{1,0:T(8,128)}, f32[256,128]{1,0:T(8,128)S(1)}, u32[]{:S(2)}, u32[]{:S(2)}) collective-permute-start(f32[256,128]{1,0:T(8,128)} %get-tuple-element.148), channel_id=1, source_target_pairs={{0,3},{4,7},{8,11},{12,15},{16,19},{20,23},{24,27},{28,31}} | collective-permute-start | bytes 393224 | tf_op jit(solution)/shard_map/ppermute | solution.py:1063
  242.8 12.6 %collective-permute-start.28 = (f32[256,128]{1,0:T(8,128)}, f32[256,128]{1,0:T(8,128)S(1)}, u32[]{:S(2)}, u32[]{:S(2)}) collective-permute-start(f32[256,128]{1,0:T(8,128)} %get-tuple-element.148), channel_id=1, source_target_pairs={{1,3},{5,7},{9,11},{13,15},{17,19},{21,23},{25,27},{29,31}} | collective-permute-start | bytes 393224 | tf_op jit(solution)/shard_map/ppermute | solution.py:1063
  243.5 11.9 %collective-permute-start.29 = (f32[256,128]{1,0:T(8,128)}, f32[256,128]{1,0:T(8,128)S(1)}, u32[]{:S(2)}, u32[]{:S(2)}) collective-permute-start(f32[256,128]{1,0:T(8,128)} %get-tuple-element.148), channel_id=1, source_target_pairs={{2,3},{6,7},{10,11},{14,15},{18,19},{22,23},{26,27},{30,31}} | collective-permute-start | bytes 393224 | tf_op jit(solution)/shard_map/ppermute | solution.py:1063
  277.8 42.4 %collective-permute-start.40 = (bf16[2,4,96,896]{3,2,1,0:T(8,128)(2,1)}, bf16[2,4,96,896]{3,2,1,0:T(8,128)(2,1)S(1)}, u32[]{:S(2)}, u32[]{:S(2)}) collective-permute-start(bf16[2,4,96,896]{3,2,1,0:T(8,128)(2,1)} %get-tuple-element.188), channel_id=1, source_target_pairs={{0,4},{4,0},{8,12},{12,8},{16,20},{20,16},{24,28},{28,24},{1,5},{5... | collective-permute-start | bytes 4128776 | tf_op jit(solution)/shard_map/y_down_1_first/ppermute | solution.py:661
  279.4 40.7 %collective-permute-start.39 = (bf16[2,4,96,768]{3,2,1,0:T(8,128)(2,1)}, bf16[2,4,96,768]{3,2,1,0:T(8,128)(2,1)}, u32[]{:S(2)}, u32[]{:S(2)}) collective-permute-start(bf16[2,4,96,768]{3,2,1,0:T(8,128)(2,1)} %get-tuple-element.186), channel_id=1, source_target_pairs={{0,2},{1,3},{2,0},{3,1},{4,6},{5,7},{6,4},{7,5},{8,10},{9,11},{10,... | collective-permute-start | bytes 3538952 | tf_op jit(solution)/shard_map/x_up_1_first/ppermute | solution.py:656
  303.6 43.5 %collective-permute-start.45 = (bf16[2,4,96,768]{3,2,1,0:T(8,128)(2,1)}, bf16[2,4,96,768]{3,2,1,0:T(8,128)(2,1)}, u32[]{:S(2)}, u32[]{:S(2)}) collective-permute-start(bf16[2,4,96,768]{3,2,1,0:T(8,128)(2,1)} %get-tuple-element.205), channel_id=1, source_target_pairs={{0,2},{1,3},{2,0},{3,1},{4,6},{5,7},{6,4},{7,5},{8,10},{9,11},{10,... | collective-permute-start | bytes 3538952 | tf_op jit(solution)/shard_map/x_att_1_first/ppermute | solution.py:656
  305.3 19.2 %collective-permute-start.44 = (bf16[2,256,768]{2,1,0:T(8,128)(2,1)}, bf16[2,256,768]{2,1,0:T(8,128)(2,1)S(1)}, u32[]{:S(2)}, u32[]{:S(2)}) collective-permute-start(bf16[2,256,768]{2,1,0:T(8,128)(2,1)} %get-tuple-element.194), channel_id=1, source_target_pairs={{0,1},{1,0},{2,3},{3,2},{4,5},{5,4},{6,7},{7,6},{8,9},{9,8},{10,11... | collective-permute-start | bytes 2359304 | tf_op jit(solution)/shard_map/core_pair/ppermute | solution.py:666
  314.9 10.1 %collective-permute-start.42 = (bf16[2,256,768]{2,1,0:T(8,128)(2,1)}, bf16[2,256,768]{2,1,0:T(8,128)(2,1)}, u32[]{:S(2)}, u32[]{:S(2)}) collective-permute-start(bf16[2,256,768]{2,1,0:T(8,128)(2,1)} %get-tuple-element.191), channel_id=1, source_target_pairs={{0,1},{1,0},{2,3},{3,2},{4,5},{5,4},{6,7},{7,6},{8,9},{9,8},{10,11... | collective-permute-start | bytes 2359304 | tf_op jit(solution)/shard_map/core_pair/ppermute | solution.py:666
  324.0 29.8 %collective-permute-start.81 = (bf16[4,96,896]{2,1,0:T(8,128)(2,1)}, bf16[4,96,896]{2,1,0:T(8,128)(2,1)}, u32[]{:S(2)}, u32[]{:S(2)}) collective-permute-start(bf16[4,96,896]{2,1,0:T(8,128)(2,1)} %fusion), channel_id=1, source_target_pairs={{0,2},{1,3},{2,0},{3,1},{4,6},{5,7},{6,4},{7,5},{8,10},{9,11},{10,... | collective-permute-start | bytes 2064392 | tf_op jit(solution)/shard_map/x_down_1_second/ppermute | solution.py:656
  324.5 25.9 %collective-permute-start.73 = (bf16[4,96,768]{2,1,0:T(8,128)(2,1)}, bf16[4,96,768]{2,1,0:T(8,128)(2,1)}, u32[]{:S(2)}, u32[]{:S(2)}) collective-permute-start(bf16[4,96,768]{2,1,0:T(8,128)(2,1)} %fusion.4), channel_id=1, source_target_pairs={{0,4},{4,0},{8,12},{12,8},{16,20},{20,16},{24,28},{28,24},{1,5},{5... | collective-permute-start | bytes 1769480 | tf_op jit(solution)/shard_map/y_up_1_second/ppermute | solution.py:661
  331.8 65.1 %collective-permute-start.47 = (bf16[2,4,96,768]{3,2,1,0:T(8,128)(2,1)}, bf16[2,4,96,768]{3,2,1,0:T(8,128)(2,1)}, u32[]{:S(2)}, u32[]{:S(2)}) collective-permute-start(bf16[2,4,96,768]{3,2,1,0:T(8,128)(2,1)} %get-tuple-element.210), channel_id=1, source_target_pairs={{0,4},{4,0},{8,12},{12,8},{16,20},{20,16},{24,28},{28,24},{1,5},{5... | collective-permute-start | bytes 3538952 | tf_op jit(solution)/shard_map/y_down_0_first/ppermute | solution.py:661
  347.1 21.4 %collective-permute-start.58 = (f32[192,768]{1,0:T(8,128)S(1)}, f32[192,768]{1,0:T(8,128)S(1)}, u32[]{:S(2)}, u32[]{:S(2)}) collective-permute-start(f32[192,768]{1,0:T(8,128)S(1)} %constant_dynamic-slice_fusion.1), channel_id=1, source_target_pairs={{0,1},{1,2},{2,3},{3,0},{4,5},{5,6},{6,7},{7,4},{8,9},{9,10},{10,1... | collective-permute-start | bytes 1769480 | tf_op jit(solution)/shard_map/ppermute | solution.py:865
  351.7 8.6 %collective-permute-start.74 = (bf16[96,768]{1,0:T(8,128)(2,1)S(1)}, bf16[96,768]{1,0:T(8,128)(2,1)S(1)}, u32[]{:S(2)}, u32[]{:S(2)}) collective-permute-start(bf16[96,768]{1,0:T(8,128)(2,1)S(1)} %get-tuple-element.339), channel_id=1, source_target_pairs={{0,8},{4,12},{8,16},{12,20},{16,24},{20,28},{24,0},{28,4},{1,9},{5... | collective-permute-start | bytes 442376 | tf_op jit(solution)/shard_map/z_up_1_1/ppermute | solution.py:672
  352.0 14.0 %collective-permute-start.75 = (bf16[96,768]{1,0:T(8,128)(2,1)S(1)}, bf16[96,768]{1,0:T(8,128)(2,1)S(1)}, u32[]{:S(2)}, u32[]{:S(2)}) collective-permute-start(bf16[96,768]{1,0:T(8,128)(2,1)S(1)} %get-tuple-element.341), channel_id=1, source_target_pairs={{0,16},{4,20},{8,24},{12,28},{16,0},{20,4},{24,8},{28,12},{1,17},{... | collective-permute-start | bytes 442376 | tf_op jit(solution)/shard_map/z_up_1_2/ppermute | solution.py:672
  353.8 12.9 %collective-permute-start.76 = (bf16[96,768]{1,0:T(8,128)(2,1)S(1)}, bf16[96,768]{1,0:T(8,128)(2,1)S(1)}, u32[]{:S(2)}, u32[]{:S(2)}) collective-permute-start(bf16[96,768]{1,0:T(8,128)(2,1)S(1)} %get-tuple-element.340), channel_id=1, source_target_pairs={{0,24},{4,28},{8,0},{12,4},{16,8},{20,12},{24,16},{28,20},{1,25},{... | collective-permute-start | bytes 442376 | tf_op jit(solution)/shard_map/z_up_1_3/ppermute | solution.py:672
  360.4 39.1 %collective-permute-start.46 = (bf16[2,4,96,768]{3,2,1,0:T(8,128)(2,1)S(1)}, bf16[2,4,96,768]{3,2,1,0:T(8,128)(2,1)S(1)}, u32[]{:S(2)}, u32[]{:S(2)}) collective-permute-start(bf16[2,4,96,768]{3,2,1,0:T(8,128)(2,1)S(1)} %copy-done.82), channel_id=1, source_target_pairs={{0,2},{1,3},{2,0},{3,1},{4,6},{5,7},{6,4},{7,5},{8,10},{9,11},{10,... | collective-permute-start | bytes 3538952 | tf_op jit(solution)/shard_map/x_up_0_first/ppermute | solution.py:656
  368.5 7.9 %collective-permute-start.82 = (bf16[96,896]{1,0:T(8,128)(2,1)S(1)}, bf16[96,896]{1,0:T(8,128)(2,1)S(1)}, u32[]{:S(2)}, u32[]{:S(2)}) collective-permute-start(bf16[96,896]{1,0:T(8,128)(2,1)S(1)} %get-tuple-element.330), channel_id=1, source_target_pairs={{0,8},{4,12},{8,16},{12,20},{16,24},{20,28},{24,0},{28,4},{1,9},{5... | collective-permute-start | bytes 516104 | tf_op jit(solution)/shard_map/z_down_1_1/ppermute | solution.py:672
  371.1 20.7 %collective-permute-start.83 = (bf16[96,896]{1,0:T(8,128)(2,1)S(1)}, bf16[96,896]{1,0:T(8,128)(2,1)S(1)}, u32[]{:S(2)}, u32[]{:S(2)}) collective-permute-start(bf16[96,896]{1,0:T(8,128)(2,1)S(1)} %get-tuple-element.332), channel_id=1, source_target_pairs={{0,16},{4,20},{8,24},{12,28},{16,0},{20,4},{24,8},{28,12},{1,17},{... | collective-permute-start | bytes 516104 | tf_op jit(solution)/shard_map/z_down_1_2/ppermute | solution.py:672
  372.1 22.7 %collective-permute-start.84 = (bf16[96,896]{1,0:T(8,128)(2,1)S(1)}, bf16[96,896]{1,0:T(8,128)(2,1)S(1)}, u32[]{:S(2)}, u32[]{:S(2)}) collective-permute-start(bf16[96,896]{1,0:T(8,128)(2,1)S(1)} %get-tuple-element.331), channel_id=1, source_target_pairs={{0,24},{4,28},{8,0},{12,4},{16,8},{20,12},{24,16},{28,20},{1,25},{... | collective-permute-start | bytes 516104 | tf_op jit(solution)/shard_map/z_down_1_3/ppermute | solution.py:672
  376.4 24.8 %collective-permute-start.48 = (bf16[768,256]{1,0:T(8,128)(2,1)S(1)}, bf16[768,256]{1,0:T(8,128)(2,1)S(1)}, u32[]{:S(2)}, u32[]{:S(2)}) collective-permute-start(bf16[768,256]{1,0:T(8,128)(2,1)S(1)} %copy-done.46), channel_id=1, source_target_pairs={{0,1},{1,0},{2,3},{3,2},{4,5},{5,4},{6,7},{7,6},{8,9},{9,8},{10,11... | collective-permute-start | bytes 1179656 | tf_op jit(solution)/shard_map/core_pair/ppermute | solution.py:666
  391.7 9.4 %collective-permute-start.49 = (bf16[2,256,768]{2,1,0:T(8,128)(2,1)S(1)}, bf16[2,256,768]{2,1,0:T(8,128)(2,1)S(1)}, u32[]{:S(2)}, u32[]{:S(2)}) collective-permute-start(bf16[2,256,768]{2,1,0:T(8,128)(2,1)S(1)} %copy-done.83), channel_id=1, source_target_pairs={{0,1},{1,0},{2,3},{3,2},{4,5},{5,4},{6,7},{7,6},{8,9},{9,8},{10,11... | collective-permute-start | bytes 2359304 | tf_op jit(solution)/shard_map/core_pair/ppermute | solution.py:666
  394.8 16.5 %collective-permute-start.65 = (bf16[4,96,768]{2,1,0:T(8,128)(2,1)}, bf16[4,96,768]{2,1,0:T(8,128)(2,1)}, u32[]{:S(2)}, u32[]{:S(2)}) collective-permute-start(bf16[4,96,768]{2,1,0:T(8,128)(2,1)} %fusion.5), channel_id=1, source_target_pairs={{0,4},{4,0},{8,12},{12,8},{16,20},{20,16},{24,28},{28,24},{1,5},{5... | collective-permute-start | bytes 1769480 | tf_op jit(solution)/shard_map/y_att_1_second/ppermute | solution.py:661
  407.4 29.7 %collective-permute-start.52 = (bf16[2,4,96,768]{3,2,1,0:T(8,128)(2,1)}, bf16[2,4,96,768]{3,2,1,0:T(8,128)(2,1)S(1)}, u32[]{:S(2)}, u32[]{:S(2)}) collective-permute-start(bf16[2,4,96,768]{3,2,1,0:T(8,128)(2,1)} %get-tuple-element.218), channel_id=1, source_target_pairs={{0,4},{4,0},{8,12},{12,8},{16,20},{20,16},{24,28},{28,24},{1,5},{5... | collective-permute-start | bytes 3538952 | tf_op jit(solution)/shard_map/y_att_0_first/ppermute | solution.py:661
  412.8 8.7 %collective-permute-start.66 = (bf16[96,768]{1,0:T(8,128)(2,1)S(1)}, bf16[96,768]{1,0:T(8,128)(2,1)S(1)}, u32[]{:S(2)}, u32[]{:S(2)}) collective-permute-start(bf16[96,768]{1,0:T(8,128)(2,1)S(1)} %get-tuple-element.345), channel_id=1, source_target_pairs={{0,8},{4,12},{8,16},{12,20},{16,24},{20,28},{24,0},{28,4},{1,9},{5... | collective-permute-start | bytes 442376 | tf_op jit(solution)/shard_map/z_att_1_1/ppermute | solution.py:672
  413.0 13.7 %collective-permute-start.67 = (bf16[96,768]{1,0:T(8,128)(2,1)S(1)}, bf16[96,768]{1,0:T(8,128)(2,1)S(1)}, u32[]{:S(2)}, u32[]{:S(2)}) collective-permute-start(bf16[96,768]{1,0:T(8,128)(2,1)S(1)} %get-tuple-element.347), channel_id=1, source_target_pairs={{0,16},{4,20},{8,24},{12,28},{16,0},{20,4},{24,8},{28,12},{1,17},{... | collective-permute-start | bytes 442376 | tf_op jit(solution)/shard_map/z_att_1_2/ppermute | solution.py:672
  415.7 10.9 %collective-permute-start.68 = (bf16[96,768]{1,0:T(8,128)(2,1)S(1)}, bf16[96,768]{1,0:T(8,128)(2,1)S(1)}, u32[]{:S(2)}, u32[]{:S(2)}) collective-permute-start(bf16[96,768]{1,0:T(8,128)(2,1)S(1)} %get-tuple-element.346), channel_id=1, source_target_pairs={{0,24},{4,28},{8,0},{12,4},{16,8},{20,12},{24,16},{28,20},{1,25},{... | collective-permute-start | bytes 442376 | tf_op jit(solution)/shard_map/z_att_1_3/ppermute | solution.py:672
  416.6 14.5 %collective-permute-start.77 = (bf16[4,96,768]{2,1,0:T(8,128)(2,1)S(1)}, bf16[4,96,768]{2,1,0:T(8,128)(2,1)S(1)}, u32[]{:S(2)}, u32[]{:S(2)}) collective-permute-start(bf16[4,96,768]{2,1,0:T(8,128)(2,1)S(1)} %copy-done.40), channel_id=1, source_target_pairs={{0,2},{1,3},{2,0},{3,1},{4,6},{5,7},{6,4},{7,5},{8,10},{9,11},{10,... | collective-permute-start | bytes 1769480 | tf_op jit(solution)/shard_map/x_down_0_second/ppermute | solution.py:656
  427.9 21.2 %collective-permute-start.69 = (bf16[4,96,768]{2,1,0:T(8,128)(2,1)S(1)}, bf16[4,96,768]{2,1,0:T(8,128)(2,1)S(1)}, u32[]{:S(2)}, u32[]{:S(2)}) collective-permute-start(bf16[4,96,768]{2,1,0:T(8,128)(2,1)S(1)} %copy-done.39), channel_id=1, source_target_pairs={{0,4},{4,0},{8,12},{12,8},{16,20},{20,16},{24,28},{28,24},{1,5},{5... | collective-permute-start | bytes 1769480 | tf_op jit(solution)/shard_map/y_up_0_second/ppermute | solution.py:661
  432.4 20.0 %collective-permute-start.78 = (bf16[96,768]{1,0:T(8,128)(2,1)S(1)}, bf16[96,768]{1,0:T(8,128)(2,1)S(1)}, u32[]{:S(2)}, u32[]{:S(2)}) collective-permute-start(bf16[96,768]{1,0:T(8,128)(2,1)S(1)} %get-tuple-element.333), channel_id=1, source_target_pairs={{0,8},{4,12},{8,16},{12,20},{16,24},{20,28},{24,0},{28,4},{1,9},{5... | collective-permute-start | bytes 442376 | tf_op jit(solution)/shard_map/z_down_0_1/ppermute | solution.py:672
  433.4 19.8 %collective-permute-start.79 = (bf16[96,768]{1,0:T(8,128)(2,1)S(1)}, bf16[96,768]{1,0:T(8,128)(2,1)S(1)}, u32[]{:S(2)}, u32[]{:S(2)}) collective-permute-start(bf16[96,768]{1,0:T(8,128)(2,1)S(1)} %get-tuple-element.335), channel_id=1, source_target_pairs={{0,16},{4,20},{8,24},{12,28},{16,0},{20,4},{24,8},{28,12},{1,17},{... | collective-permute-start | bytes 442376 | tf_op jit(solution)/shard_map/z_down_0_2/ppermute | solution.py:672
  434.3 19.0 %collective-permute-start.80 = (bf16[96,768]{1,0:T(8,128)(2,1)S(1)}, bf16[96,768]{1,0:T(8,128)(2,1)S(1)}, u32[]{:S(2)}, u32[]{:S(2)}) collective-permute-start(bf16[96,768]{1,0:T(8,128)(2,1)S(1)} %get-tuple-element.334), channel_id=1, source_target_pairs={{0,24},{4,28},{8,0},{12,4},{16,8},{20,12},{24,16},{28,20},{1,25},{... | collective-permute-start | bytes 442376 | tf_op jit(solution)/shard_map/z_down_0_3/ppermute | solution.py:672
  437.4 12.7 %collective-permute-start.53 = (f32[4,8,768]{2,1,0:T(8,128)S(1)}, f32[4,8,768]{2,1,0:T(8,128)S(1)}, u32[]{:S(2)}, u32[]{:S(2)}) collective-permute-start(f32[4,8,768]{2,1,0:T(8,128)S(1)} %maximum_add_fusion), channel_id=1, source_target_pairs={{0,1},{1,0},{2,3},{3,2},{4,5},{5,4},{6,7},{7,6},{8,9},{9,8},{10,11... | collective-permute-start | bytes 294920 | tf_op jit(solution)/shard_map/core_pair/ppermute | solution.py:666
  449.2 14.8 %collective-permute-start.70 = (bf16[96,768]{1,0:T(8,128)(2,1)S(1)}, bf16[96,768]{1,0:T(8,128)(2,1)S(1)}, u32[]{:S(2)}, u32[]{:S(2)}) collective-permute-start(bf16[96,768]{1,0:T(8,128)(2,1)S(1)} %get-tuple-element.336), channel_id=1, source_target_pairs={{0,8},{4,12},{8,16},{12,20},{16,24},{20,28},{24,0},{28,4},{1,9},{5... | collective-permute-start | bytes 442376 | tf_op jit(solution)/shard_map/z_up_0_1/ppermute | solution.py:672
  450.2 13.8 %collective-permute-start.71 = (bf16[96,768]{1,0:T(8,128)(2,1)S(1)}, bf16[96,768]{1,0:T(8,128)(2,1)S(1)}, u32[]{:S(2)}, u32[]{:S(2)}) collective-permute-start(bf16[96,768]{1,0:T(8,128)(2,1)S(1)} %get-tuple-element.338), channel_id=1, source_target_pairs={{0,16},{4,20},{8,24},{12,28},{16,0},{20,4},{24,8},{28,12},{1,17},{... | collective-permute-start | bytes 442376 | tf_op jit(solution)/shard_map/z_up_0_2/ppermute | solution.py:672
  452.4 11.6 %collective-permute-start.72 = (bf16[96,768]{1,0:T(8,128)(2,1)S(1)}, bf16[96,768]{1,0:T(8,128)(2,1)S(1)}, u32[]{:S(2)}, u32[]{:S(2)}) collective-permute-start(bf16[96,768]{1,0:T(8,128)(2,1)S(1)} %get-tuple-element.337), channel_id=1, source_target_pairs={{0,24},{4,28},{8,0},{12,4},{16,8},{20,12},{24,16},{28,20},{1,25},{... | collective-permute-start | bytes 442376 | tf_op jit(solution)/shard_map/z_up_0_3/ppermute | solution.py:672
  471.6 10.6 %collective-permute-start.61 = (bf16[4,96,768]{2,1,0:T(8,128)(2,1)S(1)}, bf16[4,96,768]{2,1,0:T(8,128)(2,1)S(1)}, u32[]{:S(2)}, u32[]{:S(2)}) collective-permute-start(bf16[4,96,768]{2,1,0:T(8,128)(2,1)S(1)} %fusion.8), channel_id=1, source_target_pairs={{0,2},{1,3},{2,0},{3,1},{4,6},{5,7},{6,4},{7,5},{8,10},{9,11},{10,... | collective-permute-start | bytes 1769480 | tf_op jit(solution)/shard_map/x_att_0_second/ppermute | solution.py:656
  482.4 7.2 %collective-permute-start.62 = (bf16[96,768]{1,0:T(8,128)(2,1)S(1)}, bf16[96,768]{1,0:T(8,128)(2,1)S(1)}, u32[]{:S(2)}, u32[]{:S(2)}) collective-permute-start(bf16[96,768]{1,0:T(8,128)(2,1)S(1)} %get-tuple-element.342), channel_id=1, source_target_pairs={{0,8},{4,12},{8,16},{12,20},{16,24},{20,28},{24,0},{28,4},{1,9},{5... | collective-permute-start | bytes 442376 | tf_op jit(solution)/shard_map/z_att_0_1/ppermute | solution.py:672
  483.9 8.8 %collective-permute-start.63 = (bf16[96,768]{1,0:T(8,128)(2,1)S(1)}, bf16[96,768]{1,0:T(8,128)(2,1)S(1)}, u32[]{:S(2)}, u32[]{:S(2)}) collective-permute-start(bf16[96,768]{1,0:T(8,128)(2,1)S(1)} %get-tuple-element.344), channel_id=1, source_target_pairs={{0,16},{4,20},{8,24},{12,28},{16,0},{20,4},{24,8},{28,12},{1,17},{... | collective-permute-start | bytes 442376 | tf_op jit(solution)/shard_map/z_att_0_2/ppermute | solution.py:672
  485.1 7.6 %collective-permute-start.64 = (bf16[96,768]{1,0:T(8,128)(2,1)S(1)}, bf16[96,768]{1,0:T(8,128)(2,1)S(1)}, u32[]{:S(2)}, u32[]{:S(2)}) collective-permute-start(bf16[96,768]{1,0:T(8,128)(2,1)S(1)} %get-tuple-element.343), channel_id=1, source_target_pairs={{0,24},{4,28},{8,0},{12,4},{16,8},{20,12},{24,16},{28,20},{1,25},{... | collective-permute-start | bytes 442376 | tf_op jit(solution)/shard_map/z_att_0_3/ppermute | solution.py:672
  (111 other events, 812.8 us)
Sparse Core Ops, SparseCore 0:
  11.6 155.8 all-gather.3

commit v3 on v2

--- a/solution.py
+++ b/solution.py
@@ -334,13 +334,13 @@
     return jnp.concatenate([ref[slot] for ref in refs], 0)
 
 
-def block_sends(stage, slot, targets, sems, place, y_first, base):
-    width = stage.shape[-1]
-    lanes = pl.ds(base, width)
+def block_sends(stage, slot, targets, sems, place, y_first, base, start=0, width=None):
+    width = stage.shape[-1] if width is None else width
+    lanes, taken = pl.ds(base, width), pl.ds(start, width)
     if len(targets) == 1:
         copies = [
             pltpu.make_async_copy(
-                stage.at[0, 0], targets[0].at[slot, :, lanes], sems.at[0, 0]
+                stage.at[0, 0, :, taken], targets[0].at[slot, :, lanes], sems.at[0, 0]
             )
         ]
     else:
@@ -350,7 +350,7 @@
             for z_rel in range(4):
                 copies.append(
                     pltpu.make_async_copy(
-                        stage.at[(place[3] + z_rel) & 3, place[2] ^ y_rel],
+                        stage.at[(place[3] + z_rel) & 3, place[2] ^ y_rel, :, taken],
                         targets[first].at[second, z_rel, :, lanes],
                         sems.at[y_rel, z_rel],
                     )
@@ -396,14 +396,17 @@
         copy.wait()
 
 
-def attention_grad_kernel(y_first, split, place, *refs):
+def attention_grad_kernel(cuts, split, place, *refs):
     sides = 2 if split else 1
     groups = []
     for _ in range(4):
         groups.append(refs[:sides])
         refs = refs[sides:]
     x_t_refs, packed_refs, low_t_refs, mixture_refs = groups
-    targets, refs = refs[:sides], refs[sides:]
+    targets = []
+    for _ in cuts:
+        targets.append(refs[:sides])
+        refs = refs[sides:]
     stage, sems = refs
     fold = stage.shape[1:]
     sends = []
@@ -419,7 +422,10 @@
             .astype(BF)
             .reshape(*fold)
         )
-        sends += block_sends(stage.at[slot], slot, targets, sems.at[slot], place, y_first, 0)
+        for at, (start, width, y_first) in enumerate(cuts):
+            sends += block_sends(
+                stage.at[slot], slot, targets[at], sems.at[at, slot], place, y_first, 0, start, width
+            )
     for copy in sends:
         copy.wait()
 
@@ -621,21 +627,28 @@
     return results[:sides], results[sides:]
 
 
-def run_attention_grad(layer_at, y_first, place, groups, split, rows_each):
+def run_attention_grad(layer_at, cuts, place, groups, split, rows_each):
     args = [value for group in groups for value in group]
-    outs = grad_shapes(split, rows_each, SLAB)
+    sides = 2 if split else 1
+    outs = []
+    for _, width, _ in cuts:
+        outs += grad_shapes(split, rows_each, width)
     fold = (4, 2, rows_each) if split else (1, 1, WIDTH)
-    slots = PARTS // (2 if split else 1)
-    return call(
-        functools.partial(attention_grad_kernel, y_first, split),
+    slots = PARTS // sides
+    results = call(
+        functools.partial(attention_grad_kernel, cuts, split),
         f"grad_attention_{layer_at}",
         5,
         place,
         args,
         outs,
-        [pltpu.VMEM((slots, *fold, SLAB), BF), pltpu.SemaphoreType.DMA((slots, 2, 4))],
+        [
+            pltpu.VMEM((slots, *fold, SLAB), BF),
+            pltpu.SemaphoreType.DMA((len(cuts), slots, 2, 4)),
+        ],
         out_hbm=range(len(outs)),
     )
+    return [results[sides * at : sides * (at + 1)] for at in range(len(cuts))]
 
 
 CORE_SWAP = [(at, at ^ 1) for at in range(PARTS)]
@@ -692,10 +705,19 @@
     def start_second(self):
         self.two = self.second(self.terms, self.name + "_second")
 
+    def block(self, step):
+        return added(self.keep[0, step], self.one[0, step], self.two[step])
+
+
+class Column:
+    def __init__(self, *items):
+        self.items = items
+        self.name = "_".join(item.name for item in items)
+
     def add_third(self):
         with jax.named_scope(f"add_{self.name}_third"):
             self.blocks = [
-                added(self.keep[0, step], self.one[0, step], self.two[step]).astype(BF)
+                jnp.concatenate([item.block(step).astype(BF) for item in self.items], 1)
                 for step in range(1, 4)
             ]
 
@@ -704,9 +726,15 @@
             along_z(block, step + 1, self.name) for step, block in enumerate(self.blocks)
         ]
 
-    def total(self):
+    def totals(self):
         with jax.named_scope(f"add_{self.name}_last"):
-            return added(self.keep[0, 0], self.one[0, 0], self.two[0], *self.arrived)
+            results, at = [], 0
+            for item in self.items:
+                own = item.block(0)
+                end = at + own.shape[1]
+                results.append(own + added(*[value[:, at:end] for value in self.arrived]))
+                at = end
+        return results
 
 
 def reduce_whole(grads, devices):
@@ -715,14 +743,20 @@
     return lax.psum_scatter(grads, BOTH, scatter_dimension=0, tiled=True)[0].astype(F32)
 
 
-def total_over_all(value, split):
-    if not split:
-        return lax.psum(value, BOTH)
-    value = value + over_core(value)
-    value = value + over_x(value, "sums")
-    value = value + over_y(value, "sums")
-    value = value + lax.ppermute(value, "dp", [(at, at ^ 2) for at in range(8)])
-    return value + lax.ppermute(value, "dp", [(at, at ^ 4) for at in range(8)])
+def total_over_plane(value):
+    with jax.named_scope("cross_sums"):
+        far = lax.ppermute(value, "tensor", [(at, at ^ 3) for at in range(PARTS)])
+    value = (value + over_core(value, "sums")) + (over_x(value, "sums") + far)
+    return value + over_y(value, "sums")
+
+
+def total_over_column(value):
+    column = jnp.stack([value, *[along_z(value, step, "sums") for step in range(1, 4)]])
+    z_at = lax.axis_index("dp") // 2
+    ordered = [
+        lax.dynamic_index_in_dim(column, (z_at - at) & 3, 0, keepdims=False) for at in range(4)
+    ]
+    return (ordered[0] + ordered[1]) + (ordered[2] + ordered[3])
 
 
 def score_kernel(count, lengths_ref, log_ref, queries_ref, passages_ref, powers_ref, sums_ref, logit_ref):
@@ -863,13 +897,14 @@
     query_rows = QDEV * QLEN // PARTS
     start = jnp.where(tensor_at == PARTS - 1, 0, ROWS - rows)
     step = lax.ppermute(
-        lax.dynamic_slice_in_dim(grad, start, rows, 0),
+        lax.dynamic_slice_in_dim(grad, start, rows, 0).astype(BF),
         "tensor",
         [(at, (at + 1) % PARTS) for at in range(PARTS)],
-    )
+    ).astype(F32)
     last = PARTS - 1
-    one = lax.ppermute(grad[query_rows : 2 * query_rows], "tensor", [(last, 1)])
-    two = lax.ppermute(grad[2 * query_rows : 3 * query_rows], "tensor", [(last, 2)])
+    sent = grad.astype(BF)
+    one = lax.ppermute(sent[query_rows : 2 * query_rows], "tensor", [(last, 1)]).astype(F32)
+    two = lax.ppermute(sent[2 * query_rows : 3 * query_rows], "tensor", [(last, 2)]).astype(F32)
     own = grad[last * query_rows :]
     query = jnp.where(
         tensor_at == 0,
@@ -1067,6 +1102,13 @@
     upstream = (grad_emb, unit, scale, top_t)
     mlp_sums, attention_sums = [None] * LAYERS, [None] * LAYERS
 
+    def stacked_sums():
+        loss_part = jnp.where(tensor_at == 0, jnp.sum(losses), 0.0)
+        sums = jnp.stack([attention_sums[0], mlp_sums[0], attention_sums[1], mlp_sums[1]])
+        row_ids = lax.broadcasted_iota(jnp.int32, sums.shape, 1)
+        sums = sums + jnp.where(row_ids == 7, loss_part, 0.0)
+        return sums
+
     def mlp_pull(layer_at, upstream):
         saved = saved_list[layer_at]
         outs = run_mlp_pull(
@@ -1105,8 +1147,8 @@
     def mlp_grad(layer_at, groups):
         return run_mlp_grad(layer_at, place, groups, split, rows_each)
 
-    def attention_grad(layer_at, y_first, groups):
-        return run_attention_grad(layer_at, y_first, place, groups, split, rows_each)
+    def attention_grad(layer_at, cuts, groups):
+        return run_attention_grad(layer_at, cuts, place, groups, split, rows_each)
 
     if split:
         grad_first, mlp_groups = mlp_pull(1, upstream)
@@ -1116,7 +1158,7 @@
         up_one.start()
         down_one.start()
         dx, att_groups = attention_pull(1, grad_first)
-        att_one = Reduction("att_1", attention_grad(1, False, att_groups), False)
+        att_one = Reduction("att_1", attention_grad(1, ((0, SLAB, False),), att_groups)[0], False)
         dx, att_one.send = tied(dx, att_one.send)
         att_one.start()
         grad_first, mlp_groups = mlp_pull(0, (dx,))
@@ -1134,31 +1176,54 @@
         up_zero.start()
         down_zero.start()
         dx, att_groups = attention_pull(0, grad_first)
+        dx, att_one.one = tied(dx, att_one.one)
         att_one.add_second()
         att_groups[0][0], att_one.terms = tied(att_groups[0][0], att_one.terms)
         att_one.start_second()
-        up_one.add_third()
-        down_one.add_third()
+        mlp_one = Column(up_one, down_one)
+        mlp_one.add_third()
         up_zero.add_second()
         down_zero.add_second()
         att_groups[0][0], up_zero.terms, down_zero.terms = tied(
             att_groups[0][0], up_zero.terms, down_zero.terms
         )
-        att_zero = Reduction("att_0", attention_grad(0, True, att_groups), True)
-        att_zero.start()
-        att_one.add_third()
-        att_zero.add_second()
-        for item in (up_one, down_one, att_one):
-            item.start_third()
-        for item in (up_zero, down_zero, att_zero):
+        half = SLAB // 2
+        left, right = attention_grad(0, ((0, half, False), (half, half, True)), att_groups)
+        halves = (Reduction("qk_0", left, False), Reduction("vo_0", right, True))
+        column_one = Column(att_one)
+        mlp_one.start_third()
+        column_one.add_third()
+        column_one.start_third()
+        for item in (up_zero, down_zero):
             item.start_second()
-        for item in (up_zero, down_zero, att_zero):
-            item.add_third()
-            item.start_third()
-        attention_sums[0] = tied(attention_sums[0], att_zero.terms)[0]
-        att_list = [att_zero.total(), att_one.total()]
-        up_list = [up_zero.total(), up_one.total()]
-        down_list = [down_zero.total(), down_one.total()]
+        qk_zero, vo_zero = halves
+        up_zero.two, down_zero.two, qk_zero.send, vo_zero.send = tied(
+            up_zero.two, down_zero.two, qk_zero.send, vo_zero.send
+        )
+        for item in halves:
+            item.start()
+        mlp_zero = Column(up_zero, down_zero)
+        mlp_zero.add_third()
+        mlp_zero.start_third()
+        for item in halves:
+            item.add_second()
+        attention_sums[0], dx, qk_zero.terms, vo_zero.terms = tied(
+            attention_sums[0], dx, qk_zero.terms, vo_zero.terms
+        )
+        for item in halves:
+            item.start_second()
+        sums = total_over_plane(stacked_sums())
+        sums, qk_zero.two, vo_zero.two = tied(sums, qk_zero.two, vo_zero.two)
+        column_zero = Column(qk_zero, vo_zero)
+        column_zero.add_third()
+        column_zero.start_third()
+        sums = total_over_column(sums)
+        att_list = [jnp.concatenate(column_zero.totals(), 1), *column_one.totals()]
+        (up_grad_zero, down_grad_zero), (up_grad_one, down_grad_one) = (
+            mlp_zero.totals(),
+            mlp_one.totals(),
+        )
+        up_list, down_list = [up_grad_zero, up_grad_one], [down_grad_zero, down_grad_one]
     else:
         att_list, up_list, down_list = [], [], []
         dx = None
@@ -1167,15 +1232,12 @@
             upstream = None
             up_grads, down_grads = mlp_grad(layer_at, groups)
             dx, groups = attention_pull(layer_at, grad_first)
-            att_grads = attention_grad(layer_at, False, groups)
+            att_grads = attention_grad(layer_at, ((0, SLAB, False),), groups)[0]
             up_list.insert(0, reduce_whole(up_grads[0], devices))
             down_list.insert(0, reduce_whole(down_grads[0], devices))
             att_list.insert(0, reduce_whole(att_grads[0], devices))
-    loss_part = jnp.where(tensor_at == 0, jnp.sum(losses), 0.0)
-    sums = jnp.stack([attention_sums[0], mlp_sums[0], attention_sums[1], mlp_sums[1]])
-    row_ids = lax.broadcasted_iota(jnp.int32, sums.shape, 1)
-    sums = sums + jnp.where(row_ids == 7, loss_part, 0.0)
-    sums = total_over_all(sums, split).reshape(LAYERS, 2, 8, WIDTH)
+        sums = lax.psum(stacked_sums(), BOTH)
+    sums = sums.reshape(LAYERS, 2, 8, WIDTH)
     norms_grad = sums[:, :, :3].reshape(LAYERS, 6, WIDTH)
     own_sums = lax.dynamic_slice_in_dim(sums, 3 + tensor_at, 1, 2)[:, :, 0]
     pair_grad = jnp.stack([own_sums[:, 0, :OWN], own_sums[:, 0, 2 * OWN : 3 * OWN]], 1)

time: 510 us -> 498 us (0.976)
  starting transfers between devices: 140 us -> 126 us
    ppermute x27 -> x24, waiting for transfers between devices: 36.4 us -> 56.1 us  [along_z(): return lax.ppermute(value, 'dp', pairs)]
    ppermute x26, starting transfers between devices: 24.1 us -> 4.93 us  [over_core(): return lax.ppermute(value, 'tensor', CORE_SWAP)]
    ppermute x10 -> x11, waiting for transfers between devices: 18.9 us -> 9.77 us  [over_y(): return lax.ppermute(value, 'dp', Y_SWAP)]
    ppermute x11 -> x12, waiting for transfers between devices: 57.9 us -> 50.1 us  [over_x(): return lax.ppermute(value, 'tensor', X_SWAP)]
    ppermute x27 -> x24, starting transfers between devices: 71 us -> 75.6 us  [along_z(): return lax.ppermute(value, 'dp', pairs)]
    unnamed x188 -> x176, local copies, waits for them, and re-layouts: 18.3 us -> 20 us
    ppermute x10 -> x11, starting transfers between devices: 9.2 us -> 10.2 us  [over_y(): return lax.ppermute(value, 'dp', Y_SWAP)]
  transfers between devices with their start and end apart: 88 -> 86, of which waited for: 37 -> 34; matrix products, arithmetic and copies ran while one was open for 10% -> 10% of each run, Pallas kernels for 16% -> 17%
where the time goes in v3:
time: 498 us; the launch traced here: 493 us
  waiting for transfers between devices  152 us (31%)
  starting transfers between devices  126 us (25%)
  Pallas kernels  119 us (24%)
  other arithmetic  42.6 us (9%)
  local copies, waits for them, and re-layouts  29.2 us (6%)
  between operations  18.3 us (4%)
  blocking collectives  5.31 us (1%)
    pallas_call x12, Pallas kernels, call(): pl.pallas_call(kernel, out_shape=outs, in_specs=[smem_spec()] + [any_spec...  111 us
    ppermute x24, starting transfers between devices, along_z(): return lax.ppermute(value, 'dp', pairs)  75.6 us
    ppermute x24, waiting for transfers between devices, along_z(): return lax.ppermute(value, 'dp', pairs)  56.1 us
    ppermute x12, waiting for transfers between devices, over_x(): return lax.ppermute(value, 'tensor', X_SWAP)  50.1 us
    unnamed x176, local copies, waits for them, and re-layouts  20 us
    ppermute x26, waiting for transfers between devices, over_core(): return lax.ppermute(value, 'tensor', CORE_SWAP)  14.2 us
    all_to_all x1, starting transfers between devices, body(): lax.all_to_all(jnp.broadcast_to(embedding[None], (devices, ROWS, DIM)), '...  13 us
    all_to_all x1, waiting for transfers between devices, body(): passage_back = lax.all_to_all(passage_terms, 'dp', 0, 0, tiled=True)  10.9 us
  transfers between devices with their start and end apart: 86, of which 34 were waited for; matrix products, arithmetic and copies ran while one was open for 10% of the time, Pallas kernels for 17%

profile of v3, /device:TPU:0, one launch (start us, length us, event | category | flops | bytes accessed | tf_op | source)
XLA Modules:
  0.0 493.0 jit_solution(1615904549703313247)
XLA Ops:
  10.8 2.9 collective-permute-start.3
  13.9 1.6 collective-permute-start
  15.5 2.6 collective-permute-start.1
  22.6 5.8 %collective-permute-done.1 = bf16[96,768]{1,0:T(8,128)(2,1)S(1)} collective-permute-done((bf16[96,768]{1,0:T(8,128)(2,1)S(1)}, bf16[96,768]{1,0:T(8,128)(2,1)S(1)}, u32[]{:S(2)}, u32[]{:S(2)}) %collective-permute-start.1) | collective-permute-done | bytes 147488 | tf_op jit(solution)/shard_map/z_att_0_2/ppermute | solution.py:685
  28.5 1.7 collective-permute-start.6
  30.2 12.2 %collective-permute-start.15 = (bf16[96,768]{1,0:T(8,128)(2,1)S(1)}, bf16[96,768]{1,0:T(8,128)(2,1)S(1)}, u32[]{:S(2)}, u32[]{:S(2)}) collective-permute-start(bf16[96,768]{1,0:T(8,128)(2,1)S(1)} %get-tuple-element.150), channel_id=1, source_target_pairs={{0,8},{4,12},{8,16},{12,20},{16,24},{20,28},{24,0},{28,4},{1,9},{5... | collective-permute-start | bytes 442376 | tf_op jit(solution)/shard_map/z_down_0_1/ppermute | solution.py:685
  45.0 13.0 %collective-permute-start.10 = (bf16[96,768]{1,0:T(8,128)(2,1)S(1)}, bf16[96,768]{1,0:T(8,128)(2,1)S(1)}, u32[]{:S(2)}, u32[]{:S(2)}) collective-permute-start(bf16[96,768]{1,0:T(8,128)(2,1)S(1)} %get-tuple-element.149), channel_id=1, source_target_pairs={{0,8},{4,12},{8,16},{12,20},{16,24},{20,28},{24,0},{28,4},{1,9},{5... | collective-permute-start | bytes 442376 | tf_op jit(solution)/shard_map/z_up_0_1/ppermute | solution.py:685
  57.9 12.3 %collective-permute-start.12 = (bf16[96,768]{1,0:T(8,128)(2,1)S(1)}, bf16[96,768]{1,0:T(8,128)(2,1)S(1)}, u32[]{:S(2)}, u32[]{:S(2)}) collective-permute-start(bf16[96,768]{1,0:T(8,128)(2,1)S(1)} %get-tuple-element.149), channel_id=1, source_target_pairs={{0,24},{4,28},{8,0},{12,4},{16,8},{20,12},{24,16},{28,20},{1,25},{... | collective-permute-start | bytes 442376 | tf_op jit(solution)/shard_map/z_up_0_3/ppermute | solution.py:685
  70.5 6.0 %collective-permute-done.11 = bf16[96,768]{1,0:T(8,128)(2,1)S(1)} collective-permute-done((bf16[96,768]{1,0:T(8,128)(2,1)S(1)}, bf16[96,768]{1,0:T(8,128)(2,1)S(1)}, u32[]{:S(2)}, u32[]{:S(2)}) %collective-permute-start.11) | collective-permute-done | bytes 147488 | tf_op jit(solution)/shard_map/z_up_0_2/ppermute | solution.py:685
  77.9 2.5 collective-permute-done.18
  81.7 22.8 %collective-permute-done.13 = bf16[4,96,768]{2,1,0:T(8,128)(2,1)S(1)} collective-permute-done((bf16[4,96,768]{2,1,0:T(8,128)(2,1)S(1)}, bf16[4,96,768]{2,1,0:T(8,128)(2,1)S(1)}, u32[]{:S(2)}, u32[]{:S(2)}) %collective-permute-start.13) | collective-permute-done | bytes 589856 | tf_op jit(solution)/shard_map/x_up_0_first/ppermute | solution.py:669
  110.8 2.2 dynamic-slice_select_fusion.refs_0_
  113.6 10.9 %attention_0.1 = (f32[256,768]{1,0:T(8,128)}, bf16[768,256]{1,0:T(8,128)(2,1)}, bf16[4,256,640]{2,1,0:T(8,128)(2,1)}, bf16[12,256,256]{2,1,0:T(8,128)(2,1)}, f32...) custom-call(s32[4]{0:T(128)} %pad_add_fusion.place, ...), custom_call_target="tpu_custom_call" | custom-call | flops 9000000 | bytes 27000 | tf_op jit(solution)/shard_map/attention_0/pallas_call | solution.py:476
  124.6 24.6 %collective-permute-done.19.refs_8_.refs_10_ = bf16[2,4,96,768]{3,2,1,0:T(8,128)(2,1)} collective-permute-done((bf16[2,4,96,768]{3,2,1,0:T(8,128)(2,1)S(1)}, bf16[2,4,96,768]{3,2,1,0:T(8,128)(2,1)}, u32[]{:S(2)}, u32[]{:S(2)}) %collective-permute-start.19) | collective-permute-done | bytes 1179680 | tf_op jit(solution)/shard_map/x_down_0_second/ppermute | solution.py:669
  153.0 2.3 collective-permute-done.21.refs_6_.refs_8_
  156.4 1.7 collective-permute-done.23.refs_10_.refs_12_
  159.1 10.0 %mlp_0.1 = (f32[256,768]{1,0:T(8,128)}, bf16[4,256,768]{2,1,0:T(8,128)(2,1)}, f32[256,768]{1,0:T(8,128)}, f32[256,128]{1,0:T(8,128)}, bf16[2,256,768]{2,1,0:T(8,128)(2,1)}, /*index=5*/bf16[2,256,768]{2,1,0:T(8,128)(2,1)}) custom-call(s32[4]{0:T(128)} %pad_add_fusion.place, f32[256,768]{1,0:T(8,128)} %get-tuple-element.151.refs_0_, ...), custom_call_target="tpu_custom_call" | custom-call | flops 9000000 | bytes 27000 | tf_op jit(solution)/shard_map/mlp_0/pallas_call | solution.py:476
  169.1 11.0 %attention_1.1 = (f32[256,768]{1,0:T(8,128)}, bf16[768,256]{1,0:T(8,128)(2,1)}, bf16[4,256,640]{2,1,0:T(8,128)(2,1)}, bf16[12,256,256]{2,1,0:T(8,128)(2,1)}, f32...) custom-call(s32[4]{0:T(128)} %pad_add_fusion.place, ...), custom_call_target="tpu_custom_call" | custom-call | flops 9000000 | bytes 27000 | tf_op jit(solution)/shard_map/attention_1/pallas_call | solution.py:476
  180.1 10.5 %mlp_1.1 = (f32[256,768]{1,0:T(8,128)}, bf16[4,256,768]{2,1,0:T(8,128)(2,1)}, f32[256,768]{1,0:T(8,128)}, f32[256,128]{1,0:T(8,128)}, bf16[2,256,768]{2,1,0:T(8,...) custom-call(s32[4]{0:T(128)} %pad_add_fusion.place, ...), custom_call_target="tpu_custom_call" | custom-call | flops 9000000 | bytes 27000 | tf_op jit(solution)/shard_map/mlp_1/pallas_call | solution.py:476
  190.7 1.8 broadcast_in_dim.55
  192.5 13.0 %all-to-all-start = ((bf16[8,256,128]{2,1,0:T(8,128)(2,1)}), bf16[8,256,128]{2,1,0:T(8,128)(2,1)S(1)}, u32[]{:S(2)}, u32[]{:S(2)}) async-start(bf16[8,256,128]{2,1,0:T(8,128)(2,1)} %broadcast_in_dim.55), calls=%async_computation | async-start | bytes 1048576 | tf_op jit(solution)/shard_map/all_to_all | solution.py:1071
  209.7 3.9 collective-permute-done.26
  214.3 6.2 %all-to-all-done.passages_ref = bf16[8,256,128]{2,1,0:T(8,128)(2,1)S(1)} async-done(((bf16[8,256,128]{2,1,0:T(8,128)(2,1)}), bf16[8,256,128]{2,1,0:T(8,128)(2,1)S(1)}, u32[]{:S(2)}, u32[]{:S(2)}) %all-to-all-start) | async-done | bytes 524320 | tf_op jit(solution)/shard_map/all_to_all | solution.py:1071
  221.3 4.0 scores.1
  225.3 5.3 %all-gather.1 = f32[32,8]{1,0:T(8,128)S(1)} all-gather(f32[8,8]{1,0:T(8,128)} %bitcast.378), channel_id=3, replica_groups=mesh['dp'=8,'tensor'=4] {'tensor'}, dimensions={0}, use_global_device_ids=true | all-gather | bytes 1280 | tf_op jit(solution)/shard_map/all_gather | solution.py:1081
  232.7 3.9 score_pulls.1
  236.6 3.6 all-to-all-start.1
  240.5 2.3 collective-permute-start.27
  244.3 10.9 %all-to-all-done.1 = bf16[8,256,128]{2,1,0:T(8,128)(2,1)S(1)} async-done(((bf16[8,256,128]{2,1,0:T(8,128)(2,1)}), bf16[8,256,128]{2,1,0:T(8,128)(2,1)S(1)}, u32[]{:S(2)}, u32[]{:S(2)}) %all-to-all-start.1) | async-done | bytes 524320 | tf_op jit(solution)/shard_map/all_to_all | solution.py:1096
  256.1 9.7 %pull_mlp_1.1 = (f32[256,768]{1,0:T(8,128)}, f32[8,768]{1,0:T(8,128)}, bf16[768,256]{1,0:T(8,128)(2,1)}, bf16[2,256,768]{2,1,0:T(8,128)(2,1)}, bf16[2,256,768]{2,1,0:T(8,128)(2,1)}, /*index=5*/f32[768,128]{1,0:T(8,128)}) custom-call(s32[4]{0:T(128)} %pad_add_fusion.place, f32[256,128]{1,0:T(8,128)} %add_select_fusion.refs_0_, ...), custom_call_target="tpu_custom_call" | custom-call | flops 8000000 | bytes 24000 | tf_op jit(solution)/shard_map/pull_mlp_1/pallas_call | solution.py:476
  266.8 2.1 collective-permute-done.30.refs_1_
  271.0 6.7 %grad_mlp_1.1 = (bf16[2,4,96,768]{3,2,1,0:T(8,128)(2,1)}, bf16[2,4,96,768]{3,2,1,0:T(8,128)(2,1)}, bf16[2,4,96,896]{3,2,1,0:T(8,128)(2,1)}, bf16[2,4,96,896]{3,2,1,0:T(8,128)(2,1)}) custom-call(s32[4]{0:T(128)} %pad_add_fusion.place, bf16[768,256]{1,0:T(8,128)(2,1)} %get-tuple-element.171.refs_0_, bf16[768,256]{1,0:T(8,128)(2,1)} %copy-done.37, ...), custom_call_target="tpu_custom_call" | custom-call | flops 8000000 | bytes 24000 | tf_op jit(solution)/shard_map/grad_mlp_1/pallas_call | solution.py:476
  279.7 13.1 %pull_attention_1.1 = (f32[256,768]{1,0:T(8,128)}, f32[8,768]{1,0:T(8,128)}, bf16[768,256]{1,0:T(8,128)(2,1)}, bf16[2,256,768]{2,1,0:T(8,128)(2,1)}, bf16[2,256,768]{2,1,0:T(8,128)(2,1)}) custom-call(s32[4]{0:T(128)} %pad_add_fusion.place, f32[256,768]{1,0:T(8,128)} %get-tuple-element.180.refs_0_, bf16[4,256,640]{2,1,0:T(8,128)(2,1)} %get-tuple-element.181.refs_1_, ...), custom_call_target="tpu_custom_call" | custom-call | flops 10000000 | bytes 30000 | tf_op jit(solution)/shard_map/pull_attention_1/pallas_call | solution.py:476
  293.5 2.1 collective-permute-done.38.refs_7_
  299.2 5.0 %grad_attention_1.1 = (bf16[2,4,96,768]{3,2,1,0:T(8,128)(2,1)}, bf16[2,4,96,768]{3,2,1,0:T(8,128)(2,1)}) custom-call(s32[4]{0:T(128)} %pad_add_fusion.place, bf16[768,256]{1,0:T(8,128)(2,1)} %get-tuple-element.186.refs_0_, bf16[768,256]{1,0:T(8,128)(2,1)} %copy-done.45, bf16[2,256,768]{2,1,0:T(8,128)(2,1)} %get-tuple-element.187.refs_2_, ...), custom_call_target="tpu_custom_call" | custom-call | flops 5000000 | bytes 15000 | tf_op jit(solution)/shard_map/grad_attention_1/pallas_call | solution.py:476
  304.2 1.6 collective-permute-start.45
  305.8 9.7 %pull_mlp_0.1 = (f32[256,768]{1,0:T(8,128)}, f32[8,768]{1,0:T(8,128)}, bf16[768,256]{1,0:T(8,128)(2,1)}, bf16[2,256,768]{2,1,0:T(8,128)(2,1)}, bf16[2,256,768]{2,1,0:T(8,128)(2,1)}) custom-call(s32[4]{0:T(128)} %pad_add_fusion.place, f32[256,768]{1,0:T(8,128)} %get-tuple-element.193.refs_0_, bf16[4,256,768]{2,1,0:T(8,128)(2,1)} %get-tuple-element.194.refs_1_, ...), custom_call_target="tpu_custom_call" | custom-call | flops 8000000 | bytes 24000 | tf_op jit(solution)/shard_map/pull_mlp_0/pallas_call | solution.py:476
  316.0 2.2 fusion.4
  320.5 1.9 copy.90
  322.5 1.7 copy.91
  326.2 6.4 %grad_mlp_0.1 = (bf16[2,4,96,768]{3,2,1,0:T(8,128)(2,1)}, bf16[2,4,96,768]{3,2,1,0:T(8,128)(2,1)}, bf16[2,4,96,768]{3,2,1,0:T(8,128)(2,1)}, bf16[2,4,96,768]{3,2,1,0:T(8,128)(2,1)}) custom-call(s32[4]{0:T(128)} %pad_add_fusion.place, bf16[768,256]{1,0:T(8,128)(2,1)} %get-tuple-element.203.refs_0_, bf16[768,256]{1,0:T(8,128)(2,1)} %copy-done.36, ...), custom_call_target="tpu_custom_call" | custom-call | flops 8000000 | bytes 24000 | tf_op jit(solution)/shard_map/grad_mlp_0/pallas_call | solution.py:476
  335.5 12.9 %pull_attention_0.1 = (f32[256,768]{1,0:T(8,128)}, f32[8,768]{1,0:T(8,128)}, bf16[768,256]{1,0:T(8,128)(2,1)}, bf16[2,256,768]{2,1,0:T(8,128)(2,1)}, bf16[2,256,768]{2,1,0:T(8,128)(2,1)}) custom-call(s32[4]{0:T(128)} %pad_add_fusion.place, f32[256,768]{1,0:T(8,128)} %get-tuple-element.211.refs_0_, bf16[4,256,640]{2,1,0:T(8,128)(2,1)} %get-tuple-element.212.refs_1_, ...), custom_call_target="tpu_custom_call" | custom-call | flops 10000000 | bytes 30000 | tf_op jit(solution)/shard_map/pull_attention_0/pallas_call | solution.py:476
  351.4 2.0 collective-permute-start.81
  353.4 1.9 collective-permute-start.82
  356.6 7.1 %collective-permute-done.80 = bf16[96,1664]{1,0:T(8,128)(2,1)S(1)} collective-permute-done((bf16[96,1664]{1,0:T(8,128)(2,1)S(1)}, bf16[96,1664]{1,0:T(8,128)(2,1)S(1)}, u32[]{:S(2)}, u32[]{:S(2)}) %collective-permute-start.80) | collective-permute-done | bytes 319520 | tf_op jit(solution)/shard_map/z_up_1_down_1_1/ppermute | solution.py:685
  364.2 11.9 %collective-permute-done.81 = bf16[96,1664]{1,0:T(8,128)(2,1)S(1)} collective-permute-done((bf16[96,1664]{1,0:T(8,128)(2,1)S(1)}, bf16[96,1664]{1,0:T(8,128)(2,1)S(1)}, u32[]{:S(2)}, u32[]{:S(2)}) %collective-permute-start.81) | collective-permute-done | bytes 319520 | tf_op jit(solution)/shard_map/z_up_1_down_1_2/ppermute | solution.py:685
  380.2 6.0 %collective-permute-start.72 = (bf16[96,768]{1,0:T(8,128)(2,1)S(1)}, bf16[96,768]{1,0:T(8,128)(2,1)S(1)}, u32[]{:S(2)}, u32[]{:S(2)}) collective-permute-start(bf16[96,768]{1,0:T(8,128)(2,1)S(1)} %get-tuple-element.370), channel_id=1, source_target_pairs={{0,8},{4,12},{8,16},{12,20},{16,24},{20,28},{24,0},{28,4},{1,9},{5... | collective-permute-start | bytes 442376 | tf_op jit(solution)/shard_map/z_att_1_1/ppermute | solution.py:685
  386.3 2.0 fusion.7
  388.3 2.4 collective-permute-start.74
  390.8 2.1 fusion.6
  394.6 1.6 collective-permute-done.73
  400.6 5.1 %grad_attention_0.1 = (bf16[2,4,96,384]{3,2,1,0:T(8,128)(2,1)}, bf16[2,4,96,384]{3,2,1,0:T(8,128)(2,1)}, bf16[2,4,96,384]{3,2,1,0:T(8,128)(2,1)}, bf16[2,4,96,384]{3,2,1,0:T(8,128)(2,1)}) custom-call(s32[4]{0:T(128)} %pad_add_fusion.place, bf16[768,256]{1,0:T(8,128)(2,1)} %get-tuple-element.228.refs_0_, bf16[768,256]{1,0:T(8,128)(2,1)} %copy-done.43, ...), custom_call_target="tpu_custom_call" | custom-call | flops 5000000 | bytes 15000 | tf_op jit(solution)/shard_map/grad_attention_0/pallas_call | solution.py:476
  405.6 2.6 collective-permute-done.52
  409.1 1.7 fusion.26
  410.9 3.2 collective-permute-start.76
  416.8 5.9 %collective-permute-done.75 = bf16[96,1536]{1,0:T(8,128)(2,1)S(1)} collective-permute-done((bf16[96,1536]{1,0:T(8,128)(2,1)S(1)}, bf16[96,1536]{1,0:T(8,128)(2,1)S(1)}, u32[]{:S(2)}, u32[]{:S(2)}) %collective-permute-start.75) | collective-permute-done | bytes 294944 | tf_op jit(solution)/shard_map/z_up_0_down_0_1/ppermute | solution.py:685
  422.8 10.7 %collective-permute-done.76 = bf16[96,1536]{1,0:T(8,128)(2,1)S(1)} collective-permute-done((bf16[96,1536]{1,0:T(8,128)(2,1)S(1)}, bf16[96,1536]{1,0:T(8,128)(2,1)S(1)}, u32[]{:S(2)}, u32[]{:S(2)}) %collective-permute-start.76) | collective-permute-done | bytes 294944 | tf_op jit(solution)/shard_map/z_up_0_down_0_2/ppermute | solution.py:685
  443.4 1.8 collective-permute-done.57
  448.3 4.7 collective-permute-done.59
  453.7 6.8 %collective-permute-start.62 = (f32[4,8,768]{2,1,0:T(8,128)S(1)}, f32[4,8,768]{2,1,0:T(8,128)S(1)}, u32[]{:S(2)}, u32[]{:S(2)}) collective-permute-start(f32[4,8,768]{2,1,0:T(8,128)S(1)} %add.594), channel_id=1, source_target_pairs={{0,8},{4,12},{8,16},{12,20},{16,24},{20,28},{24,0},{28,4},{1,9},{5... | collective-permute-start | bytes 294920 | tf_op jit(solution)/shard_map/z_sums_1/ppermute | solution.py:685
  460.8 2.5 collective-permute-start.64
  463.5 2.5 collective-permute-start.69
  467.7 1.9 collective-permute-start.70
  469.6 3.6 collective-permute-done.63
  (414 shorter events, 97.9 us)
Async XLA Ops:
  7.2 161.9 %all-gather.4.cloned.1.call-start = ((), (), s32[]{:S(2)}) async-start(), calls=%async_computation.2 | async-start | bytes 15409152 | tf_op jit(solution)/shard_map/all_gather | solution.py:868
  10.8 8.6 %collective-permute-start.3 = (f32[2,1408]{1,0:T(2,128)S(1)}, f32[2,1408]{1,0:T(2,128)S(1)}, u32[]{:S(2)}, u32[]{:S(2)}) collective-permute-start(f32[2,1408]{1,0:T(2,128)S(1)} %concatenate.43), channel_id=1, source_target_pairs={{0,2},{1,3},{2,0},{3,1},{4,6},{5,7},{6,4},{7,5},{8,10},{9,11},{10,... | collective-permute-start | bytes 33800 | tf_op jit(solution)/shard_map/x_biases/ppermute | solution.py:669
  13.9 8.7 %collective-permute-start = (bf16[96,768]{1,0:T(8,128)(2,1)S(1)}, bf16[96,768]{1,0:T(8,128)(2,1)S(1)}, u32[]{:S(2)}, u32[]{:S(2)}) collective-permute-start(bf16[96,768]{1,0:T(8,128)(2,1)S(1)} %pad_maximum_fusion.17), channel_id=1, source_target_pairs={{0,8},{4,12},{8,16},{12,20},{16,24},{20,28},{24,0},{28,4},{1,9},{5... | collective-permute-start | bytes 442376 | tf_op jit(solution)/shard_map/z_att_0_1/ppermute | solution.py:685
  15.5 12.9 %collective-permute-start.1 = (bf16[96,768]{1,0:T(8,128)(2,1)S(1)}, bf16[96,768]{1,0:T(8,128)(2,1)S(1)}, u32[]{:S(2)}, u32[]{:S(2)}) collective-permute-start(bf16[96,768]{1,0:T(8,128)(2,1)S(1)} %pad_maximum_fusion.17), channel_id=1, source_target_pairs={{0,16},{4,20},{8,24},{12,28},{16,0},{20,4},{24,8},{28,12},{1,17},{... | collective-permute-start | bytes 442376 | tf_op jit(solution)/shard_map/z_att_0_2/ppermute | solution.py:685
  18.1 10.3 %collective-permute-start.2 = (bf16[96,768]{1,0:T(8,128)(2,1)S(1)}, bf16[96,768]{1,0:T(8,128)(2,1)S(1)}, u32[]{:S(2)}, u32[]{:S(2)}) collective-permute-start(bf16[96,768]{1,0:T(8,128)(2,1)S(1)} %pad_maximum_fusion.17), channel_id=1, source_target_pairs={{0,24},{4,28},{8,0},{12,4},{16,8},{20,12},{24,16},{28,20},{1,25},{... | collective-permute-start | bytes 442376 | tf_op jit(solution)/shard_map/z_att_0_3/ppermute | solution.py:685
  28.5 16.2 %collective-permute-start.6 = (bf16[4,96,768]{2,1,0:T(8,128)(2,1)S(1)}, bf16[4,96,768]{2,1,0:T(8,128)(2,1)S(1)}, u32[]{:S(2)}, u32[]{:S(2)}) collective-permute-start(bf16[4,96,768]{2,1,0:T(8,128)(2,1)S(1)} %pad_maximum_fusion.3), channel_id=1, source_target_pairs={{0,4},{4,0},{8,12},{12,8},{16,20},{20,16},{24,28},{28,24},{1,5},{5... | collective-permute-start | bytes 1769480 | tf_op jit(solution)/shard_map/y_att_0_first/ppermute | solution.py:674
  30.2 27.7 %collective-permute-start.15 = (bf16[96,768]{1,0:T(8,128)(2,1)S(1)}, bf16[96,768]{1,0:T(8,128)(2,1)S(1)}, u32[]{:S(2)}, u32[]{:S(2)}) collective-permute-start(bf16[96,768]{1,0:T(8,128)(2,1)S(1)} %get-tuple-element.150), channel_id=1, source_target_pairs={{0,8},{4,12},{8,16},{12,20},{16,24},{20,28},{24,0},{28,4},{1,9},{5... | collective-permute-start | bytes 442376 | tf_op jit(solution)/shard_map/z_down_0_1/ppermute | solution.py:685
  42.4 15.5 %collective-permute-start.16 = (bf16[96,768]{1,0:T(8,128)(2,1)S(1)}, bf16[96,768]{1,0:T(8,128)(2,1)S(1)}, u32[]{:S(2)}, u32[]{:S(2)}) collective-permute-start(bf16[96,768]{1,0:T(8,128)(2,1)S(1)} %get-tuple-element.150), channel_id=1, source_target_pairs={{0,16},{4,20},{8,24},{12,28},{16,0},{20,4},{24,8},{28,12},{1,17},{... | collective-permute-start | bytes 442376 | tf_op jit(solution)/shard_map/z_down_0_2/ppermute | solution.py:685
  43.7 26.6 %collective-permute-start.17 = (bf16[96,768]{1,0:T(8,128)(2,1)S(1)}, bf16[96,768]{1,0:T(8,128)(2,1)S(1)}, u32[]{:S(2)}, u32[]{:S(2)}) collective-permute-start(bf16[96,768]{1,0:T(8,128)(2,1)S(1)} %get-tuple-element.150), channel_id=1, source_target_pairs={{0,24},{4,28},{8,0},{12,4},{16,8},{20,12},{24,16},{28,20},{1,25},{... | collective-permute-start | bytes 442376 | tf_op jit(solution)/shard_map/z_down_0_3/ppermute | solution.py:685
  44.9 59.8 %collective-permute-start.7 = (bf16[2,4,96,768]{3,2,1,0:T(8,128)(2,1)S(1)}, bf16[2,4,96,768]{3,2,1,0:T(8,128)(2,1)}, u32[]{:S(2)}, u32[]{:S(2)}) collective-permute-start(bf16[2,4,96,768]{3,2,1,0:T(8,128)(2,1)S(1)} %pad_maximum_fusion.refs_4_.refs_6_), channel_id=1, source_target_pairs={{0,2},{1,3},{2,0},{3,1},{4,6},{5,7},{6,4},{7,5},{8,10},{9,11},{10,... | collective-permute-start | bytes 3538952 | tf_op jit(solution)/shard_map/x_att_0_second/ppermute | solution.py:669
  45.0 25.5 %collective-permute-start.10 = (bf16[96,768]{1,0:T(8,128)(2,1)S(1)}, bf16[96,768]{1,0:T(8,128)(2,1)S(1)}, u32[]{:S(2)}, u32[]{:S(2)}) collective-permute-start(bf16[96,768]{1,0:T(8,128)(2,1)S(1)} %get-tuple-element.149), channel_id=1, source_target_pairs={{0,8},{4,12},{8,16},{12,20},{16,24},{20,28},{24,0},{28,4},{1,9},{5... | collective-permute-start | bytes 442376 | tf_op jit(solution)/shard_map/z_up_0_1/ppermute | solution.py:685
  57.9 18.6 %collective-permute-start.11 = (bf16[96,768]{1,0:T(8,128)(2,1)S(1)}, bf16[96,768]{1,0:T(8,128)(2,1)S(1)}, u32[]{:S(2)}, u32[]{:S(2)}) collective-permute-start(bf16[96,768]{1,0:T(8,128)(2,1)S(1)} %get-tuple-element.149), channel_id=1, source_target_pairs={{0,16},{4,20},{8,24},{12,28},{16,0},{20,4},{24,8},{28,12},{1,17},{... | collective-permute-start | bytes 442376 | tf_op jit(solution)/shard_map/z_up_0_2/ppermute | solution.py:685
  57.9 18.6 %collective-permute-start.12 = (bf16[96,768]{1,0:T(8,128)(2,1)S(1)}, bf16[96,768]{1,0:T(8,128)(2,1)S(1)}, u32[]{:S(2)}, u32[]{:S(2)}) collective-permute-start(bf16[96,768]{1,0:T(8,128)(2,1)S(1)} %get-tuple-element.149), channel_id=1, source_target_pairs={{0,24},{4,28},{8,0},{12,4},{16,8},{20,12},{24,16},{28,20},{1,25},{... | collective-permute-start | bytes 442376 | tf_op jit(solution)/shard_map/z_up_0_3/ppermute | solution.py:685
  70.4 10.1 %collective-permute-start.18 = (bf16[4,96,768]{2,1,0:T(8,128)(2,1)S(1)}, bf16[4,96,768]{2,1,0:T(8,128)(2,1)}, u32[]{:S(2)}, u32[]{:S(2)}) collective-permute-start(bf16[4,96,768]{2,1,0:T(8,128)(2,1)S(1)} %get-tuple-element.384), channel_id=1, source_target_pairs={{0,4},{4,0},{8,12},{12,8},{16,20},{20,16},{24,28},{28,24},{1,5},{5... | collective-permute-start | bytes 1769480 | tf_op jit(solution)/shard_map/y_down_0_first/ppermute | solution.py:674
  76.6 27.8 %collective-permute-start.13 = (bf16[4,96,768]{2,1,0:T(8,128)(2,1)S(1)}, bf16[4,96,768]{2,1,0:T(8,128)(2,1)S(1)}, u32[]{:S(2)}, u32[]{:S(2)}) collective-permute-start(bf16[4,96,768]{2,1,0:T(8,128)(2,1)S(1)} %get-tuple-element.386), channel_id=1, source_target_pairs={{0,2},{1,3},{2,0},{3,1},{4,6},{5,7},{6,4},{7,5},{8,10},{9,11},{10,... | collective-permute-start | bytes 1769480 | tf_op jit(solution)/shard_map/x_up_0_first/ppermute | solution.py:669
  77.9 35.7 %collective-permute-start.8 = (bf16[2,4,96,768]{3,2,1,0:T(8,128)(2,1)S(1)}, bf16[2,4,96,768]{3,2,1,0:T(8,128)(2,1)}, u32[]{:S(2)}, u32[]{:S(2)}) collective-permute-start(bf16[2,4,96,768]{3,2,1,0:T(8,128)(2,1)S(1)} %pad_maximum_fusion.refs_4_.refs_6_), channel_id=1, source_target_pairs={{0,1},{1,0},{2,3},{3,2},{4,5},{5,4},{6,7},{7,6},{8,9},{9,8},{10,11... | collective-permute-start | bytes 3538952 | tf_op jit(solution)/shard_map/core_att_0/ppermute | solution.py:679
  81.6 67.6 %collective-permute-start.19 = (bf16[2,4,96,768]{3,2,1,0:T(8,128)(2,1)S(1)}, bf16[2,4,96,768]{3,2,1,0:T(8,128)(2,1)}, u32[]{:S(2)}, u32[]{:S(2)}) collective-permute-start(bf16[2,4,96,768]{3,2,1,0:T(8,128)(2,1)S(1)} %pad_maximum_fusion.2.refs_7_.refs_9_), channel_id=1, source_target_pairs={{0,2},{1,3},{2,0},{3,1},{4,6},{5,7},{6,4},{7,5},{8,10},{9,11},{10,... | collective-permute-start | bytes 3538952 | tf_op jit(solution)/shard_map/x_down_0_second/ppermute | solution.py:669
  104.6 44.6 %collective-permute-start.14 = (bf16[2,4,96,768]{3,2,1,0:T(8,128)(2,1)S(1)}, bf16[2,4,96,768]{3,2,1,0:T(8,128)(2,1)}, u32[]{:S(2)}, u32[]{:S(2)}) collective-permute-start(bf16[2,4,96,768]{3,2,1,0:T(8,128)(2,1)S(1)} %pad_maximum_fusion.1.refs_3_.refs_5_), channel_id=1, source_target_pairs={{0,4},{4,0},{8,12},{12,8},{16,20},{20,16},{24,28},{28,24},{1,5},{5... | collective-permute-start | bytes 3538952 | tf_op jit(solution)/shard_map/y_up_0_second/ppermute | solution.py:674
  104.7 8.9 %collective-permute-start.9 = (bf16[2,4,96,768]{3,2,1,0:T(8,128)(2,1)}, bf16[2,4,96,768]{3,2,1,0:T(8,128)(2,1)}, u32[]{:S(2)}, u32[]{:S(2)}) collective-permute-start(bf16[2,4,96,768]{3,2,1,0:T(8,128)(2,1)} %collective-permute-done.7.refs_5_.refs_7_), channel_id=1, source_target_pairs={{0,1},{1,0},{2,3},{3,2},{4,5},{5,4},{6,7},{7,6},{8,9},{9,8},{10,11... | collective-permute-start | bytes 3538952 | tf_op jit(solution)/shard_map/core_att_0/ppermute | solution.py:679
  149.7 6.6 %collective-permute-start.22 = (bf16[2,4,96,768]{3,2,1,0:T(8,128)(2,1)S(1)}, bf16[2,4,96,768]{3,2,1,0:T(8,128)(2,1)S(1)}, u32[]{:S(2)}, u32[]{:S(2)}) collective-permute-start(bf16[2,4,96,768]{3,2,1,0:T(8,128)(2,1)S(1)} %pad_maximum_fusion.2.refs_7_.refs_9_), channel_id=1, source_target_pairs={{0,1},{1,0},{2,3},{3,2},{4,5},{5,4},{6,7},{7,6},{8,9},{9,8},{10,11... | collective-permute-start | bytes 3538952 | tf_op jit(solution)/shard_map/core_down_0/ppermute | solution.py:679
  149.8 8.3 %collective-permute-start.23 = (bf16[2,4,96,768]{3,2,1,0:T(8,128)(2,1)}, bf16[2,4,96,768]{3,2,1,0:T(8,128)(2,1)S(1)}, u32[]{:S(2)}, u32[]{:S(2)}) collective-permute-start(bf16[2,4,96,768]{3,2,1,0:T(8,128)(2,1)} %collective-permute-done.19.refs_8_.refs_10_), channel_id=1, source_target_pairs={{0,1},{1,0},{2,3},{3,2},{4,5},{5,4},{6,7},{7,6},{8,9},{9,8},{10,11... | collective-permute-start | bytes 3538952 | tf_op jit(solution)/shard_map/core_down_0/ppermute | solution.py:679
  192.5 28.0 %all-to-all-start = ((bf16[8,256,128]{2,1,0:T(8,128)(2,1)}), bf16[8,256,128]{2,1,0:T(8,128)(2,1)S(1)}, u32[]{:S(2)}, u32[]{:S(2)}) async-start(bf16[8,256,128]{2,1,0:T(8,128)(2,1)} %broadcast_in_dim.55), calls=%async_computation | async-start | bytes 1048576 | tf_op jit(solution)/shard_map/all_to_all | solution.py:1071
  236.6 18.7 %all-to-all-start.1 = ((bf16[8,256,128]{2,1,0:T(8,128)(2,1)}), bf16[8,256,128]{2,1,0:T(8,128)(2,1)S(1)}, u32[]{:S(2)}, u32[]{:S(2)}) async-start(bf16[8,256,128]{2,1,0:T(8,128)(2,1)} %get-tuple-element.163), calls=%async_computation.1 | async-start | bytes 1048576 | tf_op jit(solution)/shard_map/all_to_all | solution.py:1096
  240.2 28.7 %collective-permute-start.33 = (bf16[2,256,768]{2,1,0:T(8,128)(2,1)}, bf16[2,256,768]{2,1,0:T(8,128)(2,1)S(1)}, u32[]{:S(2)}, u32[]{:S(2)}) collective-permute-start(bf16[2,256,768]{2,1,0:T(8,128)(2,1)} %get-tuple-element.176), channel_id=1, source_target_pairs={{0,1},{1,0},{2,3},{3,2},{4,5},{5,4},{6,7},{7,6},{8,9},{9,8},{10,11... | collective-permute-start | bytes 2359304 | tf_op jit(solution)/shard_map/core_pair/ppermute | solution.py:679
  240.5 14.9 %collective-permute-start.27 = (f32[256,128]{1,0:T(8,128)}, f32[256,128]{1,0:T(8,128)S(1)}, u32[]{:S(2)}, u32[]{:S(2)}) collective-permute-start(f32[256,128]{1,0:T(8,128)} %get-tuple-element.162), channel_id=1, source_target_pairs={{0,3},{4,7},{8,11},{12,15},{16,19},{20,23},{24,27},{28,31}} | collective-permute-start | bytes 393224 | tf_op jit(solution)/shard_map/ppermute | solution.py:1098
  242.8 12.6 %collective-permute-start.28 = (f32[256,128]{1,0:T(8,128)}, f32[256,128]{1,0:T(8,128)S(1)}, u32[]{:S(2)}, u32[]{:S(2)}) collective-permute-start(f32[256,128]{1,0:T(8,128)} %get-tuple-element.162), channel_id=1, source_target_pairs={{1,3},{5,7},{9,11},{13,15},{17,19},{21,23},{25,27},{29,31}} | collective-permute-start | bytes 393224 | tf_op jit(solution)/shard_map/ppermute | solution.py:1098
  243.4 11.9 %collective-permute-start.29 = (f32[256,128]{1,0:T(8,128)}, f32[256,128]{1,0:T(8,128)S(1)}, u32[]{:S(2)}, u32[]{:S(2)}) collective-permute-start(f32[256,128]{1,0:T(8,128)} %get-tuple-element.162), channel_id=1, source_target_pairs={{2,3},{6,7},{10,11},{14,15},{18,19},{22,23},{26,27},{30,31}} | collective-permute-start | bytes 393224 | tf_op jit(solution)/shard_map/ppermute | solution.py:1098
  277.7 37.7 %collective-permute-start.39 = (bf16[2,4,96,768]{3,2,1,0:T(8,128)(2,1)}, bf16[2,4,96,768]{3,2,1,0:T(8,128)(2,1)}, u32[]{:S(2)}, u32[]{:S(2)}) collective-permute-start(bf16[2,4,96,768]{3,2,1,0:T(8,128)(2,1)} %get-tuple-element.200), channel_id=1, source_target_pairs={{0,2},{1,3},{2,0},{3,1},{4,6},{5,7},{6,4},{7,5},{8,10},{9,11},{10,... | collective-permute-start | bytes 3538952 | tf_op jit(solution)/shard_map/x_up_1_first/ppermute | solution.py:669
  278.3 40.0 %collective-permute-start.40 = (bf16[2,4,96,896]{3,2,1,0:T(8,128)(2,1)}, bf16[2,4,96,896]{3,2,1,0:T(8,128)(2,1)S(1)}, u32[]{:S(2)}, u32[]{:S(2)}) collective-permute-start(bf16[2,4,96,896]{3,2,1,0:T(8,128)(2,1)} %get-tuple-element.202), channel_id=1, source_target_pairs={{0,4},{4,0},{8,12},{12,8},{16,20},{20,16},{24,28},{28,24},{1,5},{5... | collective-permute-start | bytes 4128776 | tf_op jit(solution)/shard_map/y_down_1_first/ppermute | solution.py:674
  296.2 24.1 %collective-permute-start.44 = (bf16[2,256,768]{2,1,0:T(8,128)(2,1)}, bf16[2,256,768]{2,1,0:T(8,128)(2,1)S(1)}, u32[]{:S(2)}, u32[]{:S(2)}) collective-permute-start(bf16[2,256,768]{2,1,0:T(8,128)(2,1)} %get-tuple-element.208), channel_id=1, source_target_pairs={{0,1},{1,0},{2,3},{3,2},{4,5},{5,4},{6,7},{7,6},{8,9},{9,8},{10,11... | collective-permute-start | bytes 2359304 | tf_op jit(solution)/shard_map/core_pair/ppermute | solution.py:679
  304.2 44.2 %collective-permute-start.45 = (bf16[2,4,96,768]{3,2,1,0:T(8,128)(2,1)}, bf16[2,4,96,768]{3,2,1,0:T(8,128)(2,1)}, u32[]{:S(2)}, u32[]{:S(2)}) collective-permute-start(bf16[2,4,96,768]{3,2,1,0:T(8,128)(2,1)} %get-tuple-element.218), channel_id=1, source_target_pairs={{0,2},{1,3},{2,0},{3,1},{4,6},{5,7},{6,4},{7,5},{8,10},{9,11},{10,... | collective-permute-start | bytes 3538952 | tf_op jit(solution)/shard_map/x_att_1_first/ppermute | solution.py:669
  305.8 14.0 %collective-permute-start.41 = (bf16[768,256]{1,0:T(8,128)(2,1)}, bf16[768,256]{1,0:T(8,128)(2,1)S(1)}, u32[]{:S(2)}, u32[]{:S(2)}) collective-permute-start(bf16[768,256]{1,0:T(8,128)(2,1)} %get-tuple-element.203.refs_0_), channel_id=1, source_target_pairs={{0,1},{1,0},{2,3},{3,2},{4,5},{5,4},{6,7},{7,6},{8,9},{9,8},{10,11... | collective-permute-start | bytes 1179656 | tf_op jit(solution)/shard_map/core_pair/ppermute | solution.py:679
  315.5 10.7 %collective-permute-start.42 = (bf16[2,256,768]{2,1,0:T(8,128)(2,1)}, bf16[2,256,768]{2,1,0:T(8,128)(2,1)}, u32[]{:S(2)}, u32[]{:S(2)}) collective-permute-start(bf16[2,256,768]{2,1,0:T(8,128)(2,1)} %get-tuple-element.205), channel_id=1, source_target_pairs={{0,1},{1,0},{2,3},{3,2},{4,5},{5,4},{6,7},{7,6},{8,9},{9,8},{10,11... | collective-permute-start | bytes 2359304 | tf_op jit(solution)/shard_map/core_pair/ppermute | solution.py:679
  319.2 29.1 %collective-permute-start.78 = (bf16[4,96,768]{2,1,0:T(8,128)(2,1)}, bf16[4,96,768]{2,1,0:T(8,128)(2,1)}, u32[]{:S(2)}, u32[]{:S(2)}) collective-permute-start(bf16[4,96,768]{2,1,0:T(8,128)(2,1)} %fusion.4), channel_id=1, source_target_pairs={{0,4},{4,0},{8,12},{12,8},{16,20},{20,16},{24,28},{28,24},{1,5},{5... | collective-permute-start | bytes 1769480 | tf_op jit(solution)/shard_map/y_up_1_second/ppermute | solution.py:674
  319.8 30.1 %collective-permute-start.79 = (bf16[4,96,896]{2,1,0:T(8,128)(2,1)}, bf16[4,96,896]{2,1,0:T(8,128)(2,1)}, u32[]{:S(2)}, u32[]{:S(2)}) collective-permute-start(bf16[4,96,896]{2,1,0:T(8,128)(2,1)} %fusion), channel_id=1, source_target_pairs={{0,2},{1,3},{2,0},{3,1},{4,6},{5,7},{6,4},{7,5},{8,10},{9,11},{10,... | collective-permute-start | bytes 2064392 | tf_op jit(solution)/shard_map/x_down_1_second/ppermute | solution.py:669
  332.6 53.7 %collective-permute-start.47 = (bf16[2,4,96,768]{3,2,1,0:T(8,128)(2,1)}, bf16[2,4,96,768]{3,2,1,0:T(8,128)(2,1)}, u32[]{:S(2)}, u32[]{:S(2)}) collective-permute-start(bf16[2,4,96,768]{3,2,1,0:T(8,128)(2,1)} %get-tuple-element.227), channel_id=1, source_target_pairs={{0,4},{4,0},{8,12},{12,8},{16,20},{20,16},{24,28},{28,24},{1,5},{5... | collective-permute-start | bytes 3538952 | tf_op jit(solution)/shard_map/y_down_0_first/ppermute | solution.py:674
  334.1 54.2 %collective-permute-start.46 = (bf16[2,4,96,768]{3,2,1,0:T(8,128)(2,1)}, bf16[2,4,96,768]{3,2,1,0:T(8,128)(2,1)}, u32[]{:S(2)}, u32[]{:S(2)}) collective-permute-start(bf16[2,4,96,768]{3,2,1,0:T(8,128)(2,1)} %get-tuple-element.225), channel_id=1, source_target_pairs={{0,2},{1,3},{2,0},{3,1},{4,6},{5,7},{6,4},{7,5},{8,10},{9,11},{10,... | collective-permute-start | bytes 3538952 | tf_op jit(solution)/shard_map/x_up_0_first/ppermute | solution.py:669
  351.3 12.4 %collective-permute-start.80 = (bf16[96,1664]{1,0:T(8,128)(2,1)S(1)}, bf16[96,1664]{1,0:T(8,128)(2,1)S(1)}, u32[]{:S(2)}, u32[]{:S(2)}) collective-permute-start(bf16[96,1664]{1,0:T(8,128)(2,1)S(1)} %pad_maximum_fusion.10), channel_id=1, source_target_pairs={{0,8},{4,12},{8,16},{12,20},{16,24},{20,28},{24,0},{28,4},{1,9},{5... | collective-permute-start | bytes 958472 | tf_op jit(solution)/shard_map/z_up_1_down_1_1/ppermute | solution.py:685
  351.4 24.8 %collective-permute-start.81 = (bf16[96,1664]{1,0:T(8,128)(2,1)S(1)}, bf16[96,1664]{1,0:T(8,128)(2,1)S(1)}, u32[]{:S(2)}, u32[]{:S(2)}) collective-permute-start(bf16[96,1664]{1,0:T(8,128)(2,1)S(1)} %pad_maximum_fusion.11), channel_id=1, source_target_pairs={{0,16},{4,20},{8,24},{12,28},{16,0},{20,4},{24,8},{28,12},{1,17},{... | collective-permute-start | bytes 958472 | tf_op jit(solution)/shard_map/z_up_1_down_1_2/ppermute | solution.py:685
  353.4 22.7 %collective-permute-start.82 = (bf16[96,1664]{1,0:T(8,128)(2,1)S(1)}, bf16[96,1664]{1,0:T(8,128)(2,1)S(1)}, u32[]{:S(2)}, u32[]{:S(2)}) collective-permute-start(bf16[96,1664]{1,0:T(8,128)(2,1)S(1)} %pad_maximum_fusion.12), channel_id=1, source_target_pairs={{0,24},{4,28},{8,0},{12,4},{16,8},{20,12},{24,16},{28,20},{1,25},{... | collective-permute-start | bytes 958472 | tf_op jit(solution)/shard_map/z_up_1_down_1_3/ppermute | solution.py:685
  363.7 15.2 %collective-permute-start.71 = (bf16[4,96,768]{2,1,0:T(8,128)(2,1)S(1)}, bf16[4,96,768]{2,1,0:T(8,128)(2,1)S(1)}, u32[]{:S(2)}, u32[]{:S(2)}) collective-permute-start(bf16[4,96,768]{2,1,0:T(8,128)(2,1)S(1)} %fusion.5), channel_id=1, source_target_pairs={{0,4},{4,0},{8,12},{12,8},{16,20},{20,16},{24,28},{28,24},{1,5},{5... | collective-permute-start | bytes 1769480 | tf_op jit(solution)/shard_map/y_att_1_second/ppermute | solution.py:674
  376.1 16.7 %collective-permute-start.51 = (bf16[2,256,256]{2,1,0:T(8,128)(2,1)S(1)}, bf16[2,256,256]{2,1,0:T(8,128)(2,1)S(1)}, u32[]{:S(2)}, u32[]{:S(2)}) collective-permute-start(bf16[2,256,256]{2,1,0:T(8,128)(2,1)S(1)} %copy-done.78), channel_id=1, source_target_pairs={{0,1},{1,0},{2,3},{3,2},{4,5},{5,4},{6,7},{7,6},{8,9},{9,8},{10,11... | collective-permute-start | bytes 786440 | tf_op jit(solution)/shard_map/core_pair/ppermute | solution.py:679
  376.1 23.7 %collective-permute-start.49 = (bf16[2,256,768]{2,1,0:T(8,128)(2,1)S(1)}, bf16[2,256,768]{2,1,0:T(8,128)(2,1)}, u32[]{:S(2)}, u32[]{:S(2)}) collective-permute-start(bf16[2,256,768]{2,1,0:T(8,128)(2,1)S(1)} %copy-done.75), channel_id=1, source_target_pairs={{0,1},{1,0},{2,3},{3,2},{4,5},{5,4},{6,7},{7,6},{8,9},{9,8},{10,11... | collective-permute-start | bytes 2359304 | tf_op jit(solution)/shard_map/core_pair/ppermute | solution.py:679
  380.2 13.6 %collective-permute-start.72 = (bf16[96,768]{1,0:T(8,128)(2,1)S(1)}, bf16[96,768]{1,0:T(8,128)(2,1)S(1)}, u32[]{:S(2)}, u32[]{:S(2)}) collective-permute-start(bf16[96,768]{1,0:T(8,128)(2,1)S(1)} %get-tuple-element.370), channel_id=1, source_target_pairs={{0,8},{4,12},{8,16},{12,20},{16,24},{20,28},{24,0},{28,4},{1,9},{5... | collective-permute-start | bytes 442376 | tf_op jit(solution)/shard_map/z_att_1_1/ppermute | solution.py:685
  386.3 10.0 %collective-permute-start.73 = (bf16[96,768]{1,0:T(8,128)(2,1)S(1)}, bf16[96,768]{1,0:T(8,128)(2,1)S(1)}, u32[]{:S(2)}, u32[]{:S(2)}) collective-permute-start(bf16[96,768]{1,0:T(8,128)(2,1)S(1)} %get-tuple-element.372), channel_id=1, source_target_pairs={{0,16},{4,20},{8,24},{12,28},{16,0},{20,4},{24,8},{28,12},{1,17},{... | collective-permute-start | bytes 442376 | tf_op jit(solution)/shard_map/z_att_1_2/ppermute | solution.py:685
  388.3 9.0 %collective-permute-start.74 = (bf16[96,768]{1,0:T(8,128)(2,1)S(1)}, bf16[96,768]{1,0:T(8,128)(2,1)S(1)}, u32[]{:S(2)}, u32[]{:S(2)}) collective-permute-start(bf16[96,768]{1,0:T(8,128)(2,1)S(1)} %get-tuple-element.371), channel_id=1, source_target_pairs={{0,24},{4,28},{8,0},{12,4},{16,8},{20,12},{24,16},{28,20},{1,25},{... | collective-permute-start | bytes 442376 | tf_op jit(solution)/shard_map/z_att_1_3/ppermute | solution.py:685
  392.8 15.4 %collective-permute-start.52 = (bf16[4,96,768]{2,1,0:T(8,128)(2,1)}, bf16[4,96,768]{2,1,0:T(8,128)(2,1)S(1)}, u32[]{:S(2)}, u32[]{:S(2)}) collective-permute-start(bf16[4,96,768]{2,1,0:T(8,128)(2,1)} %fusion.6), channel_id=1, source_target_pairs={{0,4},{4,0},{8,12},{12,8},{16,20},{20,16},{24,28},{28,24},{1,5},{5... | collective-permute-start | bytes 1769480 | tf_op jit(solution)/shard_map/y_up_0_second/ppermute | solution.py:674
  393.9 15.2 %collective-permute-start.53 = (bf16[4,96,768]{2,1,0:T(8,128)(2,1)}, bf16[4,96,768]{2,1,0:T(8,128)(2,1)}, u32[]{:S(2)}, u32[]{:S(2)}) collective-permute-start(bf16[4,96,768]{2,1,0:T(8,128)(2,1)} %fusion.7), channel_id=1, source_target_pairs={{0,2},{1,3},{2,0},{3,1},{4,6},{5,7},{6,4},{7,5},{8,10},{9,11},{10,... | collective-permute-start | bytes 1769480 | tf_op jit(solution)/shard_map/x_down_0_second/ppermute | solution.py:669
  410.8 11.9 %collective-permute-start.75 = (bf16[96,1536]{1,0:T(8,128)(2,1)S(1)}, bf16[96,1536]{1,0:T(8,128)(2,1)S(1)}, u32[]{:S(2)}, u32[]{:S(2)}) collective-permute-start(bf16[96,1536]{1,0:T(8,128)(2,1)S(1)} %pad_maximum_fusion.13), channel_id=1, source_target_pairs={{0,8},{4,12},{8,16},{12,20},{16,24},{20,28},{24,0},{28,4},{1,9},{5... | collective-permute-start | bytes 884744 | tf_op jit(solution)/shard_map/z_up_0_down_0_1/ppermute | solution.py:685
  410.9 22.5 %collective-permute-start.76 = (bf16[96,1536]{1,0:T(8,128)(2,1)S(1)}, bf16[96,1536]{1,0:T(8,128)(2,1)S(1)}, u32[]{:S(2)}, u32[]{:S(2)}) collective-permute-start(bf16[96,1536]{1,0:T(8,128)(2,1)S(1)} %pad_maximum_fusion.14), channel_id=1, source_target_pairs={{0,16},{4,20},{8,24},{12,28},{16,0},{20,4},{24,8},{28,12},{1,17},{... | collective-permute-start | bytes 884744 | tf_op jit(solution)/shard_map/z_up_0_down_0_2/ppermute | solution.py:685
  414.1 19.3 %collective-permute-start.77 = (bf16[96,1536]{1,0:T(8,128)(2,1)S(1)}, bf16[96,1536]{1,0:T(8,128)(2,1)S(1)}, u32[]{:S(2)}, u32[]{:S(2)}) collective-permute-start(bf16[96,1536]{1,0:T(8,128)(2,1)S(1)} %pad_maximum_fusion.15), channel_id=1, source_target_pairs={{0,24},{4,28},{8,0},{12,4},{16,8},{20,12},{24,16},{28,20},{1,25},{... | collective-permute-start | bytes 884744 | tf_op jit(solution)/shard_map/z_up_0_down_0_3/ppermute | solution.py:685
  415.1 23.6 %collective-permute-start.55 = (bf16[2,4,96,384]{3,2,1,0:T(8,128)(2,1)S(1)}, bf16[2,4,96,384]{3,2,1,0:T(8,128)(2,1)S(1)}, u32[]{:S(2)}, u32[]{:S(2)}) collective-permute-start(bf16[2,4,96,384]{3,2,1,0:T(8,128)(2,1)S(1)} %copy-done.77), channel_id=1, source_target_pairs={{0,4},{4,0},{8,12},{12,8},{16,20},{20,16},{24,28},{28,24},{1,5},{5... | collective-permute-start | bytes 1769480 | tf_op jit(solution)/shard_map/y_vo_0_first/ppermute | solution.py:674
  416.2 22.7 %collective-permute-start.54 = (bf16[2,4,96,384]{3,2,1,0:T(8,128)(2,1)S(1)}, bf16[2,4,96,384]{3,2,1,0:T(8,128)(2,1)S(1)}, u32[]{:S(2)}, u32[]{:S(2)}) collective-permute-start(bf16[2,4,96,384]{3,2,1,0:T(8,128)(2,1)S(1)} %copy-done.76), channel_id=1, source_target_pairs={{0,2},{1,3},{2,0},{3,1},{4,6},{5,7},{6,4},{7,5},{8,10},{9,11},{10,... | collective-permute-start | bytes 1769480 | tf_op jit(solution)/shard_map/x_qk_0_first/ppermute | solution.py:669
  441.6 12.1 %collective-permute-start.60 = (bf16[4,96,384]{2,1,0:T(8,128)(2,1)S(1)}, bf16[4,96,384]{2,1,0:T(8,128)(2,1)S(1)}, u32[]{:S(2)}, u32[]{:S(2)}) collective-permute-start(bf16[4,96,384]{2,1,0:T(8,128)(2,1)S(1)} %fusion.13), channel_id=1, source_target_pairs={{0,4},{4,0},{8,12},{12,8},{16,20},{20,16},{24,28},{28,24},{1,5},{5... | collective-permute-start | bytes 884744 | tf_op jit(solution)/shard_map/y_qk_0_second/ppermute | solution.py:674
  442.6 11.1 %collective-permute-start.61 = (bf16[4,96,384]{2,1,0:T(8,128)(2,1)S(1)}, bf16[4,96,384]{2,1,0:T(8,128)(2,1)S(1)}, u32[]{:S(2)}, u32[]{:S(2)}) collective-permute-start(bf16[4,96,384]{2,1,0:T(8,128)(2,1)S(1)} %fusion.14), channel_id=1, source_target_pairs={{0,2},{1,3},{2,0},{3,1},{4,6},{5,7},{6,4},{7,5},{8,10},{9,11},{10,... | collective-permute-start | bytes 884744 | tf_op jit(solution)/shard_map/x_vo_0_second/ppermute | solution.py:669
  443.4 17.4 %collective-permute-start.65 = (bf16[192,768]{1,0:T(8,128)(2,1)S(1)}, bf16[192,768]{1,0:T(8,128)(2,1)S(1)}, u32[]{:S(2)}, u32[]{:S(2)}) collective-permute-start(bf16[192,768]{1,0:T(8,128)(2,1)S(1)} %dynamic-slice_convert_fusion), channel_id=1, source_target_pairs={{0,1},{1,2},{2,3},{3,0},{4,5},{5,6},{6,7},{7,4},{8,9},{9,10},{10,1... | collective-permute-start | bytes 884744 | tf_op jit(solution)/shard_map/ppermute | solution.py:899
  447.7 15.7 %collective-permute-start.66 = (bf16[64,768]{1,0:T(8,128)(2,1)S(1)}, bf16[64,768]{1,0:T(8,128)(2,1)S(1)}, u32[]{:S(2)}, u32[]{:S(2)}) collective-permute-start(bf16[64,768]{1,0:T(8,128)(2,1)S(1)} %get-tuple-element.389), channel_id=1, source_target_pairs={{3,1},{7,5},{11,9},{15,13},{19,17},{23,21},{27,25},{31,29}} | collective-permute-start | bytes 294920 | tf_op jit(solution)/shard_map/ppermute | solution.py:906
  453.0 10.5 %collective-permute-start.67 = (bf16[64,768]{1,0:T(8,128)(2,1)S(1)}, bf16[64,768]{1,0:T(8,128)(2,1)S(1)}, u32[]{:S(2)}, u32[]{:S(2)}) collective-permute-start(bf16[64,768]{1,0:T(8,128)(2,1)S(1)} %get-tuple-element.390), channel_id=1, source_target_pairs={{3,2},{7,6},{11,10},{15,14},{19,18},{23,22},{27,26},{31,30}} | collective-permute-start | bytes 294920 | tf_op jit(solution)/shard_map/ppermute | solution.py:907
  453.7 14.0 %collective-permute-start.62 = (f32[4,8,768]{2,1,0:T(8,128)S(1)}, f32[4,8,768]{2,1,0:T(8,128)S(1)}, u32[]{:S(2)}, u32[]{:S(2)}) collective-permute-start(f32[4,8,768]{2,1,0:T(8,128)S(1)} %add.594), channel_id=1, source_target_pairs={{0,8},{4,12},{8,16},{12,20},{16,24},{20,28},{24,0},{28,4},{1,9},{5... | collective-permute-start | bytes 294920 | tf_op jit(solution)/shard_map/z_sums_1/ppermute | solution.py:685
  460.6 12.7 %collective-permute-start.63 = (f32[4,8,768]{2,1,0:T(8,128)S(1)}, f32[4,8,768]{2,1,0:T(8,128)S(1)}, u32[]{:S(2)}, u32[]{:S(2)}) collective-permute-start(f32[4,8,768]{2,1,0:T(8,128)S(1)} %add.594), channel_id=1, source_target_pairs={{0,16},{4,20},{8,24},{12,28},{16,0},{20,4},{24,8},{28,12},{1,17},{... | collective-permute-start | bytes 294920 | tf_op jit(solution)/shard_map/z_sums_2/ppermute | solution.py:685
  460.8 12.4 %collective-permute-start.64 = (f32[4,8,768]{2,1,0:T(8,128)S(1)}, f32[4,8,768]{2,1,0:T(8,128)S(1)}, u32[]{:S(2)}, u32[]{:S(2)}) collective-permute-start(f32[4,8,768]{2,1,0:T(8,128)S(1)} %add.594), channel_id=1, source_target_pairs={{0,24},{4,28},{8,0},{12,4},{16,8},{20,12},{24,16},{28,20},{1,25},{... | collective-permute-start | bytes 294920 | tf_op jit(solution)/shard_map/z_sums_3/ppermute | solution.py:685
  463.4 15.1 %collective-permute-start.68 = (bf16[96,768]{1,0:T(8,128)(2,1)S(1)}, bf16[96,768]{1,0:T(8,128)(2,1)S(1)}, u32[]{:S(2)}, u32[]{:S(2)}) collective-permute-start(bf16[96,768]{1,0:T(8,128)(2,1)S(1)} %pad_maximum_fusion.18), channel_id=1, source_target_pairs={{0,8},{4,12},{8,16},{12,20},{16,24},{20,28},{24,0},{28,4},{1,9},{5... | collective-permute-start | bytes 442376 | tf_op jit(solution)/shard_map/z_qk_0_vo_0_1/ppermute | solution.py:685
  463.5 16.0 %collective-permute-start.69 = (bf16[96,768]{1,0:T(8,128)(2,1)S(1)}, bf16[96,768]{1,0:T(8,128)(2,1)S(1)}, u32[]{:S(2)}, u32[]{:S(2)}) collective-permute-start(bf16[96,768]{1,0:T(8,128)(2,1)S(1)} %pad_maximum_fusion.19), channel_id=1, source_target_pairs={{0,16},{4,20},{8,24},{12,28},{16,0},{20,4},{24,8},{28,12},{1,17},{... | collective-permute-start | bytes 442376 | tf_op jit(solution)/shard_map/z_qk_0_vo_0_2/ppermute | solution.py:685
  467.7 11.8 %collective-permute-start.70 = (bf16[96,768]{1,0:T(8,128)(2,1)S(1)}, bf16[96,768]{1,0:T(8,128)(2,1)S(1)}, u32[]{:S(2)}, u32[]{:S(2)}) collective-permute-start(bf16[96,768]{1,0:T(8,128)(2,1)S(1)} %pad_maximum_fusion.20), channel_id=1, source_target_pairs={{0,24},{4,28},{8,0},{12,4},{16,8},{20,12},{24,16},{28,20},{1,25},{... | collective-permute-start | bytes 442376 | tf_op jit(solution)/shard_map/z_qk_0_vo_0_3/ppermute | solution.py:685
  (103 other events, 693.6 us)
Sparse Core Ops, SparseCore 0:
  11.6 155.8 all-gather.3

commit v4 on v3

--- a/solution.py
+++ b/solution.py
@@ -212,7 +212,7 @@
         scale = lax.rsqrt(jnp.sum(embedded * embedded, -1, keepdims=True) + NORM_EPS)
         unit = embedded * scale
         unit_ref[...] = unit
-        emb_ref[...] = unit.astype(BF)
+        emb_ref[...] = jnp.broadcast_to(unit.astype(BF)[None], emb_ref.shape)
         scale_ref[...] = jnp.broadcast_to(scale, scale_ref.shape)
 
 
@@ -510,7 +510,7 @@
     )
 
 
-def run_mlp(layer_at, place, first, up_rows, norms, weights, split):
+def run_mlp(layer_at, place, first, up_rows, norms, weights, split, copies):
     top = layer_at == LAYERS - 1
     ups, up_plan = weights["up"]
     downs, down_plan = weights["down"]
@@ -523,7 +523,7 @@
     scratch = held_scratch(weights["fold"], 2)
     if top:
         outs += [
-            shaped((ROWS, DIM), BF),
+            shaped((copies, ROWS, DIM), BF),
             shaped((ROWS, DIM), F32),
             shaped((ROWS, DIM), F32),
             shaped((WIDTH, ROWS), BF),
@@ -989,9 +989,9 @@
     ]
     if split:
         last_layer = whole_weights(gather_whole(joined(*shards[1], projection), devices))
-        att = Gathering("att_0", shards[0][0], True)
-        up = Gathering("up_0", shards[0][1], False)
-        down = Gathering("down_0", shards[0][2], True)
+        att = Gathering("att_0", shards[0][0], False)
+        up = Gathering("up_0", shards[0][1], True)
+        down = Gathering("down_0", shards[0][2], False)
         att.column()
         att.held, up.shard, down.shard, small_all = tied(
             att.held, up.shard, down.shard, small_all
@@ -1052,7 +1052,14 @@
             weights[0].update(up=up.all(), down=down.all())
         mixtures = sides_of(outs[7], outs[-1])
         outs = run_mlp(
-            layer_at, place, first, up_all[:, layer_at], norm_terms[layer_at], weights[layer_at], split
+            layer_at,
+            place,
+            first,
+            up_all[:, layer_at],
+            norm_terms[layer_at],
+            weights[layer_at],
+            split,
+            devices,
         )
         hidden, slope, normal_two, factor_two = outs[:4]
         acts = sides_of(outs[4], outs[5 if split else 4])
@@ -1068,9 +1075,8 @@
         )
     embedding, unit, scale, top_t = outs[-4:]
 
-    passages = lax.all_to_all(
-        jnp.broadcast_to(embedding[None], (devices, ROWS, DIM)), "dp", 0, 0, tiled=True
-    )
+    passages = lax.all_to_all(embedding, "dp", 0, 0, tiled=True)
+    embedding = embedding[0]
     queries = embedding
     arrived = [lax.ppermute(embedding, "tensor", [(last, at)]) for at in range(last)]
     for at in range(last):

time: 498 us -> 495 us (level)
  waiting for transfers between devices: 152 us -> 146 us
    ppermute x12, waiting for transfers between devices: 50.1 us -> 2.08 us  [over_x(): return lax.ppermute(value, 'tensor', X_SWAP)]
    ppermute x11, waiting for transfers between devices: 9.77 us -> 48.6 us  [over_y(): return lax.ppermute(value, 'dp', Y_SWAP)]
    ppermute x24, waiting for transfers between devices: 56.1 us -> 61.9 us  [along_z(): return lax.ppermute(value, 'dp', pairs)]
    unnamed x176 -> x174, local copies, waits for them, and re-layouts: 20 us -> 19.8 us
  transfers between devices with their start and end apart: 86 -> 86, of which waited for: 34 -> 34; matrix products, arithmetic and copies ran while one was open for 10% -> 11% of each run, Pallas kernels for 17% -> 17%
where the time goes in v4:
time: 495 us; the launch traced here: 488 us
  waiting for transfers between devices  146 us (29%)
  starting transfers between devices  128 us (26%)
  Pallas kernels  119 us (24%)
  other arithmetic  43.3 us (9%)
  local copies, waits for them, and re-layouts  28 us (6%)
  between operations  18.2 us (4%)
  blocking collectives  5.31 us (1%)
    pallas_call x12, Pallas kernels, call(): pl.pallas_call(kernel, out_shape=outs, in_specs=[smem_spec()] + [any_spec...  111 us
    ppermute x24, starting transfers between devices, along_z(): return lax.ppermute(value, 'dp', pairs)  73.5 us
    ppermute x24, waiting for transfers between devices, along_z(): return lax.ppermute(value, 'dp', pairs)  61.9 us
    ppermute x11, waiting for transfers between devices, over_y(): return lax.ppermute(value, 'dp', Y_SWAP)  48.6 us
    unnamed x174, local copies, waits for them, and re-layouts  19.8 us
    ppermute x12, starting transfers between devices, over_x(): return lax.ppermute(value, 'tensor', X_SWAP)  14.9 us
    ppermute x26, waiting for transfers between devices, over_core(): return lax.ppermute(value, 'tensor', CORE_SWAP)  14.3 us
    ppermute x11, starting transfers between devices, over_y(): return lax.ppermute(value, 'dp', Y_SWAP)  12.2 us
  transfers between devices with their start and end apart: 86, of which 34 were waited for; matrix products, arithmetic and copies ran while one was open for 11% of the time, Pallas kernels for 17%

profile of v4, /device:TPU:0, one launch (start us, length us, event | category | flops | bytes accessed | tf_op | source)
XLA Modules:
  0.0 488.5 jit_solution(10786226368258830783)
XLA Ops:
  10.8 2.9 collective-permute-start.3
  13.9 1.6 collective-permute-start
  15.5 2.6 collective-permute-start.1
  22.6 5.8 %collective-permute-done.1 = bf16[96,768]{1,0:T(8,128)(2,1)S(1)} collective-permute-done((bf16[96,768]{1,0:T(8,128)(2,1)S(1)}, bf16[96,768]{1,0:T(8,128)(2,1)S(1)}, u32[]{:S(2)}, u32[]{:S(2)}) %collective-permute-start.1) | collective-permute-done | bytes 147488 | tf_op jit(solution)/shard_map/z_att_0_2/ppermute | solution.py:685
  28.6 12.4 %collective-permute-start.15 = (bf16[96,768]{1,0:T(8,128)(2,1)S(1)}, bf16[96,768]{1,0:T(8,128)(2,1)S(1)}, u32[]{:S(2)}, u32[]{:S(2)}) collective-permute-start(bf16[96,768]{1,0:T(8,128)(2,1)S(1)} %get-tuple-element.150), channel_id=1, source_target_pairs={{0,8},{4,12},{8,16},{12,20},{16,24},{20,28},{24,0},{28,4},{1,9},{5... | collective-permute-start | bytes 442376 | tf_op jit(solution)/shard_map/z_down_0_1/ppermute | solution.py:685
  43.5 1.7 collective-permute-start.7
  45.2 20.0 %collective-permute-start.10 = (bf16[96,768]{1,0:T(8,128)(2,1)S(1)}, bf16[96,768]{1,0:T(8,128)(2,1)S(1)}, u32[]{:S(2)}, u32[]{:S(2)}) collective-permute-start(bf16[96,768]{1,0:T(8,128)(2,1)S(1)} %get-tuple-element.149), channel_id=1, source_target_pairs={{0,8},{4,12},{8,16},{12,20},{16,24},{20,28},{24,0},{28,4},{1,9},{5... | collective-permute-start | bytes 442376 | tf_op jit(solution)/shard_map/z_up_0_1/ppermute | solution.py:685
  65.2 2.8 collective-permute-start.12
  68.8 2.5 collective-permute-done.10
  71.3 10.7 %collective-permute-done.11 = bf16[96,768]{1,0:T(8,128)(2,1)S(1)} collective-permute-done((bf16[96,768]{1,0:T(8,128)(2,1)S(1)}, bf16[96,768]{1,0:T(8,128)(2,1)S(1)}, u32[]{:S(2)}, u32[]{:S(2)}) %collective-permute-start.11) | collective-permute-done | bytes 147488 | tf_op jit(solution)/shard_map/z_up_0_2/ppermute | solution.py:685
  82.1 1.7 collective-permute-start.13
  86.7 16.2 %collective-permute-done.13 = bf16[4,96,768]{2,1,0:T(8,128)(2,1)S(1)} collective-permute-done((bf16[4,96,768]{2,1,0:T(8,128)(2,1)S(1)}, bf16[4,96,768]{2,1,0:T(8,128)(2,1)S(1)}, u32[]{:S(2)}, u32[]{:S(2)}) %collective-permute-start.13) | collective-permute-done | bytes 589856 | tf_op jit(solution)/shard_map/y_up_0_first/ppermute | solution.py:674
  110.4 2.1 dynamic-slice_select_fusion.refs_0_
  113.1 11.0 %attention_0.1 = (f32[256,768]{1,0:T(8,128)}, bf16[768,256]{1,0:T(8,128)(2,1)}, bf16[4,256,640]{2,1,0:T(8,128)(2,1)}, bf16[12,256,256]{2,1,0:T(8,128)(2,1)}, f32...) custom-call(s32[4]{0:T(128)} %pad_add_fusion.place, ...), custom_call_target="tpu_custom_call" | custom-call | flops 9000000 | bytes 27000 | tf_op jit(solution)/shard_map/attention_0/pallas_call | solution.py:476
  124.1 25.2 %collective-permute-done.19.refs_8_.refs_10_ = bf16[2,4,96,768]{3,2,1,0:T(8,128)(2,1)} collective-permute-done((bf16[2,4,96,768]{3,2,1,0:T(8,128)(2,1)S(1)}, bf16[2,4,96,768]{3,2,1,0:T(8,128)(2,1)}, u32[]{:S(2)}, u32[]{:S(2)}) %collective-permute-start.19) | collective-permute-done | bytes 1179680 | tf_op jit(solution)/shard_map/y_down_0_second/ppermute | solution.py:674
  153.1 2.3 collective-permute-done.21.refs_6_.refs_8_
  156.6 1.7 collective-permute-done.23.refs_10_.refs_12_
  159.3 10.2 %mlp_0.1 = (f32[256,768]{1,0:T(8,128)}, bf16[4,256,768]{2,1,0:T(8,128)(2,1)}, f32[256,768]{1,0:T(8,128)}, f32[256,128]{1,0:T(8,128)}, bf16[2,256,768]{2,1,0:T(8,128)(2,1)}, /*index=5*/bf16[2,256,768]{2,1,0:T(8,128)(2,1)}) custom-call(s32[4]{0:T(128)} %pad_add_fusion.place, f32[256,768]{1,0:T(8,128)} %get-tuple-element.151.refs_0_, ...), custom_call_target="tpu_custom_call" | custom-call | flops 9000000 | bytes 27000 | tf_op jit(solution)/shard_map/mlp_0/pallas_call | solution.py:476
  169.5 11.0 %attention_1.1 = (f32[256,768]{1,0:T(8,128)}, bf16[768,256]{1,0:T(8,128)(2,1)}, bf16[4,256,640]{2,1,0:T(8,128)(2,1)}, bf16[12,256,256]{2,1,0:T(8,128)(2,1)}, f32...) custom-call(s32[4]{0:T(128)} %pad_add_fusion.place, ...), custom_call_target="tpu_custom_call" | custom-call | flops 9000000 | bytes 27000 | tf_op jit(solution)/shard_map/attention_1/pallas_call | solution.py:476
  180.5 10.7 %mlp_1.1 = (f32[256,768]{1,0:T(8,128)}, bf16[4,256,768]{2,1,0:T(8,128)(2,1)}, f32[256,768]{1,0:T(8,128)}, f32[256,128]{1,0:T(8,128)}, bf16[2,256,768]{2,1,0:T(8,...) custom-call(s32[4]{0:T(128)} %pad_add_fusion.place, ...), custom_call_target="tpu_custom_call" | custom-call | flops 9000000 | bytes 27000 | tf_op jit(solution)/shard_map/mlp_1/pallas_call | solution.py:476
  191.2 9.5 %all-to-all-start = ((bf16[8,256,128]{2,1,0:T(8,128)(2,1)}), bf16[8,256,128]{2,1,0:T(8,128)(2,1)S(1)}, u32[]{:S(2)}, u32[]{:S(2)}) async-start(bf16[8,256,128]{2,1,0:T(8,128)(2,1)} %get-tuple-element.158), calls=%async_computation | async-start | bytes 1048576 | tf_op jit(solution)/shard_map/all_to_all | solution.py:1078
  205.8 4.8 collective-permute-done.26
  212.1 3.6 all-to-all-done.passages_ref
  216.5 4.0 scores.1
  220.5 5.3 %all-gather.1 = f32[32,8]{1,0:T(8,128)S(1)} all-gather(f32[8,8]{1,0:T(8,128)} %bitcast.382), channel_id=3, replica_groups=mesh['dp'=8,'tensor'=4] {'tensor'}, dimensions={0}, use_global_device_ids=true | all-gather | bytes 1280 | tf_op jit(solution)/shard_map/all_gather | solution.py:1087
  227.9 3.9 score_pulls.1
  231.9 3.6 all-to-all-start.1
  235.7 3.3 collective-permute-start.27
  240.7 9.9 %all-to-all-done.1 = bf16[8,256,128]{2,1,0:T(8,128)(2,1)S(1)} async-done(((bf16[8,256,128]{2,1,0:T(8,128)(2,1)}), bf16[8,256,128]{2,1,0:T(8,128)(2,1)S(1)}, u32[]{:S(2)}, u32[]{:S(2)}) %all-to-all-start.1) | async-done | bytes 524320 | tf_op jit(solution)/shard_map/all_to_all | solution.py:1102
  251.3 9.7 %pull_mlp_1.1 = (f32[256,768]{1,0:T(8,128)}, f32[8,768]{1,0:T(8,128)}, bf16[768,256]{1,0:T(8,128)(2,1)}, bf16[2,256,768]{2,1,0:T(8,128)(2,1)}, bf16[2,256,768]{2,1,0:T(8,128)(2,1)}, /*index=5*/f32[768,128]{1,0:T(8,128)}) custom-call(s32[4]{0:T(128)} %pad_add_fusion.place, f32[256,128]{1,0:T(8,128)} %add_select_fusion.refs_0_, ...), custom_call_target="tpu_custom_call" | custom-call | flops 8000000 | bytes 24000 | tf_op jit(solution)/shard_map/pull_mlp_1/pallas_call | solution.py:476
  262.1 2.1 collective-permute-done.30.refs_1_
  266.3 6.7 %grad_mlp_1.1 = (bf16[2,4,96,768]{3,2,1,0:T(8,128)(2,1)}, bf16[2,4,96,768]{3,2,1,0:T(8,128)(2,1)}, bf16[2,4,96,896]{3,2,1,0:T(8,128)(2,1)}, bf16[2,4,96,896]{3,2,1,0:T(8,128)(2,1)}) custom-call(s32[4]{0:T(128)} %pad_add_fusion.place, bf16[768,256]{1,0:T(8,128)(2,1)} %get-tuple-element.171.refs_0_, bf16[768,256]{1,0:T(8,128)(2,1)} %copy-done.37, ...), custom_call_target="tpu_custom_call" | custom-call | flops 8000000 | bytes 24000 | tf_op jit(solution)/shard_map/grad_mlp_1/pallas_call | solution.py:476
  273.0 1.6 collective-permute-start.39
  276.1 13.1 %pull_attention_1.1 = (f32[256,768]{1,0:T(8,128)}, f32[8,768]{1,0:T(8,128)}, bf16[768,256]{1,0:T(8,128)(2,1)}, bf16[2,256,768]{2,1,0:T(8,128)(2,1)}, bf16[2,256,768]{2,1,0:T(8,128)(2,1)}) custom-call(s32[4]{0:T(128)} %pad_add_fusion.place, f32[256,768]{1,0:T(8,128)} %get-tuple-element.180.refs_0_, bf16[4,256,640]{2,1,0:T(8,128)(2,1)} %get-tuple-element.181.refs_1_, ...), custom_call_target="tpu_custom_call" | custom-call | flops 10000000 | bytes 30000 | tf_op jit(solution)/shard_map/pull_attention_1/pallas_call | solution.py:476
  289.9 2.1 collective-permute-done.38.refs_7_
  295.5 5.0 %grad_attention_1.1 = (bf16[2,4,96,768]{3,2,1,0:T(8,128)(2,1)}, bf16[2,4,96,768]{3,2,1,0:T(8,128)(2,1)}) custom-call(s32[4]{0:T(128)} %pad_add_fusion.place, bf16[768,256]{1,0:T(8,128)(2,1)} %get-tuple-element.186.refs_0_, bf16[768,256]{1,0:T(8,128)(2,1)} %copy-done.45, bf16[2,256,768]{2,1,0:T(8,128)(2,1)} %get-tuple-element.187.refs_2_, ...), custom_call_target="tpu_custom_call" | custom-call | flops 5000000 | bytes 15000 | tf_op jit(solution)/shard_map/grad_attention_1/pallas_call | solution.py:476
  301.0 9.7 %pull_mlp_0.1 = (f32[256,768]{1,0:T(8,128)}, f32[8,768]{1,0:T(8,128)}, bf16[768,256]{1,0:T(8,128)(2,1)}, bf16[2,256,768]{2,1,0:T(8,128)(2,1)}, bf16[2,256,768]{2,1,0:T(8,128)(2,1)}) custom-call(s32[4]{0:T(128)} %pad_add_fusion.place, f32[256,768]{1,0:T(8,128)} %get-tuple-element.193.refs_0_, bf16[4,256,768]{2,1,0:T(8,128)(2,1)} %get-tuple-element.194.refs_1_, ...), custom_call_target="tpu_custom_call" | custom-call | flops 8000000 | bytes 24000 | tf_op jit(solution)/shard_map/pull_mlp_0/pallas_call | solution.py:476
  311.3 2.2 fusion.4
  315.1 1.6 collective-permute-start.79
  316.7 1.9 copy.90
  318.7 1.7 copy.91
  322.3 6.4 %grad_mlp_0.1 = (bf16[2,4,96,768]{3,2,1,0:T(8,128)(2,1)}, bf16[2,4,96,768]{3,2,1,0:T(8,128)(2,1)}, bf16[2,4,96,768]{3,2,1,0:T(8,128)(2,1)}, bf16[2,4,96,768]{3,2,1,0:T(8,128)(2,1)}) custom-call(s32[4]{0:T(128)} %pad_add_fusion.place, bf16[768,256]{1,0:T(8,128)(2,1)} %get-tuple-element.203.refs_0_, bf16[768,256]{1,0:T(8,128)(2,1)} %copy-done.36, ...), custom_call_target="tpu_custom_call" | custom-call | flops 8000000 | bytes 24000 | tf_op jit(solution)/shard_map/grad_mlp_0/pallas_call | solution.py:476
  330.9 12.9 %pull_attention_0.1 = (f32[256,768]{1,0:T(8,128)}, f32[8,768]{1,0:T(8,128)}, bf16[768,256]{1,0:T(8,128)(2,1)}, bf16[2,256,768]{2,1,0:T(8,128)(2,1)}, bf16[2,256,768]{2,1,0:T(8,128)(2,1)}) custom-call(s32[4]{0:T(128)} %pad_add_fusion.place, f32[256,768]{1,0:T(8,128)} %get-tuple-element.211.refs_0_, bf16[4,256,640]{2,1,0:T(8,128)(2,1)} %get-tuple-element.212.refs_1_, ...), custom_call_target="tpu_custom_call" | custom-call | flops 10000000 | bytes 30000 | tf_op jit(solution)/shard_map/pull_attention_0/pallas_call | solution.py:476
  346.8 2.0 collective-permute-start.81
  348.9 1.9 collective-permute-start.82
  352.0 7.1 %collective-permute-done.80 = bf16[96,1664]{1,0:T(8,128)(2,1)S(1)} collective-permute-done((bf16[96,1664]{1,0:T(8,128)(2,1)S(1)}, bf16[96,1664]{1,0:T(8,128)(2,1)S(1)}, u32[]{:S(2)}, u32[]{:S(2)}) %collective-permute-start.80) | collective-permute-done | bytes 319520 | tf_op jit(solution)/shard_map/z_up_1_down_1_1/ppermute | solution.py:685
  359.7 11.9 %collective-permute-done.81 = bf16[96,1664]{1,0:T(8,128)(2,1)S(1)} collective-permute-done((bf16[96,1664]{1,0:T(8,128)(2,1)S(1)}, bf16[96,1664]{1,0:T(8,128)(2,1)S(1)}, u32[]{:S(2)}, u32[]{:S(2)}) %collective-permute-start.81) | collective-permute-done | bytes 319520 | tf_op jit(solution)/shard_map/z_up_1_down_1_2/ppermute | solution.py:685
  375.7 6.0 %collective-permute-start.72 = (bf16[96,768]{1,0:T(8,128)(2,1)S(1)}, bf16[96,768]{1,0:T(8,128)(2,1)S(1)}, u32[]{:S(2)}, u32[]{:S(2)}) collective-permute-start(bf16[96,768]{1,0:T(8,128)(2,1)S(1)} %get-tuple-element.370), channel_id=1, source_target_pairs={{0,8},{4,12},{8,16},{12,20},{16,24},{20,28},{24,0},{28,4},{1,9},{5... | collective-permute-start | bytes 442376 | tf_op jit(solution)/shard_map/z_att_1_1/ppermute | solution.py:685
  381.7 2.0 fusion.7
  383.8 2.4 collective-permute-start.74
  386.2 2.1 fusion.6
  396.0 5.1 %grad_attention_0.1 = (bf16[2,4,96,384]{3,2,1,0:T(8,128)(2,1)}, bf16[2,4,96,384]{3,2,1,0:T(8,128)(2,1)}, bf16[2,4,96,384]{3,2,1,0:T(8,128)(2,1)}, bf16[2,4,96,384]{3,2,1,0:T(8,128)(2,1)}) custom-call(s32[4]{0:T(128)} %pad_add_fusion.place, bf16[768,256]{1,0:T(8,128)(2,1)} %get-tuple-element.228.refs_0_, bf16[768,256]{1,0:T(8,128)(2,1)} %copy-done.43, ...), custom_call_target="tpu_custom_call" | custom-call | flops 5000000 | bytes 15000 | tf_op jit(solution)/shard_map/grad_attention_0/pallas_call | solution.py:476
  401.1 2.6 collective-permute-done.52
  404.6 1.7 fusion.26
  406.4 3.1 collective-permute-start.76
  413.0 5.3 %collective-permute-done.75 = bf16[96,1536]{1,0:T(8,128)(2,1)S(1)} collective-permute-done((bf16[96,1536]{1,0:T(8,128)(2,1)S(1)}, bf16[96,1536]{1,0:T(8,128)(2,1)S(1)}, u32[]{:S(2)}, u32[]{:S(2)}) %collective-permute-start.75) | collective-permute-done | bytes 294944 | tf_op jit(solution)/shard_map/z_up_0_down_0_1/ppermute | solution.py:685
  418.3 10.7 %collective-permute-done.76 = bf16[96,1536]{1,0:T(8,128)(2,1)S(1)} collective-permute-done((bf16[96,1536]{1,0:T(8,128)(2,1)S(1)}, bf16[96,1536]{1,0:T(8,128)(2,1)S(1)}, u32[]{:S(2)}, u32[]{:S(2)}) %collective-permute-start.76) | collective-permute-done | bytes 294944 | tf_op jit(solution)/shard_map/z_up_0_down_0_2/ppermute | solution.py:685
  443.8 4.6 collective-permute-done.59
  449.2 6.8 %collective-permute-start.62 = (f32[4,8,768]{2,1,0:T(8,128)S(1)}, f32[4,8,768]{2,1,0:T(8,128)S(1)}, u32[]{:S(2)}, u32[]{:S(2)}) collective-permute-start(f32[4,8,768]{2,1,0:T(8,128)S(1)} %add.594), channel_id=1, source_target_pairs={{0,8},{4,12},{8,16},{12,20},{16,24},{20,28},{24,0},{28,4},{1,9},{5... | collective-permute-start | bytes 294920 | tf_op jit(solution)/shard_map/z_sums_1/ppermute | solution.py:685
  456.2 2.5 collective-permute-start.64
  459.0 2.5 collective-permute-start.69
  463.2 1.9 collective-permute-start.70
  465.1 3.6 collective-permute-done.63
  478.8 1.5 add_multiply_fusion.2
  (412 shorter events, 103.0 us)
Async XLA Ops:
  7.2 162.3 %all-gather.4.cloned.1.call-start = ((), (), s32[]{:S(2)}) async-start(), calls=%async_computation.2 | async-start | bytes 15409152 | tf_op jit(solution)/shard_map/all_gather | solution.py:868
  10.8 8.6 %collective-permute-start.3 = (f32[2,1408]{1,0:T(2,128)S(1)}, f32[2,1408]{1,0:T(2,128)S(1)}, u32[]{:S(2)}, u32[]{:S(2)}) collective-permute-start(f32[2,1408]{1,0:T(2,128)S(1)} %concatenate.43), channel_id=1, source_target_pairs={{0,2},{1,3},{2,0},{3,1},{4,6},{5,7},{6,4},{7,5},{8,10},{9,11},{10,... | collective-permute-start | bytes 33800 | tf_op jit(solution)/shard_map/x_biases/ppermute | solution.py:669
  13.9 8.7 %collective-permute-start = (bf16[96,768]{1,0:T(8,128)(2,1)S(1)}, bf16[96,768]{1,0:T(8,128)(2,1)S(1)}, u32[]{:S(2)}, u32[]{:S(2)}) collective-permute-start(bf16[96,768]{1,0:T(8,128)(2,1)S(1)} %pad_maximum_fusion.17), channel_id=1, source_target_pairs={{0,8},{4,12},{8,16},{12,20},{16,24},{20,28},{24,0},{28,4},{1,9},{5... | collective-permute-start | bytes 442376 | tf_op jit(solution)/shard_map/z_att_0_1/ppermute | solution.py:685
  15.5 12.9 %collective-permute-start.1 = (bf16[96,768]{1,0:T(8,128)(2,1)S(1)}, bf16[96,768]{1,0:T(8,128)(2,1)S(1)}, u32[]{:S(2)}, u32[]{:S(2)}) collective-permute-start(bf16[96,768]{1,0:T(8,128)(2,1)S(1)} %pad_maximum_fusion.17), channel_id=1, source_target_pairs={{0,16},{4,20},{8,24},{12,28},{16,0},{20,4},{24,8},{28,12},{1,17},{... | collective-permute-start | bytes 442376 | tf_op jit(solution)/shard_map/z_att_0_2/ppermute | solution.py:685
  18.1 10.3 %collective-permute-start.2 = (bf16[96,768]{1,0:T(8,128)(2,1)S(1)}, bf16[96,768]{1,0:T(8,128)(2,1)S(1)}, u32[]{:S(2)}, u32[]{:S(2)}) collective-permute-start(bf16[96,768]{1,0:T(8,128)(2,1)S(1)} %pad_maximum_fusion.17), channel_id=1, source_target_pairs={{0,24},{4,28},{8,0},{12,4},{16,8},{20,12},{24,16},{28,20},{1,25},{... | collective-permute-start | bytes 442376 | tf_op jit(solution)/shard_map/z_att_0_3/ppermute | solution.py:685
  28.5 14.9 %collective-permute-start.6 = (bf16[4,96,768]{2,1,0:T(8,128)(2,1)S(1)}, bf16[4,96,768]{2,1,0:T(8,128)(2,1)S(1)}, u32[]{:S(2)}, u32[]{:S(2)}) collective-permute-start(bf16[4,96,768]{2,1,0:T(8,128)(2,1)S(1)} %pad_maximum_fusion.3), channel_id=1, source_target_pairs={{0,2},{1,3},{2,0},{3,1},{4,6},{5,7},{6,4},{7,5},{8,10},{9,11},{10,... | collective-permute-start | bytes 1769480 | tf_op jit(solution)/shard_map/x_att_0_first/ppermute | solution.py:669
  28.6 36.6 %collective-permute-start.15 = (bf16[96,768]{1,0:T(8,128)(2,1)S(1)}, bf16[96,768]{1,0:T(8,128)(2,1)S(1)}, u32[]{:S(2)}, u32[]{:S(2)}) collective-permute-start(bf16[96,768]{1,0:T(8,128)(2,1)S(1)} %get-tuple-element.150), channel_id=1, source_target_pairs={{0,8},{4,12},{8,16},{12,20},{16,24},{20,28},{24,0},{28,4},{1,9},{5... | collective-permute-start | bytes 442376 | tf_op jit(solution)/shard_map/z_down_0_1/ppermute | solution.py:685
  41.0 24.3 %collective-permute-start.16 = (bf16[96,768]{1,0:T(8,128)(2,1)S(1)}, bf16[96,768]{1,0:T(8,128)(2,1)S(1)}, u32[]{:S(2)}, u32[]{:S(2)}) collective-permute-start(bf16[96,768]{1,0:T(8,128)(2,1)S(1)} %get-tuple-element.150), channel_id=1, source_target_pairs={{0,16},{4,20},{8,24},{12,28},{16,0},{20,4},{24,8},{28,12},{1,17},{... | collective-permute-start | bytes 442376 | tf_op jit(solution)/shard_map/z_down_0_2/ppermute | solution.py:685
  42.2 25.9 %collective-permute-start.17 = (bf16[96,768]{1,0:T(8,128)(2,1)S(1)}, bf16[96,768]{1,0:T(8,128)(2,1)S(1)}, u32[]{:S(2)}, u32[]{:S(2)}) collective-permute-start(bf16[96,768]{1,0:T(8,128)(2,1)S(1)} %get-tuple-element.150), channel_id=1, source_target_pairs={{0,24},{4,28},{8,0},{12,4},{16,8},{20,12},{24,16},{28,20},{1,25},{... | collective-permute-start | bytes 442376 | tf_op jit(solution)/shard_map/z_down_0_3/ppermute | solution.py:685
  43.5 60.9 %collective-permute-start.7 = (bf16[2,4,96,768]{3,2,1,0:T(8,128)(2,1)S(1)}, bf16[2,4,96,768]{3,2,1,0:T(8,128)(2,1)}, u32[]{:S(2)}, u32[]{:S(2)}) collective-permute-start(bf16[2,4,96,768]{3,2,1,0:T(8,128)(2,1)S(1)} %pad_maximum_fusion.refs_4_.refs_6_), channel_id=1, source_target_pairs={{0,4},{4,0},{8,12},{12,8},{16,20},{20,16},{24,28},{28,24},{1,5},{5... | collective-permute-start | bytes 3538952 | tf_op jit(solution)/shard_map/y_att_0_second/ppermute | solution.py:674
  45.2 26.1 %collective-permute-start.10 = (bf16[96,768]{1,0:T(8,128)(2,1)S(1)}, bf16[96,768]{1,0:T(8,128)(2,1)S(1)}, u32[]{:S(2)}, u32[]{:S(2)}) collective-permute-start(bf16[96,768]{1,0:T(8,128)(2,1)S(1)} %get-tuple-element.149), channel_id=1, source_target_pairs={{0,8},{4,12},{8,16},{12,20},{16,24},{20,28},{24,0},{28,4},{1,9},{5... | collective-permute-start | bytes 442376 | tf_op jit(solution)/shard_map/z_up_0_1/ppermute | solution.py:685
  65.2 16.8 %collective-permute-start.11 = (bf16[96,768]{1,0:T(8,128)(2,1)S(1)}, bf16[96,768]{1,0:T(8,128)(2,1)S(1)}, u32[]{:S(2)}, u32[]{:S(2)}) collective-permute-start(bf16[96,768]{1,0:T(8,128)(2,1)S(1)} %get-tuple-element.149), channel_id=1, source_target_pairs={{0,16},{4,20},{8,24},{12,28},{16,0},{20,4},{24,8},{28,12},{1,17},{... | collective-permute-start | bytes 442376 | tf_op jit(solution)/shard_map/z_up_0_2/ppermute | solution.py:685
  65.2 16.8 %collective-permute-start.12 = (bf16[96,768]{1,0:T(8,128)(2,1)S(1)}, bf16[96,768]{1,0:T(8,128)(2,1)S(1)}, u32[]{:S(2)}, u32[]{:S(2)}) collective-permute-start(bf16[96,768]{1,0:T(8,128)(2,1)S(1)} %get-tuple-element.149), channel_id=1, source_target_pairs={{0,24},{4,28},{8,0},{12,4},{16,8},{20,12},{24,16},{28,20},{1,25},{... | collective-permute-start | bytes 442376 | tf_op jit(solution)/shard_map/z_up_0_3/ppermute | solution.py:685
  68.2 16.9 %collective-permute-start.18 = (bf16[4,96,768]{2,1,0:T(8,128)(2,1)S(1)}, bf16[4,96,768]{2,1,0:T(8,128)(2,1)}, u32[]{:S(2)}, u32[]{:S(2)}) collective-permute-start(bf16[4,96,768]{2,1,0:T(8,128)(2,1)S(1)} %get-tuple-element.384), channel_id=1, source_target_pairs={{0,2},{1,3},{2,0},{3,1},{4,6},{5,7},{6,4},{7,5},{8,10},{9,11},{10,... | collective-permute-start | bytes 1769480 | tf_op jit(solution)/shard_map/x_down_0_first/ppermute | solution.py:669
  82.1 20.8 %collective-permute-start.13 = (bf16[4,96,768]{2,1,0:T(8,128)(2,1)S(1)}, bf16[4,96,768]{2,1,0:T(8,128)(2,1)S(1)}, u32[]{:S(2)}, u32[]{:S(2)}) collective-permute-start(bf16[4,96,768]{2,1,0:T(8,128)(2,1)S(1)} %get-tuple-element.386), channel_id=1, source_target_pairs={{0,4},{4,0},{8,12},{12,8},{16,20},{20,16},{24,28},{28,24},{1,5},{5... | collective-permute-start | bytes 1769480 | tf_op jit(solution)/shard_map/y_up_0_first/ppermute | solution.py:674
  85.0 28.1 %collective-permute-start.8 = (bf16[2,4,96,768]{3,2,1,0:T(8,128)(2,1)S(1)}, bf16[2,4,96,768]{3,2,1,0:T(8,128)(2,1)}, u32[]{:S(2)}, u32[]{:S(2)}) collective-permute-start(bf16[2,4,96,768]{3,2,1,0:T(8,128)(2,1)S(1)} %pad_maximum_fusion.refs_4_.refs_6_), channel_id=1, source_target_pairs={{0,1},{1,0},{2,3},{3,2},{4,5},{5,4},{6,7},{7,6},{8,9},{9,8},{10,11... | collective-permute-start | bytes 3538952 | tf_op jit(solution)/shard_map/core_att_0/ppermute | solution.py:679
  86.2 63.0 %collective-permute-start.19 = (bf16[2,4,96,768]{3,2,1,0:T(8,128)(2,1)S(1)}, bf16[2,4,96,768]{3,2,1,0:T(8,128)(2,1)}, u32[]{:S(2)}, u32[]{:S(2)}) collective-permute-start(bf16[2,4,96,768]{3,2,1,0:T(8,128)(2,1)S(1)} %pad_maximum_fusion.2.refs_7_.refs_9_), channel_id=1, source_target_pairs={{0,4},{4,0},{8,12},{12,8},{16,20},{20,16},{24,28},{28,24},{1,5},{5... | collective-permute-start | bytes 3538952 | tf_op jit(solution)/shard_map/y_down_0_second/ppermute | solution.py:674
  103.0 46.3 %collective-permute-start.14 = (bf16[2,4,96,768]{3,2,1,0:T(8,128)(2,1)S(1)}, bf16[2,4,96,768]{3,2,1,0:T(8,128)(2,1)}, u32[]{:S(2)}, u32[]{:S(2)}) collective-permute-start(bf16[2,4,96,768]{3,2,1,0:T(8,128)(2,1)S(1)} %pad_maximum_fusion.1.refs_3_.refs_5_), channel_id=1, source_target_pairs={{0,2},{1,3},{2,0},{3,1},{4,6},{5,7},{6,4},{7,5},{8,10},{9,11},{10,... | collective-permute-start | bytes 3538952 | tf_op jit(solution)/shard_map/x_up_0_second/ppermute | solution.py:669
  104.4 8.7 %collective-permute-start.9 = (bf16[2,4,96,768]{3,2,1,0:T(8,128)(2,1)}, bf16[2,4,96,768]{3,2,1,0:T(8,128)(2,1)}, u32[]{:S(2)}, u32[]{:S(2)}) collective-permute-start(bf16[2,4,96,768]{3,2,1,0:T(8,128)(2,1)} %collective-permute-done.7.refs_5_.refs_7_), channel_id=1, source_target_pairs={{0,1},{1,0},{2,3},{3,2},{4,5},{5,4},{6,7},{7,6},{8,9},{9,8},{10,11... | collective-permute-start | bytes 3538952 | tf_op jit(solution)/shard_map/core_att_0/ppermute | solution.py:679
  149.8 6.8 %collective-permute-start.22 = (bf16[2,4,96,768]{3,2,1,0:T(8,128)(2,1)S(1)}, bf16[2,4,96,768]{3,2,1,0:T(8,128)(2,1)S(1)}, u32[]{:S(2)}, u32[]{:S(2)}) collective-permute-start(bf16[2,4,96,768]{3,2,1,0:T(8,128)(2,1)S(1)} %pad_maximum_fusion.2.refs_7_.refs_9_), channel_id=1, source_target_pairs={{0,1},{1,0},{2,3},{3,2},{4,5},{5,4},{6,7},{7,6},{8,9},{9,8},{10,11... | collective-permute-start | bytes 3538952 | tf_op jit(solution)/shard_map/core_down_0/ppermute | solution.py:679
  149.9 8.4 %collective-permute-start.23 = (bf16[2,4,96,768]{3,2,1,0:T(8,128)(2,1)}, bf16[2,4,96,768]{3,2,1,0:T(8,128)(2,1)S(1)}, u32[]{:S(2)}, u32[]{:S(2)}) collective-permute-start(bf16[2,4,96,768]{3,2,1,0:T(8,128)(2,1)} %collective-permute-done.19.refs_8_.refs_10_), channel_id=1, source_target_pairs={{0,1},{1,0},{2,3},{3,2},{4,5},{5,4},{6,7},{7,6},{8,9},{9,8},{10,11... | collective-permute-start | bytes 3538952 | tf_op jit(solution)/shard_map/core_down_0/ppermute | solution.py:679
  191.2 24.5 %all-to-all-start = ((bf16[8,256,128]{2,1,0:T(8,128)(2,1)}), bf16[8,256,128]{2,1,0:T(8,128)(2,1)S(1)}, u32[]{:S(2)}, u32[]{:S(2)}) async-start(bf16[8,256,128]{2,1,0:T(8,128)(2,1)} %get-tuple-element.158), calls=%async_computation | async-start | bytes 1048576 | tf_op jit(solution)/shard_map/all_to_all | solution.py:1078
  231.9 18.7 %all-to-all-start.1 = ((bf16[8,256,128]{2,1,0:T(8,128)(2,1)}), bf16[8,256,128]{2,1,0:T(8,128)(2,1)S(1)}, u32[]{:S(2)}, u32[]{:S(2)}) async-start(bf16[8,256,128]{2,1,0:T(8,128)(2,1)} %get-tuple-element.163), calls=%async_computation.1 | async-start | bytes 1048576 | tf_op jit(solution)/shard_map/all_to_all | solution.py:1102
  235.5 28.7 %collective-permute-start.33 = (bf16[2,256,768]{2,1,0:T(8,128)(2,1)}, bf16[2,256,768]{2,1,0:T(8,128)(2,1)S(1)}, u32[]{:S(2)}, u32[]{:S(2)}) collective-permute-start(bf16[2,256,768]{2,1,0:T(8,128)(2,1)} %get-tuple-element.176), channel_id=1, source_target_pairs={{0,1},{1,0},{2,3},{3,2},{4,5},{5,4},{6,7},{7,6},{8,9},{9,8},{10,11... | collective-permute-start | bytes 2359304 | tf_op jit(solution)/shard_map/core_pair/ppermute | solution.py:679
  235.7 14.9 %collective-permute-start.27 = (f32[256,128]{1,0:T(8,128)}, f32[256,128]{1,0:T(8,128)S(1)}, u32[]{:S(2)}, u32[]{:S(2)}) collective-permute-start(f32[256,128]{1,0:T(8,128)} %get-tuple-element.162), channel_id=1, source_target_pairs={{0,3},{4,7},{8,11},{12,15},{16,19},{20,23},{24,27},{28,31}} | collective-permute-start | bytes 393224 | tf_op jit(solution)/shard_map/ppermute | solution.py:1104
  239.1 11.5 %collective-permute-start.28 = (f32[256,128]{1,0:T(8,128)}, f32[256,128]{1,0:T(8,128)S(1)}, u32[]{:S(2)}, u32[]{:S(2)}) collective-permute-start(f32[256,128]{1,0:T(8,128)} %get-tuple-element.162), channel_id=1, source_target_pairs={{1,3},{5,7},{9,11},{13,15},{17,19},{21,23},{25,27},{29,31}} | collective-permute-start | bytes 393224 | tf_op jit(solution)/shard_map/ppermute | solution.py:1104
  239.8 10.9 %collective-permute-start.29 = (f32[256,128]{1,0:T(8,128)}, f32[256,128]{1,0:T(8,128)S(1)}, u32[]{:S(2)}, u32[]{:S(2)}) collective-permute-start(f32[256,128]{1,0:T(8,128)} %get-tuple-element.162), channel_id=1, source_target_pairs={{2,3},{6,7},{10,11},{14,15},{18,19},{22,23},{26,27},{30,31}} | collective-permute-start | bytes 393224 | tf_op jit(solution)/shard_map/ppermute | solution.py:1104
  273.0 37.7 %collective-permute-start.39 = (bf16[2,4,96,768]{3,2,1,0:T(8,128)(2,1)}, bf16[2,4,96,768]{3,2,1,0:T(8,128)(2,1)}, u32[]{:S(2)}, u32[]{:S(2)}) collective-permute-start(bf16[2,4,96,768]{3,2,1,0:T(8,128)(2,1)} %get-tuple-element.200), channel_id=1, source_target_pairs={{0,2},{1,3},{2,0},{3,1},{4,6},{5,7},{6,4},{7,5},{8,10},{9,11},{10,... | collective-permute-start | bytes 3538952 | tf_op jit(solution)/shard_map/x_up_1_first/ppermute | solution.py:669
  274.6 38.9 %collective-permute-start.40 = (bf16[2,4,96,896]{3,2,1,0:T(8,128)(2,1)}, bf16[2,4,96,896]{3,2,1,0:T(8,128)(2,1)S(1)}, u32[]{:S(2)}, u32[]{:S(2)}) collective-permute-start(bf16[2,4,96,896]{3,2,1,0:T(8,128)(2,1)} %get-tuple-element.202), channel_id=1, source_target_pairs={{0,4},{4,0},{8,12},{12,8},{16,20},{20,16},{24,28},{28,24},{1,5},{5... | collective-permute-start | bytes 4128776 | tf_op jit(solution)/shard_map/y_down_1_first/ppermute | solution.py:674
  292.5 24.1 %collective-permute-start.44 = (bf16[2,256,768]{2,1,0:T(8,128)(2,1)}, bf16[2,256,768]{2,1,0:T(8,128)(2,1)S(1)}, u32[]{:S(2)}, u32[]{:S(2)}) collective-permute-start(bf16[2,256,768]{2,1,0:T(8,128)(2,1)} %get-tuple-element.208), channel_id=1, source_target_pairs={{0,1},{1,0},{2,3},{3,2},{4,5},{5,4},{6,7},{7,6},{8,9},{9,8},{10,11... | collective-permute-start | bytes 2359304 | tf_op jit(solution)/shard_map/core_pair/ppermute | solution.py:679
  300.5 43.3 %collective-permute-start.45 = (bf16[2,4,96,768]{3,2,1,0:T(8,128)(2,1)}, bf16[2,4,96,768]{3,2,1,0:T(8,128)(2,1)}, u32[]{:S(2)}, u32[]{:S(2)}) collective-permute-start(bf16[2,4,96,768]{3,2,1,0:T(8,128)(2,1)} %get-tuple-element.218), channel_id=1, source_target_pairs={{0,2},{1,3},{2,0},{3,1},{4,6},{5,7},{6,4},{7,5},{8,10},{9,11},{10,... | collective-permute-start | bytes 3538952 | tf_op jit(solution)/shard_map/x_att_1_first/ppermute | solution.py:669
  301.0 14.0 %collective-permute-start.41 = (bf16[768,256]{1,0:T(8,128)(2,1)}, bf16[768,256]{1,0:T(8,128)(2,1)S(1)}, u32[]{:S(2)}, u32[]{:S(2)}) collective-permute-start(bf16[768,256]{1,0:T(8,128)(2,1)} %get-tuple-element.203.refs_0_), channel_id=1, source_target_pairs={{0,1},{1,0},{2,3},{3,2},{4,5},{5,4},{6,7},{7,6},{8,9},{9,8},{10,11... | collective-permute-start | bytes 1179656 | tf_op jit(solution)/shard_map/core_pair/ppermute | solution.py:679
  310.7 11.6 %collective-permute-start.42 = (bf16[2,256,768]{2,1,0:T(8,128)(2,1)}, bf16[2,256,768]{2,1,0:T(8,128)(2,1)}, u32[]{:S(2)}, u32[]{:S(2)}) collective-permute-start(bf16[2,256,768]{2,1,0:T(8,128)(2,1)} %get-tuple-element.205), channel_id=1, source_target_pairs={{0,1},{1,0},{2,3},{3,2},{4,5},{5,4},{6,7},{7,6},{8,9},{9,8},{10,11... | collective-permute-start | bytes 2359304 | tf_op jit(solution)/shard_map/core_pair/ppermute | solution.py:679
  314.5 29.3 %collective-permute-start.78 = (bf16[4,96,768]{2,1,0:T(8,128)(2,1)}, bf16[4,96,768]{2,1,0:T(8,128)(2,1)}, u32[]{:S(2)}, u32[]{:S(2)}) collective-permute-start(bf16[4,96,768]{2,1,0:T(8,128)(2,1)} %fusion.4), channel_id=1, source_target_pairs={{0,4},{4,0},{8,12},{12,8},{16,20},{20,16},{24,28},{28,24},{1,5},{5... | collective-permute-start | bytes 1769480 | tf_op jit(solution)/shard_map/y_up_1_second/ppermute | solution.py:674
  315.1 30.3 %collective-permute-start.79 = (bf16[4,96,896]{2,1,0:T(8,128)(2,1)}, bf16[4,96,896]{2,1,0:T(8,128)(2,1)}, u32[]{:S(2)}, u32[]{:S(2)}) collective-permute-start(bf16[4,96,896]{2,1,0:T(8,128)(2,1)} %fusion), channel_id=1, source_target_pairs={{0,2},{1,3},{2,0},{3,1},{4,6},{5,7},{6,4},{7,5},{8,10},{9,11},{10,... | collective-permute-start | bytes 2064392 | tf_op jit(solution)/shard_map/x_down_1_second/ppermute | solution.py:669
  328.7 53.0 %collective-permute-start.47 = (bf16[2,4,96,768]{3,2,1,0:T(8,128)(2,1)}, bf16[2,4,96,768]{3,2,1,0:T(8,128)(2,1)}, u32[]{:S(2)}, u32[]{:S(2)}) collective-permute-start(bf16[2,4,96,768]{3,2,1,0:T(8,128)(2,1)} %get-tuple-element.227), channel_id=1, source_target_pairs={{0,4},{4,0},{8,12},{12,8},{16,20},{20,16},{24,28},{28,24},{1,5},{5... | collective-permute-start | bytes 3538952 | tf_op jit(solution)/shard_map/y_down_0_first/ppermute | solution.py:674
  330.2 53.5 %collective-permute-start.46 = (bf16[2,4,96,768]{3,2,1,0:T(8,128)(2,1)}, bf16[2,4,96,768]{3,2,1,0:T(8,128)(2,1)}, u32[]{:S(2)}, u32[]{:S(2)}) collective-permute-start(bf16[2,4,96,768]{3,2,1,0:T(8,128)(2,1)} %get-tuple-element.225), channel_id=1, source_target_pairs={{0,2},{1,3},{2,0},{3,1},{4,6},{5,7},{6,4},{7,5},{8,10},{9,11},{10,... | collective-permute-start | bytes 3538952 | tf_op jit(solution)/shard_map/x_up_0_first/ppermute | solution.py:669
  346.7 12.4 %collective-permute-start.80 = (bf16[96,1664]{1,0:T(8,128)(2,1)S(1)}, bf16[96,1664]{1,0:T(8,128)(2,1)S(1)}, u32[]{:S(2)}, u32[]{:S(2)}) collective-permute-start(bf16[96,1664]{1,0:T(8,128)(2,1)S(1)} %pad_maximum_fusion.10), channel_id=1, source_target_pairs={{0,8},{4,12},{8,16},{12,20},{16,24},{20,28},{24,0},{28,4},{1,9},{5... | collective-permute-start | bytes 958472 | tf_op jit(solution)/shard_map/z_up_1_down_1_1/ppermute | solution.py:685
  346.8 24.8 %collective-permute-start.81 = (bf16[96,1664]{1,0:T(8,128)(2,1)S(1)}, bf16[96,1664]{1,0:T(8,128)(2,1)S(1)}, u32[]{:S(2)}, u32[]{:S(2)}) collective-permute-start(bf16[96,1664]{1,0:T(8,128)(2,1)S(1)} %pad_maximum_fusion.11), channel_id=1, source_target_pairs={{0,16},{4,20},{8,24},{12,28},{16,0},{20,4},{24,8},{28,12},{1,17},{... | collective-permute-start | bytes 958472 | tf_op jit(solution)/shard_map/z_up_1_down_1_2/ppermute | solution.py:685
  348.9 22.7 %collective-permute-start.82 = (bf16[96,1664]{1,0:T(8,128)(2,1)S(1)}, bf16[96,1664]{1,0:T(8,128)(2,1)S(1)}, u32[]{:S(2)}, u32[]{:S(2)}) collective-permute-start(bf16[96,1664]{1,0:T(8,128)(2,1)S(1)} %pad_maximum_fusion.12), channel_id=1, source_target_pairs={{0,24},{4,28},{8,0},{12,4},{16,8},{20,12},{24,16},{28,20},{1,25},{... | collective-permute-start | bytes 958472 | tf_op jit(solution)/shard_map/z_up_1_down_1_3/ppermute | solution.py:685
  359.1 15.3 %collective-permute-start.71 = (bf16[4,96,768]{2,1,0:T(8,128)(2,1)S(1)}, bf16[4,96,768]{2,1,0:T(8,128)(2,1)S(1)}, u32[]{:S(2)}, u32[]{:S(2)}) collective-permute-start(bf16[4,96,768]{2,1,0:T(8,128)(2,1)S(1)} %fusion.5), channel_id=1, source_target_pairs={{0,4},{4,0},{8,12},{12,8},{16,20},{20,16},{24,28},{28,24},{1,5},{5... | collective-permute-start | bytes 1769480 | tf_op jit(solution)/shard_map/y_att_1_second/ppermute | solution.py:674
  371.6 16.7 %collective-permute-start.51 = (bf16[2,256,256]{2,1,0:T(8,128)(2,1)S(1)}, bf16[2,256,256]{2,1,0:T(8,128)(2,1)S(1)}, u32[]{:S(2)}, u32[]{:S(2)}) collective-permute-start(bf16[2,256,256]{2,1,0:T(8,128)(2,1)S(1)} %copy-done.77), channel_id=1, source_target_pairs={{0,1},{1,0},{2,3},{3,2},{4,5},{5,4},{6,7},{7,6},{8,9},{9,8},{10,11... | collective-permute-start | bytes 786440 | tf_op jit(solution)/shard_map/core_pair/ppermute | solution.py:679
  371.6 23.7 %collective-permute-start.49 = (bf16[2,256,768]{2,1,0:T(8,128)(2,1)S(1)}, bf16[2,256,768]{2,1,0:T(8,128)(2,1)}, u32[]{:S(2)}, u32[]{:S(2)}) collective-permute-start(bf16[2,256,768]{2,1,0:T(8,128)(2,1)S(1)} %copy-done.74), channel_id=1, source_target_pairs={{0,1},{1,0},{2,3},{3,2},{4,5},{5,4},{6,7},{7,6},{8,9},{9,8},{10,11... | collective-permute-start | bytes 2359304 | tf_op jit(solution)/shard_map/core_pair/ppermute | solution.py:679
  375.7 13.7 %collective-permute-start.72 = (bf16[96,768]{1,0:T(8,128)(2,1)S(1)}, bf16[96,768]{1,0:T(8,128)(2,1)S(1)}, u32[]{:S(2)}, u32[]{:S(2)}) collective-permute-start(bf16[96,768]{1,0:T(8,128)(2,1)S(1)} %get-tuple-element.370), channel_id=1, source_target_pairs={{0,8},{4,12},{8,16},{12,20},{16,24},{20,28},{24,0},{28,4},{1,9},{5... | collective-permute-start | bytes 442376 | tf_op jit(solution)/shard_map/z_att_1_1/ppermute | solution.py:685
  381.7 10.0 %collective-permute-start.73 = (bf16[96,768]{1,0:T(8,128)(2,1)S(1)}, bf16[96,768]{1,0:T(8,128)(2,1)S(1)}, u32[]{:S(2)}, u32[]{:S(2)}) collective-permute-start(bf16[96,768]{1,0:T(8,128)(2,1)S(1)} %get-tuple-element.372), channel_id=1, source_target_pairs={{0,16},{4,20},{8,24},{12,28},{16,0},{20,4},{24,8},{28,12},{1,17},{... | collective-permute-start | bytes 442376 | tf_op jit(solution)/shard_map/z_att_1_2/ppermute | solution.py:685
  383.8 9.0 %collective-permute-start.74 = (bf16[96,768]{1,0:T(8,128)(2,1)S(1)}, bf16[96,768]{1,0:T(8,128)(2,1)S(1)}, u32[]{:S(2)}, u32[]{:S(2)}) collective-permute-start(bf16[96,768]{1,0:T(8,128)(2,1)S(1)} %get-tuple-element.371), channel_id=1, source_target_pairs={{0,24},{4,28},{8,0},{12,4},{16,8},{20,12},{24,16},{28,20},{1,25},{... | collective-permute-start | bytes 442376 | tf_op jit(solution)/shard_map/z_att_1_3/ppermute | solution.py:685
  388.3 15.4 %collective-permute-start.52 = (bf16[4,96,768]{2,1,0:T(8,128)(2,1)}, bf16[4,96,768]{2,1,0:T(8,128)(2,1)S(1)}, u32[]{:S(2)}, u32[]{:S(2)}) collective-permute-start(bf16[4,96,768]{2,1,0:T(8,128)(2,1)} %fusion.6), channel_id=1, source_target_pairs={{0,4},{4,0},{8,12},{12,8},{16,20},{20,16},{24,28},{28,24},{1,5},{5... | collective-permute-start | bytes 1769480 | tf_op jit(solution)/shard_map/y_up_0_second/ppermute | solution.py:674
  389.4 15.2 %collective-permute-start.53 = (bf16[4,96,768]{2,1,0:T(8,128)(2,1)}, bf16[4,96,768]{2,1,0:T(8,128)(2,1)}, u32[]{:S(2)}, u32[]{:S(2)}) collective-permute-start(bf16[4,96,768]{2,1,0:T(8,128)(2,1)} %fusion.7), channel_id=1, source_target_pairs={{0,2},{1,3},{2,0},{3,1},{4,6},{5,7},{6,4},{7,5},{8,10},{9,11},{10,... | collective-permute-start | bytes 1769480 | tf_op jit(solution)/shard_map/x_down_0_second/ppermute | solution.py:669
  406.3 11.9 %collective-permute-start.75 = (bf16[96,1536]{1,0:T(8,128)(2,1)S(1)}, bf16[96,1536]{1,0:T(8,128)(2,1)S(1)}, u32[]{:S(2)}, u32[]{:S(2)}) collective-permute-start(bf16[96,1536]{1,0:T(8,128)(2,1)S(1)} %pad_maximum_fusion.13), channel_id=1, source_target_pairs={{0,8},{4,12},{8,16},{12,20},{16,24},{20,28},{24,0},{28,4},{1,9},{5... | collective-permute-start | bytes 884744 | tf_op jit(solution)/shard_map/z_up_0_down_0_1/ppermute | solution.py:685
  406.4 22.5 %collective-permute-start.76 = (bf16[96,1536]{1,0:T(8,128)(2,1)S(1)}, bf16[96,1536]{1,0:T(8,128)(2,1)S(1)}, u32[]{:S(2)}, u32[]{:S(2)}) collective-permute-start(bf16[96,1536]{1,0:T(8,128)(2,1)S(1)} %pad_maximum_fusion.14), channel_id=1, source_target_pairs={{0,16},{4,20},{8,24},{12,28},{16,0},{20,4},{24,8},{28,12},{1,17},{... | collective-permute-start | bytes 884744 | tf_op jit(solution)/shard_map/z_up_0_down_0_2/ppermute | solution.py:685
  409.6 19.3 %collective-permute-start.77 = (bf16[96,1536]{1,0:T(8,128)(2,1)S(1)}, bf16[96,1536]{1,0:T(8,128)(2,1)S(1)}, u32[]{:S(2)}, u32[]{:S(2)}) collective-permute-start(bf16[96,1536]{1,0:T(8,128)(2,1)S(1)} %pad_maximum_fusion.15), channel_id=1, source_target_pairs={{0,24},{4,28},{8,0},{12,4},{16,8},{20,12},{24,16},{28,20},{1,25},{... | collective-permute-start | bytes 884744 | tf_op jit(solution)/shard_map/z_up_0_down_0_3/ppermute | solution.py:685
  410.6 23.6 %collective-permute-start.55 = (bf16[2,4,96,384]{3,2,1,0:T(8,128)(2,1)S(1)}, bf16[2,4,96,384]{3,2,1,0:T(8,128)(2,1)S(1)}, u32[]{:S(2)}, u32[]{:S(2)}) collective-permute-start(bf16[2,4,96,384]{3,2,1,0:T(8,128)(2,1)S(1)} %copy-done.76), channel_id=1, source_target_pairs={{0,4},{4,0},{8,12},{12,8},{16,20},{20,16},{24,28},{28,24},{1,5},{5... | collective-permute-start | bytes 1769480 | tf_op jit(solution)/shard_map/y_vo_0_first/ppermute | solution.py:674
  411.6 22.7 %collective-permute-start.54 = (bf16[2,4,96,384]{3,2,1,0:T(8,128)(2,1)S(1)}, bf16[2,4,96,384]{3,2,1,0:T(8,128)(2,1)S(1)}, u32[]{:S(2)}, u32[]{:S(2)}) collective-permute-start(bf16[2,4,96,384]{3,2,1,0:T(8,128)(2,1)S(1)} %copy-done.75), channel_id=1, source_target_pairs={{0,2},{1,3},{2,0},{3,1},{4,6},{5,7},{6,4},{7,5},{8,10},{9,11},{10,... | collective-permute-start | bytes 1769480 | tf_op jit(solution)/shard_map/x_qk_0_first/ppermute | solution.py:669
  437.0 12.1 %collective-permute-start.60 = (bf16[4,96,384]{2,1,0:T(8,128)(2,1)S(1)}, bf16[4,96,384]{2,1,0:T(8,128)(2,1)S(1)}, u32[]{:S(2)}, u32[]{:S(2)}) collective-permute-start(bf16[4,96,384]{2,1,0:T(8,128)(2,1)S(1)} %fusion.13), channel_id=1, source_target_pairs={{0,4},{4,0},{8,12},{12,8},{16,20},{20,16},{24,28},{28,24},{1,5},{5... | collective-permute-start | bytes 884744 | tf_op jit(solution)/shard_map/y_qk_0_second/ppermute | solution.py:674
  438.1 11.1 %collective-permute-start.61 = (bf16[4,96,384]{2,1,0:T(8,128)(2,1)S(1)}, bf16[4,96,384]{2,1,0:T(8,128)(2,1)S(1)}, u32[]{:S(2)}, u32[]{:S(2)}) collective-permute-start(bf16[4,96,384]{2,1,0:T(8,128)(2,1)S(1)} %fusion.14), channel_id=1, source_target_pairs={{0,2},{1,3},{2,0},{3,1},{4,6},{5,7},{6,4},{7,5},{8,10},{9,11},{10,... | collective-permute-start | bytes 884744 | tf_op jit(solution)/shard_map/x_vo_0_second/ppermute | solution.py:669
  439.5 16.7 %collective-permute-start.65 = (bf16[192,768]{1,0:T(8,128)(2,1)S(1)}, bf16[192,768]{1,0:T(8,128)(2,1)S(1)}, u32[]{:S(2)}, u32[]{:S(2)}) collective-permute-start(bf16[192,768]{1,0:T(8,128)(2,1)S(1)} %dynamic-slice_convert_fusion), channel_id=1, source_target_pairs={{0,1},{1,2},{2,3},{3,0},{4,5},{5,6},{6,7},{7,4},{8,9},{9,10},{10,1... | collective-permute-start | bytes 884744 | tf_op jit(solution)/shard_map/ppermute | solution.py:899
  443.2 15.7 %collective-permute-start.66 = (bf16[64,768]{1,0:T(8,128)(2,1)S(1)}, bf16[64,768]{1,0:T(8,128)(2,1)S(1)}, u32[]{:S(2)}, u32[]{:S(2)}) collective-permute-start(bf16[64,768]{1,0:T(8,128)(2,1)S(1)} %get-tuple-element.389), channel_id=1, source_target_pairs={{3,1},{7,5},{11,9},{15,13},{19,17},{23,21},{27,25},{31,29}} | collective-permute-start | bytes 294920 | tf_op jit(solution)/shard_map/ppermute | solution.py:906
  448.5 10.5 %collective-permute-start.67 = (bf16[64,768]{1,0:T(8,128)(2,1)S(1)}, bf16[64,768]{1,0:T(8,128)(2,1)S(1)}, u32[]{:S(2)}, u32[]{:S(2)}) collective-permute-start(bf16[64,768]{1,0:T(8,128)(2,1)S(1)} %get-tuple-element.390), channel_id=1, source_target_pairs={{3,2},{7,6},{11,10},{15,14},{19,18},{23,22},{27,26},{31,30}} | collective-permute-start | bytes 294920 | tf_op jit(solution)/shard_map/ppermute | solution.py:907
  449.2 14.0 %collective-permute-start.62 = (f32[4,8,768]{2,1,0:T(8,128)S(1)}, f32[4,8,768]{2,1,0:T(8,128)S(1)}, u32[]{:S(2)}, u32[]{:S(2)}) collective-permute-start(f32[4,8,768]{2,1,0:T(8,128)S(1)} %add.594), channel_id=1, source_target_pairs={{0,8},{4,12},{8,16},{12,20},{16,24},{20,28},{24,0},{28,4},{1,9},{5... | collective-permute-start | bytes 294920 | tf_op jit(solution)/shard_map/z_sums_1/ppermute | solution.py:685
  456.0 12.7 %collective-permute-start.63 = (f32[4,8,768]{2,1,0:T(8,128)S(1)}, f32[4,8,768]{2,1,0:T(8,128)S(1)}, u32[]{:S(2)}, u32[]{:S(2)}) collective-permute-start(f32[4,8,768]{2,1,0:T(8,128)S(1)} %add.594), channel_id=1, source_target_pairs={{0,16},{4,20},{8,24},{12,28},{16,0},{20,4},{24,8},{28,12},{1,17},{... | collective-permute-start | bytes 294920 | tf_op jit(solution)/shard_map/z_sums_2/ppermute | solution.py:685
  456.2 12.4 %collective-permute-start.64 = (f32[4,8,768]{2,1,0:T(8,128)S(1)}, f32[4,8,768]{2,1,0:T(8,128)S(1)}, u32[]{:S(2)}, u32[]{:S(2)}) collective-permute-start(f32[4,8,768]{2,1,0:T(8,128)S(1)} %add.594), channel_id=1, source_target_pairs={{0,24},{4,28},{8,0},{12,4},{16,8},{20,12},{24,16},{28,20},{1,25},{... | collective-permute-start | bytes 294920 | tf_op jit(solution)/shard_map/z_sums_3/ppermute | solution.py:685
  458.9 15.1 %collective-permute-start.68 = (bf16[96,768]{1,0:T(8,128)(2,1)S(1)}, bf16[96,768]{1,0:T(8,128)(2,1)S(1)}, u32[]{:S(2)}, u32[]{:S(2)}) collective-permute-start(bf16[96,768]{1,0:T(8,128)(2,1)S(1)} %pad_maximum_fusion.18), channel_id=1, source_target_pairs={{0,8},{4,12},{8,16},{12,20},{16,24},{20,28},{24,0},{28,4},{1,9},{5... | collective-permute-start | bytes 442376 | tf_op jit(solution)/shard_map/z_qk_0_vo_0_1/ppermute | solution.py:685
  459.0 16.0 %collective-permute-start.69 = (bf16[96,768]{1,0:T(8,128)(2,1)S(1)}, bf16[96,768]{1,0:T(8,128)(2,1)S(1)}, u32[]{:S(2)}, u32[]{:S(2)}) collective-permute-start(bf16[96,768]{1,0:T(8,128)(2,1)S(1)} %pad_maximum_fusion.19), channel_id=1, source_target_pairs={{0,16},{4,20},{8,24},{12,28},{16,0},{20,4},{24,8},{28,12},{1,17},{... | collective-permute-start | bytes 442376 | tf_op jit(solution)/shard_map/z_qk_0_vo_0_2/ppermute | solution.py:685
  463.2 11.8 %collective-permute-start.70 = (bf16[96,768]{1,0:T(8,128)(2,1)S(1)}, bf16[96,768]{1,0:T(8,128)(2,1)S(1)}, u32[]{:S(2)}, u32[]{:S(2)}) collective-permute-start(bf16[96,768]{1,0:T(8,128)(2,1)S(1)} %pad_maximum_fusion.20), channel_id=1, source_target_pairs={{0,24},{4,28},{8,0},{12,4},{16,8},{20,12},{24,16},{28,20},{1,25},{... | collective-permute-start | bytes 442376 | tf_op jit(solution)/shard_map/z_qk_0_vo_0_3/ppermute | solution.py:685
  (102 other events, 715.7 us)
Sparse Core Ops, SparseCore 0:
  11.6 155.9 all-gather.3

commit v5 on v4

--- a/solution.py
+++ b/solution.py
@@ -1184,15 +1184,11 @@
         dx, att_groups = attention_pull(0, grad_first)
         dx, att_one.one = tied(dx, att_one.one)
         att_one.add_second()
-        att_groups[0][0], att_one.terms = tied(att_groups[0][0], att_one.terms)
         att_one.start_second()
         mlp_one = Column(up_one, down_one)
         mlp_one.add_third()
         up_zero.add_second()
         down_zero.add_second()
-        att_groups[0][0], up_zero.terms, down_zero.terms = tied(
-            att_groups[0][0], up_zero.terms, down_zero.terms
-        )
         half = SLAB // 2
         left, right = attention_grad(0, ((0, half, False), (half, half, True)), att_groups)
         halves = (Reduction("qk_0", left, False), Reduction("vo_0", right, True))

time: 495 us -> 493 us (level)
    ppermute x12, waiting for transfers between devices: 2.08 us -> 16.6 us  [over_x(): return lax.ppermute(value, 'tensor', X_SWAP)]
    ppermute x24, waiting for transfers between devices: 61.9 us -> 51.8 us  [along_z(): return lax.ppermute(value, 'dp', pairs)]
    unnamed x174 -> x166, local copies, waits for them, and re-layouts: 19.8 us -> 18.9 us
  transfers between devices with their start and end apart: 86 -> 86, of which waited for: 34 -> 33; matrix products, arithmetic and copies ran while one was open for 11% -> 11% of each run, Pallas kernels for 17% -> 17%
where the time goes in v5:
time: 493 us; the launch traced here: 487 us
  waiting for transfers between devices  147 us (30%)
  starting transfers between devices  125 us (25%)
  Pallas kernels  119 us (24%)
  other arithmetic  45.6 us (9%)
  local copies, waits for them, and re-layouts  27.2 us (6%)
  between operations  18.1 us (4%)
  blocking collectives  5.31 us (1%)
    pallas_call x12, Pallas kernels, call(): pl.pallas_call(kernel, out_shape=outs, in_specs=[smem_spec()] + [any_spec...  111 us
    ppermute x24, starting transfers between devices, along_z(): return lax.ppermute(value, 'dp', pairs)  69.8 us
    ppermute x24, waiting for transfers between devices, along_z(): return lax.ppermute(value, 'dp', pairs)  51.8 us
    ppermute x11, waiting for transfers between devices, over_y(): return lax.ppermute(value, 'dp', Y_SWAP)  44.5 us
    unnamed x166, local copies, waits for them, and re-layouts  18.9 us
    ppermute x12, waiting for transfers between devices, over_x(): return lax.ppermute(value, 'tensor', X_SWAP)  16.6 us
    ppermute x11, starting transfers between devices, over_y(): return lax.ppermute(value, 'dp', Y_SWAP)  14.3 us
    ppermute x26, waiting for transfers between devices, over_core(): return lax.ppermute(value, 'tensor', CORE_SWAP)  14.3 us
  transfers between devices with their start and end apart: 86, of which 33 were waited for; matrix products, arithmetic and copies ran while one was open for 11% of the time, Pallas kernels for 17%

profile of v5, /device:TPU:0, one launch (start us, length us, event | category | flops | bytes accessed | tf_op | source)
XLA Modules:
  0.0 487.2 jit_solution(9967490410038839470)
XLA Ops:
  10.8 2.9 collective-permute-start.3
  13.9 1.6 collective-permute-start
  15.5 2.6 collective-permute-start.1
  22.6 5.8 %collective-permute-done.1 = bf16[96,768]{1,0:T(8,128)(2,1)S(1)} collective-permute-done((bf16[96,768]{1,0:T(8,128)(2,1)S(1)}, bf16[96,768]{1,0:T(8,128)(2,1)S(1)}, u32[]{:S(2)}, u32[]{:S(2)}) %collective-permute-start.1) | collective-permute-done | bytes 147488 | tf_op jit(solution)/shard_map/z_att_0_2/ppermute | solution.py:685
  28.6 12.4 %collective-permute-start.15 = (bf16[96,768]{1,0:T(8,128)(2,1)S(1)}, bf16[96,768]{1,0:T(8,128)(2,1)S(1)}, u32[]{:S(2)}, u32[]{:S(2)}) collective-permute-start(bf16[96,768]{1,0:T(8,128)(2,1)S(1)} %get-tuple-element.145), channel_id=1, source_target_pairs={{0,8},{4,12},{8,16},{12,20},{16,24},{20,28},{24,0},{28,4},{1,9},{5... | collective-permute-start | bytes 442376 | tf_op jit(solution)/shard_map/z_down_0_1/ppermute | solution.py:685
  43.5 1.7 collective-permute-start.7
  45.2 20.0 %collective-permute-start.10 = (bf16[96,768]{1,0:T(8,128)(2,1)S(1)}, bf16[96,768]{1,0:T(8,128)(2,1)S(1)}, u32[]{:S(2)}, u32[]{:S(2)}) collective-permute-start(bf16[96,768]{1,0:T(8,128)(2,1)S(1)} %get-tuple-element.144), channel_id=1, source_target_pairs={{0,8},{4,12},{8,16},{12,20},{16,24},{20,28},{24,0},{28,4},{1,9},{5... | collective-permute-start | bytes 442376 | tf_op jit(solution)/shard_map/z_up_0_1/ppermute | solution.py:685
  65.2 2.8 collective-permute-start.12
  68.8 2.5 collective-permute-done.10
  71.3 10.7 %collective-permute-done.11 = bf16[96,768]{1,0:T(8,128)(2,1)S(1)} collective-permute-done((bf16[96,768]{1,0:T(8,128)(2,1)S(1)}, bf16[96,768]{1,0:T(8,128)(2,1)S(1)}, u32[]{:S(2)}, u32[]{:S(2)}) %collective-permute-start.11) | collective-permute-done | bytes 147488 | tf_op jit(solution)/shard_map/z_up_0_2/ppermute | solution.py:685
  82.1 1.7 collective-permute-start.13
  88.2 14.7 %collective-permute-done.13 = bf16[4,96,768]{2,1,0:T(8,128)(2,1)S(1)} collective-permute-done((bf16[4,96,768]{2,1,0:T(8,128)(2,1)S(1)}, bf16[4,96,768]{2,1,0:T(8,128)(2,1)S(1)}, u32[]{:S(2)}, u32[]{:S(2)}) %collective-permute-start.13) | collective-permute-done | bytes 589856 | tf_op jit(solution)/shard_map/y_up_0_first/ppermute | solution.py:674
  110.4 2.1 dynamic-slice_select_fusion.refs_0_
  113.1 11.0 %attention_0.1 = (f32[256,768]{1,0:T(8,128)}, bf16[768,256]{1,0:T(8,128)(2,1)}, bf16[4,256,640]{2,1,0:T(8,128)(2,1)}, bf16[12,256,256]{2,1,0:T(8,128)(2,1)}, f32...) custom-call(s32[4]{0:T(128)} %pad_add_fusion.place, ...), custom_call_target="tpu_custom_call" | custom-call | flops 9000000 | bytes 27000 | tf_op jit(solution)/shard_map/attention_0/pallas_call | solution.py:476
  124.1 25.2 %collective-permute-done.19.refs_8_.refs_10_ = bf16[2,4,96,768]{3,2,1,0:T(8,128)(2,1)} collective-permute-done((bf16[2,4,96,768]{3,2,1,0:T(8,128)(2,1)S(1)}, bf16[2,4,96,768]{3,2,1,0:T(8,128)(2,1)}, u32[]{:S(2)}, u32[]{:S(2)}) %collective-permute-start.19) | collective-permute-done | bytes 1179680 | tf_op jit(solution)/shard_map/y_down_0_second/ppermute | solution.py:674
  153.1 2.3 collective-permute-done.21.refs_6_.refs_8_
  156.6 1.7 collective-permute-done.23.refs_10_.refs_12_
  159.3 10.1 %mlp_0.1 = (f32[256,768]{1,0:T(8,128)}, bf16[4,256,768]{2,1,0:T(8,128)(2,1)}, f32[256,768]{1,0:T(8,128)}, f32[256,128]{1,0:T(8,128)}, bf16[2,256,768]{2,1,0:T(8,128)(2,1)}, /*index=5*/bf16[2,256,768]{2,1,0:T(8,128)(2,1)}) custom-call(s32[4]{0:T(128)} %pad_add_fusion.place, f32[256,768]{1,0:T(8,128)} %get-tuple-element.146.refs_0_, ...), custom_call_target="tpu_custom_call" | custom-call | flops 9000000 | bytes 27000 | tf_op jit(solution)/shard_map/mlp_0/pallas_call | solution.py:476
  169.5 11.0 %attention_1.1 = (f32[256,768]{1,0:T(8,128)}, bf16[768,256]{1,0:T(8,128)(2,1)}, bf16[4,256,640]{2,1,0:T(8,128)(2,1)}, bf16[12,256,256]{2,1,0:T(8,128)(2,1)}, f32...) custom-call(s32[4]{0:T(128)} %pad_add_fusion.place, ...), custom_call_target="tpu_custom_call" | custom-call | flops 9000000 | bytes 27000 | tf_op jit(solution)/shard_map/attention_1/pallas_call | solution.py:476
  180.5 10.7 %mlp_1.1 = (f32[256,768]{1,0:T(8,128)}, bf16[4,256,768]{2,1,0:T(8,128)(2,1)}, f32[256,768]{1,0:T(8,128)}, f32[256,128]{1,0:T(8,128)}, bf16[2,256,768]{2,1,0:T(8,...) custom-call(s32[4]{0:T(128)} %pad_add_fusion.place, ...), custom_call_target="tpu_custom_call" | custom-call | flops 9000000 | bytes 27000 | tf_op jit(solution)/shard_map/mlp_1/pallas_call | solution.py:476
  191.2 9.4 %all-to-all-start = ((bf16[8,256,128]{2,1,0:T(8,128)(2,1)}), bf16[8,256,128]{2,1,0:T(8,128)(2,1)S(1)}, u32[]{:S(2)}, u32[]{:S(2)}) async-start(bf16[8,256,128]{2,1,0:T(8,128)(2,1)} %get-tuple-element.153), calls=%async_computation | async-start | bytes 1048576 | tf_op jit(solution)/shard_map/all_to_all | solution.py:1078
  205.7 4.8 collective-permute-done.26
  212.0 3.6 all-to-all-done.passages_ref
  216.4 4.0 scores.1
  220.4 5.3 %all-gather.1 = f32[32,8]{1,0:T(8,128)S(1)} all-gather(f32[8,8]{1,0:T(8,128)} %bitcast.383), channel_id=3, replica_groups=mesh['dp'=8,'tensor'=4] {'tensor'}, dimensions={0}, use_global_device_ids=true | all-gather | bytes 1280 | tf_op jit(solution)/shard_map/all_gather | solution.py:1087
  227.8 3.9 score_pulls.1
  231.8 3.6 all-to-all-start.1
  235.6 3.3 collective-permute-start.27
  240.5 9.9 %all-to-all-done.1 = bf16[8,256,128]{2,1,0:T(8,128)(2,1)S(1)} async-done(((bf16[8,256,128]{2,1,0:T(8,128)(2,1)}), bf16[8,256,128]{2,1,0:T(8,128)(2,1)S(1)}, u32[]{:S(2)}, u32[]{:S(2)}) %all-to-all-start.1) | async-done | bytes 524320 | tf_op jit(solution)/shard_map/all_to_all | solution.py:1102
  251.2 9.7 %pull_mlp_1.1 = (f32[256,768]{1,0:T(8,128)}, f32[8,768]{1,0:T(8,128)}, bf16[768,256]{1,0:T(8,128)(2,1)}, bf16[2,256,768]{2,1,0:T(8,128)(2,1)}, bf16[2,256,768]{2,1,0:T(8,128)(2,1)}, /*index=5*/f32[768,128]{1,0:T(8,128)}) custom-call(s32[4]{0:T(128)} %pad_add_fusion.place, f32[256,128]{1,0:T(8,128)} %add_select_fusion.refs_0_, ...), custom_call_target="tpu_custom_call" | custom-call | flops 8000000 | bytes 24000 | tf_op jit(solution)/shard_map/pull_mlp_1/pallas_call | solution.py:476
  262.0 2.1 collective-permute-done.30.refs_1_
  266.2 6.7 %grad_mlp_1.1 = (bf16[2,4,96,768]{3,2,1,0:T(8,128)(2,1)}, bf16[2,4,96,768]{3,2,1,0:T(8,128)(2,1)}, bf16[2,4,96,896]{3,2,1,0:T(8,128)(2,1)}, bf16[2,4,96,896]{3,2,1,0:T(8,128)(2,1)}) custom-call(s32[4]{0:T(128)} %pad_add_fusion.place, bf16[768,256]{1,0:T(8,128)(2,1)} %get-tuple-element.166.refs_0_, bf16[768,256]{1,0:T(8,128)(2,1)} %copy-done.38, ...), custom_call_target="tpu_custom_call" | custom-call | flops 8000000 | bytes 24000 | tf_op jit(solution)/shard_map/grad_mlp_1/pallas_call | solution.py:476
  272.9 1.6 collective-permute-start.39
  276.0 13.1 %pull_attention_1.1 = (f32[256,768]{1,0:T(8,128)}, f32[8,768]{1,0:T(8,128)}, bf16[768,256]{1,0:T(8,128)(2,1)}, bf16[2,256,768]{2,1,0:T(8,128)(2,1)}, bf16[2,256,768]{2,1,0:T(8,128)(2,1)}) custom-call(s32[4]{0:T(128)} %pad_add_fusion.place, f32[256,768]{1,0:T(8,128)} %get-tuple-element.175.refs_0_, bf16[4,256,640]{2,1,0:T(8,128)(2,1)} %get-tuple-element.176.refs_1_, ...), custom_call_target="tpu_custom_call" | custom-call | flops 10000000 | bytes 30000 | tf_op jit(solution)/shard_map/pull_attention_1/pallas_call | solution.py:476
  289.8 2.1 collective-permute-done.38.refs_7_
  295.4 4.9 %grad_attention_1.1 = (bf16[2,4,96,768]{3,2,1,0:T(8,128)(2,1)}, bf16[2,4,96,768]{3,2,1,0:T(8,128)(2,1)}) custom-call(s32[4]{0:T(128)} %pad_add_fusion.place, bf16[768,256]{1,0:T(8,128)(2,1)} %get-tuple-element.181.refs_0_, bf16[768,256]{1,0:T(8,128)(2,1)} %copy-done.45, bf16[2,256,768]{2,1,0:T(8,128)(2,1)} %get-tuple-element.182.refs_2_, ...), custom_call_target="tpu_custom_call" | custom-call | flops 5000000 | bytes 15000 | tf_op jit(solution)/shard_map/grad_attention_1/pallas_call | solution.py:476
  300.3 9.7 %pull_mlp_0.1 = (f32[256,768]{1,0:T(8,128)}, f32[8,768]{1,0:T(8,128)}, bf16[768,256]{1,0:T(8,128)(2,1)}, bf16[2,256,768]{2,1,0:T(8,128)(2,1)}, bf16[2,256,768]{2,1,0:T(8,128)(2,1)}) custom-call(s32[4]{0:T(128)} %pad_add_fusion.place, f32[256,768]{1,0:T(8,128)} %get-tuple-element.188.refs_0_, bf16[4,256,768]{2,1,0:T(8,128)(2,1)} %get-tuple-element.189.refs_1_, ...), custom_call_target="tpu_custom_call" | custom-call | flops 8000000 | bytes 24000 | tf_op jit(solution)/shard_map/pull_mlp_0/pallas_call | solution.py:476
  310.2 2.3 fusion.4
  314.5 1.7 copy.90
  316.3 1.7 copy.91
  322.2 6.4 %grad_mlp_0.1 = (bf16[2,4,96,768]{3,2,1,0:T(8,128)(2,1)}, bf16[2,4,96,768]{3,2,1,0:T(8,128)(2,1)}, bf16[2,4,96,768]{3,2,1,0:T(8,128)(2,1)}, bf16[2,4,96,768]{3,2,1,0:T(8,128)(2,1)}) custom-call(s32[4]{0:T(128)} %pad_add_fusion.place, bf16[768,256]{1,0:T(8,128)(2,1)} %get-tuple-element.198.refs_0_, bf16[768,256]{1,0:T(8,128)(2,1)} %collective-permute-done.41.refs_1_, ...), custom_call_target="tpu_custom_call" | custom-call | flops 8000000 | bytes 24000 | tf_op jit(solution)/shard_map/grad_mlp_0/pallas_call | solution.py:476
  328.6 12.8 %pull_attention_0.1 = (f32[256,768]{1,0:T(8,128)}, f32[8,768]{1,0:T(8,128)}, bf16[768,256]{1,0:T(8,128)(2,1)}, bf16[2,256,768]{2,1,0:T(8,128)(2,1)}, bf16[2,256,768]{2,1,0:T(8,128)(2,1)}) custom-call(s32[4]{0:T(128)} %pad_add_fusion.place, f32[256,768]{1,0:T(8,128)} %get-tuple-element.206.refs_0_, bf16[4,256,640]{2,1,0:T(8,128)(2,1)} %get-tuple-element.207.refs_1_, ...), custom_call_target="tpu_custom_call" | custom-call | flops 10000000 | bytes 30000 | tf_op jit(solution)/shard_map/pull_attention_0/pallas_call | solution.py:476
  348.6 2.0 collective-permute-start.81
  350.6 6.4 %collective-permute-done.45 = bf16[2,4,96,768]{3,2,1,0:T(8,128)(2,1)} collective-permute-done((bf16[2,4,96,768]{3,2,1,0:T(8,128)(2,1)}, bf16[2,4,96,768]{3,2,1,0:T(8,128)(2,1)}, u32[]{:S(2)}, u32[]{:S(2)}) %collective-permute-start.45) | collective-permute-done | bytes 1179680 | tf_op jit(solution)/shard_map/x_att_1_first/ppermute | solution.py:669
  358.7 2.0 fusion.7
  360.8 5.1 %grad_attention_0.1 = (bf16[2,4,96,384]{3,2,1,0:T(8,128)(2,1)}, bf16[2,4,96,384]{3,2,1,0:T(8,128)(2,1)}, bf16[2,4,96,384]{3,2,1,0:T(8,128)(2,1)}, bf16[2,4,96,384]{3,2,1,0:T(8,128)(2,1)}) custom-call(s32[4]{0:T(128)} %pad_add_fusion.place, bf16[768,256]{1,0:T(8,128)(2,1)} %get-tuple-element.215.refs_0_, bf16[768,256]{1,0:T(8,128)(2,1)} %copy-done.42, ...), custom_call_target="tpu_custom_call" | custom-call | flops 5000000 | bytes 15000 | tf_op jit(solution)/shard_map/grad_attention_0/pallas_call | solution.py:476
  365.8 1.8 collective-permute-start.71
  367.6 6.3 %collective-permute-done.81 = bf16[96,1664]{1,0:T(8,128)(2,1)} collective-permute-done((bf16[96,1664]{1,0:T(8,128)(2,1)}, bf16[96,1664]{1,0:T(8,128)(2,1)}, u32[]{:S(2)}, u32[]{:S(2)}) %collective-permute-start.81) | collective-permute-done | bytes 319520 | tf_op jit(solution)/shard_map/z_up_1_down_1_2/ppermute | solution.py:685
  378.8 8.7 %collective-permute-done.50 = bf16[2,4,96,768]{3,2,1,0:T(8,128)(2,1)} collective-permute-done((bf16[2,4,96,768]{3,2,1,0:T(8,128)(2,1)}, bf16[2,4,96,768]{3,2,1,0:T(8,128)(2,1)}, u32[]{:S(2)}, u32[]{:S(2)}) %collective-permute-start.50) | collective-permute-done | bytes 1179680 | tf_op jit(solution)/shard_map/x_up_0_first/ppermute | solution.py:669
  388.7 1.8 collective-permute-start.51
  391.9 3.7 collective-permute-start.74
  396.3 2.7 collective-permute-done.72
  399.0 3.7 collective-permute-done.73
  403.7 1.6 fusion.26
  405.4 2.5 collective-permute-start.75
  408.5 1.8 collective-permute-start.77
  412.7 4.6 collective-permute-done.75
  417.3 9.7 %collective-permute-done.76 = bf16[96,1536]{1,0:T(8,128)(2,1)S(1)} collective-permute-done((bf16[96,1536]{1,0:T(8,128)(2,1)S(1)}, bf16[96,1536]{1,0:T(8,128)(2,1)S(1)}, u32[]{:S(2)}, u32[]{:S(2)}) %collective-permute-start.76) | collective-permute-done | bytes 294944 | tf_op jit(solution)/shard_map/z_up_0_down_0_2/ppermute | solution.py:685
  441.8 4.6 collective-permute-done.59
  447.1 6.8 %collective-permute-start.62 = (f32[4,8,768]{2,1,0:T(8,128)S(1)}, f32[4,8,768]{2,1,0:T(8,128)S(1)}, u32[]{:S(2)}, u32[]{:S(2)}) collective-permute-start(f32[4,8,768]{2,1,0:T(8,128)S(1)} %add.593), channel_id=1, source_target_pairs={{0,8},{4,12},{8,16},{12,20},{16,24},{20,28},{24,0},{28,4},{1,9},{5... | collective-permute-start | bytes 294920 | tf_op jit(solution)/shard_map/z_sums_1/ppermute | solution.py:685
  453.9 1.9 collective-permute-start.63
  456.0 1.9 collective-permute-start.64
  461.1 2.7 collective-permute-start.70
  463.7 3.2 collective-permute-done.63
  (404 shorter events, 107.6 us)
Async XLA Ops:
  7.2 162.2 %all-gather.4.cloned.1.call-start = ((), (), s32[]{:S(2)}) async-start(), calls=%async_computation.2 | async-start | bytes 15409152 | tf_op jit(solution)/shard_map/all_gather | solution.py:868
  10.8 8.6 %collective-permute-start.3 = (f32[2,1408]{1,0:T(2,128)S(1)}, f32[2,1408]{1,0:T(2,128)S(1)}, u32[]{:S(2)}, u32[]{:S(2)}) collective-permute-start(f32[2,1408]{1,0:T(2,128)S(1)} %concatenate.43), channel_id=1, source_target_pairs={{0,2},{1,3},{2,0},{3,1},{4,6},{5,7},{6,4},{7,5},{8,10},{9,11},{10,... | collective-permute-start | bytes 33800 | tf_op jit(solution)/shard_map/x_biases/ppermute | solution.py:669
  13.9 8.7 %collective-permute-start = (bf16[96,768]{1,0:T(8,128)(2,1)S(1)}, bf16[96,768]{1,0:T(8,128)(2,1)S(1)}, u32[]{:S(2)}, u32[]{:S(2)}) collective-permute-start(bf16[96,768]{1,0:T(8,128)(2,1)S(1)} %pad_maximum_fusion.17), channel_id=1, source_target_pairs={{0,8},{4,12},{8,16},{12,20},{16,24},{20,28},{24,0},{28,4},{1,9},{5... | collective-permute-start | bytes 442376 | tf_op jit(solution)/shard_map/z_att_0_1/ppermute | solution.py:685
  15.5 12.9 %collective-permute-start.1 = (bf16[96,768]{1,0:T(8,128)(2,1)S(1)}, bf16[96,768]{1,0:T(8,128)(2,1)S(1)}, u32[]{:S(2)}, u32[]{:S(2)}) collective-permute-start(bf16[96,768]{1,0:T(8,128)(2,1)S(1)} %pad_maximum_fusion.17), channel_id=1, source_target_pairs={{0,16},{4,20},{8,24},{12,28},{16,0},{20,4},{24,8},{28,12},{1,17},{... | collective-permute-start | bytes 442376 | tf_op jit(solution)/shard_map/z_att_0_2/ppermute | solution.py:685
  18.1 10.3 %collective-permute-start.2 = (bf16[96,768]{1,0:T(8,128)(2,1)S(1)}, bf16[96,768]{1,0:T(8,128)(2,1)S(1)}, u32[]{:S(2)}, u32[]{:S(2)}) collective-permute-start(bf16[96,768]{1,0:T(8,128)(2,1)S(1)} %pad_maximum_fusion.17), channel_id=1, source_target_pairs={{0,24},{4,28},{8,0},{12,4},{16,8},{20,12},{24,16},{28,20},{1,25},{... | collective-permute-start | bytes 442376 | tf_op jit(solution)/shard_map/z_att_0_3/ppermute | solution.py:685
  28.5 14.9 %collective-permute-start.6 = (bf16[4,96,768]{2,1,0:T(8,128)(2,1)S(1)}, bf16[4,96,768]{2,1,0:T(8,128)(2,1)S(1)}, u32[]{:S(2)}, u32[]{:S(2)}) collective-permute-start(bf16[4,96,768]{2,1,0:T(8,128)(2,1)S(1)} %pad_maximum_fusion.3), channel_id=1, source_target_pairs={{0,2},{1,3},{2,0},{3,1},{4,6},{5,7},{6,4},{7,5},{8,10},{9,11},{10,... | collective-permute-start | bytes 1769480 | tf_op jit(solution)/shard_map/x_att_0_first/ppermute | solution.py:669
  28.6 36.6 %collective-permute-start.15 = (bf16[96,768]{1,0:T(8,128)(2,1)S(1)}, bf16[96,768]{1,0:T(8,128)(2,1)S(1)}, u32[]{:S(2)}, u32[]{:S(2)}) collective-permute-start(bf16[96,768]{1,0:T(8,128)(2,1)S(1)} %get-tuple-element.145), channel_id=1, source_target_pairs={{0,8},{4,12},{8,16},{12,20},{16,24},{20,28},{24,0},{28,4},{1,9},{5... | collective-permute-start | bytes 442376 | tf_op jit(solution)/shard_map/z_down_0_1/ppermute | solution.py:685
  41.0 24.3 %collective-permute-start.16 = (bf16[96,768]{1,0:T(8,128)(2,1)S(1)}, bf16[96,768]{1,0:T(8,128)(2,1)S(1)}, u32[]{:S(2)}, u32[]{:S(2)}) collective-permute-start(bf16[96,768]{1,0:T(8,128)(2,1)S(1)} %get-tuple-element.145), channel_id=1, source_target_pairs={{0,16},{4,20},{8,24},{12,28},{16,0},{20,4},{24,8},{28,12},{1,17},{... | collective-permute-start | bytes 442376 | tf_op jit(solution)/shard_map/z_down_0_2/ppermute | solution.py:685
  42.2 25.9 %collective-permute-start.17 = (bf16[96,768]{1,0:T(8,128)(2,1)S(1)}, bf16[96,768]{1,0:T(8,128)(2,1)S(1)}, u32[]{:S(2)}, u32[]{:S(2)}) collective-permute-start(bf16[96,768]{1,0:T(8,128)(2,1)S(1)} %get-tuple-element.145), channel_id=1, source_target_pairs={{0,24},{4,28},{8,0},{12,4},{16,8},{20,12},{24,16},{28,20},{1,25},{... | collective-permute-start | bytes 442376 | tf_op jit(solution)/shard_map/z_down_0_3/ppermute | solution.py:685
  43.5 60.9 %collective-permute-start.7 = (bf16[2,4,96,768]{3,2,1,0:T(8,128)(2,1)S(1)}, bf16[2,4,96,768]{3,2,1,0:T(8,128)(2,1)}, u32[]{:S(2)}, u32[]{:S(2)}) collective-permute-start(bf16[2,4,96,768]{3,2,1,0:T(8,128)(2,1)S(1)} %pad_maximum_fusion.refs_4_.refs_6_), channel_id=1, source_target_pairs={{0,4},{4,0},{8,12},{12,8},{16,20},{20,16},{24,28},{28,24},{1,5},{5... | collective-permute-start | bytes 3538952 | tf_op jit(solution)/shard_map/y_att_0_second/ppermute | solution.py:674
  45.2 26.1 %collective-permute-start.10 = (bf16[96,768]{1,0:T(8,128)(2,1)S(1)}, bf16[96,768]{1,0:T(8,128)(2,1)S(1)}, u32[]{:S(2)}, u32[]{:S(2)}) collective-permute-start(bf16[96,768]{1,0:T(8,128)(2,1)S(1)} %get-tuple-element.144), channel_id=1, source_target_pairs={{0,8},{4,12},{8,16},{12,20},{16,24},{20,28},{24,0},{28,4},{1,9},{5... | collective-permute-start | bytes 442376 | tf_op jit(solution)/shard_map/z_up_0_1/ppermute | solution.py:685
  65.2 16.8 %collective-permute-start.11 = (bf16[96,768]{1,0:T(8,128)(2,1)S(1)}, bf16[96,768]{1,0:T(8,128)(2,1)S(1)}, u32[]{:S(2)}, u32[]{:S(2)}) collective-permute-start(bf16[96,768]{1,0:T(8,128)(2,1)S(1)} %get-tuple-element.144), channel_id=1, source_target_pairs={{0,16},{4,20},{8,24},{12,28},{16,0},{20,4},{24,8},{28,12},{1,17},{... | collective-permute-start | bytes 442376 | tf_op jit(solution)/shard_map/z_up_0_2/ppermute | solution.py:685
  65.2 16.8 %collective-permute-start.12 = (bf16[96,768]{1,0:T(8,128)(2,1)S(1)}, bf16[96,768]{1,0:T(8,128)(2,1)S(1)}, u32[]{:S(2)}, u32[]{:S(2)}) collective-permute-start(bf16[96,768]{1,0:T(8,128)(2,1)S(1)} %get-tuple-element.144), channel_id=1, source_target_pairs={{0,24},{4,28},{8,0},{12,4},{16,8},{20,12},{24,16},{28,20},{1,25},{... | collective-permute-start | bytes 442376 | tf_op jit(solution)/shard_map/z_up_0_3/ppermute | solution.py:685
  68.1 17.6 %collective-permute-start.18 = (bf16[4,96,768]{2,1,0:T(8,128)(2,1)S(1)}, bf16[4,96,768]{2,1,0:T(8,128)(2,1)S(1)}, u32[]{:S(2)}, u32[]{:S(2)}) collective-permute-start(bf16[4,96,768]{2,1,0:T(8,128)(2,1)S(1)} %get-tuple-element.374), channel_id=1, source_target_pairs={{0,2},{1,3},{2,0},{3,1},{4,6},{5,7},{6,4},{7,5},{8,10},{9,11},{10,... | collective-permute-start | bytes 1769480 | tf_op jit(solution)/shard_map/x_down_0_first/ppermute | solution.py:669
  82.1 20.8 %collective-permute-start.13 = (bf16[4,96,768]{2,1,0:T(8,128)(2,1)S(1)}, bf16[4,96,768]{2,1,0:T(8,128)(2,1)S(1)}, u32[]{:S(2)}, u32[]{:S(2)}) collective-permute-start(bf16[4,96,768]{2,1,0:T(8,128)(2,1)S(1)} %get-tuple-element.376), channel_id=1, source_target_pairs={{0,4},{4,0},{8,12},{12,8},{16,20},{20,16},{24,28},{28,24},{1,5},{5... | collective-permute-start | bytes 1769480 | tf_op jit(solution)/shard_map/y_up_0_first/ppermute | solution.py:674
  85.7 27.4 %collective-permute-start.8 = (bf16[2,4,96,768]{3,2,1,0:T(8,128)(2,1)S(1)}, bf16[2,4,96,768]{3,2,1,0:T(8,128)(2,1)}, u32[]{:S(2)}, u32[]{:S(2)}) collective-permute-start(bf16[2,4,96,768]{3,2,1,0:T(8,128)(2,1)S(1)} %pad_maximum_fusion.refs_4_.refs_6_), channel_id=1, source_target_pairs={{0,1},{1,0},{2,3},{3,2},{4,5},{5,4},{6,7},{7,6},{8,9},{9,8},{10,11... | collective-permute-start | bytes 3538952 | tf_op jit(solution)/shard_map/core_att_0/ppermute | solution.py:679
  87.7 61.5 %collective-permute-start.19 = (bf16[2,4,96,768]{3,2,1,0:T(8,128)(2,1)S(1)}, bf16[2,4,96,768]{3,2,1,0:T(8,128)(2,1)}, u32[]{:S(2)}, u32[]{:S(2)}) collective-permute-start(bf16[2,4,96,768]{3,2,1,0:T(8,128)(2,1)S(1)} %pad_maximum_fusion.2.refs_7_.refs_9_), channel_id=1, source_target_pairs={{0,4},{4,0},{8,12},{12,8},{16,20},{20,16},{24,28},{28,24},{1,5},{5... | collective-permute-start | bytes 3538952 | tf_op jit(solution)/shard_map/y_down_0_second/ppermute | solution.py:674
  103.0 46.3 %collective-permute-start.14 = (bf16[2,4,96,768]{3,2,1,0:T(8,128)(2,1)S(1)}, bf16[2,4,96,768]{3,2,1,0:T(8,128)(2,1)}, u32[]{:S(2)}, u32[]{:S(2)}) collective-permute-start(bf16[2,4,96,768]{3,2,1,0:T(8,128)(2,1)S(1)} %pad_maximum_fusion.1.refs_3_.refs_5_), channel_id=1, source_target_pairs={{0,2},{1,3},{2,0},{3,1},{4,6},{5,7},{6,4},{7,5},{8,10},{9,11},{10,... | collective-permute-start | bytes 3538952 | tf_op jit(solution)/shard_map/x_up_0_second/ppermute | solution.py:669
  104.4 8.7 %collective-permute-start.9 = (bf16[2,4,96,768]{3,2,1,0:T(8,128)(2,1)}, bf16[2,4,96,768]{3,2,1,0:T(8,128)(2,1)}, u32[]{:S(2)}, u32[]{:S(2)}) collective-permute-start(bf16[2,4,96,768]{3,2,1,0:T(8,128)(2,1)} %collective-permute-done.7.refs_5_.refs_7_), channel_id=1, source_target_pairs={{0,1},{1,0},{2,3},{3,2},{4,5},{5,4},{6,7},{7,6},{8,9},{9,8},{10,11... | collective-permute-start | bytes 3538952 | tf_op jit(solution)/shard_map/core_att_0/ppermute | solution.py:679
  149.9 8.4 %collective-permute-start.23 = (bf16[2,4,96,768]{3,2,1,0:T(8,128)(2,1)}, bf16[2,4,96,768]{3,2,1,0:T(8,128)(2,1)S(1)}, u32[]{:S(2)}, u32[]{:S(2)}) collective-permute-start(bf16[2,4,96,768]{3,2,1,0:T(8,128)(2,1)} %collective-permute-done.19.refs_8_.refs_10_), channel_id=1, source_target_pairs={{0,1},{1,0},{2,3},{3,2},{4,5},{5,4},{6,7},{7,6},{8,9},{9,8},{10,11... | collective-permute-start | bytes 3538952 | tf_op jit(solution)/shard_map/core_down_0/ppermute | solution.py:679
  191.2 24.4 %all-to-all-start = ((bf16[8,256,128]{2,1,0:T(8,128)(2,1)}), bf16[8,256,128]{2,1,0:T(8,128)(2,1)S(1)}, u32[]{:S(2)}, u32[]{:S(2)}) async-start(bf16[8,256,128]{2,1,0:T(8,128)(2,1)} %get-tuple-element.153), calls=%async_computation | async-start | bytes 1048576 | tf_op jit(solution)/shard_map/all_to_all | solution.py:1078
  231.8 18.7 %all-to-all-start.1 = ((bf16[8,256,128]{2,1,0:T(8,128)(2,1)}), bf16[8,256,128]{2,1,0:T(8,128)(2,1)S(1)}, u32[]{:S(2)}, u32[]{:S(2)}) async-start(bf16[8,256,128]{2,1,0:T(8,128)(2,1)} %get-tuple-element.158), calls=%async_computation.1 | async-start | bytes 1048576 | tf_op jit(solution)/shard_map/all_to_all | solution.py:1102
  235.4 28.8 %collective-permute-start.33 = (bf16[2,256,768]{2,1,0:T(8,128)(2,1)}, bf16[2,256,768]{2,1,0:T(8,128)(2,1)S(1)}, u32[]{:S(2)}, u32[]{:S(2)}) collective-permute-start(bf16[2,256,768]{2,1,0:T(8,128)(2,1)} %get-tuple-element.171), channel_id=1, source_target_pairs={{0,1},{1,0},{2,3},{3,2},{4,5},{5,4},{6,7},{7,6},{8,9},{9,8},{10,11... | collective-permute-start | bytes 2359304 | tf_op jit(solution)/shard_map/core_pair/ppermute | solution.py:679
  235.6 14.9 %collective-permute-start.27 = (f32[256,128]{1,0:T(8,128)}, f32[256,128]{1,0:T(8,128)S(1)}, u32[]{:S(2)}, u32[]{:S(2)}) collective-permute-start(f32[256,128]{1,0:T(8,128)} %get-tuple-element.157), channel_id=1, source_target_pairs={{0,3},{4,7},{8,11},{12,15},{16,19},{20,23},{24,27},{28,31}} | collective-permute-start | bytes 393224 | tf_op jit(solution)/shard_map/ppermute | solution.py:1104
  239.0 11.5 %collective-permute-start.28 = (f32[256,128]{1,0:T(8,128)}, f32[256,128]{1,0:T(8,128)S(1)}, u32[]{:S(2)}, u32[]{:S(2)}) collective-permute-start(f32[256,128]{1,0:T(8,128)} %get-tuple-element.157), channel_id=1, source_target_pairs={{1,3},{5,7},{9,11},{13,15},{17,19},{21,23},{25,27},{29,31}} | collective-permute-start | bytes 393224 | tf_op jit(solution)/shard_map/ppermute | solution.py:1104
  239.7 10.9 %collective-permute-start.29 = (f32[256,128]{1,0:T(8,128)}, f32[256,128]{1,0:T(8,128)S(1)}, u32[]{:S(2)}, u32[]{:S(2)}) collective-permute-start(f32[256,128]{1,0:T(8,128)} %get-tuple-element.157), channel_id=1, source_target_pairs={{2,3},{6,7},{10,11},{14,15},{18,19},{22,23},{26,27},{30,31}} | collective-permute-start | bytes 393224 | tf_op jit(solution)/shard_map/ppermute | solution.py:1104
  272.9 37.3 %collective-permute-start.39 = (bf16[2,4,96,768]{3,2,1,0:T(8,128)(2,1)}, bf16[2,4,96,768]{3,2,1,0:T(8,128)(2,1)}, u32[]{:S(2)}, u32[]{:S(2)}) collective-permute-start(bf16[2,4,96,768]{3,2,1,0:T(8,128)(2,1)} %get-tuple-element.195), channel_id=1, source_target_pairs={{0,2},{1,3},{2,0},{3,1},{4,6},{5,7},{6,4},{7,5},{8,10},{9,11},{10,... | collective-permute-start | bytes 3538952 | tf_op jit(solution)/shard_map/x_up_1_first/ppermute | solution.py:669
  274.5 38.0 %collective-permute-start.40 = (bf16[2,4,96,896]{3,2,1,0:T(8,128)(2,1)}, bf16[2,4,96,896]{3,2,1,0:T(8,128)(2,1)S(1)}, u32[]{:S(2)}, u32[]{:S(2)}) collective-permute-start(bf16[2,4,96,896]{3,2,1,0:T(8,128)(2,1)} %get-tuple-element.197), channel_id=1, source_target_pairs={{0,4},{4,0},{8,12},{12,8},{16,20},{20,16},{24,28},{28,24},{1,5},{5... | collective-permute-start | bytes 4128776 | tf_op jit(solution)/shard_map/y_down_1_first/ppermute | solution.py:674
  292.4 22.2 %collective-permute-start.41 = (bf16[768,256]{1,0:T(8,128)(2,1)}, bf16[768,256]{1,0:T(8,128)(2,1)}, u32[]{:S(2)}, u32[]{:S(2)}) collective-permute-start(bf16[768,256]{1,0:T(8,128)(2,1)} %get-tuple-element.198.refs_0_), channel_id=1, source_target_pairs={{0,1},{1,0},{2,3},{3,2},{4,5},{5,4},{6,7},{7,6},{8,9},{9,8},{10,11... | collective-permute-start | bytes 1179656 | tf_op jit(solution)/shard_map/core_pair/ppermute | solution.py:679
  293.7 26.2 %collective-permute-start.44 = (bf16[2,256,768]{2,1,0:T(8,128)(2,1)}, bf16[2,256,768]{2,1,0:T(8,128)(2,1)S(1)}, u32[]{:S(2)}, u32[]{:S(2)}) collective-permute-start(bf16[2,256,768]{2,1,0:T(8,128)(2,1)} %get-tuple-element.203), channel_id=1, source_target_pairs={{0,1},{1,0},{2,3},{3,2},{4,5},{5,4},{6,7},{7,6},{8,9},{9,8},{10,11... | collective-permute-start | bytes 2359304 | tf_op jit(solution)/shard_map/core_pair/ppermute | solution.py:679
  310.0 10.6 %collective-permute-start.42 = (bf16[2,256,768]{2,1,0:T(8,128)(2,1)}, bf16[2,256,768]{2,1,0:T(8,128)(2,1)}, u32[]{:S(2)}, u32[]{:S(2)}) collective-permute-start(bf16[2,256,768]{2,1,0:T(8,128)(2,1)} %get-tuple-element.200), channel_id=1, source_target_pairs={{0,1},{1,0},{2,3},{3,2},{4,5},{5,4},{6,7},{7,6},{8,9},{9,8},{10,11... | collective-permute-start | bytes 2359304 | tf_op jit(solution)/shard_map/core_pair/ppermute | solution.py:679
  313.5 27.9 %collective-permute-start.78 = (bf16[4,96,768]{2,1,0:T(8,128)(2,1)}, bf16[4,96,768]{2,1,0:T(8,128)(2,1)}, u32[]{:S(2)}, u32[]{:S(2)}) collective-permute-start(bf16[4,96,768]{2,1,0:T(8,128)(2,1)} %fusion.4), channel_id=1, source_target_pairs={{0,4},{4,0},{8,12},{12,8},{16,20},{20,16},{24,28},{28,24},{1,5},{5... | collective-permute-start | bytes 1769480 | tf_op jit(solution)/shard_map/y_up_1_second/ppermute | solution.py:674
  314.1 29.1 %collective-permute-start.79 = (bf16[4,96,896]{2,1,0:T(8,128)(2,1)}, bf16[4,96,896]{2,1,0:T(8,128)(2,1)}, u32[]{:S(2)}, u32[]{:S(2)}) collective-permute-start(bf16[4,96,896]{2,1,0:T(8,128)(2,1)} %fusion), channel_id=1, source_target_pairs={{0,2},{1,3},{2,0},{3,1},{4,6},{5,7},{6,4},{7,5},{8,10},{9,11},{10,... | collective-permute-start | bytes 2064392 | tf_op jit(solution)/shard_map/x_down_1_second/ppermute | solution.py:669
  320.0 28.7 %collective-permute-start.46 = (bf16[768,256]{1,0:T(8,128)(2,1)}, bf16[768,256]{1,0:T(8,128)(2,1)S(1)}, u32[]{:S(2)}, u32[]{:S(2)}) collective-permute-start(bf16[768,256]{1,0:T(8,128)(2,1)} %get-tuple-element.215.refs_0_), channel_id=1, source_target_pairs={{0,1},{1,0},{2,3},{3,2},{4,5},{5,4},{6,7},{7,6},{8,9},{9,8},{10,11... | collective-permute-start | bytes 1179656 | tf_op jit(solution)/shard_map/core_pair/ppermute | solution.py:679
  320.5 25.9 %collective-permute-start.49 = (bf16[2,256,256]{2,1,0:T(8,128)(2,1)}, bf16[2,256,256]{2,1,0:T(8,128)(2,1)}, u32[]{:S(2)}, u32[]{:S(2)}) collective-permute-start(bf16[2,256,256]{2,1,0:T(8,128)(2,1)} %get-tuple-element.220), channel_id=1, source_target_pairs={{0,1},{1,0},{2,3},{3,2},{4,5},{5,4},{6,7},{7,6},{8,9},{9,8},{10,11... | collective-permute-start | bytes 786440 | tf_op jit(solution)/shard_map/core_pair/ppermute | solution.py:679
  320.6 36.4 %collective-permute-start.45 = (bf16[2,4,96,768]{3,2,1,0:T(8,128)(2,1)}, bf16[2,4,96,768]{3,2,1,0:T(8,128)(2,1)}, u32[]{:S(2)}, u32[]{:S(2)}) collective-permute-start(bf16[2,4,96,768]{3,2,1,0:T(8,128)(2,1)} %get-tuple-element.213), channel_id=1, source_target_pairs={{0,2},{1,3},{2,0},{3,1},{4,6},{5,7},{6,4},{7,5},{8,10},{9,11},{10,... | collective-permute-start | bytes 3538952 | tf_op jit(solution)/shard_map/x_att_1_first/ppermute | solution.py:669
  341.4 16.8 %collective-permute-start.47 = (bf16[2,256,768]{2,1,0:T(8,128)(2,1)}, bf16[2,256,768]{2,1,0:T(8,128)(2,1)S(1)}, u32[]{:S(2)}, u32[]{:S(2)}) collective-permute-start(bf16[2,256,768]{2,1,0:T(8,128)(2,1)} %get-tuple-element.217), channel_id=1, source_target_pairs={{0,1},{1,0},{2,3},{3,2},{4,5},{5,4},{6,7},{7,6},{8,9},{9,8},{10,11... | collective-permute-start | bytes 2359304 | tf_op jit(solution)/shard_map/core_pair/ppermute | solution.py:679
  346.4 30.3 %collective-permute-start.52 = (bf16[2,4,96,768]{3,2,1,0:T(8,128)(2,1)}, bf16[2,4,96,768]{3,2,1,0:T(8,128)(2,1)}, u32[]{:S(2)}, u32[]{:S(2)}) collective-permute-start(bf16[2,4,96,768]{3,2,1,0:T(8,128)(2,1)} %get-tuple-element.225), channel_id=1, source_target_pairs={{0,4},{4,0},{8,12},{12,8},{16,20},{20,16},{24,28},{28,24},{1,5},{5... | collective-permute-start | bytes 3538952 | tf_op jit(solution)/shard_map/y_down_0_first/ppermute | solution.py:674
  348.6 17.2 %collective-permute-start.80 = (bf16[96,1664]{1,0:T(8,128)(2,1)}, bf16[96,1664]{1,0:T(8,128)(2,1)}, u32[]{:S(2)}, u32[]{:S(2)}) collective-permute-start(bf16[96,1664]{1,0:T(8,128)(2,1)} %pad_maximum_fusion.10), channel_id=1, source_target_pairs={{0,8},{4,12},{8,16},{12,20},{16,24},{20,28},{24,0},{28,4},{1,9},{5... | collective-permute-start | bytes 958472 | tf_op jit(solution)/shard_map/z_up_1_down_1_1/ppermute | solution.py:685
  348.6 25.2 %collective-permute-start.81 = (bf16[96,1664]{1,0:T(8,128)(2,1)}, bf16[96,1664]{1,0:T(8,128)(2,1)}, u32[]{:S(2)}, u32[]{:S(2)}) collective-permute-start(bf16[96,1664]{1,0:T(8,128)(2,1)} %pad_maximum_fusion.11), channel_id=1, source_target_pairs={{0,16},{4,20},{8,24},{12,28},{16,0},{20,4},{24,8},{28,12},{1,17},{... | collective-permute-start | bytes 958472 | tf_op jit(solution)/shard_map/z_up_1_down_1_2/ppermute | solution.py:685
  357.0 16.9 %collective-permute-start.82 = (bf16[96,1664]{1,0:T(8,128)(2,1)}, bf16[96,1664]{1,0:T(8,128)(2,1)}, u32[]{:S(2)}, u32[]{:S(2)}) collective-permute-start(bf16[96,1664]{1,0:T(8,128)(2,1)} %pad_maximum_fusion.12), channel_id=1, source_target_pairs={{0,24},{4,28},{8,0},{12,4},{16,8},{20,12},{24,16},{28,20},{1,25},{... | collective-permute-start | bytes 958472 | tf_op jit(solution)/shard_map/z_up_1_down_1_3/ppermute | solution.py:685
  358.2 29.3 %collective-permute-start.50 = (bf16[2,4,96,768]{3,2,1,0:T(8,128)(2,1)}, bf16[2,4,96,768]{3,2,1,0:T(8,128)(2,1)}, u32[]{:S(2)}, u32[]{:S(2)}) collective-permute-start(bf16[2,4,96,768]{3,2,1,0:T(8,128)(2,1)} %get-tuple-element.223), channel_id=1, source_target_pairs={{0,2},{1,3},{2,0},{3,1},{4,6},{5,7},{6,4},{7,5},{8,10},{9,11},{10,... | collective-permute-start | bytes 3538952 | tf_op jit(solution)/shard_map/x_up_0_first/ppermute | solution.py:669
  365.8 24.6 %collective-permute-start.71 = (bf16[4,96,768]{2,1,0:T(8,128)(2,1)}, bf16[4,96,768]{2,1,0:T(8,128)(2,1)S(1)}, u32[]{:S(2)}, u32[]{:S(2)}) collective-permute-start(bf16[4,96,768]{2,1,0:T(8,128)(2,1)} %fusion.7), channel_id=1, source_target_pairs={{0,4},{4,0},{8,12},{12,8},{16,20},{20,16},{24,28},{28,24},{1,5},{5... | collective-permute-start | bytes 1769480 | tf_op jit(solution)/shard_map/y_att_1_second/ppermute | solution.py:674
  378.1 25.6 %collective-permute-start.53 = (bf16[4,96,768]{2,1,0:T(8,128)(2,1)S(1)}, bf16[4,96,768]{2,1,0:T(8,128)(2,1)S(1)}, u32[]{:S(2)}, u32[]{:S(2)}) collective-permute-start(bf16[4,96,768]{2,1,0:T(8,128)(2,1)S(1)} %fusion.6), channel_id=1, source_target_pairs={{0,2},{1,3},{2,0},{3,1},{4,6},{5,7},{6,4},{7,5},{8,10},{9,11},{10,... | collective-permute-start | bytes 1769480 | tf_op jit(solution)/shard_map/x_down_0_second/ppermute | solution.py:669
  388.7 15.0 %collective-permute-start.51 = (bf16[4,96,768]{2,1,0:T(8,128)(2,1)S(1)}, bf16[4,96,768]{2,1,0:T(8,128)(2,1)S(1)}, u32[]{:S(2)}, u32[]{:S(2)}) collective-permute-start(bf16[4,96,768]{2,1,0:T(8,128)(2,1)S(1)} %fusion.5), channel_id=1, source_target_pairs={{0,4},{4,0},{8,12},{12,8},{16,20},{20,16},{24,28},{28,24},{1,5},{5... | collective-permute-start | bytes 1769480 | tf_op jit(solution)/shard_map/y_up_0_second/ppermute | solution.py:674
  391.7 7.3 %collective-permute-start.72 = (bf16[96,768]{1,0:T(8,128)(2,1)S(1)}, bf16[96,768]{1,0:T(8,128)(2,1)S(1)}, u32[]{:S(2)}, u32[]{:S(2)}) collective-permute-start(bf16[96,768]{1,0:T(8,128)(2,1)S(1)} %get-tuple-element.360), channel_id=1, source_target_pairs={{0,8},{4,12},{8,16},{12,20},{16,24},{20,28},{24,0},{28,4},{1,9},{5... | collective-permute-start | bytes 442376 | tf_op jit(solution)/shard_map/z_att_1_1/ppermute | solution.py:685
  391.8 10.9 %collective-permute-start.73 = (bf16[96,768]{1,0:T(8,128)(2,1)S(1)}, bf16[96,768]{1,0:T(8,128)(2,1)S(1)}, u32[]{:S(2)}, u32[]{:S(2)}) collective-permute-start(bf16[96,768]{1,0:T(8,128)(2,1)S(1)} %get-tuple-element.362), channel_id=1, source_target_pairs={{0,16},{4,20},{8,24},{12,28},{16,0},{20,4},{24,8},{28,12},{1,17},{... | collective-permute-start | bytes 442376 | tf_op jit(solution)/shard_map/z_att_1_2/ppermute | solution.py:685
  391.9 10.8 %collective-permute-start.74 = (bf16[96,768]{1,0:T(8,128)(2,1)S(1)}, bf16[96,768]{1,0:T(8,128)(2,1)S(1)}, u32[]{:S(2)}, u32[]{:S(2)}) collective-permute-start(bf16[96,768]{1,0:T(8,128)(2,1)S(1)} %get-tuple-element.361), channel_id=1, source_target_pairs={{0,24},{4,28},{8,0},{12,4},{16,8},{20,12},{24,16},{28,20},{1,25},{... | collective-permute-start | bytes 442376 | tf_op jit(solution)/shard_map/z_att_1_3/ppermute | solution.py:685
  405.4 11.9 %collective-permute-start.75 = (bf16[96,1536]{1,0:T(8,128)(2,1)S(1)}, bf16[96,1536]{1,0:T(8,128)(2,1)S(1)}, u32[]{:S(2)}, u32[]{:S(2)}) collective-permute-start(bf16[96,1536]{1,0:T(8,128)(2,1)S(1)} %pad_maximum_fusion.13), channel_id=1, source_target_pairs={{0,8},{4,12},{8,16},{12,20},{16,24},{20,28},{24,0},{28,4},{1,9},{5... | collective-permute-start | bytes 884744 | tf_op jit(solution)/shard_map/z_up_0_down_0_1/ppermute | solution.py:685
  407.8 19.1 %collective-permute-start.76 = (bf16[96,1536]{1,0:T(8,128)(2,1)S(1)}, bf16[96,1536]{1,0:T(8,128)(2,1)S(1)}, u32[]{:S(2)}, u32[]{:S(2)}) collective-permute-start(bf16[96,1536]{1,0:T(8,128)(2,1)S(1)} %pad_maximum_fusion.14), channel_id=1, source_target_pairs={{0,16},{4,20},{8,24},{12,28},{16,0},{20,4},{24,8},{28,12},{1,17},{... | collective-permute-start | bytes 884744 | tf_op jit(solution)/shard_map/z_up_0_down_0_2/ppermute | solution.py:685
  408.5 18.4 %collective-permute-start.77 = (bf16[96,1536]{1,0:T(8,128)(2,1)S(1)}, bf16[96,1536]{1,0:T(8,128)(2,1)S(1)}, u32[]{:S(2)}, u32[]{:S(2)}) collective-permute-start(bf16[96,1536]{1,0:T(8,128)(2,1)S(1)} %pad_maximum_fusion.15), channel_id=1, source_target_pairs={{0,24},{4,28},{8,0},{12,4},{16,8},{20,12},{24,16},{28,20},{1,25},{... | collective-permute-start | bytes 884744 | tf_op jit(solution)/shard_map/z_up_0_down_0_3/ppermute | solution.py:685
  410.6 21.5 %collective-permute-start.55 = (bf16[2,4,96,384]{3,2,1,0:T(8,128)(2,1)S(1)}, bf16[2,4,96,384]{3,2,1,0:T(8,128)(2,1)S(1)}, u32[]{:S(2)}, u32[]{:S(2)}) collective-permute-start(bf16[2,4,96,384]{3,2,1,0:T(8,128)(2,1)S(1)} %copy-done.73), channel_id=1, source_target_pairs={{0,4},{4,0},{8,12},{12,8},{16,20},{20,16},{24,28},{28,24},{1,5},{5... | collective-permute-start | bytes 1769480 | tf_op jit(solution)/shard_map/y_vo_0_first/ppermute | solution.py:674
  411.8 20.4 %collective-permute-start.54 = (bf16[2,4,96,384]{3,2,1,0:T(8,128)(2,1)S(1)}, bf16[2,4,96,384]{3,2,1,0:T(8,128)(2,1)S(1)}, u32[]{:S(2)}, u32[]{:S(2)}) collective-permute-start(bf16[2,4,96,384]{3,2,1,0:T(8,128)(2,1)S(1)} %copy-done.72), channel_id=1, source_target_pairs={{0,2},{1,3},{2,0},{3,1},{4,6},{5,7},{6,4},{7,5},{8,10},{9,11},{10,... | collective-permute-start | bytes 1769480 | tf_op jit(solution)/shard_map/x_qk_0_first/ppermute | solution.py:669
  434.9 12.1 %collective-permute-start.60 = (bf16[4,96,384]{2,1,0:T(8,128)(2,1)S(1)}, bf16[4,96,384]{2,1,0:T(8,128)(2,1)S(1)}, u32[]{:S(2)}, u32[]{:S(2)}) collective-permute-start(bf16[4,96,384]{2,1,0:T(8,128)(2,1)S(1)} %fusion.13), channel_id=1, source_target_pairs={{0,4},{4,0},{8,12},{12,8},{16,20},{20,16},{24,28},{28,24},{1,5},{5... | collective-permute-start | bytes 884744 | tf_op jit(solution)/shard_map/y_qk_0_second/ppermute | solution.py:674
  436.1 11.0 %collective-permute-start.61 = (bf16[4,96,384]{2,1,0:T(8,128)(2,1)S(1)}, bf16[4,96,384]{2,1,0:T(8,128)(2,1)S(1)}, u32[]{:S(2)}, u32[]{:S(2)}) collective-permute-start(bf16[4,96,384]{2,1,0:T(8,128)(2,1)S(1)} %fusion.14), channel_id=1, source_target_pairs={{0,2},{1,3},{2,0},{3,1},{4,6},{5,7},{6,4},{7,5},{8,10},{9,11},{10,... | collective-permute-start | bytes 884744 | tf_op jit(solution)/shard_map/x_vo_0_second/ppermute | solution.py:669
  437.0 19.0 %collective-permute-start.65 = (bf16[192,768]{1,0:T(8,128)(2,1)S(1)}, bf16[192,768]{1,0:T(8,128)(2,1)S(1)}, u32[]{:S(2)}, u32[]{:S(2)}) collective-permute-start(bf16[192,768]{1,0:T(8,128)(2,1)S(1)} %dynamic-slice_convert_fusion), channel_id=1, source_target_pairs={{0,1},{1,2},{2,3},{3,0},{4,5},{5,6},{6,7},{7,4},{8,9},{9,10},{10,1... | collective-permute-start | bytes 884744 | tf_op jit(solution)/shard_map/ppermute | solution.py:899
  441.1 16.9 %collective-permute-start.66 = (bf16[64,768]{1,0:T(8,128)(2,1)S(1)}, bf16[64,768]{1,0:T(8,128)(2,1)S(1)}, u32[]{:S(2)}, u32[]{:S(2)}) collective-permute-start(bf16[64,768]{1,0:T(8,128)(2,1)S(1)} %get-tuple-element.379), channel_id=1, source_target_pairs={{3,1},{7,5},{11,9},{15,13},{19,17},{23,21},{27,25},{31,29}} | collective-permute-start | bytes 294920 | tf_op jit(solution)/shard_map/ppermute | solution.py:906
  446.4 11.9 %collective-permute-start.67 = (bf16[64,768]{1,0:T(8,128)(2,1)S(1)}, bf16[64,768]{1,0:T(8,128)(2,1)S(1)}, u32[]{:S(2)}, u32[]{:S(2)}) collective-permute-start(bf16[64,768]{1,0:T(8,128)(2,1)S(1)} %get-tuple-element.380), channel_id=1, source_target_pairs={{3,2},{7,6},{11,10},{15,14},{19,18},{23,22},{27,26},{31,30}} | collective-permute-start | bytes 294920 | tf_op jit(solution)/shard_map/ppermute | solution.py:907
  447.1 14.0 %collective-permute-start.62 = (f32[4,8,768]{2,1,0:T(8,128)S(1)}, f32[4,8,768]{2,1,0:T(8,128)S(1)}, u32[]{:S(2)}, u32[]{:S(2)}) collective-permute-start(f32[4,8,768]{2,1,0:T(8,128)S(1)} %add.593), channel_id=1, source_target_pairs={{0,8},{4,12},{8,16},{12,20},{16,24},{20,28},{24,0},{28,4},{1,9},{5... | collective-permute-start | bytes 294920 | tf_op jit(solution)/shard_map/z_sums_1/ppermute | solution.py:685
  453.9 13.0 %collective-permute-start.63 = (f32[4,8,768]{2,1,0:T(8,128)S(1)}, f32[4,8,768]{2,1,0:T(8,128)S(1)}, u32[]{:S(2)}, u32[]{:S(2)}) collective-permute-start(f32[4,8,768]{2,1,0:T(8,128)S(1)} %add.593), channel_id=1, source_target_pairs={{0,16},{4,20},{8,24},{12,28},{16,0},{20,4},{24,8},{28,12},{1,17},{... | collective-permute-start | bytes 294920 | tf_op jit(solution)/shard_map/z_sums_2/ppermute | solution.py:685
  456.0 10.9 %collective-permute-start.64 = (f32[4,8,768]{2,1,0:T(8,128)S(1)}, f32[4,8,768]{2,1,0:T(8,128)S(1)}, u32[]{:S(2)}, u32[]{:S(2)}) collective-permute-start(f32[4,8,768]{2,1,0:T(8,128)S(1)} %add.593), channel_id=1, source_target_pairs={{0,24},{4,28},{8,0},{12,4},{16,8},{20,12},{24,16},{28,20},{1,25},{... | collective-permute-start | bytes 294920 | tf_op jit(solution)/shard_map/z_sums_3/ppermute | solution.py:685
  458.0 14.1 %collective-permute-start.68 = (bf16[96,768]{1,0:T(8,128)(2,1)S(1)}, bf16[96,768]{1,0:T(8,128)(2,1)S(1)}, u32[]{:S(2)}, u32[]{:S(2)}) collective-permute-start(bf16[96,768]{1,0:T(8,128)(2,1)S(1)} %pad_maximum_fusion.18), channel_id=1, source_target_pairs={{0,8},{4,12},{8,16},{12,20},{16,24},{20,28},{24,0},{28,4},{1,9},{5... | collective-permute-start | bytes 442376 | tf_op jit(solution)/shard_map/z_qk_0_vo_0_1/ppermute | solution.py:685
  458.3 15.4 %collective-permute-start.69 = (bf16[96,768]{1,0:T(8,128)(2,1)S(1)}, bf16[96,768]{1,0:T(8,128)(2,1)S(1)}, u32[]{:S(2)}, u32[]{:S(2)}) collective-permute-start(bf16[96,768]{1,0:T(8,128)(2,1)S(1)} %pad_maximum_fusion.19), channel_id=1, source_target_pairs={{0,16},{4,20},{8,24},{12,28},{16,0},{20,4},{24,8},{28,12},{1,17},{... | collective-permute-start | bytes 442376 | tf_op jit(solution)/shard_map/z_qk_0_vo_0_2/ppermute | solution.py:685
  461.1 12.6 %collective-permute-start.70 = (bf16[96,768]{1,0:T(8,128)(2,1)S(1)}, bf16[96,768]{1,0:T(8,128)(2,1)S(1)}, u32[]{:S(2)}, u32[]{:S(2)}) collective-permute-start(bf16[96,768]{1,0:T(8,128)(2,1)S(1)} %pad_maximum_fusion.20), channel_id=1, source_target_pairs={{0,24},{4,28},{8,0},{12,4},{16,8},{20,12},{24,16},{28,20},{1,25},{... | collective-permute-start | bytes 442376 | tf_op jit(solution)/shard_map/z_qk_0_vo_0_3/ppermute | solution.py:685
  (98 other events, 675.4 us)
Sparse Core Ops, SparseCore 0:
  11.6 155.9 all-gather.3
